TPU v7x, 32 devices: a whole 2x2x4 slice. The times are simulated.
32 devices in a mesh: dp: 4 (over z), ctx: 8 (over y, x, core).
Axes of the slice: x: 2, y: 2, z: 4, core: 2. Of those that a mesh axis runs over, the one named last changes fastest.
Arguments:
- hidden: bfloat16 [8192, 1536], P(('dp', 'ctx')), may hold values from -6 to 6
- gain_attn: bfloat16 [1536], P(('dp', 'ctx')), may hold values from 0.5 to 1.5
- w_query: bfloat16 [1536, 1536], P(('dp', 'ctx')), may hold values from -0.625 to 0.625
- w_key: bfloat16 [1536, 512], P(('dp', 'ctx')), may hold values from -0.625 to 0.625
- w_value: bfloat16 [1536, 512], P(('dp', 'ctx')), may hold values from -0.15625 to 0.15625
- w_out: bfloat16 [1536, 1536], P(('dp', 'ctx')), may hold values from -4 to 4
- gain_ffn: bfloat16 [1536], P(('dp', 'ctx')), may hold values from 0.5 to 1.5
- router: bfloat16 [1536, 16], P(('dp', 'ctx')), may hold values from -0.078125 to 0.078125
- routes: int32 [8192, 8], P(('dp', 'ctx')), may hold values from 0 to 15, all different within a row; in each aligned block of 256 rows (0 to 255, 256 to 511, ...) at most 160 rows name the same one
- slot_order: int32 [32, 256], P(('dp', 'ctx')), may hold values from 0 to 255, each once within a row
- w_gate: bfloat16 [16, 1536, 512], P('ctx', 'dp'), may hold values from -0.15625 to 0.15625
- w_up: bfloat16 [16, 1536, 512], P('ctx', 'dp'), may hold values from -0.15625 to 0.15625
- w_down: bfloat16 [16, 1536, 512], P('ctx', 'dp'), may hold values from -6 to 6
- grad_out: bfloat16 [8192, 1536], P(('dp', 'ctx')), may hold values from -6 to 6
Outputs:
- output: bfloat16 [8192, 1536], P(('dp', 'ctx'))
- grad_hidden: float32 [8192, 1536], P(('dp', 'ctx'))
- grad_gain_attn: float32 [1536], P(('dp', 'ctx'))
- grad_query: float32 [1536, 1536], P(('dp', 'ctx'))
- grad_key: float32 [1536, 512], P(('dp', 'ctx'))
- grad_value: float32 [1536, 512], P(('dp', 'ctx'))
- grad_out_proj: float32 [1536, 1536], P(('dp', 'ctx'))
- grad_gain_ffn: float32 [1536], P(('dp', 'ctx'))
- grad_router: float32 [1536, 16], P(('dp', 'ctx'))
- grad_gate: float32 [16, 1536, 512], P('ctx', 'dp')
- grad_up: float32 [16, 1536, 512], P('ctx', 'dp')
- grad_down: float32 [16, 1536, 512], P('ctx', 'dp')
Inputs may be any that keep to these rules, and one draw needn't show every extreme that they name: `routes`: each row names 8 different experts. Among the 256 rows of one device (aligned blocks) no expert is named by more than 160 rows, a bound that some block reaches. `slot_order`: each row is a permutation of 0 to 255.
All inputs are finite; a program needn't handle non-finite values.
Results may differ from a plain program's by a relative error of at most 0.025.
Values may be sent and summed in bfloat16 or wider, within the bound.
No kernel may reach another device: no remote copies, remote signals or barrier semaphores. Data moves between devices by JAX's collectives and lax.ppermute only.
A program may use at most 192 MiB of HBM per device.

v0:
```python
import jax
import jax.numpy as jnp
from jax import lax
from jax.sharding import PartitionSpec as P

H = 24
KV = 8
HD = 64
TOP = 8
CAP = 1024


EPS = 1e-06
NEG_FILL = -1e30
SCORE_SCALE = 0.015625
RESIDUAL_SCALE = 0.22


def carried_in(value, axis, join, neutral):
    count, mine = (lax.axis_size(axis), lax.axis_index(axis))
    pieces = lax.all_gather(value, axis)
    so_far = jnp.full_like(value, 0) + jnp.asarray(neutral, value.dtype)

    def hop(position, so_far):
        longer = join(so_far, pieces[position])
        return jnp.where(position < mine, longer, so_far)

    return lax.fori_loop(0, count - 1, hop, so_far)


def shifted(value, axis, steps):
    count = lax.axis_size(axis)
    leading, last = (max(0, -steps), min(count, count - steps))
    return lax.ppermute(value, axis, [(source, source + steps) for source in range(leading, last)])


def shifted_2(array, axis, by):
    size = lax.axis_size(axis)
    return lax.ppermute(array, axis, [(i, (i + by) % size) for i in range(size)])


def rope_tables(positions, head_dim):
    half_dim = head_dim // 2
    exponents = jnp.arange(half_dim, dtype=jnp.float32) * (2.0 / head_dim)
    inverse = jnp.power(10000.0, -exponents)
    angles = positions.astype(jnp.float32)[:, None] * inverse[None, :]
    return (jnp.cos(angles), jnp.sin(angles))


def rotate(values_in, cos_table, sin_table):
    row_total = values_in.shape[0]
    split = values_in.reshape(row_total, -1, 2, cos_table.shape[1])
    first_half = split[:, :, 0, :]
    second_half = split[:, :, 1, :]
    cos_wide = cos_table[:, None, :]
    sin_wide = sin_table[:, None, :]
    turned = jnp.stack(
        [
            first_half * cos_wide - second_half * sin_wide,
            second_half * cos_wide + first_half * sin_wide,
        ],
        axis=2,
    )
    return turned.reshape(row_total, -1)


def rotate_back(grads_in, cos_table, sin_table):
    row_total = grads_in.shape[0]
    split = grads_in.reshape(row_total, -1, 2, cos_table.shape[1])
    first_half = split[:, :, 0, :]
    second_half = split[:, :, 1, :]
    cos_wide = cos_table[:, None, :]
    sin_wide = sin_table[:, None, :]
    turned = jnp.stack(
        [
            first_half * cos_wide + second_half * sin_wide,
            second_half * cos_wide - first_half * sin_wide,
        ],
        axis=2,
    )
    return turned.reshape(row_total, -1)


def unchanged(carry_state):
    return carry_state


def over_blocks(step_fn, carry_state, pieces, first_row):
    row_count = pieces[0].shape[0]
    block_rows = 512 if row_count > 512 and row_count % 512 == 0 else row_count
    if block_rows == row_count:
        return step_fn(carry_state, pieces, first_row)

    def advance(state_now, block_index):
        block_begin = block_index * block_rows
        sub_pieces = tuple(
            (lax.dynamic_slice_in_dim(member, block_begin, block_rows, 0) for member in pieces)
        )
        return (step_fn(state_now, sub_pieces, block_begin), None)

    carry_state, ignored = lax.scan(
        advance, carry_state, jnp.arange(row_count // block_rows, dtype=jnp.int32)
    )
    return carry_state


def add_counts(earlier_part, later_part):
    return earlier_part + later_part


def shards(
    hidden,
    gain_attn,
    w_query,
    w_key,
    w_value,
    w_out,
    gain_ffn,
    router,
    routes,
    slot_order,
    w_gate,
    w_up,
    w_down,
    grad_out,
):
    tok_rows = hidden.shape[0]
    model_width = hidden.shape[1]
    ctx_size = lax.axis_size("ctx")
    ctx_index = lax.axis_index("ctx")
    gain_a_all, query_w, key_w, value_w, out_w, gain_f_all, router_w = (
        lax.all_gather(gain_attn, ("dp", "ctx"), axis=0, tiled=True),
        lax.all_gather(w_query, ("dp", "ctx"), axis=0, tiled=True),
        lax.all_gather(w_key, ("dp", "ctx"), axis=0, tiled=True),
        lax.all_gather(w_value, ("dp", "ctx"), axis=0, tiled=True),
        lax.all_gather(w_out, ("dp", "ctx"), axis=0, tiled=True),
        lax.all_gather(gain_ffn, ("dp", "ctx"), axis=0, tiled=True),
        lax.all_gather(router, ("dp", "ctx"), axis=0, tiled=True),
    )
    gate_w, up_w, down_w = (
        lax.all_gather(w_gate, "dp", axis=1, tiled=True),
        lax.all_gather(w_up, "dp", axis=1, tiled=True),
        lax.all_gather(w_down, "dp", axis=1, tiled=True),
    )
    group_size = H // KV
    query_rows = tok_rows * group_size
    kv_width = KV * HD
    hidden_f = hidden.astype(jnp.float32)
    inv_attn = lax.rsqrt(jnp.mean(hidden_f * hidden_f, axis=-1, keepdims=True) + EPS)
    normed_a = hidden_f * inv_attn
    gain_a = gain_a_all.astype(jnp.float32)
    attn_in = (normed_a * gain_a).astype(jnp.bfloat16)
    positions = ctx_index * tok_rows + jnp.arange(tok_rows, dtype=jnp.int32)
    cos_table, sin_table = rope_tables(positions, HD)
    query_b = rotate(
        jnp.dot(attn_in, query_w, preferred_element_type=jnp.float32), cos_table, sin_table
    ).astype(jnp.bfloat16)
    key_b = rotate(
        jnp.dot(attn_in, key_w, preferred_element_type=jnp.float32), cos_table, sin_table
    ).astype(jnp.bfloat16)
    value_b = jnp.dot(attn_in, value_w, preferred_element_type=jnp.float32).astype(jnp.bfloat16)
    queries = (
        query_b.reshape(tok_rows, KV, group_size, HD)
        .transpose(1, 0, 2, 3)
        .reshape(KV, query_rows, HD)
    )
    query_pos = jnp.repeat(positions, group_size)
    query_last = ctx_index * tok_rows + tok_rows - 1

    def forward_step(state_now, pieces, first_row):
        key_rows, value_rows = pieces
        row_count = key_rows.shape[0]

        def attend(state_in):
            run_max, row_sum, weighted = state_in
            key_heads = key_rows.reshape(row_count, KV, HD)
            value_heads = value_rows.reshape(row_count, KV, HD)
            scores = (
                jnp.einsum("grd,kgd->grk", queries, key_heads, preferred_element_type=jnp.float32)
                * SCORE_SCALE
            )
            key_pos = first_row + jnp.arange(row_count, dtype=jnp.int32)
            allowed = key_pos[None, None, :] <= query_pos[None, :, None]
            scores = jnp.where(allowed, scores, NEG_FILL)
            new_max = jnp.maximum(run_max, jnp.max(scores, axis=-1))
            exp_scores = jnp.where(allowed, jnp.exp(scores - new_max[..., None]), 0.0)
            rescale = jnp.exp(run_max - new_max)
            row_sum = row_sum * rescale + jnp.sum(exp_scores, axis=-1)
            weighted = weighted * rescale[..., None] + jnp.einsum(
                "grk,kgd->grd",
                exp_scores.astype(jnp.bfloat16),
                value_heads,
                preferred_element_type=jnp.float32,
            )
            return (new_max, row_sum, weighted)

        return lax.cond(first_row <= query_last, attend, unchanged, state_now)

    start_state = (
        jnp.full((KV, query_rows), NEG_FILL, jnp.float32),
        jnp.zeros((KV, query_rows), jnp.float32),
        jnp.zeros((KV, query_rows, HD), jnp.float32),
    )
    run_max, row_sum, weighted = over_blocks(
        forward_step,
        start_state,
        (
            lax.all_gather(key_b, "ctx", axis=0, tiled=True),
            lax.all_gather(value_b, "ctx", axis=0, tiled=True),
        ),
        jnp.int32(0),
    )
    attn_heads = weighted / row_sum[..., None]
    log_total = run_max + jnp.log(row_sum)
    attn_flat = (
        attn_heads.reshape(KV, tok_rows, group_size, HD)
        .transpose(1, 0, 2, 3)
        .reshape(tok_rows, H * HD)
    )
    attn_b = attn_flat.astype(jnp.bfloat16)
    branch = jnp.dot(attn_b, out_w, preferred_element_type=jnp.float32)
    resid = hidden_f + RESIDUAL_SCALE * branch
    inv_ffn = lax.rsqrt(jnp.mean(resid * resid, axis=-1, keepdims=True) + EPS)
    normed_f = resid * inv_ffn
    gain_f = gain_f_all.astype(jnp.float32)
    moe_in = (normed_f * gain_f).astype(jnp.bfloat16)
    logits = jnp.dot(moe_in, router_w, preferred_element_type=jnp.float32)
    n_experts = router_w.shape[1]
    exp_local = gate_w.shape[0]
    most_slots = 5 * tok_rows * TOP // (4 * n_experts)
    n_slots = n_experts * most_slots
    chosen = (routes[:, :, None] == jnp.arange(n_experts, dtype=jnp.int32)[None, None, :]).astype(
        jnp.float32
    )
    route_logit = jnp.sum(chosen * logits[:, None, :], axis=-1)
    gates = jax.nn.softmax(route_logit, axis=-1)
    per_token = jnp.sum(chosen, axis=1)
    device_load = jnp.sum(per_token, axis=0).astype(jnp.int32)
    earlier = carried_in(device_load, "ctx", add_counts, jnp.zeros_like(device_load))
    ranks = slot_order.reshape(-1)
    before = (ranks[None, :] < ranks[:, None]).astype(jnp.bfloat16)
    local_slot = jnp.dot(before, per_token.astype(jnp.bfloat16), preferred_element_type=jnp.float32)
    slot_local = jnp.sum(chosen * local_slot[:, None, :], axis=-1).astype(jnp.int32)
    slot_seq = (
        jnp.sum(chosen * earlier.astype(jnp.float32)[None, None, :], axis=-1).astype(jnp.int32)
        + slot_local
    )
    kept = (slot_seq < CAP).astype(jnp.float32)
    dest = jnp.where(slot_seq < CAP, routes * most_slots + slot_local, n_slots).reshape(-1)
    pair_ids = jnp.arange(tok_rows * TOP, dtype=jnp.int32)
    slot_pair = jnp.zeros((n_slots,), jnp.int32).at[dest].set(pair_ids, mode="drop")
    slot_used = jnp.zeros((n_slots,), jnp.bfloat16).at[dest].set(1.0, mode="drop")
    gather_index = jnp.minimum(dest, n_slots - 1).reshape(tok_rows, TOP)
    send_rows = (moe_in[slot_pair // TOP] * slot_used[:, None]).reshape(
        ctx_size, exp_local, most_slots, model_width
    )
    arrived = lax.all_to_all(send_rows, "ctx", split_axis=0, concat_axis=0, tiled=True)
    gate_pre = jnp.einsum("cemd,edf->cemf", arrived, gate_w, preferred_element_type=jnp.float32)
    up_pre = jnp.einsum("cemd,edf->cemf", arrived, up_w, preferred_element_type=jnp.float32)
    activated = jax.nn.silu(gate_pre)
    inner_b = (activated * up_pre).astype(jnp.bfloat16)
    expert_out = jnp.einsum(
        "cemf,edf->cemd", inner_b, down_w, preferred_element_type=jnp.float32
    ).astype(jnp.bfloat16)
    returned = lax.all_to_all(expert_out, "ctx", split_axis=0, concat_axis=0, tiled=True).reshape(
        n_slots, model_width
    )
    routed_out = returned[gather_index]
    weight_pair = kept * gates
    mixed = jnp.einsum("tk,tkd->td", weight_pair, routed_out, preferred_element_type=jnp.float32)
    output = (resid + RESIDUAL_SCALE * mixed).astype(jnp.bfloat16)
    grad_f = grad_out.astype(jnp.float32)
    slot_grad = (RESIDUAL_SCALE * weight_pair[:, :, None] * grad_f[:, None, :]).astype(jnp.bfloat16)
    gate_grad = (
        RESIDUAL_SCALE
        * kept
        * jnp.einsum("td,tkd->tk", grad_f, routed_out, preferred_element_type=jnp.float32)
    )
    logit_grad = gates * (gate_grad - jnp.sum(gates * gate_grad, axis=-1, keepdims=True))
    router_grad_b = jnp.einsum("tk,tke->te", logit_grad, chosen).astype(jnp.bfloat16)
    d_router = jnp.einsum("td,te->de", moe_in, router_grad_b, preferred_element_type=jnp.float32)
    d_from_router = jnp.einsum(
        "te,de->td", router_grad_b, router_w, preferred_element_type=jnp.float32
    )
    grad_send = (
        slot_grad.reshape(tok_rows * TOP, model_width)[slot_pair] * slot_used[:, None]
    ).reshape(ctx_size, exp_local, most_slots, model_width)
    grad_arrived = lax.all_to_all(grad_send, "ctx", split_axis=0, concat_axis=0, tiled=True)
    d_inner = jnp.einsum("cemd,edf->cemf", grad_arrived, down_w, preferred_element_type=jnp.float32)
    d_down = jnp.einsum("cemd,cemf->edf", grad_arrived, inner_b, preferred_element_type=jnp.float32)
    sigmoid_gate = jax.nn.sigmoid(gate_pre)
    d_gate_b = (d_inner * up_pre * sigmoid_gate * (1.0 + gate_pre * (1.0 - sigmoid_gate))).astype(
        jnp.bfloat16
    )
    d_up_b = (d_inner * activated).astype(jnp.bfloat16)
    d_wgate = jnp.einsum("cemd,cemf->edf", arrived, d_gate_b, preferred_element_type=jnp.float32)
    d_wup = jnp.einsum("cemd,cemf->edf", arrived, d_up_b, preferred_element_type=jnp.float32)
    d_arrived = (
        jnp.einsum("cemf,edf->cemd", d_gate_b, gate_w, preferred_element_type=jnp.float32)
        + jnp.einsum("cemf,edf->cemd", d_up_b, up_w, preferred_element_type=jnp.float32)
    ).astype(jnp.bfloat16)
    d_returned = lax.all_to_all(d_arrived, "ctx", split_axis=0, concat_axis=0, tiled=True).reshape(
        n_slots, model_width
    )
    d_routed = d_returned[gather_index]
    d_moe_in = d_from_router + jnp.einsum(
        "tk,tkd->td", kept, d_routed, preferred_element_type=jnp.float32
    )
    d_gain_ffn = jnp.sum(d_moe_in * normed_f, axis=0)
    d_normed_f = d_moe_in * gain_f
    d_resid = grad_f + inv_ffn * (
        d_normed_f - normed_f * jnp.mean(d_normed_f * normed_f, axis=-1, keepdims=True)
    )
    d_branch_b = (RESIDUAL_SCALE * d_resid).astype(jnp.bfloat16)
    d_wout = jnp.einsum("tc,td->cd", attn_b, d_branch_b, preferred_element_type=jnp.float32)
    d_attn_b = jnp.einsum(
        "td,cd->tc", d_branch_b, out_w, preferred_element_type=jnp.float32
    ).astype(jnp.bfloat16)
    d_out_heads = (
        d_attn_b.reshape(tok_rows, KV, group_size, HD)
        .transpose(1, 0, 2, 3)
        .reshape(KV, query_rows, HD)
    )
    row_delta = jnp.sum(d_out_heads.astype(jnp.float32) * attn_heads, axis=-1)

    def grad_core(key_rows, value_rows, first_row):
        row_count = key_rows.shape[0]
        key_heads = key_rows.reshape(row_count, KV, HD)
        value_heads = value_rows.reshape(row_count, KV, HD)
        scores = (
            jnp.einsum("grd,kgd->grk", queries, key_heads, preferred_element_type=jnp.float32)
            * SCORE_SCALE
        )
        key_pos = first_row + jnp.arange(row_count, dtype=jnp.int32)
        allowed = key_pos[None, None, :] <= query_pos[None, :, None]
        probs = jnp.where(allowed, jnp.exp(scores - log_total[..., None]), 0.0)
        d_value = jnp.einsum(
            "grk,grd->kgd",
            probs.astype(jnp.bfloat16),
            d_out_heads,
            preferred_element_type=jnp.float32,
        )
        d_probs = jnp.einsum(
            "grd,kgd->grk", d_out_heads, value_heads, preferred_element_type=jnp.float32
        )
        d_scores = (probs * (d_probs - row_delta[..., None])).astype(jnp.bfloat16)
        query_add = jnp.einsum(
            "grk,kgd->grd", d_scores, key_heads, preferred_element_type=jnp.float32
        )
        d_key = jnp.einsum("grk,grd->kgd", d_scores, queries, preferred_element_type=jnp.float32)
        update = jnp.concatenate(
            [d_key.reshape(row_count, kv_width), d_value.reshape(row_count, kv_width)], axis=1
        )
        return (query_add, update)

    query_zero = jnp.zeros((KV, query_rows, HD), jnp.float32)

    def cycle_turn(turn, cycle_state):
        d_query, key_rows, value_rows, grad_acc = cycle_state
        source = (ctx_index - turn + ctx_size) % ctx_size
        cycle_base = source * tok_rows

        def cycle_step(state_now, pieces, first_row):

            def attend_cycle(state_in):
                query_now, acc_now = state_in
                query_add, update = grad_core(pieces[0], pieces[1], first_row)
                current = acc_now
                acc_now = current + update
                return (query_now + query_add, acc_now)

            return lax.cond(first_row <= query_last, attend_cycle, unchanged, state_now)

        d_query, grad_acc = over_blocks(
            cycle_step, (d_query, grad_acc), (key_rows, value_rows), cycle_base
        )
        key_rows, value_rows = shifted((key_rows, value_rows), "ctx", 1)
        grad_acc = shifted_2(grad_acc.astype(jnp.bfloat16), "ctx", 1).astype(grad_acc.dtype)
        return (d_query, key_rows, value_rows, grad_acc)

    cycle_start = (query_zero, key_b, value_b, jnp.zeros((tok_rows, 2 * kv_width), jnp.float32))
    d_query, ignored_keys, ignored_values, own_keyval = lax.fori_loop(
        0, ctx_size, cycle_turn, cycle_start
    )
    d_query_flat = (
        (d_query * SCORE_SCALE)
        .reshape(KV, tok_rows, group_size, HD)
        .transpose(1, 0, 2, 3)
        .reshape(tok_rows, H * HD)
    )
    d_qpre_b = rotate_back(d_query_flat, cos_table, sin_table).astype(jnp.bfloat16)
    d_kpre_b = rotate_back(own_keyval[:, :kv_width] * SCORE_SCALE, cos_table, sin_table).astype(
        jnp.bfloat16
    )
    d_value_b = own_keyval[:, kv_width:].astype(jnp.bfloat16)
    d_wquery = jnp.einsum("td,tc->dc", attn_in, d_qpre_b, preferred_element_type=jnp.float32)
    d_wkey = jnp.einsum("td,tc->dc", attn_in, d_kpre_b, preferred_element_type=jnp.float32)
    d_wvalue = jnp.einsum("td,tc->dc", attn_in, d_value_b, preferred_element_type=jnp.float32)
    d_attn_in = (
        jnp.einsum("tc,dc->td", d_qpre_b, query_w, preferred_element_type=jnp.float32)
        + jnp.einsum("tc,dc->td", d_kpre_b, key_w, preferred_element_type=jnp.float32)
        + jnp.einsum("tc,dc->td", d_value_b, value_w, preferred_element_type=jnp.float32)
    )
    d_gain_attn = jnp.sum(d_attn_in * normed_a, axis=0)
    d_normed_a = d_attn_in * gain_a
    d_hidden = d_resid + inv_attn * (
        d_normed_a - normed_a * jnp.mean(d_normed_a * normed_a, axis=-1, keepdims=True)
    )
    owned = (
        lax.psum_scatter(d_gain_attn, ("dp", "ctx"), scatter_dimension=0, tiled=True),
        lax.psum_scatter(d_wquery, ("dp", "ctx"), scatter_dimension=0, tiled=True),
        lax.psum_scatter(d_wkey, ("dp", "ctx"), scatter_dimension=0, tiled=True),
        lax.psum_scatter(d_wvalue, ("dp", "ctx"), scatter_dimension=0, tiled=True),
        lax.psum_scatter(d_wout, ("dp", "ctx"), scatter_dimension=0, tiled=True),
        lax.psum_scatter(d_gain_ffn, ("dp", "ctx"), scatter_dimension=0, tiled=True),
        lax.psum_scatter(d_router, ("dp", "ctx"), scatter_dimension=0, tiled=True),
    )
    owned_experts = (
        lax.psum_scatter(
            d_wgate.astype(jnp.bfloat16), "dp", scatter_dimension=1, tiled=True
        ).astype(jnp.float32),
        lax.psum_scatter(d_wup.astype(jnp.bfloat16), "dp", scatter_dimension=1, tiled=True).astype(
            jnp.float32
        ),
        lax.psum_scatter(d_down.astype(jnp.bfloat16), "dp", scatter_dimension=1, tiled=True).astype(
            jnp.float32
        ),
    )
    return (
        output,
        d_hidden,
        owned[0],
        owned[1],
        owned[2],
        owned[3],
        owned[4],
        owned[5],
        owned[6],
        owned_experts[0],
        owned_experts[1],
        owned_experts[2],
    )


def solution(mesh):
    return jax.shard_map(
        shards,
        mesh=mesh,
        in_specs=(
            P(("dp", "ctx"), None),
            P(("dp", "ctx")),
            P(("dp", "ctx"), None),
            P(("dp", "ctx"), None),
            P(("dp", "ctx"), None),
            P(("dp", "ctx"), None),
            P(("dp", "ctx")),
            P(("dp", "ctx"), None),
            P(("dp", "ctx"), None),
            P(("dp", "ctx"), None),
            P("ctx", "dp", None),
            P("ctx", "dp", None),
            P("ctx", "dp", None),
            P(("dp", "ctx"), None),
        ),
        out_specs=(
            P(("dp", "ctx"), None),
            P(("dp", "ctx"), None),
            P(("dp", "ctx")),
            P(("dp", "ctx"), None),
            P(("dp", "ctx"), None),
            P(("dp", "ctx"), None),
            P(("dp", "ctx"), None),
            P(("dp", "ctx")),
            P(("dp", "ctx"), None),
            P("ctx", "dp", None),
            P("ctx", "dp", None),
            P("ctx", "dp", None),
        ),
        check_vma=False,
    )
```

profile of v0, /device:TPU:0, one launch (start us, length us, event | category | flops | bytes accessed | tf_op | source)
XLA Modules:
  0.0 1574.8 jit_solution(8077085205849853573)
XLA Ops:
  10.4 42.1 %all-reduce.6 = (bf16[1536]{0:T(1024)(128)(2,1)S(1)}, bf16[1536]{0:T(1024)(128)(2,1)S(1)}) all-reduce(bf16[1536]{0:T(1024)(128)(2,1)S(1)} %dynamic-update-slice, bf16[1536]{0:T(1024)(128)(2,1)S(1)} %dynamic-update-slice.2), channel_id=1, replica_groups=mesh['dp'=4,'ctx'=8] {'dp','ctx'}, use_global_device_ids=true, to_apply=%add | all-reduce | flops 3072 | bytes 12288
  53.9 14.6 all-gather.18.cloned.1.call-done
  72.5 52.8 %all-gather.12.cloned.1.call-done = bf16[1536,512]{1,0:T(8,128)(2,1)} async-done(((bf16[48,512]{1,0:T(8,128)(2,1)}), bf16[1536,512]{1,0:T(8,128)(2,1)}) %all-gather.12.cloned.1.call-update) | async-done | bytes 1572880 | tf_op jit(solution)/shard_map/all_gather | solution.py:134
  131.2 7.3 all-reduce.1
  138.9 40.1 %all-gather.1 = bf16[32,48,16]{1,2,0:T(8,128)(2,1)S(1)} all-gather(bf16[1,48,16]{1,2,0:T(8,128)(2,1)S(1)} %bitcast.239), channel_id=1, replica_groups=mesh['dp'=4,'ctx'=8] {'dp','ctx'}, dimensions={0}, use_global_device_ids=true | all-gather | bytes 50688 | tf_op jit(solution)/shard_map/all_gather | solution.py:138
  184.5 36.7 %all-gather.16.cloned.1.call-done = bf16[1536,1536]{1,0:T(8,128)(2,1)} async-done(((bf16[48,1536]{1,0:T(8,128)(2,1)}), bf16[1536,1536]{1,0:T(8,128)(2,1)}) %all-gather.16.cloned.1.call-update) | async-done | bytes 4718608 | tf_op jit(solution)/shard_map/all_gather | solution.py:133
  228.0 22.0 %all-gather.14.cloned.1.call-done = bf16[2048,512]{0,1:T(8,128)(2,1)} async-done(((bf16[256,512]{0,1:T(8,128)(2,1)}), bf16[2048,512]{0,1:T(8,128)(2,1)}) %all-gather.14.cloned.1.call-update) | async-done | bytes 2097168 | tf_op jit(solution)/shard_map/all_gather | solution.py:208
  250.2 16.4 %while.51 = (s32[]{:T(128)}, f32[8,768]{1,0:T(8,128)S(1)}, f32[8,768]{1,0:T(8,128)S(1)}, f32[8,768,64]{1,2,0:T(8,128)S(1)}, s32[4]{0:T(128)S(1)}, /*index=5*/s32...) while((s32[]{:T(128)}, f32[8,768]{1,0:T(8,128)S(1)}, ...), condition=%wide.region_6.7_spmd.clone, body=%wide.region_1.6_spmd.clone.sunk | while | flops 847393280 | bytes 46810432 | solution.py:101
  251.4 11.3 conditional.6
  273.8 42.6 %all-gather.22.cloned.1.call-done = bf16[1536,1536]{1,0:T(8,128)(2,1)} async-done(((bf16[48,1536]{1,0:T(8,128)(2,1)}), bf16[1536,1536]{1,0:T(8,128)(2,1)}) %all-gather.22.cloned.1.call-update) | async-done | bytes 4718608 | tf_op jit(solution)/shard_map/all_gather | solution.py:136
  323.6 8.1 scatter_custom_fusion
  331.7 14.6 scatter_custom_fusion.1
  346.4 9.6 gather_fusion
  359.9 20.0 %gather_fusion.2 = bf16[2560,1536]{1,0:T(8,128)(2,1)} fusion(bf16[2048,1536]{1,0:T(8,128)(2,1)} %fusion.21, s32[3072]{0:T(1024)S(1)} %get-tuple-element.858), kind=kCustom, calls=%fused_computation.2 | custom fusion | bytes 15738880 | tf_op jit(solution)/shard_map/gather | solution.py:286
  379.9 11.1 broadcast_multiply_fusion
  396.7 87.7 %all-to-all-done = bf16[8,2,160,1536]{3,2,1,0:T(8,128)(2,1)} async-done(((bf16[8,2,160,1536]{3,2,1,0:T(8,128)(2,1)}), bf16[8,2,160,1536]{3,2,1,0:T(8,128)(2,1)}, u32[]{:S(2)}, u32[]{:S(2)}) %all-to-all-start) | async-done | bytes 7864352 | tf_op jit(solution)/shard_map/all_to_all | solution.py:257
  490.3 10.6 fusion.25
  500.9 10.7 fusion.27
  511.7 43.6 %all-gather.28.cloned.1.call-done = bf16[2,1536,512]{2,1,0:T(8,128)(2,1)} async-done(((bf16[2,384,512]{2,1,0:T(8,128)(2,1)}), bf16[2,1536,512]{2,1,0:T(8,128)(2,1)}) %all-gather.28.cloned.1.call-update) | async-done | bytes 3145744 | tf_op jit(solution)/shard_map/all_gather | solution.py:143
  555.3 22.4 %all-to-all-done.2 = bf16[8,2,160,1536]{3,2,1,0:T(8,128)(2,1)} async-done(((bf16[8,2,160,1536]{3,2,1,0:T(8,128)(2,1)}), bf16[8,2,160,1536]{3,2,1,0:T(8,128)(2,1)}, u32[]{:S(2)}, u32[]{:S(2)}) %all-to-all-start.2) | async-done | bytes 7864352 | tf_op jit(solution)/shard_map/all_to_all | solution.py:288
  577.8 12.4 fusion.38
  591.7 10.9 bitcast_convert_fusion
  602.6 7.0 convert_bitcast_fusion
  618.4 11.2 bitcast_convert_fusion.1
  629.7 12.5 fusion.46
  642.2 10.7 fusion.22
  652.8 7.1 copy.115
  659.9 46.9 %all-to-all-done.1 = bf16[8,2,160,1536]{3,2,1,0:T(8,128)(2,1)} async-done(((bf16[8,2,160,1536]{3,2,1,0:T(8,128)(2,1)}), bf16[8,2,160,1536]{3,2,1,0:T(8,128)(2,1)}, u32[]{:S(2)}, u32[]{:S(2)}) %all-to-all-start.1) | async-done | bytes 7864352 | tf_op jit(solution)/shard_map/all_to_all | solution.py:265
  711.8 10.8 bitcast_convert_fusion.2
  725.9 17.7 %gather_fusion.1 = bf16[2048,1536]{1,0:T(8,128)(2,1)} fusion(bf16[2560,1536]{1,0:T(8,128)(2,1)} %bitcast.33, s32[2048]{0:T(1024)S(1)} %broadcast_clamp_fusion), kind=kCustom, calls=%fused_computation.1 | custom fusion | bytes 12591104 | tf_op jit(solution)/shard_map/gather | solution.py:268
  750.1 50.2 %all-to-all-done.3 = bf16[8,2,160,1536]{3,2,1,0:T(8,128)(2,1)} async-done(((bf16[8,2,160,1536]{3,2,1,0:T(8,128)(2,1)}), bf16[8,2,160,1536]{3,2,1,0:T(8,128)(2,1)}, u32[]{:S(2)}, u32[]{:S(2)}) %all-to-all-start.3) | async-done | bytes 7864352 | tf_op jit(solution)/shard_map/all_to_all | solution.py:302
  800.2 17.5 %gather_fusion.3 = bf16[2048,1536]{1,0:T(8,128)(2,1)} fusion(bf16[2560,1536]{1,0:T(8,128)(2,1)} %bitcast.46, s32[2048]{0:T(1024)S(1)} %broadcast_clamp_fusion), kind=kCustom, calls=%fused_computation.3 | custom fusion | bytes 12591104 | tf_op jit(solution)/shard_map/gather | solution.py:305
  838.7 231.1 %while.53 = (s32[]{:T(128)}, f32[8,768,64]{1,2,0:T(8,128)S(1)}, bf16[256,512]{0,1:T(8,128)(2,1)}, bf16[256,512]{0,1:T(8,128)(2,1)}, f32[256,1024]{0,1:T(8,128)},...) while((s32[]{:T(128)}, f32[8,768,64]{1,2,0:T(8,128)S(1)}, ...), condition=%wide.region_25.26_spmd.clone, body=%wide.region_22.25_spmd.clone.sunk | while | flops 1024262400 | bytes 56188612 | solution.py:382
  842.2 10.8 conditional.7
  870.1 12.7 collective-permute-start.2
  902.9 15.9 %collective-permute-start = (bf16[256,512]{0,1:T(8,128)(2,1)}, bf16[256,512]{0,1:T(8,128)(2,1)}, u32[]{:S(2)}, u32[]{:S(2)}) collective-permute-start(bf16[256,512]{0,1:T(8,128)(2,1)} %copy.203), channel_id=1, source_target_pairs={{0,1},{1,2},{2,3},{3,4},{4,5},{5,6},{6,7},{8,9},{9,10},{10,11},{11... | collective-permute-start | bytes 786440 | tf_op jit(solution)/shard_map/while/body/eval_jaxpr/ppermute | solution.py:34
  927.3 6.6 collective-permute-start.2
  939.0 13.6 collective-permute-start.1
  982.9 13.2 collective-permute-start.2
  1029.2 8.8 collective-permute-done.2
  1046.5 13.4 collective-permute-start.1
  1060.0 8.8 collective-permute-done.2
  1077.7 6.7 fusion.70
  1112.4 43.3 %all-reduce.5 = (f32[1536]{0:T(1024)S(1)}, f32[1536]{0:T(1024)S(1)}) all-reduce(f32[1536]{0:T(1024)S(1)} %get-tuple-element.764, f32[1536]{0:T(1024)S(1)} %copy-done.51), channel_id=3, replica_groups=mesh['dp'=4,'ctx'=8] {'dp','ctx'}, use_global_device_ids=true, to_apply=%region_28.29.clone | all-reduce | flops 3072 | bytes 24576
  1161.3 17.5 %reduce-scatter.15.cloned.1.call-done = f32[48,512]{1,0:T(8,128)} async-done(((f32[1536,512]{1,0:T(8,128)}), f32[48,512]{1,0:T(8,128)}) %reduce-scatter.15.cloned.1.call-update) | async-done | bytes 98320 | tf_op jit(solution)/shard_map/reduce_scatter | solution.py:413
  1178.7 106.3 %reduce-scatter.13.cloned.1.call-done = f32[48,512]{1,0:T(8,128)} async-done(((f32[1536,512]{1,0:T(8,128)}), f32[48,512]{1,0:T(8,128)}) %reduce-scatter.13.cloned.1.call-update) | async-done | bytes 98320 | tf_op jit(solution)/shard_map/reduce_scatter | solution.py:412
  1285.1 141.0 %reduce-scatter.17.cloned.1.call-done = f32[48,1536]{1,0:T(8,128)} async-done(((f32[1536,1536]{1,0:T(8,128)}), f32[48,1536]{1,0:T(8,128)}) %reduce-scatter.17.cloned.1.call-update) | async-done | bytes 294928 | tf_op jit(solution)/shard_map/reduce_scatter | solution.py:414
  1426.1 141.9 %reduce-scatter.11.cloned.1.call-done = f32[48,1536]{1,0:T(8,128)} async-done(((f32[1536,1536]{1,0:T(8,128)}), f32[48,1536]{1,0:T(8,128)}) %reduce-scatter.11.cloned.1.call-update) | async-done | bytes 294928 | tf_op jit(solution)/shard_map/reduce_scatter | solution.py:411
  (418 shorter events, 294.5 us)
Async XLA Ops:
  7.2 61.4 %all-gather.18.cloned.1.call-start = ((), (), s32[]{:S(2)}) async-start(), calls=%async_computation.15 | async-start | bytes 1622016 | tf_op jit(solution)/shard_map/all_gather | solution.py:135
  7.9 117.4 %all-gather.12.cloned.1.call-start = ((), (), s32[]{:S(2)}) async-start(), calls=%async_computation.12 | async-start | bytes 1622016 | tf_op jit(solution)/shard_map/all_gather | solution.py:134
  8.7 171.9 %all-gather.20.cloned.1.call-start = ((), (), s32[]{:S(2)}) async-start(), calls=%async_computation.16 | async-start | bytes 2359296 | tf_op jit(solution)/shard_map/all_gather | solution.py:209
  52.5 168.7 %copy-start.37 = (f32[1536]{0:T(1024)}, f32[1536]{0:T(1024)S(1)}, u32[]{:S(2)}) copy-start(f32[1536]{0:T(1024)S(1)} %convert_element_type.202) | copy-start | bytes 18436
  71.6 149.7 %all-gather.16.cloned.1.call-start = ((), (), s32[]{:S(2)}) async-start(), calls=%async_computation.14 | async-start | bytes 4866048 | tf_op jit(solution)/shard_map/all_gather | solution.py:133
  72.2 177.9 %all-gather.14.cloned.1.call-start = ((), (), s32[]{:S(2)}) async-start(), calls=%async_computation.13 | async-start | bytes 2359296 | tf_op jit(solution)/shard_map/all_gather | solution.py:208
  128.3 188.1 %all-gather.22.cloned.1.call-start = ((), (), s32[]{:S(2)}) async-start(), calls=%async_computation.17 | async-start | bytes 4866048 | tf_op jit(solution)/shard_map/all_gather | solution.py:136
  128.9 361.4 %all-gather.26.cloned.1.call-start = ((), (), s32[]{:S(2)}) async-start(), calls=%async_computation.19 | async-start | bytes 3932160 | tf_op jit(solution)/shard_map/all_gather | solution.py:142
  138.9 181.5 %copy-start.41 = (f32[1536]{0:T(1024)}, f32[1536]{0:T(1024)S(1)}, u32[]{:S(2)}) copy-start(f32[1536]{0:T(1024)S(1)} %convert_element_type.219) | copy-start | bytes 18436
  391.0 93.3 %all-to-all-start = ((bf16[8,2,160,1536]{3,2,1,0:T(8,128)(2,1)}), bf16[8,2,160,1536]{3,2,1,0:T(8,128)(2,1)}, u32[]{:S(2)}, u32[]{:S(2)}) async-start(bf16[8,2,160,1536]{3,2,1,0:T(8,128)(2,1)} %get-tuple-element.851), calls=%async_computation | async-start | bytes 15728640 | tf_op jit(solution)/shard_map/all_to_all | solution.py:257
  395.9 105.0 %all-gather.24.cloned.1.call-start = ((), (), s32[]{:S(2)}) async-start(), calls=%async_computation.18 | async-start | bytes 3932160 | tf_op jit(solution)/shard_map/all_gather | solution.py:141
  484.4 93.4 %all-to-all-start.2 = ((bf16[8,2,160,1536]{3,2,1,0:T(8,128)(2,1)}), bf16[8,2,160,1536]{3,2,1,0:T(8,128)(2,1)}, u32[]{:S(2)}, u32[]{:S(2)}) async-start(bf16[8,2,160,1536]{3,2,1,0:T(8,128)(2,1)} %get-tuple-element.850), calls=%async_computation.2 | async-start | bytes 15728640 | tf_op jit(solution)/shard_map/all_to_all | solution.py:288
  489.3 66.0 %all-gather.28.cloned.1.call-start = ((), (), s32[]{:S(2)}) async-start(), calls=%async_computation.20 | async-start | bytes 3932160 | tf_op jit(solution)/shard_map/all_gather | solution.py:143
  490.1 607.3 %reduce-scatter.23.cloned.1.call-start = ((), (), s32[]{:S(2)}) async-start(), calls=%async_computation.27 | async-start | bytes 3932160 | tf_op jit(solution)/shard_map/reduce_scatter | solution.py:425
  613.1 93.7 %all-to-all-start.1 = ((bf16[8,2,160,1536]{3,2,1,0:T(8,128)(2,1)}), bf16[8,2,160,1536]{3,2,1,0:T(8,128)(2,1)}, u32[]{:S(2)}, u32[]{:S(2)}) async-start(bf16[8,2,160,1536]{3,2,1,0:T(8,128)(2,1)} %copy.111), calls=%async_computation.1 | async-start | bytes 15728640 | tf_op jit(solution)/shard_map/all_to_all | solution.py:265
  618.4 481.5 %reduce-scatter.21.cloned.1.call-start = ((), (), s32[]{:S(2)}) async-start(), calls=%async_computation.26 | async-start | bytes 3932160 | tf_op jit(solution)/shard_map/reduce_scatter | solution.py:422
  706.8 93.4 %all-to-all-start.3 = ((bf16[8,2,160,1536]{3,2,1,0:T(8,128)(2,1)}), bf16[8,2,160,1536]{3,2,1,0:T(8,128)(2,1)}, u32[]{:S(2)}, u32[]{:S(2)}) async-start(bf16[8,2,160,1536]{3,2,1,0:T(8,128)(2,1)} %copy.115), calls=%async_computation.3 | async-start | bytes 15728640 | tf_op jit(solution)/shard_map/all_to_all | solution.py:302
  711.8 390.6 %reduce-scatter.19.cloned.1.call-start = ((), (), s32[]{:S(2)}) async-start(), calls=%async_computation.25 | async-start | bytes 3932160 | tf_op jit(solution)/shard_map/reduce_scatter | solution.py:419
  722.7 437.1 %reduce-scatter.25.cloned.1.call-start = ((), (), s32[]{:S(2)}) async-start(), calls=%async_computation.28 | async-start | bytes 811008
  838.5 340.2 %reduce-scatter.15.cloned.1.call-start = ((), (), s32[]{:S(2)}) async-start(), calls=%async_computation.23 | async-start | bytes 3244032 | tf_op jit(solution)/shard_map/reduce_scatter | solution.py:413
  838.7 231.2 %copy-start.38 = (f32[1536]{0:T(1024)S(1)}, f32[1536]{0:T(1024)}, u32[]{:S(2)}) copy-start(f32[1536]{0:T(1024)} %copy-done.37) | copy-start | bytes 18436
  853.8 9.7 collective-permute-start.2
  853.8 10.8 collective-permute-start
  857.1 7.5 collective-permute-start.1
  870.1 19.8 %collective-permute-start.2 = (bf16[256,1024]{0,1:T(8,128)(2,1)}, bf16[256,1024]{0,1:T(8,128)(2,1)S(1)}, u32[]{:S(2)}, u32[]{:S(2)}) collective-permute-start(bf16[256,1024]{0,1:T(8,128)(2,1)} %convert_element_type.335), channel_id=1, source_target_pairs={{0,1},{1,2},{2,3},{3,4},{4,5},{5,6},{6,7},{7,0},{8,9},{9,10},{10,1... | collective-permute-start | bytes 1572872 | tf_op jit(solution)/shard_map/while/body/eval_jaxpr/ppermute | solution.py:39
  882.8 8.1 collective-permute-start
  887.9 3.1 collective-permute-start.1
  896.5 24.3 %collective-permute-start.2 = (bf16[256,1024]{0,1:T(8,128)(2,1)}, bf16[256,1024]{0,1:T(8,128)(2,1)S(1)}, u32[]{:S(2)}, u32[]{:S(2)}) collective-permute-start(bf16[256,1024]{0,1:T(8,128)(2,1)} %convert_element_type.335), channel_id=1, source_target_pairs={{0,1},{1,2},{2,3},{3,4},{4,5},{5,6},{6,7},{7,0},{8,9},{9,10},{10,1... | collective-permute-start | bytes 1572872 | tf_op jit(solution)/shard_map/while/body/eval_jaxpr/ppermute | solution.py:39
  902.9 18.9 %collective-permute-start = (bf16[256,512]{0,1:T(8,128)(2,1)}, bf16[256,512]{0,1:T(8,128)(2,1)}, u32[]{:S(2)}, u32[]{:S(2)}) collective-permute-start(bf16[256,512]{0,1:T(8,128)(2,1)} %copy.203), channel_id=1, source_target_pairs={{0,1},{1,2},{2,3},{3,4},{4,5},{5,6},{6,7},{8,9},{9,10},{10,11},{11... | collective-permute-start | bytes 786440 | tf_op jit(solution)/shard_map/while/body/eval_jaxpr/ppermute | solution.py:34
  918.7 3.1 collective-permute-start.1
  927.3 25.3 %collective-permute-start.2 = (bf16[256,1024]{0,1:T(8,128)(2,1)}, bf16[256,1024]{0,1:T(8,128)(2,1)S(1)}, u32[]{:S(2)}, u32[]{:S(2)}) collective-permute-start(bf16[256,1024]{0,1:T(8,128)(2,1)} %convert_element_type.335), channel_id=1, source_target_pairs={{0,1},{1,2},{2,3},{3,4},{4,5},{5,6},{6,7},{7,0},{8,9},{9,10},{10,1... | collective-permute-start | bytes 1572872 | tf_op jit(solution)/shard_map/while/body/eval_jaxpr/ppermute | solution.py:39
  933.9 19.8 %collective-permute-start = (bf16[256,512]{0,1:T(8,128)(2,1)}, bf16[256,512]{0,1:T(8,128)(2,1)}, u32[]{:S(2)}, u32[]{:S(2)}) collective-permute-start(bf16[256,512]{0,1:T(8,128)(2,1)} %copy.203), channel_id=1, source_target_pairs={{0,1},{1,2},{2,3},{3,4},{4,5},{5,6},{6,7},{8,9},{9,10},{10,11},{11... | collective-permute-start | bytes 786440 | tf_op jit(solution)/shard_map/while/body/eval_jaxpr/ppermute | solution.py:34
  939.0 14.7 collective-permute-start.1
  959.1 17.2 %collective-permute-start.2 = (bf16[256,1024]{0,1:T(8,128)(2,1)}, bf16[256,1024]{0,1:T(8,128)(2,1)S(1)}, u32[]{:S(2)}, u32[]{:S(2)}) collective-permute-start(bf16[256,1024]{0,1:T(8,128)(2,1)} %convert_element_type.335), channel_id=1, source_target_pairs={{0,1},{1,2},{2,3},{3,4},{4,5},{5,6},{6,7},{7,0},{8,9},{9,10},{10,1... | collective-permute-start | bytes 1572872 | tf_op jit(solution)/shard_map/while/body/eval_jaxpr/ppermute | solution.py:39
  964.4 13.0 collective-permute-start
  969.4 8.0 collective-permute-start.1
  982.9 24.3 %collective-permute-start.2 = (bf16[256,1024]{0,1:T(8,128)(2,1)}, bf16[256,1024]{0,1:T(8,128)(2,1)S(1)}, u32[]{:S(2)}, u32[]{:S(2)}) collective-permute-start(bf16[256,1024]{0,1:T(8,128)(2,1)} %convert_element_type.335), channel_id=1, source_target_pairs={{0,1},{1,2},{2,3},{3,4},{4,5},{5,6},{6,7},{7,0},{8,9},{9,10},{10,1... | collective-permute-start | bytes 1572872 | tf_op jit(solution)/shard_map/while/body/eval_jaxpr/ppermute | solution.py:39
  996.1 12.1 collective-permute-start
  1001.2 7.0 collective-permute-start.1
  1013.7 24.3 %collective-permute-start.2 = (bf16[256,1024]{0,1:T(8,128)(2,1)}, bf16[256,1024]{0,1:T(8,128)(2,1)S(1)}, u32[]{:S(2)}, u32[]{:S(2)}) collective-permute-start(bf16[256,1024]{0,1:T(8,128)(2,1)} %convert_element_type.335), channel_id=1, source_target_pairs={{0,1},{1,2},{2,3},{3,4},{4,5},{5,6},{6,7},{7,0},{8,9},{9,10},{10,1... | collective-permute-start | bytes 1572872 | tf_op jit(solution)/shard_map/while/body/eval_jaxpr/ppermute | solution.py:39
  1017.0 22.0 %collective-permute-start = (bf16[256,512]{0,1:T(8,128)(2,1)}, bf16[256,512]{0,1:T(8,128)(2,1)}, u32[]{:S(2)}, u32[]{:S(2)}) collective-permute-start(bf16[256,512]{0,1:T(8,128)(2,1)} %copy.203), channel_id=1, source_target_pairs={{0,1},{1,2},{2,3},{3,4},{4,5},{5,6},{6,7},{8,9},{9,10},{10,11},{11... | collective-permute-start | bytes 786440 | tf_op jit(solution)/shard_map/while/body/eval_jaxpr/ppermute | solution.py:34
  1022.6 16.4 %collective-permute-start.1 = (bf16[256,512]{0,1:T(8,128)(2,1)}, bf16[256,512]{0,1:T(8,128)(2,1)}, u32[]{:S(2)}, u32[]{:S(2)}) collective-permute-start(bf16[256,512]{0,1:T(8,128)(2,1)} %copy.204), channel_id=1, source_target_pairs={{0,1},{1,2},{2,3},{3,4},{4,5},{5,6},{6,7},{8,9},{9,10},{10,11},{11... | collective-permute-start | bytes 786440 | tf_op jit(solution)/shard_map/while/body/eval_jaxpr/ppermute | solution.py:34
  1044.5 24.3 %collective-permute-start.2 = (bf16[256,1024]{0,1:T(8,128)(2,1)}, bf16[256,1024]{0,1:T(8,128)(2,1)S(1)}, u32[]{:S(2)}, u32[]{:S(2)}) collective-permute-start(bf16[256,1024]{0,1:T(8,128)(2,1)} %convert_element_type.335), channel_id=1, source_target_pairs={{0,1},{1,2},{2,3},{3,4},{4,5},{5,6},{6,7},{7,0},{8,9},{9,10},{10,1... | collective-permute-start | bytes 1572872 | tf_op jit(solution)/shard_map/while/body/eval_jaxpr/ppermute | solution.py:39
  1044.5 25.3 %collective-permute-start = (bf16[256,512]{0,1:T(8,128)(2,1)}, bf16[256,512]{0,1:T(8,128)(2,1)}, u32[]{:S(2)}, u32[]{:S(2)}) collective-permute-start(bf16[256,512]{0,1:T(8,128)(2,1)} %copy.203), channel_id=1, source_target_pairs={{0,1},{1,2},{2,3},{3,4},{4,5},{5,6},{6,7},{8,9},{9,10},{10,11},{11... | collective-permute-start | bytes 786440 | tf_op jit(solution)/shard_map/while/body/eval_jaxpr/ppermute | solution.py:34
  1046.5 23.3 %collective-permute-start.1 = (bf16[256,512]{0,1:T(8,128)(2,1)}, bf16[256,512]{0,1:T(8,128)(2,1)}, u32[]{:S(2)}, u32[]{:S(2)}) collective-permute-start(bf16[256,512]{0,1:T(8,128)(2,1)} %copy.204), channel_id=1, source_target_pairs={{0,1},{1,2},{2,3},{3,4},{4,5},{5,6},{6,7},{8,9},{9,10},{10,11},{11... | collective-permute-start | bytes 786440 | tf_op jit(solution)/shard_map/while/body/eval_jaxpr/ppermute | solution.py:34
  1073.6 211.5 %reduce-scatter.13.cloned.1.call-start = ((), (), s32[]{:S(2)}) async-start(), calls=%async_computation.22 | async-start | bytes 3244032 | tf_op jit(solution)/shard_map/reduce_scatter | solution.py:412
  1077.6 348.4 %reduce-scatter.17.cloned.1.call-start = ((), (), s32[]{:S(2)}) async-start(), calls=%async_computation.24 | async-start | bytes 9732096 | tf_op jit(solution)/shard_map/reduce_scatter | solution.py:414
  1084.4 483.6 %reduce-scatter.11.cloned.1.call-start = ((), (), s32[]{:S(2)}) async-start(), calls=%async_computation.21 | async-start | bytes 9732096 | tf_op jit(solution)/shard_map/reduce_scatter | solution.py:411
  (65 other events, 1506.0 us)
Sparse Core Ops, SparseCore 0:
  10.9 57.6 all-gather.17
  71.4 53.8 all-gather.11
  127.7 27.0 all-gather.19
  157.6 63.5 all-gather.15
  223.0 26.9 all-gather.13
  252.8 63.5 all-gather.21
  318.0 62.2 all-gather.25
  398.3 63.5 all-gather.23
  491.7 63.5 all-gather.27
  602.7 58.1 reduce-scatter.22
  663.2 60.2 reduce-scatter.20
  725.6 60.2 reduce-scatter.18
  838.6 93.4 reduce-scatter.24
  1073.8 104.9 reduce-scatter.14
  1184.6 100.4 reduce-scatter.12
  1291.4 134.6 reduce-scatter.16
  1433.4 134.5 reduce-scatter.10
where the time goes:
time: 1580 us; the launch traced here: 1570 us
  waiting for transfers between devices  858 us (54%)
  matrix products  166 us (11%)
  local copies, waits for them, and re-layouts  165 us (10%)
  starting transfers between devices  163 us (10%)
  blocking collectives  133 us (8%)
  other arithmetic  70.5 us (4%)
  between operations  16 us (1%)
    reduce_scatter x1, waiting for transfers between devices, shards(): lax.psum_scatter(d_wquery, ('dp', 'ctx'), scatter_dimension=0, tiled=True)  142 us
    reduce_scatter x1, waiting for transfers between devices, shards(): lax.psum_scatter(d_wout, ('dp', 'ctx'), scatter_dimension=0, tiled=True)  141 us
    reduce_scatter x1, waiting for transfers between devices, shards(): lax.psum_scatter(d_wkey, ('dp', 'ctx'), scatter_dimension=0, tiled=True)  106 us
    ppermute x16, starting transfers between devices, shifted(): lax.ppermute(value, axis, [(source, source + steps) for source in range(l...  94.8 us
    unnamed x3, blocking collectives  92.7 us
    all_to_all x1, waiting for transfers between devices, shards(): lax.all_to_all(send_rows, 'ctx', split_axis=0, concat_axis=0, tiled=True)  87.7 us
    all_gather x1, waiting for transfers between devices, shards(): lax.all_gather(w_key, ('dp', 'ctx'), axis=0, tiled=True)  52.8 us
    all_to_all x1, waiting for transfers between devices, shards(): lax.all_to_all(d_arrived, 'ctx', split_axis=0, concat_axis=0, tiled=True)  50.2 us
  transfers between devices with their start and end apart: 45, of which 19 were waited for; matrix products, arithmetic and copies ran while one was open for 24% of the time, Pallas kernels for 0%

commit v1 on v0

v1 whole, which is shorter than its diff:
```python
import functools

import jax
import jax.numpy as jnp
from jax import lax
from jax.experimental import pallas as pl
from jax.experimental.pallas import tpu as pltpu
from jax.sharding import PartitionSpec as P

H = 24
KV = 8
HD = 64
TOP = 8
CAP = 1024

EPS = 1e-06
NEG_FILL = -1e30
SCORE_SCALE = 0.015625
RESIDUAL_SCALE = 0.22

GROUP = H // KV
HALF = HD // 2
QW = GROUP * HD
QKV = QW + 2 * HD
LOW = 64
EXTRA = 128

f32 = jnp.float32
bf16 = jnp.bfloat16
i32 = jnp.int32
VMEM_LIMIT = 58 * 1024 * 1024


def dot_nn(a, b):
    return lax.dot_general(a, b, (((1,), (0,)), ((), ())), preferred_element_type=f32)


def dot_nt(a, b):
    return lax.dot_general(a, b, (((1,), (1,)), ((), ())), preferred_element_type=f32)


def dot_tn(a, b):
    return lax.dot_general(a, b, (((0,), (0,)), ((), ())), preferred_element_type=f32)


def params(limit=VMEM_LIMIT):
    return pltpu.CompilerParams(dimension_semantics=("arbitrary",), vmem_limit_bytes=limit)


def lane_orders(count):
    bits = []
    bit = 2
    while bit < count:
        bits.append(bit)
        bit *= 2
    return (bits[::-1] + [1], bits + [1])


def slots_of(order):
    slots = [0]
    for bit in order:
        slots = slots + [s ^ bit for s in slots]
    return slots


def swap(value, bit, count):
    return lax.ppermute(value, "ctx", [(i, i ^ bit) for i in range(count)])


def plane_gather(first, second, count):
    order_a, order_b = lane_orders(count)
    a, b = (first[None], second[None])
    for bit_a, bit_b in zip(order_a, order_b):
        got_a, got_b = (swap(a, bit_a, count), swap(b, bit_b, count))
        a = jnp.concatenate([a, got_a], axis=0)
        b = jnp.concatenate([b, got_b], axis=0)
    return a, b


def plane_scatter(a, b, count):
    order_a, order_b = lane_orders(count)
    for bit_a, bit_b in zip(order_a[::-1], order_b[::-1]):
        half = a.shape[0] // 2
        got_a, got_b = (swap(a[half:], bit_a, count), swap(b[half:], bit_b, count))
        a = a[:half].astype(f32) + got_a.astype(f32)
        b = b[:half].astype(f32) + got_b.astype(f32)
        if half > 1:
            a, b = (a.astype(bf16), b.astype(bf16))
    return a[0], b[0]


def qkv_kernel(slot_ref, xa, xb, gain, wt, cos, sin, ain_o, qt_o, k_o, kt_o, v_o, vt_o):
    x = jnp.concatenate([xa[0], xb[0]], axis=0).astype(f32)
    inv = lax.rsqrt(jnp.mean(x * x, axis=-1, keepdims=True) + EPS)
    a = (x * inv * gain[...]).astype(bf16)
    ain_o[0] = a
    y = dot_nt(wt[...], a)
    c, s = (cos[0], sin[0])

    def turn(rows):
        lo, hi = (rows[:HALF], rows[HALF:])
        return jnp.concatenate([lo * c - hi * s, hi * c + lo * s], axis=0)

    for h in range(GROUP):
        q = turn(y[h * HD : (h + 1) * HD]).astype(bf16).astype(f32) * SCORE_SCALE
        qt_o[0, h * HD : (h + 1) * HD, :] = q.astype(bf16)
    k = turn(y[QW : QW + HD])
    kt_o[0] = k.astype(bf16)
    k_o[0] = k.T.astype(bf16)
    v = y[QW + HD :]
    vt_o[0] = v.astype(bf16)
    v_o[0] = v.T.astype(bf16)


def heads_wide(rows):
    return jnp.concatenate([rows[h * HD : (h + 1) * HD] for h in range(GROUP)], axis=1)


def causal(shape, width):
    key = lax.broadcasted_iota(i32, shape, 0)
    query = lax.broadcasted_iota(i32, shape, 1)
    for _ in range(GROUP - 1):
        query = jnp.where(query >= width, query - width, query)
    return key <= query


def attn_fwd_kernel(qt, k, vt, of_o, ob_o, lse_o):
    a = pl.program_id(0)
    tok = qt.shape[2]
    q = heads_wide(qt[0])
    s = dot_nn(k[a], q)
    s = jnp.where(causal(s.shape, tok), s, NEG_FILL)
    m = jnp.max(s, axis=0, keepdims=True)
    p = jnp.exp(s - m)
    l = jnp.sum(p, axis=0, keepdims=True)
    o = dot_nn(vt[a], p.astype(bf16))

    def step(b, carry):
        m, l, o = carry
        s = dot_nn(k[b], q)
        new = jnp.maximum(m, jnp.max(s, axis=0, keepdims=True))
        p = jnp.exp(s - new)
        back = jnp.exp(m - new)
        l = l * back + jnp.sum(p, axis=0, keepdims=True)
        o = o * back + dot_nn(vt[b], p.astype(bf16))
        return (new, l, o)

    m, l, o = lax.fori_loop(0, a, step, (m, l, o))
    o = o / l
    lse_o[0] = m + jnp.log(l)
    for h in range(GROUP):
        part = o[:, h * tok : (h + 1) * tok]
        of_o[0, h * HD : (h + 1) * HD, :] = part
        ob_o[0, h * HD : (h + 1) * HD, :] = part.astype(bf16)


def attn_bwd_kernel(qt, dot_, of, lse, k, kt, v, cos, sin, dq_o, dk_o, dv_o, dk_s, dv_s):
    a = pl.program_id(0)
    tok = qt.shape[2]
    count = k.shape[0]
    q = heads_wide(qt[0])
    do = heads_wide(dot_[0])
    delta = jnp.sum(do.astype(f32) * heads_wide(of[0]), axis=0, keepdims=True)
    total = lse[0]

    def pair(b, mask):
        s = dot_nn(k[b], q)
        p = jnp.exp(s - total)
        if mask:
            p = jnp.where(causal(s.shape, tok), p, 0.0)
        dp = dot_nn(v[b], do)
        ds = (p * (dp - delta)).astype(bf16)
        return dot_nt(ds, q), dot_nt(p.astype(bf16), do), dot_nn(kt[b], ds)

    dk, dv, dq = pair(a, True)
    dk_s[a] = dk
    dv_s[a] = dv

    def step(b, dq):
        dk, dv, more = pair(b, False)
        dk_s[b] += dk
        dv_s[b] += dv
        return dq + more

    dq = lax.fori_loop(0, a, step, dq) * SCORE_SCALE

    def back(rows, c, s):
        lo, hi = (rows[:HALF], rows[HALF:])
        return jnp.concatenate([lo * c + hi * s, hi * c - lo * s], axis=0)

    for h in range(GROUP):
        dq_o[0, h * HD : (h + 1) * HD, :] = back(
            dq[:, h * tok : (h + 1) * tok], cos[a], sin[a]
        ).astype(bf16)

    @pl.when(a == count - 1)
    def _():
        @pl.loop(0, count)
        def _(b):
            dk_o[b] = back(dk_s[b].T, cos[b], sin[b]).astype(bf16)
            dv_o[b] = dv_s[b].T.astype(bf16)


def qkv_bwd_kernel(share, slot_ref, dq, dk, dv, ain, xa, xb, wt, da_o, db_o, gw_o, gg_o, acc, gacc):
    a = pl.program_id(0)
    d = jnp.concatenate([dq[0], dk[0], dv[0]], axis=0)
    part = dot_tn(d, wt[...]) * share
    x = jnp.concatenate([xa[0], xb[0]], axis=0).astype(f32)
    inv = lax.rsqrt(jnp.mean(x * x, axis=-1, keepdims=True) + EPS)
    half = xa.shape[1]
    da_o[0] = part[:half].astype(bf16)
    db_o[0] = part[half:].astype(bf16)

    @pl.when(a == 0)
    def _():
        acc[...] = jnp.zeros_like(acc)
        gacc[...] = jnp.zeros_like(gacc)

    acc[...] += dot_nn(d, ain[0])
    gacc[...] += jnp.sum(part * (x * inv), axis=0, keepdims=True)

    @pl.when(a == pl.num_programs(0) - 1)
    def _():
        width = gw_o.shape[2]
        for z in range(gw_o.shape[0]):
            gw_o[z] = acc[:, z * width : (z + 1) * width].astype(bf16)
        gg_o[...] = gacc[...]


def moe_kernel(second, which, *refs):
    xa, xb, ya, yb, router, code, weights = refs[:7]
    refs = refs[7:]
    if second:
        din_pa, din_pb, out_pa, out_pb = refs[:4]
        refs = refs[4:]
    din_a, din_b, out_a, out_b, grad_o, acc_g, acc_u, acc_d = refs
    i = pl.program_id(0)
    expert = which[0]
    x = jnp.concatenate([xa[0], xb[0]], axis=0)
    y = jnp.concatenate([ya[0], yb[0]], axis=0)
    shards, _, depth, ff = weights.shape
    width = shards * depth
    w_gate = weights[:, 0].reshape(width, ff)
    w_up = weights[:, 1].reshape(width, ff)
    w_down = weights[:, 2].reshape(width, ff)

    logits = dot_nt(x, router[...])
    named = code[0] > 0.5
    logits = jnp.where(named, logits, NEG_FILL)
    top = jnp.max(logits, axis=-1, keepdims=True)
    raised = jnp.where(named, jnp.exp(logits - top), 0.0)
    gates = raised / jnp.sum(raised, axis=-1, keepdims=True)
    mine = (lax.broadcasted_iota(i32, gates.shape, 1) == expert) & (code[0] > 1.5)
    weight = RESIDUAL_SCALE * jnp.sum(jnp.where(mine, gates, 0.0), axis=-1, keepdims=True)
    kept = RESIDUAL_SCALE * jnp.sum(jnp.where(mine, 1.0, 0.0), axis=-1, keepdims=True)

    gate_pre = dot_nn(x, w_gate)
    up_pre = dot_nn(x, w_up)
    back = dot_nn(y, w_down)
    sig = jax.nn.sigmoid(gate_pre)
    act = gate_pre * sig
    inner = act * up_pre
    gate_grad = kept * jnp.sum(inner * back, axis=-1, keepdims=True)
    inner_w = (inner * weight).astype(bf16)
    d_inner = back * weight
    d_gate = (d_inner * up_pre * sig * (1.0 + gate_pre * (1.0 - sig))).astype(bf16)
    d_up = (d_inner * act).astype(bf16)

    out = dot_nt(inner_w, w_down)
    din = dot_nt(d_gate, w_gate) + dot_nt(d_up, w_up)
    high = gate_grad.astype(bf16)
    low = (gate_grad - high.astype(f32)).astype(bf16)
    lane = lax.broadcasted_iota(i32, (x.shape[0], EXTRA), 1)
    side = jnp.where(lane == expert, high.astype(f32), 0.0) + jnp.where(
        lane == expert + LOW, low.astype(f32), 0.0
    )
    half = xa.shape[1]
    for part, din_o, out_o in ((slice(0, half), din_a, out_a), (slice(half, None), din_b, out_b)):
        d, o, s = (din[part], out[part], side[part])
        if second:
            din_p, out_p = (din_pa, out_pa) if din_o is din_a else (din_pb, out_pb)
            d = d + din_p[0, :, :width].astype(f32)
            s = s + din_p[0, :, width:].astype(f32)
            o = o + out_p[0].astype(f32)
        din_o[0, :, :width] = d.astype(bf16)
        din_o[0, :, width:] = s.astype(bf16)
        out_o[0] = o.astype(bf16)

    @pl.when(i == 0)
    def _():
        acc_g[...] = jnp.zeros_like(acc_g)
        acc_u[...] = jnp.zeros_like(acc_u)
        acc_d[...] = jnp.zeros_like(acc_d)

    acc_g[...] += dot_tn(x, d_gate)
    acc_u[...] += dot_tn(x, d_up)
    acc_d[...] += dot_tn(y, inner_w)

    @pl.when(i == pl.num_programs(0) - 1)
    def _():
        for z in range(shards):
            rows = slice(z * depth, (z + 1) * depth)
            grad_o[z, 0] = acc_g[rows, :].astype(bf16)
            grad_o[z, 1] = acc_u[rows, :].astype(bf16)
            grad_o[z, 2] = acc_d[rows, :].astype(bf16)


def place_kernel(slot_ref, a, b, out):
    half = a.shape[1]
    for z in range(half):
        out[z, 0] = a[0, z]
        out[half + z, 0] = b[0, z]


def whole(shape):
    zeros = (0,) * len(shape)
    return pl.BlockSpec(shape, lambda i, *refs: zeros)


def at_step(shape):
    zeros = (0,) * (len(shape) - 1)
    return pl.BlockSpec(shape, lambda i, *refs: (i,) + zeros)


def at_slot(shape, lane):
    zeros = (0,) * (len(shape) - 1)
    return pl.BlockSpec(shape, lambda i, slots: (slots[lane, i],) + zeros)


def shape_of(*dims, dtype=bf16):
    return jax.ShapeDtypeStruct(dims, dtype)


def shards(
    hidden,
    gain_attn,
    w_query,
    w_key,
    w_value,
    w_out,
    gain_ffn,
    router,
    routes,
    slot_order,
    w_gate,
    w_up,
    w_down,
    grad_out,
):
    tok, width = hidden.shape
    n = lax.axis_size("ctx")
    dp = lax.axis_size("dp")
    me = lax.axis_index("ctx")
    copies = n // KV
    rp = w_query.shape[0]
    slab = rp * n
    experts = router.shape[1]
    half = tok // 2
    ff = w_gate.shape[2]
    depth = w_gate.shape[1]
    order_a, order_b = lane_orders(n)
    slots_a, slots_b = (slots_of(order_a), slots_of(order_b))
    absolute = jnp.arange(n, dtype=i32)
    inverse_a = jnp.zeros((n,), i32).at[jnp.array(slots_a)].set(absolute)
    inverse_b = jnp.zeros((n,), i32).at[jnp.array(slots_b)].set(absolute)
    slot_at = jnp.stack([inverse_a[absolute ^ me], inverse_b[absolute ^ me]])
    block_a = jnp.array(slots_a, i32) ^ me
    block_b = jnp.array(slots_b, i32) ^ me

    by_head = jnp.concatenate(
        [
            w_query.reshape(rp, KV, QW),
            w_key.reshape(rp, KV, HD),
            w_value.reshape(rp, KV, HD),
        ],
        axis=2,
    ).transpose(1, 0, 2)
    extras = jnp.concatenate([gain_attn[:, None], gain_ffn[:, None], router], axis=1)
    send = jnp.concatenate(
        [
            jnp.repeat(by_head, copies, axis=0),
            jnp.broadcast_to(extras[None], (n,) + extras.shape),
        ],
        axis=2,
    )
    took = lax.all_to_all(send, "ctx", split_axis=0, concat_axis=0, tiled=True)
    side = took.shape[2]
    pad = -(side + rp * dp) % 16
    pack = jnp.concatenate(
        [took.reshape(slab, side).T, w_out.reshape(rp * dp, slab)], axis=0
    )
    packs = lax.all_gather(pack, "dp", axis=0)
    wt = packs[:, :QKV].transpose(1, 0, 2).reshape(QKV, width)
    gains = packs[:, QKV : QKV + 2].transpose(1, 0, 2).reshape(2, width).astype(f32)
    router_t = packs[:, QKV + 2 : side].transpose(1, 0, 2).reshape(experts, width)
    gain_a, gain_f = (gains[0:1], gains[1:2])
    out_rows = packs[:, side:].reshape(dp, rp, width)

    expert_w = [
        lax.all_gather(jnp.stack([w_gate[e], w_up[e], w_down[e]]), "dp", axis=0)
        for e in range(w_gate.shape[0])
    ]

    xa, xb = plane_gather(hidden[:half], hidden[half:], n)
    ya, yb = plane_gather(grad_out[:half], grad_out[half:], n)
    oa, ob = plane_gather(out_rows[: dp // 2], out_rows[dp // 2 :], n)

    table = lax.all_gather(
        jnp.concatenate([routes, slot_order.reshape(tok, 1)], axis=1), "ctx", axis=0
    )
    names = jnp.arange(experts, dtype=i32)
    named = jnp.sum(
        (table[:, :, :TOP, None] == names).astype(f32), axis=2
    )
    ranks = table[:, :, TOP]
    before = (ranks[:, None, :] < ranks[:, :, None]).astype(bf16)
    local = jnp.einsum("btu,bue->bte", before, named.astype(bf16), preferred_element_type=f32)
    load = jnp.sum(named, axis=1)
    earlier = jnp.cumsum(load, axis=0) - load
    slot = local + earlier[:, None, :]
    code_all = named * (1.0 + (slot < CAP).astype(f32))
    code = jnp.concatenate([code_all[block_a, :half], code_all[block_b, half:]], axis=1)
    code_mine = code_all[me]

    exponents = jnp.arange(HALF, dtype=f32) * (2.0 / HD)
    inverse_freq = jnp.power(10000.0, -exponents)
    positions = jnp.arange(n * tok, dtype=f32).reshape(n, 1, tok)
    angles = positions * inverse_freq[None, :, None]
    cos, sin = (jnp.cos(angles), jnp.sin(angles))

    grid_spec = pltpu.PrefetchScalarGridSpec

    ain, qt, k, kt, v, vt = pl.pallas_call(
        qkv_kernel,
        grid_spec=grid_spec(
            num_scalar_prefetch=1,
            grid=(n,),
            in_specs=[
                at_slot((1, half, width), 0),
                at_slot((1, half, width), 1),
                whole((1, width)),
                whole((QKV, width)),
                at_step((1, HALF, tok)),
                at_step((1, HALF, tok)),
            ],
            out_specs=[
                at_step((1, tok, width)),
                at_step((1, QW, tok)),
                at_step((1, tok, HD)),
                at_step((1, HD, tok)),
                at_step((1, tok, HD)),
                at_step((1, HD, tok)),
            ],
        ),
        out_shape=[
            shape_of(n, tok, width),
            shape_of(n, QW, tok),
            shape_of(n, tok, HD),
            shape_of(n, HD, tok),
            shape_of(n, tok, HD),
            shape_of(n, HD, tok),
        ],
        compiler_params=params(32 * 1024 * 1024),
        name="qkv",
    )(slot_at, xa, xb, gain_a, wt, cos, sin)

    of, attn_t, lse = pl.pallas_call(
        attn_fwd_kernel,
        grid=(n,),
        in_specs=[at_step((1, QW, tok)), whole((n, tok, HD)), whole((n, HD, tok))],
        out_specs=[
            at_step((1, QW, tok)),
            at_step((1, QW, tok)),
            at_step((1, 1, GROUP * tok)),
        ],
        out_shape=[
            shape_of(n, QW, tok, dtype=f32),
            shape_of(n, QW, tok),
            shape_of(n, 1, GROUP * tok, dtype=f32),
        ],
        compiler_params=params(32 * 1024 * 1024),
        name="attn_fwd",
    )(qt, k, vt)

    attn_b = lax.all_to_all(attn_t, "ctx", split_axis=0, concat_axis=0, tiled=True)
    attn_b = attn_b[::copies].reshape(KV * QW, tok)

    w_out_all = pl.pallas_call(
        place_kernel,
        grid_spec=grid_spec(
            num_scalar_prefetch=1,
            grid=(n,),
            in_specs=[
                at_slot((1, dp // 2, rp, width), 0),
                at_slot((1, dp // 2, rp, width), 1),
            ],
            out_specs=pl.BlockSpec((dp, 1, rp, width), lambda i, slots: (0, i, 0, 0)),
        ),
        out_shape=shape_of(dp, n, rp, width),
        compiler_params=params(16 * 1024 * 1024),
        name="place",
    )(slot_at, oa, ob).reshape(KV * QW, width)

    hidden_f = hidden.astype(f32)
    branch = dot_tn(attn_b, w_out_all)
    resid = hidden_f + RESIDUAL_SCALE * branch
    inv_ffn = lax.rsqrt(jnp.mean(resid * resid, axis=-1, keepdims=True) + EPS)
    normed_f = resid * inv_ffn
    moe_in = (normed_f * gain_f).astype(bf16)

    ma, mb = plane_gather(moe_in[:half], moe_in[half:], n)

    side_w = width + EXTRA
    din = None
    expert_grads = []
    for e, gathered in enumerate(expert_w):
        operands = [ma, mb, ya, yb, router_t, code, gathered]
        in_specs = [at_step((1, half, width))] * 4 + [
            whole((experts, width)),
            at_step((1, tok, experts)),
            whole((dp, 3, depth, ff)),
        ]
        if din is not None:
            operands += [din[0], din[1], din[2], din[3]]
            in_specs += [at_step((1, half, side_w))] * 2 + [at_step((1, half, width))] * 2
        *din, grads = pl.pallas_call(
            functools.partial(moe_kernel, din is not None),
            grid_spec=grid_spec(
                num_scalar_prefetch=1,
                grid=(n,),
                in_specs=in_specs,
                out_specs=[at_step((1, half, side_w))] * 2
                + [at_step((1, half, width))] * 2
                + [whole((dp, 3, depth, ff))],
                scratch_shapes=[pltpu.VMEM((width, ff), f32)] * 3,
            ),
            out_shape=[shape_of(n, half, side_w)] * 2
            + [shape_of(n, half, width)] * 2
            + [shape_of(dp, 3, depth, ff)],
            compiler_params=params(),
            name="moe",
        )((me * len(expert_w) + e).reshape(1).astype(i32), *operands)
        expert_grads.append(
            lax.psum_scatter(grads, "dp", scatter_dimension=0, tiled=True)[0].astype(f32)
        )

    back_a, back_b = plane_scatter(din[0], din[1], n)
    back = jnp.concatenate([back_a, back_b], axis=0)
    mix_a, mix_b = plane_scatter(din[2], din[3], n)
    output = (resid + jnp.concatenate([mix_a, mix_b], axis=0)).astype(bf16)

    grad_f = grad_out.astype(f32)
    chosen = code_mine > 0.5
    logits = jnp.where(chosen, dot_nt(moe_in, router_t), NEG_FILL)
    gates = jnp.where(chosen, jax.nn.softmax(logits, axis=-1), 0.0)
    gate_grad = (
        back[:, width : width + experts] + back[:, width + LOW : width + LOW + experts]
    )
    logit_grad = gates * (gate_grad - jnp.sum(gates * gate_grad, axis=-1, keepdims=True))
    dlogits = logit_grad.astype(bf16)
    d_router = dot_tn(dlogits, moe_in)
    d_moe_in = back[:, :width] + dot_nn(dlogits, router_t)
    d_gain_ffn = jnp.sum(d_moe_in * normed_f, axis=0, keepdims=True)
    d_normed_f = d_moe_in * gain_f
    d_resid = grad_f + inv_ffn * (
        d_normed_f - normed_f * jnp.mean(d_normed_f * normed_f, axis=-1, keepdims=True)
    )
    d_branch = (RESIDUAL_SCALE * d_resid).astype(bf16)
    d_attn = dot_nt(w_out_all, d_branch).astype(bf16).reshape(KV, QW, tok)
    d_heads = lax.all_to_all(
        jnp.repeat(d_attn, copies, axis=0), "ctx", split_axis=0, concat_axis=0, tiled=True
    )

    d_wout = dot_nn(attn_b, d_branch).astype(bf16).reshape(dp, n, rp, width)
    wout_a, wout_b = plane_scatter(
        d_wout[: dp // 2].transpose(1, 0, 2, 3)[block_a],
        d_wout[dp // 2 :].transpose(1, 0, 2, 3)[block_b],
        n,
    )
    d_wout = jnp.concatenate([wout_a, wout_b], axis=0).astype(bf16)

    dq, dk, dv = pl.pallas_call(
        attn_bwd_kernel,
        grid=(n,),
        in_specs=[
            at_step((1, QW, tok)),
            at_step((1, QW, tok)),
            at_step((1, QW, tok)),
            at_step((1, 1, GROUP * tok)),
            whole((n, tok, HD)),
            whole((n, HD, tok)),
            whole((n, tok, HD)),
            whole((n, HALF, tok)),
            whole((n, HALF, tok)),
        ],
        out_specs=[at_step((1, QW, tok)), whole((n, HD, tok)), whole((n, HD, tok))],
        out_shape=[shape_of(n, QW, tok), shape_of(n, HD, tok), shape_of(n, HD, tok)],
        scratch_shapes=[pltpu.VMEM((n, tok, HD), f32), pltpu.VMEM((n, tok, HD), f32)],
        compiler_params=params(40 * 1024 * 1024),
        name="attn_bwd",
    )(qt, d_heads, of, lse, k, kt, v, cos, sin)

    da, db, gw, d_gain_attn = pl.pallas_call(
        functools.partial(qkv_bwd_kernel, 1.0 / copies),
        grid_spec=grid_spec(
            num_scalar_prefetch=1,
            grid=(n,),
            in_specs=[
                at_step((1, QW, tok)),
                at_step((1, HD, tok)),
                at_step((1, HD, tok)),
                at_step((1, tok, width)),
                at_slot((1, half, width), 0),
                at_slot((1, half, width), 1),
                whole((QKV, width)),
            ],
            out_specs=[
                at_slot((1, half, width), 0),
                at_slot((1, half, width), 1),
                whole((dp, QKV, slab)),
                whole((1, width)),
            ],
            scratch_shapes=[pltpu.VMEM((QKV, width), f32), pltpu.VMEM((1, width), f32)],
        ),
        out_shape=[
            shape_of(n, half, width),
            shape_of(n, half, width),
            shape_of(dp, QKV, slab),
            shape_of(1, width, dtype=f32),
        ],
        compiler_params=params(40 * 1024 * 1024),
        name="qkv_bwd",
    )(slot_at, dq, dk, dv, ain, xa, xb, wt)

    rest = jnp.concatenate([d_gain_attn, d_gain_ffn, d_router], axis=0).astype(bf16)
    grads = jnp.concatenate(
        [
            gw,
            rest.reshape(2 + experts, dp, slab).transpose(1, 0, 2),
            d_wout.reshape(dp, rp * dp, slab),
            jnp.zeros((dp, pad, slab), bf16),
        ],
        axis=1,
    )
    own = lax.psum_scatter(grads, "dp", scatter_dimension=0, tiled=True)[0]
    given = lax.all_to_all(
        own[:side].T.reshape(n, rp, side), "ctx", split_axis=0, concat_axis=0, tiled=True
    ).astype(f32)
    heads = given[::copies].transpose(1, 0, 2)
    grad_query = heads[:, :, :QW].reshape(rp, KV * QW)
    grad_key = heads[:, :, QW : QW + HD].reshape(rp, KV * HD)
    grad_value = heads[:, :, QW + HD : QKV].reshape(rp, KV * HD)
    sums = jnp.sum(given[:, :, QKV:], axis=0)
    grad_out_proj = own[side : side + rp * dp].reshape(rp, width).astype(f32)

    in_a, in_b = plane_scatter(da, db, n)
    d_attn_in = jnp.concatenate([in_a, in_b], axis=0)
    inv_attn = lax.rsqrt(jnp.mean(hidden_f * hidden_f, axis=-1, keepdims=True) + EPS)
    normed_a = hidden_f * inv_attn
    d_normed_a = d_attn_in * gain_a
    d_hidden = d_resid + inv_attn * (
        d_normed_a - normed_a * jnp.mean(d_normed_a * normed_a, axis=-1, keepdims=True)
    )
    expert_grads = jnp.stack(expert_grads)
    return (
        output,
        d_hidden,
        sums[:, 0],
        grad_query,
        grad_key,
        grad_value,
        grad_out_proj,
        sums[:, 1],
        sums[:, 2:],
        expert_grads[:, 0],
        expert_grads[:, 1],
        expert_grads[:, 2],
    )


def solution(mesh):
    rows = P(("dp", "ctx"), None)
    flat = P(("dp", "ctx"))
    expert = P("ctx", "dp", None)
    return jax.shard_map(
        shards,
        mesh=mesh,
        in_specs=(
            rows,
            flat,
            rows,
            rows,
            rows,
            rows,
            flat,
            rows,
            rows,
            rows,
            expert,
            expert,
            expert,
            rows,
        ),
        out_specs=(
            rows,
            rows,
            flat,
            rows,
            rows,
            rows,
            rows,
            flat,
            rows,
            expert,
            expert,
            expert,
        ),
        check_vma=False,
    )
```

time: 1580 us -> 738 us (0.47)
  waiting for transfers between devices: 858 us -> 319 us
  matrix products: 166 us -> 14.2 us
  Pallas kernels: 0 us -> 150 us
  blocking collectives: 133 us -> 16.2 us
  starting transfers between devices: 163 us -> 50.9 us
  local copies, waits for them, and re-layouts: 165 us -> 81.7 us
    reduce_scatter x7 -> x3, waiting for transfers between devices: 407 us -> 150 us  [the longest x2 150 us: shards(): lax.psum_scatter(grads, 'dp', scatter_dimension=0, tiled=True)[0]]
    all_gather x9 -> x3, waiting for transfers between devices: 212 us -> 0.02 us  [the longest x2 0.02 us: shards(): lax.all_gather(jnp.stack([w_gate[e], w_up[e], w_down[e]]), 'dp', axis=0)]
    all_to_all x4, waiting for transfers between devices: 207 us -> 19 us  [the longest x1 6.97 us: shards(): took = lax.all_to_all(send, 'ctx', split_axis=0, concat_axis=0, tiled=True)]
    dot_general x34 -> x7, matrix products: 165 us -> 14.2 us  [the longest x2 5.05 us: dot_nt(): lax.dot_general(a, b, (((1,), (1,)), ((), ())), preferred_element_type=f32)]
    pallas_call x0 -> x7, Pallas kernels: none -> 150 us  [the longest x2 85.8 us: shards(): pl.pallas_call(functools.partial(moe_kernel, din is not None), grid_spec=...]
    ppermute x24 -> x48, waiting for transfers between devices: 26.9 us -> 148 us  [swap(): return lax.ppermute(value, 'ctx', [(i, i ^ bit) for i in range(count)])]
    ppermute x24 -> x48, starting transfers between devices: 142 us -> 33.9 us  [swap(): return lax.ppermute(value, 'ctx', [(i, i ^ bit) for i in range(count)])]
    unnamed x3 -> x0, blocking collectives: 92.7 us -> none
  transfers between devices with their start and end apart: 45 -> 58, of which waited for: 19 -> 28; matrix products, arithmetic and copies ran while one was open for 24% -> 18% of each run, Pallas kernels for 0% -> 15%
where the time goes in v1:
time: 738 us; the launch traced here: 729 us
  waiting for transfers between devices  319 us (43%)
  Pallas kernels  150 us (20%)
  local copies, waits for them, and re-layouts  81.7 us (11%)
  other arithmetic  80.9 us (11%)
  starting transfers between devices  50.9 us (7%)
  blocking collectives  16.2 us (2%)
  between operations  15.9 us (2%)
  matrix products  14.2 us (2%)
    reduce_scatter x2, waiting for transfers between devices, shards(): lax.psum_scatter(grads, 'dp', scatter_dimension=0, tiled=True)[0]  150 us
    ppermute x48, waiting for transfers between devices, swap(): return lax.ppermute(value, 'ctx', [(i, i ^ bit) for i in range(count)])  148 us
    pallas_call x2, Pallas kernels, shards(): pl.pallas_call(functools.partial(moe_kernel, din is not None), grid_spec=...  85.8 us
    ppermute x48, starting transfers between devices, swap(): return lax.ppermute(value, 'ctx', [(i, i ^ bit) for i in range(count)])  33.9 us
    concatenate x12, other arithmetic, plane_gather(): a = jnp.concatenate([a, got_a], axis=0)  24.8 us
    pallas_call x1, Pallas kernels, shards(): pl.pallas_call(attn_bwd_kernel, grid=(n,), in_specs=[at_step((1, QW, tok)...  23.8 us
    concatenate x12, other arithmetic, plane_gather(): b = jnp.concatenate([b, got_b], axis=0)  20.3 us
    pallas_call x1, Pallas kernels, shards(): pl.pallas_call(attn_fwd_kernel, grid=(n,), in_specs=[at_step((1, QW, tok)...  19.6 us
  transfers between devices with their start and end apart: 58, of which 28 were waited for; matrix products, arithmetic and copies ran while one was open for 18% of the time, Pallas kernels for 15%

profile of v1, /device:TPU:0, one launch (start us, length us, event | category | flops | bytes accessed | tf_op | source)
XLA Modules:
  0.0 728.6 jit_solution(14498391257386471022)
XLA Ops:
  12.1 5.2 all-to-all-start
  17.6 7.0 all-to-all-done
  36.1 16.2 %all-gather.1 = s32[2048,9]{0,1:T(8,128)S(1)} all-gather(s32[256,9]{0,1:T(8,128)S(1)} %pad_add_fusion), channel_id=3, replica_groups=mesh['dp'=4,'ctx'=8] {'ctx'}, dimensions={0}, use_global_device_ids=true | all-gather | bytes 82944 | tf_op jit(solution)/shard_map/all_gather | solution.py:408
  58.1 14.6 %collective-permute-done.4 = bf16[2,128,1536]{2,1,0:T(8,128)(2,1)S(1)} collective-permute-done((bf16[2,128,1536]{2,1,0:T(8,128)(2,1)S(1)}, bf16[2,128,1536]{2,1,0:T(8,128)(2,1)S(1)}, u32[]{:S(2)}, u32[]{:S(2)}) %collective-permute-start.4) | collective-permute-done | bytes 786464 | tf_op jit(solution)/shard_map/ppermute | solution.py:67
  89.3 4.1 collective-permute-done.9
  95.1 10.3 %collective-permute-done.7 = bf16[2,2,48,1536]{3,2,1,0:T(8,128)(2,1)S(1)} collective-permute-done((bf16[2,2,48,1536]{3,2,1,0:T(8,128)(2,1)S(1)}, bf16[2,2,48,1536]{3,2,1,0:T(8,128)(2,1)S(1)}, u32[]{:S(2)}, u32[]{:S(2)}) %collective-permute-start.7) | collective-permute-done | bytes 589856 | tf_op jit(solution)/shard_map/ppermute | solution.py:67
  111.6 2.9 pad_maximum_fusion.xa
  114.6 6.4 qkv.1
  123.5 19.6 %attn_fwd.1 = (f32[8,192,256]{2,1,0:T(8,128)S(1)}, bf16[8,192,256]{2,1,0:T(8,128)(2,1)}, f32[8,1,768]{2,1,0:T(1,128)S(1)}) custom-call(bf16[8,192,256]{2,1,0:T(8,128)(2,1)S(1)} %get-tuple-element.38.qt, bf16[8,256,64]{2,1,0:T(8,128)(2,1)S(1)} %get-tuple-element.39.k, bf16[8,64,256]{2,1,0:T(8,128)(2,1)S(1)} %get-tuple-element.40.vt), custom_call_target="tpu_custom_call" | custom-call | tf_op jit(solution)/shard_map/attn_fwd/pallas_call | solution.py:467
  145.2 4.7 all-to-all-start.1
  162.9 4.4 multiply_reduce_fusion.2
  180.6 6.3 collective-permute-done.15
  189.6 2.6 pad_maximum_fusion.12
  192.3 7.7 %collective-permute-done.12 = bf16[1,128,1536]{2,1,0:T(8,128)(2,1)S(1)} collective-permute-done((bf16[1,128,1536]{2,1,0:T(8,128)(2,1)}, bf16[1,128,1536]{2,1,0:T(8,128)(2,1)S(1)}, u32[]{:S(2)}, u32[]{:S(2)}) %collective-permute-start.12) | collective-permute-done | bytes 393248 | tf_op jit(solution)/shard_map/ppermute | solution.py:67
  205.4 10.3 %collective-permute-done.16 = bf16[2,128,1536]{2,1,0:T(8,128)(2,1)S(1)} collective-permute-done((bf16[2,128,1536]{2,1,0:T(8,128)(2,1)S(1)}, bf16[2,128,1536]{2,1,0:T(8,128)(2,1)S(1)}, u32[]{:S(2)}, u32[]{:S(2)}) %collective-permute-start.16) | collective-permute-done | bytes 786464 | tf_op jit(solution)/shard_map/ppermute | solution.py:67
  215.6 2.7 pad_maximum_fusion.11
  225.3 3.1 pad_maximum_fusion.4.refs_2_
  228.4 3.1 pad_maximum_fusion.5.refs_3_
  231.6 3.1 pad_maximum_fusion.3.refs_1_
  234.7 2.8 pad_maximum_fusion.2.refs_0_
  237.5 42.4 %moe.2 = (bf16[8,128,1664]{2,1,0:T(8,128)(2,1)}, bf16[8,128,1664]{2,1,0:T(8,128)(2,1)}, bf16[8,128,1536]{2,1,0:T(8,128)(2,1)}, bf16[8,128,1536]{2,1,0:T(8,128)(2,1)}, bf16[4,3,384,512]{3,2,1,0:T(8,128)(2,1)}) custom-call(s32[1]{0:T(128)} %bitcast.25.which, bf16[8,128,1536]{2,1,0:T(8,128)(2,1)} %pad_maximum_fusion.2.refs_0_, ...), custom_call_target="tpu_custom_call" | custom-call | tf_op jit(solution)/shard_map/moe/pallas_call | solution.py:526
  280.0 43.4 %moe.3 = (bf16[8,128,1664]{2,1,0:T(8,128)(2,1)}, bf16[8,128,1664]{2,1,0:T(8,128)(2,1)}, bf16[8,128,1536]{2,1,0:T(8,128)(2,1)}, bf16[8,128,1536]{2,1,0:T(8,128)(2,1)}, bf16[4,3,384,512]{3,2,1,0:T(8,128)(2,1)}) custom-call(s32[1]{0:T(128)} %bitcast.16.which, bf16[8,128,1536]{2,1,0:T(8,128)(2,1)} %pad_maximum_fusion.2.refs_0_, ...), custom_call_target="tpu_custom_call" | custom-call | tf_op jit(solution)/shard_map/moe/pallas_call | solution.py:526
  323.4 2.8 slice.300
  326.3 2.7 slice.306
  345.7 11.5 %collective-permute-done.25 = bf16[2,128,1536]{2,1,0:T(8,128)(2,1)S(1)} collective-permute-done((bf16[2,128,1536]{2,1,0:T(8,128)(2,1)S(1)}, bf16[2,128,1536]{2,1,0:T(8,128)(2,1)S(1)}, u32[]{:S(2)}, u32[]{:S(2)}) %collective-permute-start.25) | collective-permute-done | bytes 786464 | tf_op jit(solution)/shard_map/ppermute | solution.py:67
  361.6 13.8 %collective-permute-done.31 = bf16[2,128,1664]{2,1,0:T(8,128)(2,1)S(1)} collective-permute-done((bf16[2,128,1664]{2,1,0:T(8,128)(2,1)S(1)}, bf16[2,128,1664]{2,1,0:T(8,128)(2,1)S(1)}, u32[]{:S(2)}, u32[]{:S(2)}) %collective-permute-start.31) | collective-permute-done | bytes 852000 | tf_op jit(solution)/shard_map/ppermute | solution.py:67
  379.9 6.4 collective-permute-done.26
  386.5 8.3 %collective-permute-done.32 = bf16[1,128,1664]{2,1,0:T(8,128)(2,1)S(1)} collective-permute-done((bf16[1,128,1664]{2,1,0:T(8,128)(2,1)S(1)}, bf16[1,128,1664]{2,1,0:T(8,128)(2,1)S(1)}, u32[]{:S(2)}, u32[]{:S(2)}) %collective-permute-start.32) | collective-permute-done | bytes 426016 | tf_op jit(solution)/shard_map/ppermute | solution.py:67
  405.1 3.8 gather_fusion.4
  411.4 4.6 convolution_convert_fusion.1
  416.1 3.5 all-to-all-start.2
  419.7 3.8 gather_fusion.5
  427.6 4.6 all-to-all-done.2.dot_
  433.6 23.8 %attn_bwd.1 = (bf16[8,192,256]{2,1,0:T(8,128)(2,1)S(1)}, bf16[8,64,256]{2,1,0:T(8,128)(2,1)S(1)}, bf16[8,64,256]{2,1,0:T(8,128)(2,1)S(1)}) custom-call(bf16[8,192,256]{2,1,0:T(8,128)(2,1)S(1)} %copy-done.8, bf16[8,192,256]{2,1,0:T(8,128)(2,1)S(1)} %all-to-all-done.2.dot_, f32[8,192,256]{2,1,0:T(8,128)S(1)} %copy-done.12, ...), custom_call_target="tpu_custom_call" | custom-call | tf_op jit(solution)/shard_map/attn_bwd/pallas_call | solution.py:582
  457.4 12.7 %qkv_bwd.1 = (bf16[8,128,1536]{2,1,0:T(8,128)(2,1)S(1)}, bf16[8,128,1536]{2,1,0:T(8,128)(2,1)S(1)}, bf16[4,320,384]{2,1,0:T(8,128)(2,1)S(1)}, f32[1,1536]{1,0:T(1,128)S(1)}) custom-call(s32[2,8]{1,0:T(2,128)S(1)} %pad_add_fusion.1.slot_ref, bf16[8,192,256]{2,1,0:T(8,128)(2,1)S(1)} %get-tuple-element.54.dq, bf16[8,64,256]{2,1,0:T(8,128)(2,1)S(1)} %get-tuple-element.55.dk, ...), custom_call_target="tpu_custom_call" | custom-call | tf_op jit(solution)/shard_map/qkv_bwd/pallas_call | solution.py:603
  471.1 2.6 add_convert_fusion.7
  476.8 11.2 %collective-permute-done.43 = bf16[2,2,48,1536]{3,2,1,0:T(8,128)(2,1)S(1)} collective-permute-done((bf16[2,2,48,1536]{3,2,1,0:T(8,128)(2,1)S(1)}, bf16[2,2,48,1536]{3,2,1,0:T(8,128)(2,1)S(1)}, u32[]{:S(2)}, u32[]{:S(2)}) %collective-permute-start.43) | collective-permute-done | bytes 589856 | tf_op jit(solution)/shard_map/ppermute | solution.py:67
  488.6 3.7 collective-permute-done.46
  494.0 3.4 collective-permute-done.44
  498.4 2.6 collective-permute-done.47
  503.1 3.0 maximum_maximum_fusion
  509.5 2.7 collective-permute-done.36
  517.0 16.6 %collective-permute-done.37 = bf16[2,128,1536]{2,1,0:T(8,128)(2,1)} collective-permute-done((bf16[2,128,1536]{2,1,0:T(8,128)(2,1)}, bf16[2,128,1536]{2,1,0:T(8,128)(2,1)}, u32[]{:S(2)}, u32[]{:S(2)}) %collective-permute-start.37) | collective-permute-done | bytes 786464 | tf_op jit(solution)/shard_map/ppermute | solution.py:67
  536.8 8.7 %collective-permute-done.38 = bf16[1,128,1536]{2,1,0:T(8,128)(2,1)S(1)} collective-permute-done((bf16[1,128,1536]{2,1,0:T(8,128)(2,1)S(1)}, bf16[1,128,1536]{2,1,0:T(8,128)(2,1)S(1)}, u32[]{:S(2)}, u32[]{:S(2)}) %collective-permute-start.38) | collective-permute-done | bytes 393248 | tf_op jit(solution)/shard_map/ppermute | solution.py:67
  551.4 3.4 all-to-all-start.3
  556.6 5.5 all-to-all-done.3
  566.6 62.5 %reduce-scatter.8.cloned.1.call-done = bf16[1,3,384,512]{3,2,1,0:T(8,128)(2,1)} async-done(((bf16[4,3,384,512]{3,2,1,0:T(8,128)(2,1)}), bf16[1,3,384,512]{3,2,1,0:T(8,128)(2,1)}) %reduce-scatter.8.cloned.1.call-update) | async-done | bytes 1179664 | tf_op jit(solution)/shard_map/reduce_scatter | solution.py:544
  629.1 88.0 %reduce-scatter.6.cloned.1.call-done = bf16[1,3,384,512]{3,2,1,0:T(8,128)(2,1)} async-done(((bf16[4,3,384,512]{3,2,1,0:T(8,128)(2,1)}), bf16[1,3,384,512]{3,2,1,0:T(8,128)(2,1)}) %reduce-scatter.6.cloned.1.call-update) | async-done | bytes 1179664 | tf_op jit(solution)/shard_map/reduce_scatter | solution.py:544
  (423 shorter events, 173.6 us)
Async XLA Ops:
  12.1 12.5 %all-to-all-start = ((bf16[8,48,338]{2,1,0:T(8,128)(2,1)}), bf16[8,48,338]{2,1,0:T(8,128)(2,1)S(1)}, u32[]{:S(2)}, u32[]{:S(2)}) async-start(bf16[8,48,338]{2,1,0:T(8,128)(2,1)} %pad_maximum_fusion.27), calls=%async_computation | async-start | bytes 589824 | tf_op jit(solution)/shard_map/all_to_all | solution.py:386
  17.3 56.8 %all-gather.13.cloned.1.call-start = ((), (), s32[]{:S(2)}) async-start(), calls=%async_computation.12 | async-start | bytes 2058240 | tf_op jit(solution)/shard_map/all_gather | solution.py:392
  25.7 211.8 %all-gather.11.cloned.1.call-start = ((), (), s32[]{:S(2)}) async-start(), calls=%async_computation.11 | async-start | bytes 5898240 | tf_op jit(solution)/shard_map/all_gather | solution.py:400
  28.7 251.3 %all-gather.9.cloned.1.call-start = ((), (), s32[]{:S(2)}) async-start(), calls=%async_computation.10 | async-start | bytes 5898240 | tf_op jit(solution)/shard_map/all_gather | solution.py:400
  28.9 23.8 %collective-permute-start.3 = (bf16[1,128,1536]{2,1,0:T(8,128)(2,1)S(1)}, bf16[1,128,1536]{2,1,0:T(8,128)(2,1)S(1)}, u32[]{:S(2)}, u32[]{:S(2)}) collective-permute-start(bf16[1,128,1536]{2,1,0:T(8,128)(2,1)S(1)} %get-tuple-element.145), channel_id=1, source_target_pairs={{0,2},{1,3},{2,0},{3,1},{4,6},{5,7},{6,4},{7,5},{8,10},{9,11},{10,... | collective-permute-start | bytes 1179656 | tf_op jit(solution)/shard_map/ppermute | solution.py:67
  29.6 25.8 %collective-permute-start = (bf16[1,128,1536]{2,1,0:T(8,128)(2,1)S(1)}, bf16[1,128,1536]{2,1,0:T(8,128)(2,1)S(1)}, u32[]{:S(2)}, u32[]{:S(2)}) collective-permute-start(bf16[1,128,1536]{2,1,0:T(8,128)(2,1)S(1)} %get-tuple-element.146), channel_id=1, source_target_pairs={{0,4},{1,5},{2,6},{3,7},{4,0},{5,1},{6,2},{7,3},{8,12},{9,13},{10,... | collective-permute-start | bytes 1179656 | tf_op jit(solution)/shard_map/ppermute | solution.py:67
  32.0 117.8 %collective-permute-start.18 = (bf16[1,128,1536]{2,1,0:T(8,128)(2,1)}, bf16[1,128,1536]{2,1,0:T(8,128)(2,1)}, u32[]{:S(2)}, u32[]{:S(2)}) collective-permute-start(bf16[1,128,1536]{2,1,0:T(8,128)(2,1)} %get-tuple-element.142), channel_id=1, source_target_pairs={{0,4},{1,5},{2,6},{3,7},{4,0},{5,1},{6,2},{7,3},{8,12},{9,13},{10,... | collective-permute-start | bytes 1179656 | tf_op jit(solution)/shard_map/ppermute | solution.py:67
  52.8 19.9 %collective-permute-start.4 = (bf16[2,128,1536]{2,1,0:T(8,128)(2,1)S(1)}, bf16[2,128,1536]{2,1,0:T(8,128)(2,1)S(1)}, u32[]{:S(2)}, u32[]{:S(2)}) collective-permute-start(bf16[2,128,1536]{2,1,0:T(8,128)(2,1)S(1)} %pad_maximum_fusion.19), channel_id=1, source_target_pairs={{0,4},{1,5},{2,6},{3,7},{4,0},{5,1},{6,2},{7,3},{8,12},{9,13},{10,... | collective-permute-start | bytes 2359304 | tf_op jit(solution)/shard_map/ppermute | solution.py:67
  56.4 22.3 %collective-permute-start.1 = (bf16[2,128,1536]{2,1,0:T(8,128)(2,1)}, bf16[2,128,1536]{2,1,0:T(8,128)(2,1)}, u32[]{:S(2)}, u32[]{:S(2)}) collective-permute-start(bf16[2,128,1536]{2,1,0:T(8,128)(2,1)} %pad_maximum_fusion.18), channel_id=1, source_target_pairs={{0,2},{1,3},{2,0},{3,1},{4,6},{5,7},{6,4},{7,5},{8,10},{9,11},{10,... | collective-permute-start | bytes 2359304 | tf_op jit(solution)/shard_map/ppermute | solution.py:67
  74.1 35.3 %collective-permute-start.5 = (bf16[4,128,1536]{2,1,0:T(8,128)(2,1)}, bf16[4,128,1536]{2,1,0:T(8,128)(2,1)}, u32[]{:S(2)}, u32[]{:S(2)}) collective-permute-start(bf16[4,128,1536]{2,1,0:T(8,128)(2,1)} %pad_maximum_fusion.9), channel_id=1, source_target_pairs={{0,1},{1,0},{2,3},{3,2},{4,5},{5,4},{6,7},{7,6},{8,9},{9,8},{10,11... | collective-permute-start | bytes 4718600 | tf_op jit(solution)/shard_map/ppermute | solution.py:67
  81.2 30.4 %collective-permute-start.2 = (bf16[4,128,1536]{2,1,0:T(8,128)(2,1)}, bf16[4,128,1536]{2,1,0:T(8,128)(2,1)}, u32[]{:S(2)}, u32[]{:S(2)}) collective-permute-start(bf16[4,128,1536]{2,1,0:T(8,128)(2,1)} %pad_maximum_fusion.8), channel_id=1, source_target_pairs={{0,1},{1,0},{2,3},{3,2},{4,5},{5,4},{6,7},{7,6},{8,9},{9,8},{10,11... | collective-permute-start | bytes 4718600 | tf_op jit(solution)/shard_map/ppermute | solution.py:67
  87.9 17.5 %collective-permute-start.7 = (bf16[2,2,48,1536]{3,2,1,0:T(8,128)(2,1)S(1)}, bf16[2,2,48,1536]{3,2,1,0:T(8,128)(2,1)S(1)}, u32[]{:S(2)}, u32[]{:S(2)}) collective-permute-start(bf16[2,2,48,1536]{3,2,1,0:T(8,128)(2,1)S(1)} %pad_maximum_fusion.24), channel_id=1, source_target_pairs={{0,2},{1,3},{2,0},{3,1},{4,6},{5,7},{6,4},{7,5},{8,10},{9,11},{10,... | collective-permute-start | bytes 1769480 | tf_op jit(solution)/shard_map/ppermute | solution.py:67
  93.5 14.7 %collective-permute-start.10 = (bf16[2,2,48,1536]{3,2,1,0:T(8,128)(2,1)S(1)}, bf16[2,2,48,1536]{3,2,1,0:T(8,128)(2,1)S(1)}, u32[]{:S(2)}, u32[]{:S(2)}) collective-permute-start(bf16[2,2,48,1536]{3,2,1,0:T(8,128)(2,1)S(1)} %pad_maximum_fusion.25), channel_id=1, source_target_pairs={{0,4},{1,5},{2,6},{3,7},{4,0},{5,1},{6,2},{7,3},{8,12},{9,13},{10,... | collective-permute-start | bytes 1769480 | tf_op jit(solution)/shard_map/ppermute | solution.py:67
  105.4 63.5 %collective-permute-start.21 = (bf16[1,128,1536]{2,1,0:T(8,128)(2,1)S(1)}, bf16[1,128,1536]{2,1,0:T(8,128)(2,1)}, u32[]{:S(2)}, u32[]{:S(2)}) collective-permute-start(bf16[1,128,1536]{2,1,0:T(8,128)(2,1)S(1)} %get-tuple-element.141), channel_id=1, source_target_pairs={{0,2},{1,3},{2,0},{3,1},{4,6},{5,7},{6,4},{7,5},{8,10},{9,11},{10,... | collective-permute-start | bytes 1179656 | tf_op jit(solution)/shard_map/ppermute | solution.py:67
  108.1 45.8 %collective-permute-start.8 = (bf16[4,2,48,1536]{3,2,1,0:T(8,128)(2,1)}, bf16[4,2,48,1536]{3,2,1,0:T(8,128)(2,1)}, u32[]{:S(2)}, u32[]{:S(2)}) collective-permute-start(bf16[4,2,48,1536]{3,2,1,0:T(8,128)(2,1)} %pad_maximum_fusion.14), channel_id=1, source_target_pairs={{0,1},{1,0},{2,3},{3,2},{4,5},{5,4},{6,7},{7,6},{8,9},{9,8},{10,11... | collective-permute-start | bytes 3538952 | tf_op jit(solution)/shard_map/ppermute | solution.py:67
  109.4 46.5 %collective-permute-start.11 = (bf16[4,2,48,1536]{3,2,1,0:T(8,128)(2,1)}, bf16[4,2,48,1536]{3,2,1,0:T(8,128)(2,1)}, u32[]{:S(2)}, u32[]{:S(2)}) collective-permute-start(bf16[4,2,48,1536]{3,2,1,0:T(8,128)(2,1)} %pad_maximum_fusion.15), channel_id=1, source_target_pairs={{0,1},{1,0},{2,3},{3,2},{4,5},{5,4},{6,7},{7,6},{8,9},{9,8},{10,11... | collective-permute-start | bytes 3538952 | tf_op jit(solution)/shard_map/ppermute | solution.py:67
  145.2 17.8 %all-to-all-start.1 = ((bf16[8,192,256]{2,1,0:T(8,128)(2,1)}), bf16[8,192,256]{2,1,0:T(8,128)(2,1)}, u32[]{:S(2)}, u32[]{:S(2)}) async-start(bf16[8,192,256]{2,1,0:T(8,128)(2,1)} %get-tuple-element.41), calls=%async_computation.1 | async-start | bytes 1572864 | tf_op jit(solution)/shard_map/all_to_all | solution.py:485
  152.0 37.6 %collective-permute-start.19 = (bf16[2,128,1536]{2,1,0:T(8,128)(2,1)}, bf16[2,128,1536]{2,1,0:T(8,128)(2,1)}, u32[]{:S(2)}, u32[]{:S(2)}) collective-permute-start(bf16[2,128,1536]{2,1,0:T(8,128)(2,1)} %pad_maximum_fusion.22), channel_id=1, source_target_pairs={{0,2},{1,3},{2,0},{3,1},{4,6},{5,7},{6,4},{7,5},{8,10},{9,11},{10,... | collective-permute-start | bytes 2359304 | tf_op jit(solution)/shard_map/ppermute | solution.py:67
  168.7 18.1 %collective-permute-start.15 = (bf16[1,128,1536]{2,1,0:T(8,128)(2,1)}, bf16[1,128,1536]{2,1,0:T(8,128)(2,1)}, u32[]{:S(2)}, u32[]{:S(2)}) collective-permute-start(bf16[1,128,1536]{2,1,0:T(8,128)(2,1)} %get-tuple-element.143), channel_id=1, source_target_pairs={{0,2},{1,3},{2,0},{3,1},{4,6},{5,7},{6,4},{7,5},{8,10},{9,11},{10,... | collective-permute-start | bytes 1179656 | tf_op jit(solution)/shard_map/ppermute | solution.py:67
  170.9 31.9 %collective-permute-start.22 = (bf16[2,128,1536]{2,1,0:T(8,128)(2,1)}, bf16[2,128,1536]{2,1,0:T(8,128)(2,1)}, u32[]{:S(2)}, u32[]{:S(2)}) collective-permute-start(bf16[2,128,1536]{2,1,0:T(8,128)(2,1)} %pad_maximum_fusion.23), channel_id=1, source_target_pairs={{0,4},{1,5},{2,6},{3,7},{4,0},{5,1},{6,2},{7,3},{8,12},{9,13},{10,... | collective-permute-start | bytes 2359304 | tf_op jit(solution)/shard_map/ppermute | solution.py:67
  179.7 20.3 %collective-permute-start.12 = (bf16[1,128,1536]{2,1,0:T(8,128)(2,1)}, bf16[1,128,1536]{2,1,0:T(8,128)(2,1)S(1)}, u32[]{:S(2)}, u32[]{:S(2)}) collective-permute-start(bf16[1,128,1536]{2,1,0:T(8,128)(2,1)} %get-tuple-element.144), channel_id=1, source_target_pairs={{0,4},{1,5},{2,6},{3,7},{4,0},{5,1},{6,2},{7,3},{8,12},{9,13},{10,... | collective-permute-start | bytes 1179656 | tf_op jit(solution)/shard_map/ppermute | solution.py:67
  188.0 27.6 %collective-permute-start.16 = (bf16[2,128,1536]{2,1,0:T(8,128)(2,1)S(1)}, bf16[2,128,1536]{2,1,0:T(8,128)(2,1)S(1)}, u32[]{:S(2)}, u32[]{:S(2)}) collective-permute-start(bf16[2,128,1536]{2,1,0:T(8,128)(2,1)S(1)} %pad_maximum_fusion.21), channel_id=1, source_target_pairs={{0,4},{1,5},{2,6},{3,7},{4,0},{5,1},{6,2},{7,3},{8,12},{9,13},{10,... | collective-permute-start | bytes 2359304 | tf_op jit(solution)/shard_map/ppermute | solution.py:67
  192.2 33.0 %collective-permute-start.20 = (bf16[4,128,1536]{2,1,0:T(8,128)(2,1)}, bf16[4,128,1536]{2,1,0:T(8,128)(2,1)}, u32[]{:S(2)}, u32[]{:S(2)}) collective-permute-start(bf16[4,128,1536]{2,1,0:T(8,128)(2,1)} %pad_maximum_fusion.12), channel_id=1, source_target_pairs={{0,1},{1,0},{2,3},{3,2},{4,5},{5,4},{6,7},{7,6},{8,9},{9,8},{10,11... | collective-permute-start | bytes 4718600 | tf_op jit(solution)/shard_map/ppermute | solution.py:67
  201.0 20.4 %collective-permute-start.13 = (bf16[2,128,1536]{2,1,0:T(8,128)(2,1)}, bf16[2,128,1536]{2,1,0:T(8,128)(2,1)}, u32[]{:S(2)}, u32[]{:S(2)}) collective-permute-start(bf16[2,128,1536]{2,1,0:T(8,128)(2,1)} %pad_maximum_fusion.20), channel_id=1, source_target_pairs={{0,2},{1,3},{2,0},{3,1},{4,6},{5,7},{6,4},{7,5},{8,10},{9,11},{10,... | collective-permute-start | bytes 2359304 | tf_op jit(solution)/shard_map/ppermute | solution.py:67
  205.3 23.1 %collective-permute-start.23 = (bf16[4,128,1536]{2,1,0:T(8,128)(2,1)}, bf16[4,128,1536]{2,1,0:T(8,128)(2,1)}, u32[]{:S(2)}, u32[]{:S(2)}) collective-permute-start(bf16[4,128,1536]{2,1,0:T(8,128)(2,1)} %pad_maximum_fusion.13), channel_id=1, source_target_pairs={{0,1},{1,0},{2,3},{3,2},{4,5},{5,4},{6,7},{7,6},{8,9},{9,8},{10,11... | collective-permute-start | bytes 4718600 | tf_op jit(solution)/shard_map/ppermute | solution.py:67
  218.3 13.3 %collective-permute-start.17 = (bf16[4,128,1536]{2,1,0:T(8,128)(2,1)}, bf16[4,128,1536]{2,1,0:T(8,128)(2,1)}, u32[]{:S(2)}, u32[]{:S(2)}) collective-permute-start(bf16[4,128,1536]{2,1,0:T(8,128)(2,1)} %pad_maximum_fusion.11), channel_id=1, source_target_pairs={{0,1},{1,0},{2,3},{3,2},{4,5},{5,4},{6,7},{7,6},{8,9},{9,8},{10,11... | collective-permute-start | bytes 4718600 | tf_op jit(solution)/shard_map/ppermute | solution.py:67
  223.0 11.7 %collective-permute-start.14 = (bf16[4,128,1536]{2,1,0:T(8,128)(2,1)S(1)}, bf16[4,128,1536]{2,1,0:T(8,128)(2,1)S(1)}, u32[]{:S(2)}, u32[]{:S(2)}) collective-permute-start(bf16[4,128,1536]{2,1,0:T(8,128)(2,1)S(1)} %pad_maximum_fusion.10), channel_id=1, source_target_pairs={{0,1},{1,0},{2,3},{3,2},{4,5},{5,4},{6,7},{7,6},{8,9},{9,8},{10,11... | collective-permute-start | bytes 4718600 | tf_op jit(solution)/shard_map/ppermute | solution.py:67
  336.8 20.4 %collective-permute-start.25 = (bf16[2,128,1536]{2,1,0:T(8,128)(2,1)S(1)}, bf16[2,128,1536]{2,1,0:T(8,128)(2,1)S(1)}, u32[]{:S(2)}, u32[]{:S(2)}) collective-permute-start(bf16[2,128,1536]{2,1,0:T(8,128)(2,1)S(1)} %slice.391), channel_id=1, source_target_pairs={{0,2},{1,3},{2,0},{3,1},{4,6},{5,7},{6,4},{7,5},{8,10},{9,11},{10,... | collective-permute-start | bytes 2359304 | tf_op jit(solution)/shard_map/ppermute | solution.py:67
  339.2 20.4 %collective-permute-start.28 = (bf16[2,128,1536]{2,1,0:T(8,128)(2,1)S(1)}, bf16[2,128,1536]{2,1,0:T(8,128)(2,1)S(1)}, u32[]{:S(2)}, u32[]{:S(2)}) collective-permute-start(bf16[2,128,1536]{2,1,0:T(8,128)(2,1)S(1)} %slice.395), channel_id=1, source_target_pairs={{0,4},{1,5},{2,6},{3,7},{4,0},{5,1},{6,2},{7,3},{8,12},{9,13},{10,... | collective-permute-start | bytes 2359304 | tf_op jit(solution)/shard_map/ppermute | solution.py:67
  342.4 33.0 %collective-permute-start.31 = (bf16[2,128,1664]{2,1,0:T(8,128)(2,1)S(1)}, bf16[2,128,1664]{2,1,0:T(8,128)(2,1)S(1)}, u32[]{:S(2)}, u32[]{:S(2)}) collective-permute-start(bf16[2,128,1664]{2,1,0:T(8,128)(2,1)S(1)} %slice.399), channel_id=1, source_target_pairs={{0,2},{1,3},{2,0},{3,1},{4,6},{5,7},{6,4},{7,5},{8,10},{9,11},{10,... | collective-permute-start | bytes 2555912 | tf_op jit(solution)/shard_map/ppermute | solution.py:67
  344.1 33.8 %collective-permute-start.34 = (bf16[2,128,1664]{2,1,0:T(8,128)(2,1)S(1)}, bf16[2,128,1664]{2,1,0:T(8,128)(2,1)S(1)}, u32[]{:S(2)}, u32[]{:S(2)}) collective-permute-start(bf16[2,128,1664]{2,1,0:T(8,128)(2,1)S(1)} %slice.403), channel_id=1, source_target_pairs={{0,4},{1,5},{2,6},{3,7},{4,0},{5,1},{6,2},{7,3},{8,12},{9,13},{10,... | collective-permute-start | bytes 2555912 | tf_op jit(solution)/shard_map/ppermute | solution.py:67
  357.4 28.9 %collective-permute-start.26 = (bf16[1,128,1536]{2,1,0:T(8,128)(2,1)S(1)}, bf16[1,128,1536]{2,1,0:T(8,128)(2,1)S(1)}, u32[]{:S(2)}, u32[]{:S(2)}) collective-permute-start(bf16[1,128,1536]{2,1,0:T(8,128)(2,1)S(1)} %slice.393), channel_id=1, source_target_pairs={{0,4},{1,5},{2,6},{3,7},{4,0},{5,1},{6,2},{7,3},{8,12},{9,13},{10,... | collective-permute-start | bytes 1179656 | tf_op jit(solution)/shard_map/ppermute | solution.py:67
  359.9 26.6 %collective-permute-start.29 = (bf16[1,128,1536]{2,1,0:T(8,128)(2,1)S(1)}, bf16[1,128,1536]{2,1,0:T(8,128)(2,1)S(1)}, u32[]{:S(2)}, u32[]{:S(2)}) collective-permute-start(bf16[1,128,1536]{2,1,0:T(8,128)(2,1)S(1)} %slice.397), channel_id=1, source_target_pairs={{0,2},{1,3},{2,0},{3,1},{4,6},{5,7},{6,4},{7,5},{8,10},{9,11},{10,... | collective-permute-start | bytes 1179656 | tf_op jit(solution)/shard_map/ppermute | solution.py:67
  375.7 19.2 %collective-permute-start.32 = (bf16[1,128,1664]{2,1,0:T(8,128)(2,1)S(1)}, bf16[1,128,1664]{2,1,0:T(8,128)(2,1)S(1)}, u32[]{:S(2)}, u32[]{:S(2)}) collective-permute-start(bf16[1,128,1664]{2,1,0:T(8,128)(2,1)S(1)} %slice.401), channel_id=1, source_target_pairs={{0,4},{1,5},{2,6},{3,7},{4,0},{5,1},{6,2},{7,3},{8,12},{9,13},{10,... | collective-permute-start | bytes 1277960 | tf_op jit(solution)/shard_map/ppermute | solution.py:67
  378.1 16.8 %collective-permute-start.35 = (bf16[1,128,1664]{2,1,0:T(8,128)(2,1)S(1)}, bf16[1,128,1664]{2,1,0:T(8,128)(2,1)S(1)}, u32[]{:S(2)}, u32[]{:S(2)}) collective-permute-start(bf16[1,128,1664]{2,1,0:T(8,128)(2,1)S(1)} %slice.405), channel_id=1, source_target_pairs={{0,2},{1,3},{2,0},{3,1},{4,6},{5,7},{6,4},{7,5},{8,10},{9,11},{10,... | collective-permute-start | bytes 1277960 | tf_op jit(solution)/shard_map/ppermute | solution.py:67
  411.4 59.7 %collective-permute-start.42 = (bf16[4,2,48,1536]{3,2,1,0:T(8,128)(2,1)}, bf16[4,2,48,1536]{3,2,1,0:T(8,128)(2,1)}, u32[]{:S(2)}, u32[]{:S(2)}) collective-permute-start(bf16[4,2,48,1536]{3,2,1,0:T(8,128)(2,1)} %slice.420), channel_id=1, source_target_pairs={{0,1},{1,0},{2,3},{3,2},{4,5},{5,4},{6,7},{7,6},{8,9},{9,8},{10,11... | collective-permute-start | bytes 3538952 | tf_op jit(solution)/shard_map/ppermute | solution.py:67
  416.1 16.1 %all-to-all-start.2 = ((bf16[8,192,256]{2,1,0:T(8,128)(2,1)}), bf16[8,192,256]{2,1,0:T(8,128)(2,1)S(1)}, u32[]{:S(2)}, u32[]{:S(2)}) async-start(bf16[8,192,256]{2,1,0:T(8,128)(2,1)} %bitcast.32), calls=%async_computation.2 | async-start | bytes 1572864 | tf_op jit(solution)/shard_map/all_to_all | solution.py:570
  419.6 129.8 %reduce-scatter.4.cloned.1.call-start = ((), (), s32[]{:S(2)}) async-start(), calls=%async_computation.7 | async-start | bytes 2088960 | tf_op jit(solution)/shard_map/reduce_scatter | solution.py:645
  426.0 48.4 %collective-permute-start.45 = (bf16[4,2,48,1536]{3,2,1,0:T(8,128)(2,1)}, bf16[4,2,48,1536]{3,2,1,0:T(8,128)(2,1)}, u32[]{:S(2)}, u32[]{:S(2)}) collective-permute-start(bf16[4,2,48,1536]{3,2,1,0:T(8,128)(2,1)} %slice.427), channel_id=1, source_target_pairs={{0,1},{1,0},{2,3},{3,2},{4,5},{5,4},{6,7},{7,6},{8,9},{9,8},{10,11... | collective-permute-start | bytes 3538952 | tf_op jit(solution)/shard_map/ppermute | solution.py:67
  473.8 14.1 %collective-permute-start.43 = (bf16[2,2,48,1536]{3,2,1,0:T(8,128)(2,1)S(1)}, bf16[2,2,48,1536]{3,2,1,0:T(8,128)(2,1)S(1)}, u32[]{:S(2)}, u32[]{:S(2)}) collective-permute-start(bf16[2,2,48,1536]{3,2,1,0:T(8,128)(2,1)S(1)} %slice.422), channel_id=1, source_target_pairs={{0,2},{1,3},{2,0},{3,1},{4,6},{5,7},{6,4},{7,5},{8,10},{9,11},{10,... | collective-permute-start | bytes 1769480 | tf_op jit(solution)/shard_map/ppermute | solution.py:67
  476.0 16.3 %collective-permute-start.46 = (bf16[2,2,48,1536]{3,2,1,0:T(8,128)(2,1)S(1)}, bf16[2,2,48,1536]{3,2,1,0:T(8,128)(2,1)S(1)}, u32[]{:S(2)}, u32[]{:S(2)}) collective-permute-start(bf16[2,2,48,1536]{3,2,1,0:T(8,128)(2,1)S(1)} %slice.429), channel_id=1, source_target_pairs={{0,4},{1,5},{2,6},{3,7},{4,0},{5,1},{6,2},{7,3},{8,12},{9,13},{10,... | collective-permute-start | bytes 1769480 | tf_op jit(solution)/shard_map/ppermute | solution.py:67
  506.1 123.0 %reduce-scatter.8.cloned.1.call-start = ((), (), s32[]{:S(2)}) async-start(), calls=%async_computation.9 | async-start | bytes 5898240 | tf_op jit(solution)/shard_map/reduce_scatter | solution.py:544
  506.7 210.4 %reduce-scatter.6.cloned.1.call-start = ((), (), s32[]{:S(2)}) async-start(), calls=%async_computation.8 | async-start | bytes 5898240 | tf_op jit(solution)/shard_map/reduce_scatter | solution.py:544
  513.7 19.9 %collective-permute-start.37 = (bf16[2,128,1536]{2,1,0:T(8,128)(2,1)}, bf16[2,128,1536]{2,1,0:T(8,128)(2,1)}, u32[]{:S(2)}, u32[]{:S(2)}) collective-permute-start(bf16[2,128,1536]{2,1,0:T(8,128)(2,1)} %slice.411), channel_id=1, source_target_pairs={{0,2},{1,3},{2,0},{3,1},{4,6},{5,7},{6,4},{7,5},{8,10},{9,11},{10,... | collective-permute-start | bytes 2359304 | tf_op jit(solution)/shard_map/ppermute | solution.py:67
  516.1 19.8 %collective-permute-start.40 = (bf16[2,128,1536]{2,1,0:T(8,128)(2,1)S(1)}, bf16[2,128,1536]{2,1,0:T(8,128)(2,1)S(1)}, u32[]{:S(2)}, u32[]{:S(2)}) collective-permute-start(bf16[2,128,1536]{2,1,0:T(8,128)(2,1)S(1)} %slice.415), channel_id=1, source_target_pairs={{0,4},{1,5},{2,6},{3,7},{4,0},{5,1},{6,2},{7,3},{8,12},{9,13},{10,... | collective-permute-start | bytes 2359304 | tf_op jit(solution)/shard_map/ppermute | solution.py:67
  535.1 10.4 %collective-permute-start.38 = (bf16[1,128,1536]{2,1,0:T(8,128)(2,1)S(1)}, bf16[1,128,1536]{2,1,0:T(8,128)(2,1)S(1)}, u32[]{:S(2)}, u32[]{:S(2)}) collective-permute-start(bf16[1,128,1536]{2,1,0:T(8,128)(2,1)S(1)} %slice.413), channel_id=1, source_target_pairs={{0,4},{1,5},{2,6},{3,7},{4,0},{5,1},{6,2},{7,3},{8,12},{9,13},{10,... | collective-permute-start | bytes 1179656 | tf_op jit(solution)/shard_map/ppermute | solution.py:67
  536.1 10.2 %collective-permute-start.41 = (bf16[1,128,1536]{2,1,0:T(8,128)(2,1)S(1)}, bf16[1,128,1536]{2,1,0:T(8,128)(2,1)S(1)}, u32[]{:S(2)}, u32[]{:S(2)}) collective-permute-start(bf16[1,128,1536]{2,1,0:T(8,128)(2,1)S(1)} %slice.417), channel_id=1, source_target_pairs={{0,2},{1,3},{2,0},{3,1},{4,6},{5,7},{6,4},{7,5},{8,10},{9,11},{10,... | collective-permute-start | bytes 1179656 | tf_op jit(solution)/shard_map/ppermute | solution.py:67
  551.4 10.6 %all-to-all-start.3 = ((bf16[8,48,338]{2,1,0:T(8,128)(2,1)}), bf16[8,48,338]{2,1,0:T(8,128)(2,1)S(1)}, u32[]{:S(2)}, u32[]{:S(2)}) async-start(bf16[8,48,338]{2,1,0:T(8,128)(2,1)} %bitcast.43), calls=%async_computation.4 | async-start | bytes 589824 | tf_op jit(solution)/shard_map/all_to_all | solution.py:646
  (89 other events, 527.7 us)
Sparse Core Ops, SparseCore 0:
  25.8 37.6 all-gather.12
  65.1 88.2 all-gather.10
  154.9 87.8 all-gather.8
  506.2 36.3 reduce-scatter.3
  544.7 84.3 reduce-scatter.7
  631.2 85.7 reduce-scatter.5

commit v2 on v1

v2 whole, which is shorter than its diff:
```python
import functools

import jax
import jax.numpy as jnp
from jax import lax
from jax.experimental import pallas as pl
from jax.experimental.pallas import tpu as pltpu
from jax.sharding import PartitionSpec as P

H = 24
KV = 8
HD = 64
TOP = 8
CAP = 1024

EPS = 1e-06
NEG_FILL = -1e30
SCORE_SCALE = 0.015625
RESIDUAL_SCALE = 0.22

GROUP = H // KV
HALF = HD // 2
QW = GROUP * HD
QKV = QW + 2 * HD
LOW = 64
EXTRA = 128

f32 = jnp.float32
bf16 = jnp.bfloat16
i32 = jnp.int32
VMEM_LIMIT = 58 * 1024 * 1024


def dot_nn(a, b):
    return lax.dot_general(a, b, (((1,), (0,)), ((), ())), preferred_element_type=f32)


def dot_nt(a, b):
    return lax.dot_general(a, b, (((1,), (1,)), ((), ())), preferred_element_type=f32)


def dot_tn(a, b):
    return lax.dot_general(a, b, (((0,), (0,)), ((), ())), preferred_element_type=f32)


def params(limit=VMEM_LIMIT):
    return pltpu.CompilerParams(dimension_semantics=("arbitrary",), vmem_limit_bytes=limit)


def lane_orders(count):
    bits = []
    bit = 2
    while bit < count:
        bits.append(bit)
        bit *= 2
    return (bits[::-1] + [1], bits + [1])


def slots_of(order):
    slots = [0]
    for bit in order:
        slots = slots + [s ^ bit for s in slots]
    return slots


def swap(value, bit, count):
    return lax.ppermute(value, "ctx", [(i, i ^ bit) for i in range(count)])


class Gather:
    def __init__(self, first, second, count):
        self.count = count
        self.orders = lane_orders(count)
        self.have = [first[None], second[None]]
        self.at = 0
        self.start()

    def start(self):
        self.got = [
            swap(have, order[self.at], self.count)
            for have, order in zip(self.have, self.orders)
        ]
        self.at += 1

    def step(self):
        self.have = [
            jnp.concatenate([have, got], axis=0) for have, got in zip(self.have, self.got)
        ]
        self.start()

    def run(self):
        while self.at < len(self.orders[0]):
            self.step()
        return [self.have[0], self.got[0], self.have[1], self.got[1]]


def add_up(x, y):
    return (x.astype(f32) + y.astype(f32)).astype(bf16)


def fold_kernel(*refs):
    ins, outs = (refs[:8], refs[8:])
    for lane in range(2):
        near, got, near_far, got_far = ins[4 * lane : 4 * lane + 4]
        outs[2 * lane][...] = add_up(near[...], got[...])
        outs[2 * lane + 1][...] = add_up(near_far[...], got_far[...])


def fold(keep, got):
    size, *rest = keep[0].shape
    half = size // 2
    zeros = (0,) * len(rest)
    near = pl.BlockSpec((1, *rest), lambda i: (i,) + zeros)
    far = pl.BlockSpec((1, *rest), lambda i: (i + half,) + zeros)
    out = [jax.ShapeDtypeStruct((half, *rest), bf16)] * 4
    kept_a, sent_a, kept_b, sent_b = pl.pallas_call(
        fold_kernel,
        grid=(half,),
        in_specs=[near, near, far, far] * 2,
        out_specs=[near] * 4,
        out_shape=out,
        compiler_params=params(16 * 1024 * 1024),
        cost_estimate=pl.CostEstimate(flops=int(3e9), bytes_accessed=int(3e6), transcendentals=0),
        name="fold",
    )(keep[0], got[0], keep[0], got[0], keep[1], got[1], keep[1], got[1])
    return [kept_a, kept_b], [sent_a, sent_b]


class Scatter:
    def __init__(self, pieces, count):
        a, a_far, b, b_far = pieces
        self.count = count
        self.orders = [order[::-1] for order in lane_orders(count)]
        self.keep = [a, b]
        self.got = [swap(a_far, 1, count), swap(b_far, 1, count)]
        self.at = 1

    def step(self):
        self.keep, send = fold(self.keep, self.got)
        self.got = [
            swap(part, order[self.at], self.count) for part, order in zip(send, self.orders)
        ]
        self.at += 1

    def run(self):
        while self.at < len(self.orders[0]):
            self.step()
        return [(keep[0], got[0]) for keep, got in zip(self.keep, self.got)]


def after(values, *others):
    return lax.optimization_barrier((values, others))[0]


def near(slots, lane, step, far):
    return slots[lane, step] < far


def pick(flags, pieces):
    a, a_far, b, b_far = pieces
    return jnp.concatenate(
        [lax.select(flags[0], a[0], a_far[0]), lax.select(flags[1], b[0], b_far[0])], axis=0
    )


def put(flags, outs, rows):
    a, a_far, b, b_far = outs
    half = a.shape[1]
    for flag, near_o, far_o, part in (
        (flags[0], a, a_far, rows[:half]),
        (flags[1], b, b_far, rows[half:]),
    ):

        @pl.when(flag)
        def _():
            near_o[0] = part

        @pl.when(jnp.logical_not(flag))
        def _():
            far_o[0] = part


def prep_kernel(query, key, value, gain_a, gain_f, router, routes, order, out):
    rp = query.shape[0]
    count, _, columns = out.shape
    small = [x[...].astype(f32) for x in (gain_a, gain_f, router)]
    side = jnp.concatenate(small, axis=0).T.astype(bf16)
    tail = jnp.zeros((rp, columns - QKV - side.shape[1]), bf16)
    rows = [x[...].astype(f32) for x in (routes, order)]
    tok = order.shape[1]
    ranks = out.shape[1] - rp
    rows.append(jnp.zeros((ranks - TOP - 1, tok), f32))
    rows = jnp.concatenate(rows, axis=0).astype(bf16)
    rows = jnp.concatenate([rows, jnp.zeros((ranks, columns - tok), bf16)], axis=1)
    for c in range(count):
        g = c * KV // count
        out[c, :rp, :] = jnp.concatenate(
            [
                query[:, g * QW : (g + 1) * QW],
                key[:, g * HD : (g + 1) * HD],
                value[:, g * HD : (g + 1) * HD],
                side,
                tail,
            ],
            axis=1,
        )
        out[c, rp : rp + ranks, :] = rows


def pack_kernel(took, w_out, out):
    count, _, columns = took.shape
    rp, width = w_out.shape
    slab = count * rp
    chunks = width // slab
    for j in range(chunks):
        out[j * rp : (j + 1) * rp, :] = w_out[:, j * slab : (j + 1) * slab]
    rows = took[:, :rp, :].astype(f32).reshape(slab, columns).T
    out[chunks * rp :, :] = rows[: out.shape[0] - chunks * rp].astype(bf16)


def unpack_kernel(shards, rp, where, *refs):
    pieces, (wt_o, gains_o, router_o, rows_o) = (refs[: 2 * shards - 1], refs[2 * shards - 1 :])
    slab = pieces[0].shape[1]
    first = shards * rp
    experts = router_o.shape[0]
    for z in range(shards):

        @pl.when(where[0] == z)
        def _():
            for p in range(shards):
                piece = pieces[p - z + shards - 1]
                columns = slice(p * slab, (p + 1) * slab)
                wt_o[:, columns] = piece[first : first + QKV]
                gains_o[:, columns] = piece[first + QKV : first + QKV + 2].astype(f32)
                router_o[:, columns] = piece[first + QKV + 2 : first + QKV + 2 + experts]
                for j in range(shards):
                    rows_o[p, :, j * slab : (j + 1) * slab] = piece[j * rp : (j + 1) * rp]


def code_kernel(first, table, out, load):
    i = pl.program_id(0)
    tok, experts = out.shape[1:]

    @pl.when(i == 0)
    def _():
        load[...] = jnp.zeros_like(load)

    rows = table[0, first : first + TOP + 1, :tok].astype(f32)
    names = lax.broadcasted_iota(i32, (experts, tok), 0).astype(f32)
    named = jnp.zeros((experts, tok), f32)
    for k in range(TOP):
        named += jnp.where(rows[k : k + 1] == names, 1.0, 0.0)
    ranks = jnp.broadcast_to(rows[TOP : TOP + 1], (tok, tok))
    before = jnp.where(ranks.T < ranks, 1.0, 0.0).astype(bf16)
    slot = dot_nn(named.astype(bf16), before) + load[:, :1]
    out[0] = (named * (1.0 + jnp.where(slot < CAP, 1.0, 0.0))).T
    load[...] += jnp.sum(named, axis=1, keepdims=True)


def qkv_kernel(
    far, slot_ref, xa, xaf, xb, xbf, gain, wt, cos, sin, ain_o, qt_o, k_o, kt_o, v_o, vt_o
):
    i = pl.program_id(0)
    flags = (near(slot_ref, 0, i, far), near(slot_ref, 1, i, far))
    x = pick(flags, (xa, xaf, xb, xbf)).astype(f32)
    inv = lax.rsqrt(jnp.mean(x * x, axis=-1, keepdims=True) + EPS)
    a = (x * inv * gain[...]).astype(bf16)
    ain_o[0] = a
    y = dot_nt(wt[...], a)
    c, s = (cos[0], sin[0])

    def turn(rows):
        lo, hi = (rows[:HALF], rows[HALF:])
        return jnp.concatenate([lo * c - hi * s, hi * c + lo * s], axis=0)

    for h in range(GROUP):
        q = turn(y[h * HD : (h + 1) * HD]).astype(bf16).astype(f32) * SCORE_SCALE
        qt_o[0, h * HD : (h + 1) * HD, :] = q.astype(bf16)
    k = turn(y[QW : QW + HD])
    kt_o[0] = k.astype(bf16)
    k_o[0] = k.T.astype(bf16)
    v = y[QW + HD :]
    vt_o[0] = v.astype(bf16)
    v_o[0] = v.T.astype(bf16)


def heads_wide(rows):
    return jnp.concatenate([rows[h * HD : (h + 1) * HD] for h in range(GROUP)], axis=1)


def causal(shape, width):
    key = lax.broadcasted_iota(i32, shape, 0)
    query = lax.broadcasted_iota(i32, shape, 1)
    for _ in range(GROUP - 1):
        query = jnp.where(query >= width, query - width, query)
    return key <= query


def attn_fwd_kernel(qt, k, vt, of_o, ob_o, lse_o):
    a = pl.program_id(0)
    tok = qt.shape[2]
    q = heads_wide(qt[0])
    s = dot_nn(k[a], q)
    s = jnp.where(causal(s.shape, tok), s, NEG_FILL)
    m = jnp.max(s, axis=0, keepdims=True)
    p = jnp.exp(s - m)
    l = jnp.sum(p, axis=0, keepdims=True)
    o = dot_nn(vt[a], p.astype(bf16))

    def step(b, carry):
        m, l, o = carry
        s = dot_nn(k[b], q)
        new = jnp.maximum(m, jnp.max(s, axis=0, keepdims=True))
        p = jnp.exp(s - new)
        back = jnp.exp(m - new)
        l = l * back + jnp.sum(p, axis=0, keepdims=True)
        o = o * back + dot_nn(vt[b], p.astype(bf16))
        return (new, l, o)

    m, l, o = lax.fori_loop(0, a, step, (m, l, o))
    o = o / l
    lse_o[0] = m + jnp.log(l)
    for h in range(GROUP):
        part = o[:, h * tok : (h + 1) * tok]
        of_o[0, h * HD : (h + 1) * HD, :] = part
        ob_o[0, h * HD : (h + 1) * HD, :] = part.astype(bf16)


def attn_bwd_kernel(qt, dot_, of, lse, k, kt, v, cos, sin, dq_o, dk_o, dv_o, dk_s, dv_s):
    a = pl.program_id(0)
    tok = qt.shape[2]
    count = k.shape[0]
    q = heads_wide(qt[0])
    do = heads_wide(dot_[0])
    delta = jnp.sum(do.astype(f32) * heads_wide(of[0]), axis=0, keepdims=True)
    total = lse[0]

    def pair(b, mask):
        s = dot_nn(k[b], q)
        p = jnp.exp(s - total)
        if mask:
            p = jnp.where(causal(s.shape, tok), p, 0.0)
        dp = dot_nn(v[b], do)
        ds = (p * (dp - delta)).astype(bf16)
        return dot_nt(ds, q), dot_nt(p.astype(bf16), do), dot_nn(kt[b], ds)

    dk, dv, dq = pair(a, True)
    dk_s[a] = dk
    dv_s[a] = dv

    def step(b, dq):
        dk, dv, more = pair(b, False)
        dk_s[b] += dk
        dv_s[b] += dv
        return dq + more

    dq = lax.fori_loop(0, a, step, dq) * SCORE_SCALE

    def back(rows, c, s):
        lo, hi = (rows[:HALF], rows[HALF:])
        return jnp.concatenate([lo * c + hi * s, hi * c - lo * s], axis=0)

    for h in range(GROUP):
        dq_o[0, h * HD : (h + 1) * HD, :] = back(
            dq[:, h * tok : (h + 1) * tok], cos[a], sin[a]
        ).astype(bf16)

    @pl.when(a == count - 1)
    def _():
        @pl.loop(0, count)
        def _(b):
            dk_o[b] = back(dk_s[b].T, cos[b], sin[b]).astype(bf16)
            dv_o[b] = dv_s[b].T.astype(bf16)


def qkv_bwd_kernel(
    share, far, blocks_ref, dqa, dka, dva, dqb, dkb, dvb, aa, ab, xa, xaf, xb, xbf, wt,
    da_o, daf_o, db_o, dbf_o, gw_o, gg_o, acc, gacc,
):
    i = pl.program_id(0)
    flags = (i < far, i < far)
    d = jnp.concatenate(
        [
            jnp.concatenate([dqa[0], dka[0], dva[0]], axis=0),
            jnp.concatenate([dqb[0], dkb[0], dvb[0]], axis=0),
        ],
        axis=1,
    )
    part = dot_tn(d, wt[...]) * share
    x = pick(flags, (xa, xaf, xb, xbf)).astype(f32)
    inv = lax.rsqrt(jnp.mean(x * x, axis=-1, keepdims=True) + EPS)
    put(flags, (da_o, daf_o, db_o, dbf_o), part.astype(bf16))

    @pl.when(i == 0)
    def _():
        acc[...] = jnp.zeros_like(acc)
        gacc[...] = jnp.zeros_like(gacc)

    acc[...] += dot_nn(d, jnp.concatenate([aa[0], ab[0]], axis=0))
    gacc[...] += jnp.sum(part * (x * inv), axis=0, keepdims=True)

    @pl.when(i == pl.num_programs(0) - 1)
    def _():
        width = gw_o.shape[2]
        for z in range(gw_o.shape[0]):
            gw_o[z] = acc[:, z * width : (z + 1) * width].astype(bf16)
        gg_o[...] = gacc[...]


def expert_terms(expert, x, y, router, code, w_gate, w_up, w_down):
    logits = dot_nt(x, router)
    named = code > 0.5
    logits = jnp.where(named, logits, NEG_FILL)
    top = jnp.max(logits, axis=-1, keepdims=True)
    raised = jnp.where(named, jnp.exp(logits - top), 0.0)
    gates = raised / jnp.sum(raised, axis=-1, keepdims=True)
    mine = (lax.broadcasted_iota(i32, gates.shape, 1) == expert) & (code > 1.5)
    weight = RESIDUAL_SCALE * jnp.sum(jnp.where(mine, gates, 0.0), axis=-1, keepdims=True)
    kept = RESIDUAL_SCALE * jnp.sum(jnp.where(mine, 1.0, 0.0), axis=-1, keepdims=True)

    gate_pre = dot_nn(x, w_gate)
    up_pre = dot_nn(x, w_up)
    back = dot_nn(y, w_down)
    sig = jax.nn.sigmoid(gate_pre)
    act = gate_pre * sig
    inner = act * up_pre
    gate_grad = kept * jnp.sum(inner * back, axis=-1, keepdims=True)
    inner_w = (inner * weight).astype(bf16)
    d_inner = back * weight
    d_gate = (d_inner * up_pre * sig * (1.0 + gate_pre * (1.0 - sig))).astype(bf16)
    d_up = (d_inner * act).astype(bf16)
    din = dot_nt(d_gate, w_gate) + dot_nt(d_up, w_up)
    high = gate_grad.astype(bf16).astype(f32)
    low = (gate_grad - high).astype(bf16).astype(f32)
    lane = lax.broadcasted_iota(i32, (x.shape[0], EXTRA), 1)
    side = jnp.where(lane == expert, high, 0.0) + jnp.where(lane == expert + LOW, low, 0.0)
    return inner_w, d_gate, d_up, jnp.concatenate([din, side], axis=1)


def weight_of(weights, which):
    shards, _, depth, ff = weights.shape
    return weights[:, which].reshape(shards * depth, ff)


def clear(accs, i):
    @pl.when(i == 0)
    def _():
        for acc in accs:
            acc[...] = jnp.zeros_like(acc)


def flush(accs, grad_o, i):
    @pl.when(i == pl.num_programs(0) - 1)
    def _():
        shards, _, depth, _ = grad_o.shape
        for which, acc in enumerate(accs):
            for z in range(shards):
                grad_o[z, which] = acc[z * depth : (z + 1) * depth, :].astype(bf16)


def moe_first_kernel(far, which, blocks, *refs):
    xs, ys, (router, code_a, code_b, weights) = (refs[:4], refs[4:8], refs[8:12])
    outs, (b_o, grad_o), accs = (refs[12:16], refs[16:18], refs[18:])
    i = pl.program_id(0)
    flags = (i < far, i < far)
    x, y = (pick(flags, xs), pick(flags, ys))
    code = jnp.concatenate([code_a[0], code_b[0]], axis=0)
    inner_w, d_gate, d_up, din = expert_terms(
        which[0], x, y, router[...], code, *[weight_of(weights, m) for m in range(3)]
    )
    put(flags, outs, din.astype(bf16))
    b_o[0] = inner_w
    clear(accs, i)
    accs[0][...] += dot_tn(x, d_gate)
    accs[1][...] += dot_tn(x, d_up)
    accs[2][...] += dot_tn(y, inner_w)
    flush(accs, grad_o, i)


def moe_second_kernel(far, which, blocks, *refs):
    xs, ys, (router, code_a, code_b, weights) = (refs[:4], refs[4:8], refs[8:12])
    prev, outs, (b_o, dg_o, du_o) = (refs[12:16], refs[16:20], refs[20:])
    i = pl.program_id(0)
    flags = (i < far, i < far)
    x, y = (pick(flags, xs), pick(flags, ys))
    code = jnp.concatenate([code_a[0], code_b[0]], axis=0)
    inner_w, d_gate, d_up, din = expert_terms(
        which[0], x, y, router[...], code, *[weight_of(weights, m) for m in range(3)]
    )
    put(flags, outs, (din + pick(flags, prev).astype(f32)).astype(bf16))
    b_o[0] = inner_w
    dg_o[0] = d_gate
    du_o[0] = d_up


def moe_grads_kernel(far, *refs):
    xs, ys, (b, dg, du), grad_o, accs = (refs[:4], refs[4:8], refs[8:11], refs[11], refs[12:])
    i = pl.program_id(0)
    flags = (i < far, i < far)
    x, y = (pick(flags, xs), pick(flags, ys))
    clear(accs, i)
    accs[0][...] += dot_tn(x, dg[0])
    accs[1][...] += dot_tn(x, du[0])
    accs[2][...] += dot_tn(y, b[0])
    flush(accs, grad_o, i)


def moe_out_kernel(far, b0, b1, w0, w1, *outs):
    i = pl.program_id(0)
    flags = (i < far, i < far)
    out = dot_nt(b0[0], weight_of(w0, 0)) + dot_nt(b1[0], weight_of(w1, 0))
    put(flags, outs, out.astype(bf16))


def place_kernel(far, slot_ref, a, af, b, bf, out):
    i = pl.program_id(0)
    flags = (near(slot_ref, 0, i, far), near(slot_ref, 1, i, far))
    half = a.shape[1]
    for z in range(half):
        out[z, 0] = lax.select(flags[0], a[0, z], af[0, z])
        out[half + z, 0] = lax.select(flags[1], b[0, z], bf[0, z])


def after_attn_kernel(attn, w_out, hidden, gain, resid_o, ma_o, mb_o):
    resid = hidden[...].astype(f32) + RESIDUAL_SCALE * dot_tn(attn[...], w_out[...])
    resid_o[...] = resid
    inv = lax.rsqrt(jnp.mean(resid * resid, axis=-1, keepdims=True) + EPS)
    moe_in = (resid * inv * gain[...]).astype(bf16)
    half = ma_o.shape[1]
    ma_o[0] = moe_in[:half]
    mb_o[0] = moe_in[half:]


def before_attn_kernel(
    a0, a1, b0, b1, resid, ma, mb, grad_out, code, router, gain, w_out,
    d_resid_o, d_branch_o, d_attn_o, d_router_o, d_gain_o,
):
    width = resid.shape[1]
    experts = router.shape[0]
    back = jnp.concatenate(
        [
            a0[...].astype(f32) + a1[...].astype(f32),
            b0[...].astype(f32) + b1[...].astype(f32),
        ],
        axis=0,
    )
    moe_in = jnp.concatenate([ma[0], mb[0]], axis=0)
    chosen = code[...] > 0.5
    logits = jnp.where(chosen, dot_nt(moe_in, router[...]), NEG_FILL)
    raised = jnp.where(chosen, jnp.exp(logits - jnp.max(logits, axis=-1, keepdims=True)), 0.0)
    gates = raised / jnp.sum(raised, axis=-1, keepdims=True)
    gate_grad = (
        back[:, width : width + experts] + back[:, width + LOW : width + LOW + experts]
    )
    logit_grad = gates * (gate_grad - jnp.sum(gates * gate_grad, axis=-1, keepdims=True))
    dlogits = logit_grad.astype(bf16)
    d_router_o[...] = dot_tn(dlogits, moe_in)
    d_moe_in = back[:, :width] + dot_nn(dlogits, router[...])
    r = resid[...]
    inv = lax.rsqrt(jnp.mean(r * r, axis=-1, keepdims=True) + EPS)
    normed = r * inv
    d_gain_o[...] = jnp.sum(d_moe_in * normed, axis=0, keepdims=True)
    d_normed = d_moe_in * gain[...]
    d_resid = grad_out[...].astype(f32) + inv * (
        d_normed - normed * jnp.mean(d_normed * normed, axis=-1, keepdims=True)
    )
    d_resid_o[...] = d_resid
    d_branch = (RESIDUAL_SCALE * d_resid).astype(bf16)
    d_branch_o[...] = d_branch
    d_attn_o[...] = dot_nt(w_out[...], d_branch).astype(bf16)


def wout_grad_kernel(far, slot_ref, attn, d_branch, a, af, b, bf):
    n2, half, rp, width = a.shape
    n = 2 * n2
    d = d_branch[...]
    for z in range(2 * half):
        rows = dot_nn(attn[z * n * rp : (z + 1) * n * rp, :], d).astype(bf16)
        lane = 0 if z < half else 1
        near_o, far_o = ((a, af), (b, bf))[lane]
        for c in range(n):
            part = rows[c * rp : (c + 1) * rp]
            slot = slot_ref[lane, c]

            @pl.when(slot < far)
            def _():
                near_o[slot, z % half] = part

            @pl.when(slot >= far)
            def _():
                far_o[slot - far, z % half] = part


def last_kernel(a0, a1, b0, b1, d_resid, hidden, gain, out):
    d = jnp.concatenate(
        [
            a0[...].astype(f32) + a1[...].astype(f32),
            b0[...].astype(f32) + b1[...].astype(f32),
        ],
        axis=0,
    )
    x = hidden[...].astype(f32)
    inv = lax.rsqrt(jnp.mean(x * x, axis=-1, keepdims=True) + EPS)
    normed = x * inv
    d = d * gain[...]
    out[...] = d_resid[...] + inv * (
        d - normed * jnp.mean(d * normed, axis=-1, keepdims=True)
    )


def whole(shape):
    zeros = (0,) * len(shape)
    return pl.BlockSpec(shape, lambda *at: zeros)


def at_step(shape):
    zeros = (0,) * (len(shape) - 1)
    return pl.BlockSpec(shape, lambda i, *refs: (i,) + zeros)


def lanes_at_step(shape, far):
    zeros = (0,) * (len(shape) - 1)
    first = pl.BlockSpec(shape, lambda i, *refs: (jnp.minimum(i, far - 1),) + zeros)
    second = pl.BlockSpec(shape, lambda i, *refs: (jnp.maximum(i - far, 0),) + zeros)
    return [first, second, first, second]


def lanes_at_slot(shape, far):
    zeros = (0,) * (len(shape) - 1)

    def spec(lane, second):
        def index(i, slots):
            slot = slots[lane, i]
            slot = jnp.maximum(slot - far, 0) if second else jnp.minimum(slot, far - 1)
            return (slot,) + zeros

        return pl.BlockSpec(shape, index)

    return [spec(0, False), spec(0, True), spec(1, False), spec(1, True)]


def shape_of(*dims, dtype=bf16):
    return jax.ShapeDtypeStruct(dims, dtype)


def micros(us):
    return pl.CostEstimate(
        flops=int(us * 1.1e9), bytes_accessed=int(us * 1e6), transcendentals=0
    )


def call(kernel, name, us, out_shape, operands, *, grid=None, specs=None, out_specs=None,
         scratch=(), tables=(), limit=58):
    if grid is None:
        specs = [whole(x.shape) for x in operands]
        out_specs = jax.tree.map(lambda x: whole(x.shape), out_shape)
        grid = 1
    return pl.pallas_call(
        kernel,
        grid_spec=pltpu.PrefetchScalarGridSpec(
            num_scalar_prefetch=len(tables),
            grid=(grid,),
            in_specs=specs,
            out_specs=out_specs,
            scratch_shapes=list(scratch),
        ),
        out_shape=out_shape,
        compiler_params=params(limit * 1024 * 1024),
        cost_estimate=micros(us),
        name=name,
    )(*tables, *operands)


def shards(
    hidden,
    gain_attn,
    w_query,
    w_key,
    w_value,
    w_out,
    gain_ffn,
    router,
    routes,
    slot_order,
    w_gate,
    w_up,
    w_down,
    grad_out,
):
    tok, width = hidden.shape
    n = lax.axis_size("ctx")
    dp = lax.axis_size("dp")
    me = lax.axis_index("ctx")
    copies = n // KV
    far = n // 2
    rp = w_query.shape[0]
    slab = rp * n
    experts = router.shape[1]
    half = tok // 2
    ff = w_gate.shape[2]
    depth = w_gate.shape[1]
    orders = lane_orders(n)
    slots = [slots_of(order) for order in orders]
    blocks = jnp.array(slots, i32) ^ me
    inverse = jnp.array([[lane.index(j) for j in range(n)] for lane in slots], i32)
    slot_at = jnp.take(inverse, jnp.arange(n, dtype=i32) ^ me, axis=1)


    side = QKV + 2 + experts
    pad = -(side + rp * dp) % 16
    send = call(
        prep_kernel,
        "prep",
        2,
        shape_of(n, rp + 16, max(slab, tok, -(-side // 128) * 128)),
        [
            w_query,
            w_key,
            w_value,
            gain_attn[None],
            gain_ffn[None],
            router.T,
            routes.T,
            slot_order,
        ],
        limit=58,
    )
    took = lax.all_to_all(send, "ctx", split_axis=0, concat_axis=0, tiled=True)
    pack = call(
        pack_kernel,
        "pack",
        2,
        shape_of(side + rp * dp, slab),
        [took, w_out],
        limit=58,
    )

    def along(value, by):
        pairs = [(z, z + by) for z in range(dp) if 0 <= z + by < dp]
        return lax.ppermute(value, "dp", pairs)

    below, above = ([], [])
    for _ in range(dp - 1):
        below.append(along(below[-1] if below else pack, 1))
        above.append(along(above[-1] if above else pack, -1))
    wt, gains, router_t, out_rows = call(
        functools.partial(unpack_kernel, dp, rp),
        "unpack",
        2,
        [
            shape_of(QKV, width),
            shape_of(2, width, dtype=f32),
            shape_of(experts, width),
            shape_of(dp, rp, width),
        ],
        [*below[::-1], pack, *above],
        grid=1,
        specs=[whole(pack.shape)] * (2 * dp - 1),
        out_specs=[
            whole((QKV, width)),
            whole((2, width)),
            whole((experts, width)),
            whole((dp, rp, width)),
        ],
        tables=[lax.axis_index("dp").reshape(1).astype(i32)],
        limit=58,
    )
    gain_a, gain_f = (gains[0:1], gains[1:2])

    stacks = [jnp.stack([w_gate[e], w_up[e], w_down[e]]) for e in range(w_gate.shape[0])]
    stacks = after(stacks, below[:-1], above[:-1])
    expert_w = [lax.all_gather(stack, "dp", axis=0) for stack in stacks]

    code = call(
        functools.partial(code_kernel, rp),
        "code",
        6,
        shape_of(n, tok, experts, dtype=f32),
        [took],
        grid=n,
        specs=[at_step((1,) + took.shape[1:])],
        out_specs=at_step((1, tok, experts)),
        scratch=[pltpu.VMEM((experts, 1), f32)],
        limit=58,
    )
    code_mine = lax.dynamic_index_in_dim(code, me, 0, keepdims=False)

    x_rows = after(hidden, took)
    x_rows = Gather(x_rows[:half], x_rows[half:], n)
    xs = x_rows.run()
    y_rows = after(grad_out, x_rows.have)
    y_rows = Gather(y_rows[:half], y_rows[half:], n)

    exponents = jnp.arange(HALF, dtype=f32) * (2.0 / HD)
    inverse_freq = jnp.power(10000.0, -exponents)
    positions = jnp.arange(n * tok, dtype=f32).reshape(n, 1, tok)
    angles = positions * inverse_freq[None, :, None]
    cos, sin = (jnp.cos(angles), jnp.sin(angles))

    o_rows = Gather(out_rows[: dp // 2], out_rows[dp // 2 :], n)
    gain_a, code, y_rows.got = after((gain_a, code, y_rows.got))

    ain, qt, k, kt, v, vt = call(
        functools.partial(qkv_kernel, far),
        "qkv",
        6,
        [
            shape_of(n, tok, width),
            shape_of(n, QW, tok),
            shape_of(n, tok, HD),
            shape_of(n, HD, tok),
            shape_of(n, tok, HD),
            shape_of(n, HD, tok),
        ],
        [*xs, gain_a, wt, cos, sin],
        grid=n,
        specs=lanes_at_slot((1, half, width), far)
        + [whole((1, width)), whole((QKV, width))]
        + [at_step((1, HALF, tok))] * 2,
        out_specs=[
            at_step((1, tok, width)),
            at_step((1, QW, tok)),
            at_step((1, tok, HD)),
            at_step((1, HD, tok)),
            at_step((1, tok, HD)),
            at_step((1, HD, tok)),
        ],
        tables=[slot_at],
        limit=58,
    )

    qt, y_rows.have, y_rows.got, o_rows.have, o_rows.got = after(
        (qt, y_rows.have, y_rows.got, o_rows.have, o_rows.got)
    )
    y_rows.step()
    o_rows.step()
    qt = after(qt, y_rows.have, o_rows.have)
    of, attn_t, lse = call(
        attn_fwd_kernel,
        "attn_fwd",
        19,
        [
            shape_of(n, QW, tok, dtype=f32),
            shape_of(n, QW, tok),
            shape_of(n, 1, GROUP * tok, dtype=f32),
        ],
        [qt, k, vt],
        grid=n,
        specs=[at_step((1, QW, tok)), whole((n, tok, HD)), whole((n, HD, tok))],
        out_specs=[at_step((1, QW, tok))] * 2 + [at_step((1, 1, GROUP * tok))],
        limit=58,
    )

    attn_t, y_rows.got, o_rows.got = after((attn_t, y_rows.got, o_rows.got))
    os = o_rows.run()
    ys = y_rows.run()
    attn_b = lax.all_to_all(attn_t, "ctx", split_axis=0, concat_axis=0, tiled=True)
    attn_b = attn_b[::copies].reshape(KV * QW, tok)

    w_out_all = call(
        functools.partial(place_kernel, far),
        "place",
        4,
        shape_of(dp, n, rp, width),
        os,
        grid=n,
        specs=lanes_at_slot((1, dp // 2, rp, width), far),
        out_specs=pl.BlockSpec((dp, 1, rp, width), lambda i, slots: (0, i, 0, 0)),
        tables=[slot_at],
        limit=58,
    ).reshape(KV * QW, width)

    resid, ma, mb = call(
        after_attn_kernel,
        "after_attn",
        6,
        [shape_of(tok, width, dtype=f32)] + [shape_of(1, half, width)] * 2,
        [attn_b, w_out_all, hidden, gain_f],
        limit=58,
    )
    ms = Gather(ma[0], mb[0], n).run()

    side_w = width + EXTRA
    wide = [shape_of(far, half, side_w)] * 4
    rows_in = lanes_at_step((1, half, width), far) * 2 + [
        whole((experts, width)),
        *[
            pl.BlockSpec((1, half, experts), lambda i, which, blocks, lane=lane: (blocks[lane, i], lane, 0))
            for lane in range(2)
        ],
        whole((dp, 3, depth, ff)),
    ]
    hidden_o = [at_step((1, tok, ff))]
    hidden_s = [shape_of(n, tok, ff)]
    accs = [pltpu.VMEM((width, ff), f32)] * 3
    first = (me * len(expert_w)).reshape(1).astype(i32)
    *din, inner_0, grads_0 = call(
        functools.partial(moe_first_kernel, far),
        "moe_first",
        38,
        wide + hidden_s + [shape_of(dp, 3, depth, ff)],
        [*ms, *ys, router_t, code, code, expert_w[0]],
        grid=n,
        specs=rows_in,
        out_specs=lanes_at_step((1, half, side_w), far) + hidden_o + [whole((dp, 3, depth, ff))],
        scratch=accs,
        tables=[first, blocks],
        limit=58,
    )
    *din, inner_1, d_gate_1, d_up_1 = call(
        functools.partial(moe_second_kernel, far),
        "moe_second",
        25,
        wide + hidden_s * 3,
        [*ms, *ys, router_t, code, code, expert_w[1], *din],
        grid=n,
        specs=rows_in + lanes_at_step((1, half, side_w), far),
        out_specs=lanes_at_step((1, half, side_w), far) + hidden_o * 3,
        tables=[first + 1, blocks],
        limit=58,
    )
    back = Scatter(din, n)
    back.step()
    inner_1 = after(inner_1, back.keep)
    grads_1 = call(
        functools.partial(moe_grads_kernel, far),
        "moe_grads",
        15,
        shape_of(dp, 3, depth, ff),
        [*ms, *ys, inner_1, d_gate_1, d_up_1],
        grid=n,
        specs=lanes_at_step((1, half, width), far) * 2 + hidden_o * 3,
        out_specs=whole((dp, 3, depth, ff)),
        scratch=accs,
        limit=58,
    )
    expert_grads = [
        lax.psum_scatter(grads, "dp", scatter_dimension=0, tiled=True)
        for grads in (grads_0, grads_1)
    ]

    back.got = after(back.got, grads_1)
    (a0, a1), (b0, b1) = back.run()
    inner_1 = after(inner_1, back.keep)
    down = pl.BlockSpec((dp, 1, depth, ff), lambda i: (0, 2, 0, 0))
    outs = call(
        functools.partial(moe_out_kernel, far),
        "moe_out",
        8,
        [shape_of(far, half, width)] * 4,
        [inner_0, inner_1, *expert_w],
        grid=n,
        specs=hidden_o * 2 + [down] * 2,
        out_specs=lanes_at_step((1, half, width), far),
        limit=58,
    )
    mix = Scatter(outs, n)
    resid_in = after(resid, expert_grads[0], outs)
    d_resid, d_branch, d_attn, d_router, d_gain_ffn = call(
        before_attn_kernel,
        "before_attn",
        8,
        [
            shape_of(tok, width, dtype=f32),
            shape_of(tok, width),
            shape_of(KV * QW, tok),
            shape_of(experts, width, dtype=f32),
            shape_of(1, width, dtype=f32),
        ],
        [a0, a1, b0, b1, resid_in, ma, mb, grad_out, code_mine, router_t, gain_f, w_out_all],
        limit=58,
    )
    d_heads = lax.all_to_all(
        jnp.repeat(d_attn.reshape(KV, QW, tok), copies, axis=0),
        "ctx",
        split_axis=0,
        concat_axis=0,
        tiled=True,
    )
    d_wout = call(
        functools.partial(wout_grad_kernel, far),
        "wout_grad",
        6,
        [shape_of(far, dp // 2, rp, width)] * 4,
        [attn_b, d_branch],
        grid=1,
        specs=[whole((KV * QW, tok)), whole((tok, width))],
        out_specs=[whole((far, dp // 2, rp, width))] * 4,
        tables=[slot_at],
        limit=58,
    )

    wout = Scatter(d_wout, n)
    d_heads, wout.got, mix.got = after((d_heads, wout.got, mix.got))
    wout.step()
    mix.step()
    d_heads = after(d_heads, wout.keep, mix.keep)
    dq, dk, dv = call(
        attn_bwd_kernel,
        "attn_bwd",
        24,
        [shape_of(n, QW, tok), shape_of(n, HD, tok), shape_of(n, HD, tok)],
        [qt, d_heads, of, lse, k, kt, v, cos, sin],
        grid=n,
        specs=[
            at_step((1, QW, tok)),
            at_step((1, QW, tok)),
            at_step((1, QW, tok)),
            at_step((1, 1, GROUP * tok)),
            whole((n, tok, HD)),
            whole((n, HD, tok)),
            whole((n, tok, HD)),
            whole((n, HALF, tok)),
            whole((n, HALF, tok)),
        ],
        out_specs=[at_step((1, QW, tok)), whole((n, HD, tok)), whole((n, HD, tok))],
        scratch=[pltpu.VMEM((n, tok, HD), f32), pltpu.VMEM((n, tok, HD), f32)],
        limit=58,
    )

    dq, wout.got, mix.got = after((dq, wout.got, mix.got))
    (p0, p1), (q0, q1) = wout.run()
    (r0, r1), (s0, s1) = mix.run()
    dq = after(dq, wout.keep, mix.keep)

    def columns(rows, lane):
        return pl.BlockSpec((1, rows, half), lambda i, blocks: (blocks[lane, i], 0, lane))

    def tokens(lane):
        return pl.BlockSpec((1, half, width), lambda i, blocks: (blocks[lane, i], lane, 0))

    *d_in, gw, d_gain_attn = call(
        functools.partial(qkv_bwd_kernel, 1.0 / copies, far),
        "qkv_bwd",
        12,
        [shape_of(far, half, width)] * 4
        + [shape_of(dp, QKV, slab), shape_of(1, width, dtype=f32)],
        [dq, dk, dv, dq, dk, dv, ain, ain, *xs, wt],
        grid=n,
        specs=[columns(rows, lane) for lane in range(2) for rows in (QW, HD, HD)]
        + [tokens(0), tokens(1)]
        + lanes_at_step((1, half, width), far)
        + [whole((QKV, width))],
        out_specs=lanes_at_step((1, half, width), far)
        + [whole((dp, QKV, slab)), whole((1, width))],
        scratch=[pltpu.VMEM((QKV, width), f32), pltpu.VMEM((1, width), f32)],
        tables=[blocks],
        limit=58,
    )

    d_wout = jnp.concatenate([add_up(p0, p1), add_up(q0, q1)], axis=0)
    rest = jnp.concatenate([d_gain_attn, d_gain_ffn, d_router], axis=0).astype(bf16)
    grads = jnp.concatenate(
        [
            gw,
            rest.reshape(2 + experts, dp, slab).transpose(1, 0, 2),
            d_wout.reshape(dp, rp * dp, slab),
            jnp.zeros((dp, pad, slab), bf16),
        ],
        axis=1,
    )
    own = lax.psum_scatter(grads, "dp", scatter_dimension=0, tiled=True)[0]
    (c0, c1), (e0, e1) = Scatter(d_in, n).run()
    d_hidden = call(
        last_kernel,
        "last",
        3,
        shape_of(tok, width, dtype=f32),
        [c0, c1, e0, e1, after(d_resid, own), hidden, gain_a],
        limit=58,
    )

    given = lax.all_to_all(
        own[:side].T.reshape(n, rp, side), "ctx", split_axis=0, concat_axis=0, tiled=True
    ).astype(f32)
    heads = given[::copies].transpose(1, 0, 2)
    grad_query = heads[:, :, :QW].reshape(rp, KV * QW)
    grad_key = heads[:, :, QW : QW + HD].reshape(rp, KV * HD)
    grad_value = heads[:, :, QW + HD : QKV].reshape(rp, KV * HD)
    sums = jnp.sum(given[:, :, QKV:], axis=0)
    grad_out_proj = own[side : side + rp * dp].reshape(rp, width).astype(f32)

    mixed = jnp.concatenate(
        [r0.astype(f32) + r1.astype(f32), s0.astype(f32) + s1.astype(f32)], axis=0
    )
    output = (resid + mixed).astype(bf16)

    expert_grads = jnp.concatenate(expert_grads, axis=0).astype(f32)
    return (
        output,
        d_hidden,
        sums[:, 0],
        grad_query,
        grad_key,
        grad_value,
        grad_out_proj,
        sums[:, 1],
        sums[:, 2:],
        expert_grads[:, 0],
        expert_grads[:, 1],
        expert_grads[:, 2],
    )


def solution(mesh):
    rows = P(("dp", "ctx"), None)
    flat = P(("dp", "ctx"))
    expert = P("ctx", "dp", None)
    return jax.shard_map(
        shards,
        mesh=mesh,
        in_specs=(
            rows,
            flat,
            rows,
            rows,
            rows,
            rows,
            flat,
            rows,
            rows,
            rows,
            expert,
            expert,
            expert,
            rows,
        ),
        out_specs=(
            rows,
            rows,
            flat,
            rows,
            rows,
            rows,
            rows,
            flat,
            rows,
            expert,
            expert,
            expert,
        ),
        check_vma=False,
    )
```

time: 738 us -> 513 us (0.70)
  waiting for transfers between devices: 319 us -> 107 us
  Pallas kernels: 150 us -> 243 us
  other arithmetic: 80.9 us -> 19.9 us
  local copies, waits for them, and re-layouts: 81.7 us -> 47.7 us
  starting transfers between devices: 50.9 us -> 72.1 us
  blocking collectives: 16.2 us -> 0 us
  matrix products: 14.2 us -> 0 us
    reduce_scatter x2, waiting for transfers between devices: 150 us -> 1.33 us  [shards(): lax.psum_scatter(grads, 'dp', scatter_dimension=0, tiled=True)]
    pallas_call x7 -> x25, Pallas kernels: 150 us -> 243 us  [the longest x17 232 us: call(): pl.pallas_call(kernel, grid_spec=pltpu.PrefetchScalarGridSpec(num_scalar_...]
    ppermute x48, waiting for transfers between devices: 148 us -> 69.4 us  [swap(): return lax.ppermute(value, 'ctx', [(i, i ^ bit) for i in range(count)])]
    concatenate x29 -> x6, other arithmetic: 46.8 us -> 3.71 us  [step(): jnp.concatenate([have, got], axis=0)]
    slice x27 -> x1, local copies, waits for them, and re-layouts: 21.9 us -> 0.05 us  [shards(): w_up[e]]
    ppermute x0 -> x6, starting transfers between devices: none -> 18.8 us  [along(): return lax.ppermute(value, 'dp', pairs)]
    all_gather x1 -> x0, blocking collectives: 16.2 us -> none  [shards(): lax.all_gather(jnp.concatenate([routes, slot_order.reshape(tok, 1)], axis...]
    dot_general x7 -> x0, matrix products: 14.2 us -> none  [the longest x2 5.05 us: dot_nt(): lax.dot_general(a, b, (((1,), (1,)), ((), ())), preferred_element_type=f32)]
  transfers between devices with their start and end apart: 58 -> 63, of which waited for: 28 -> 29; matrix products, arithmetic and copies ran while one was open for 18% -> 8% of each run, Pallas kernels for 15% -> 48%
where the time goes in v2:
time: 513 us; the launch traced here: 505 us
  Pallas kernels  243 us (47%)
  waiting for transfers between devices  107 us (21%)
  starting transfers between devices  72.1 us (14%)
  local copies, waits for them, and re-layouts  47.7 us (9%)
  other arithmetic  19.9 us (4%)
  between operations  15.1 us (3%)
    pallas_call x17, Pallas kernels, call(): pl.pallas_call(kernel, grid_spec=pltpu.PrefetchScalarGridSpec(num_scalar_...  232 us
    ppermute x48, waiting for transfers between devices, swap(): return lax.ppermute(value, 'ctx', [(i, i ^ bit) for i in range(count)])  69.4 us
    ppermute x48, starting transfers between devices, swap(): return lax.ppermute(value, 'ctx', [(i, i ^ bit) for i in range(count)])  36.2 us
    unnamed x126, local copies, waits for them, and re-layouts  24.8 us
    ppermute x6, starting transfers between devices, along(): return lax.ppermute(value, 'dp', pairs)  18.8 us
    all_to_all x1, waiting for transfers between devices, shards(): lax.all_to_all(jnp.repeat(d_attn.reshape(KV, QW, tok), copies, axis=0), '...  11.8 us
    pallas_call x8, Pallas kernels, fold(): pl.pallas_call(fold_kernel, grid=(half,), in_specs=[near, near, far, far]...  10.7 us
  transfers between devices with their start and end apart: 63, of which 29 were waited for; matrix products, arithmetic and copies ran while one was open for 8% of the time, Pallas kernels for 48%

profile of v2, /device:TPU:0, one launch (start us, length us, event | category | flops | bytes accessed | tf_op | source)
XLA Modules:
  0.0 504.8 jit_solution(10656758935855669469)
XLA Ops:
  9.2 5.3 %all-to-all-start = ((bf16[8,64,384]{2,1,0:T(8,128)(2,1)}), bf16[8,64,384]{2,1,0:T(8,128)(2,1)S(1)}, u32[]{:S(2)}, u32[]{:S(2)}) async-start(bf16[8,64,384]{2,1,0:T(8,128)(2,1)} %prep.1), calls=%async_computation | async-start | bytes 786432 | tf_op jit(solution)/shard_map/all_to_all | solution.py:728
  17.3 5.6 %all-to-all-done.took.table = bf16[8,64,384]{2,1,0:T(8,128)(2,1)S(1)} async-done(((bf16[8,64,384]{2,1,0:T(8,128)(2,1)}), bf16[8,64,384]{2,1,0:T(8,128)(2,1)S(1)}, u32[]{:S(2)}, u32[]{:S(2)}) %all-to-all-start) | async-done | bytes 393248 | tf_op jit(solution)/shard_map/all_to_all | solution.py:728
  30.8 4.6 collective-permute-start.6
  38.6 3.7 collective-permute-done.9.refs_4_
  43.6 4.6 collective-permute-start.7
  48.2 6.0 %code.1.refs_9_.refs_10_ = f32[8,256,16]{2,1,0:T(8,128)} custom-call(bf16[8,64,384]{2,1,0:T(8,128)(2,1)} %copy-done.37), custom_call_target="tpu_custom_call" | custom-call | flops 6600000000 | bytes 6000000 | tf_op jit(solution)/shard_map/code/pallas_call | solution.py:658
  57.4 5.8 %collective-permute-start.8 = (bf16[530,384]{1,0:T(8,128)(2,1)}, bf16[530,384]{1,0:T(8,128)(2,1)}, u32[]{:S(2)}, u32[]{:S(2)}) collective-permute-start(bf16[530,384]{1,0:T(8,128)(2,1)} %copy-done.53), channel_id=1, source_target_pairs={{0,8},{8,16},{16,24},{1,9},{9,17},{17,25},{2,10},{10,18},{18,26},{... | collective-permute-start | bytes 1221128 | tf_op jit(solution)/shard_map/ppermute | solution.py:740
  64.6 2.1 pad_maximum_fusion.1.xb
  68.5 2.1 collective-permute-start.12
  70.6 2.5 collective-permute-done.8.refs_0_
  73.1 3.1 unpack.1
  78.9 2.8 collective-permute-start.14
  81.6 12.3 %qkv.1 = (bf16[8,256,1536]{2,1,0:T(8,128)(2,1)}, bf16[8,192,256]{2,1,0:T(8,128)(2,1)}, bf16[8,256,64]{2,1,0:T(8,128)(2,1)}, bf16[8,64,256]{2,1,0:T(8,128)(2,1)},...) custom-call(s32[2,8]{1,0:T(2,128)} %select_bitcast_fusion.slot_ref, bf16[4,128,1536]{2,1,0:T(8,128)(2,1)} %copy-done.27, ...), custom_call_target="tpu_custom_call" | custom-call | flops 6600000000 | bytes 6000000 | tf_op jit(solution)/shard_map/qkv/pallas_call | solution.py:658
  95.5 2.1 collective-permute-start.18
  105.5 21.0 %attn_fwd.1 = (f32[8,192,256]{2,1,0:T(8,128)}, bf16[8,192,256]{2,1,0:T(8,128)(2,1)}, f32[8,1,768]{2,1,0:T(1,128)}) custom-call(bf16[8,192,256]{2,1,0:T(8,128)(2,1)} %get-tuple-element.153.qt, bf16[8,256,64]{2,1,0:T(8,128)(2,1)} %get-tuple-element.154.k, bf16[8,64,256]{2,1,0:T(8,128)(2,1)} %get-tuple-element.155.vt), custom_call_target="tpu_custom_call" | custom-call | flops 20899999744 | bytes 19000000 | tf_op jit(solution)/shard_map/attn_fwd/pallas_call | solution.py:658
  126.5 2.8 collective-permute-done.17
  131.6 3.5 all-to-all-start.1
  137.1 8.0 %place.1 = bf16[4,8,48,1536]{3,2,1,0:T(8,128)(2,1)} custom-call(s32[2,8]{1,0:T(2,128)} %select_bitcast_fusion.slot_ref, bf16[4,2,48,1536]{3,2,1,0:T(8,128)(2,1)} %constant_dynamic-update-slice_fusion.8.a, bf16[4,2,48,1536]{3,2,1,0:T(8,128)(2,1)} %copy-done.47, bf16[4,2,48,1536]{3,2,1,0:T(8,128)(2,1)} %constant_dynamic-update-slice_fusion.11.b, ...), custom_call_target="tpu_custom_call" | custom-call | flops 4400000000 | bytes 4000000 | tf_op jit(solution)/shard_map/place/pallas_call | solution.py:658
  145.1 2.5 all-to-all-done.1
  148.5 5.7 %after_attn.1 = (f32[256,1536]{1,0:T(8,128)}, bf16[1,128,1536]{2,1,0:T(8,128)(2,1)}, bf16[1,128,1536]{2,1,0:T(8,128)(2,1)}) custom-call(bf16[1536,256]{1,0:T(8,128)(2,1)} %bitcast.70, bf16[1536,1536]{1,0:T(8,128)(2,1)} %bitcast.89, bf16[256,1536]{1,0:T(8,128)(2,1)} %hidden.3, f32[1,1536]{1,0:T(1,128)} %get-tuple-element.319.gain), custom_call_target="tpu_custom_call" | custom-call | flops 6600000000 | bytes 6000000 | tf_op jit(solution)/shard_map/after_attn/pallas_call | solution.py:658
  157.7 6.7 %collective-permute-done.25 = bf16[1,128,1536]{2,1,0:T(8,128)(2,1)S(1)} collective-permute-done((bf16[1,128,1536]{2,1,0:T(8,128)(2,1)}, bf16[1,128,1536]{2,1,0:T(8,128)(2,1)S(1)}, u32[]{:S(2)}, u32[]{:S(2)}) %collective-permute-start.25) | collective-permute-done | bytes 393248 | tf_op jit(solution)/shard_map/ppermute | solution.py:67
  169.5 14.6 %collective-permute-done.26 = bf16[2,128,1536]{2,1,0:T(8,128)(2,1)S(1)} collective-permute-done((bf16[2,128,1536]{2,1,0:T(8,128)(2,1)S(1)}, bf16[2,128,1536]{2,1,0:T(8,128)(2,1)S(1)}, u32[]{:S(2)}, u32[]{:S(2)}) %collective-permute-start.26) | collective-permute-done | bytes 786464 | tf_op jit(solution)/shard_map/ppermute | solution.py:67
  184.2 2.4 collective-permute-done.23
  187.8 2.6 collective-permute-done.24.refs_1_
  190.3 45.6 %moe_first.1 = (bf16[4,128,1664]{2,1,0:T(8,128)(2,1)}, bf16[4,128,1664]{2,1,0:T(8,128)(2,1)}, bf16[4,128,1664]{2,1,0:T(8,128)(2,1)}, bf16[4,128,1664]{2,1,0:T(8,...) custom-call(s32[1]{0:T(128)} %bitcast.15.which, s32[2,8]{1,0:T(2,128)} %broadcast_xor_fusion.blocks.blocks_ref, ...), custom_call_target="tpu_custom_call" | custom-call | flops 41799999488 | bytes 38000000 | tf_op jit(solution)/shard_map/moe_first/pallas_call | solution.py:658
  236.2 2.2 all-gather.7.cloned.1.call-done
  238.4 32.5 %moe_second.1 = (bf16[4,128,1664]{2,1,0:T(8,128)(2,1)}, bf16[4,128,1664]{2,1,0:T(8,128)(2,1)}, bf16[4,128,1664]{2,1,0:T(8,128)(2,1)}, bf16[4,128,1664]{2,1,0:T(8...) custom-call(s32[1]{0:T(128)S(6)} %add.64.which, ...), custom_call_target="tpu_custom_call" | custom-call | flops 27499999232 | bytes 25000000 | tf_op jit(solution)/shard_map/moe_second/pallas_call | solution.py:658
  274.8 2.4 collective-permute-done.31.refs_5_.refs_7_
  286.6 18.4 %moe_grads.1 = bf16[4,3,384,512]{3,2,1,0:T(8,128)(2,1)} custom-call(bf16[4,128,1536]{2,1,0:T(8,128)(2,1)} %copy-done.41, bf16[4,128,1536]{2,1,0:T(8,128)(2,1)} %collective-permute-done.24.refs_1_, bf16[4,128,1536]{2,1,0:T(8,128)(2,1)} %copy-done.40, bf16[4,128,1536]{2,1,0:T(8,128)(2,1)} %collective-permute-done.27.refs_3_, ...), custom_call_target="tpu_custom_call" | custom-call | flops 16499999744 | bytes 15000000 | tf_op jit(solution)/shard_map/moe_grads/pallas_call | solution.py:658
  310.6 12.7 %moe_out.1 = (bf16[4,128,1536]{2,1,0:T(8,128)(2,1)}, bf16[4,128,1536]{2,1,0:T(8,128)(2,1)}, bf16[4,128,1536]{2,1,0:T(8,128)(2,1)}, bf16[4,128,1536]{2,1,0:T(8,128)(2,1)}) custom-call(bf16[8,256,512]{2,1,0:T(8,128)(2,1)} %get-tuple-element.168.b0, bf16[8,256,512]{2,1,0:T(8,128)(2,1)} %get-tuple-element.190.refs_8_.b1, bf16[4,3,384,512]{3,2,1,0:T(8,128)(2,1)} %bitcast.78, ...), custom_call_target="tpu_custom_call" | custom-call | flops 8800000000 | bytes 8000000 | tf_op jit(solution)/shard_map/moe_out/pallas_call | solution.py:658
  326.1 7.9 %before_attn.1 = (f32[256,1536]{1,0:T(8,128)}, bf16[256,1536]{1,0:T(8,128)(2,1)}, bf16[1536,256]{1,0:T(8,128)(2,1)}, f32[16,1536]{1,0:T(8,128)}, f32[1,1536]{1,0:T(1,128)}) custom-call(bf16[128,1664]{1,0:T(8,128)(2,1)} %bitcast.66, bf16[128,1664]{1,0:T(8,128)(2,1)} %bitcast.81, bf16[128,1664]{1,0:T(8,128)(2,1)} %bitcast.67, bf16[128,1664]{1,0:T(8,128)(2,1)} %bitcast.82, ...), custom_call_target="tpu_custom_call" | custom-call | flops 8800000000 | bytes 8000000 | tf_op jit(solution)/shard_map/before_attn/pallas_call | solution.py:658
  334.0 7.2 %wout_grad.1 = (bf16[4,2,48,1536]{3,2,1,0:T(8,128)(2,1)}, bf16[4,2,48,1536]{3,2,1,0:T(8,128)(2,1)}, bf16[4,2,48,1536]{3,2,1,0:T(8,128)(2,1)}, bf16[4,2,48,1536]{3,2,1,0:T(8,128)(2,1)}) custom-call(s32[2,8]{1,0:T(2,128)} %select_bitcast_fusion.slot_ref, bf16[1536,256]{1,0:T(8,128)(2,1)} %bitcast.71, bf16[256,1536]{1,0:T(8,128)(2,1)} %get-tuple-element.200.d_branch), custom_call_target="tpu_custom_call" | custom-call | flops 6600000000 | bytes 6000000 | tf_op jit(solution)/shard_map/wout_grad/pallas_call | solution.py:658
  341.7 4.2 all-to-all-start.2
  346.7 11.8 %all-to-all-done.2.dot_ = bf16[8,192,256]{2,1,0:T(8,128)(2,1)} async-done(((bf16[8,192,256]{2,1,0:T(8,128)(2,1)}), bf16[8,192,256]{2,1,0:T(8,128)(2,1)}, u32[]{:S(2)}, u32[]{:S(2)}) %all-to-all-start.2) | async-done | bytes 786464 | tf_op jit(solution)/shard_map/all_to_all | solution.py:973
  358.6 3.0 fold.10
  361.6 2.5 fold.11
  369.9 26.5 %attn_bwd.1 = (bf16[8,192,256]{2,1,0:T(8,128)(2,1)}, bf16[8,64,256]{2,1,0:T(8,128)(2,1)}, bf16[8,64,256]{2,1,0:T(8,128)(2,1)}) custom-call(bf16[8,192,256]{2,1,0:T(8,128)(2,1)} %get-tuple-element.153.qt, bf16[8,192,256]{2,1,0:T(8,128)(2,1)} %all-to-all-done.2.dot_, f32[8,192,256]{2,1,0:T(8,128)} %get-tuple-element.215.of, ...), custom_call_target="tpu_custom_call" | custom-call | flops 26400000000 | bytes 24000000 | tf_op jit(solution)/shard_map/attn_bwd/pallas_call | solution.py:658
  401.5 17.3 %qkv_bwd.1 = (bf16[4,128,1536]{2,1,0:T(8,128)(2,1)}, bf16[4,128,1536]{2,1,0:T(8,128)(2,1)}, bf16[4,128,1536]{2,1,0:T(8,128)(2,1)}, bf16[4,128,1536]{2,1,0:T(8,12...) custom-call(s32[2,8]{1,0:T(2,128)} %broadcast_xor_fusion.blocks.blocks_ref, ...), custom_call_target="tpu_custom_call" | custom-call | flops 13200000000 | bytes 12000000 | tf_op jit(solution)/shard_map/qkv_bwd/pallas_call | solution.py:658
  423.8 3.6 collective-permute-done.53
  431.1 3.0 maximum_maximum_fusion
  438.0 2.3 slice_bitcast_fusion
  443.5 3.9 collective-permute-done.44
  447.5 4.9 collective-permute-done.45
  452.4 13.3 %collective-permute-done.48.refs_1_.refs_3_ = bf16[2,128,1536]{2,1,0:T(8,128)(2,1)S(1)} collective-permute-done((bf16[2,128,1536]{2,1,0:T(8,128)(2,1)S(1)}, bf16[2,128,1536]{2,1,0:T(8,128)(2,1)S(1)}, u32[]{:S(2)}, u32[]{:S(2)}) %collective-permute-start.48) | collective-permute-done | bytes 786464 | tf_op jit(solution)/shard_map/ppermute | solution.py:67
  470.3 5.0 collective-permute-done.50
  476.6 4.1 last.1
  482.6 3.4 all-to-all-start.3
  487.7 5.5 %all-to-all-done.3 = bf16[8,48,338]{2,1,0:T(8,128)(2,1)S(1)} async-done(((bf16[8,48,338]{2,1,0:T(8,128)(2,1)}), bf16[8,48,338]{2,1,0:T(8,128)(2,1)S(1)}, u32[]{:S(2)}, u32[]{:S(2)}) %all-to-all-start.3) | async-done | bytes 259616 | tf_op jit(solution)/shard_map/all_to_all | solution.py:1073
  (298 shorter events, 114.1 us)
Async XLA Ops:
  9.2 13.6 %all-to-all-start = ((bf16[8,64,384]{2,1,0:T(8,128)(2,1)}), bf16[8,64,384]{2,1,0:T(8,128)(2,1)S(1)}, u32[]{:S(2)}, u32[]{:S(2)}) async-start(bf16[8,64,384]{2,1,0:T(8,128)(2,1)} %prep.1), calls=%async_computation | async-start | bytes 786432 | tf_op jit(solution)/shard_map/all_to_all | solution.py:728
  14.5 175.8 %all-gather.5.cloned.1.call-start = ((), (), s32[]{:S(2)}) async-start(), calls=%async_computation.10 | async-start | bytes 5898240 | tf_op jit(solution)/shard_map/all_gather | solution.py:772
  29.5 12.8 %collective-permute-start.9 = (bf16[530,384]{1,0:T(8,128)(2,1)}, bf16[530,384]{1,0:T(8,128)(2,1)S(1)}, u32[]{:S(2)}, u32[]{:S(2)}) collective-permute-start(bf16[530,384]{1,0:T(8,128)(2,1)} %pack.1.refs_3_), channel_id=1, source_target_pairs={{8,0},{16,8},{24,16},{9,1},{17,9},{25,17},{10,2},{18,10},{26,18},{... | collective-permute-start | bytes 1221128 | tf_op jit(solution)/shard_map/ppermute | solution.py:740
  30.8 12.8 %collective-permute-start.6 = (bf16[530,384]{1,0:T(8,128)(2,1)}, bf16[530,384]{1,0:T(8,128)(2,1)S(1)}, u32[]{:S(2)}, u32[]{:S(2)}) collective-permute-start(bf16[530,384]{1,0:T(8,128)(2,1)} %pack.1.refs_3_), channel_id=1, source_target_pairs={{0,8},{8,16},{16,24},{1,9},{9,17},{17,25},{2,10},{10,18},{18,26},{... | collective-permute-start | bytes 1221128 | tf_op jit(solution)/shard_map/ppermute | solution.py:740
  35.5 27.7 %collective-permute-start.1 = (bf16[2,128,1536]{2,1,0:T(8,128)(2,1)S(1)}, bf16[2,128,1536]{2,1,0:T(8,128)(2,1)}, u32[]{:S(2)}, u32[]{:S(2)}) collective-permute-start(bf16[2,128,1536]{2,1,0:T(8,128)(2,1)S(1)} %pad_maximum_fusion.4), channel_id=1, source_target_pairs={{0,2},{1,3},{2,0},{3,1},{4,6},{5,7},{6,4},{7,5},{8,10},{9,11},{10,... | collective-permute-start | bytes 2359304 | tf_op jit(solution)/shard_map/ppermute | solution.py:67
  37.1 27.6 %collective-permute-start.4 = (bf16[2,128,1536]{2,1,0:T(8,128)(2,1)S(1)}, bf16[2,128,1536]{2,1,0:T(8,128)(2,1)}, u32[]{:S(2)}, u32[]{:S(2)}) collective-permute-start(bf16[2,128,1536]{2,1,0:T(8,128)(2,1)S(1)} %pad_maximum_fusion.5), channel_id=1, source_target_pairs={{0,4},{1,5},{2,6},{3,7},{4,0},{5,1},{6,2},{7,3},{8,12},{9,13},{10,... | collective-permute-start | bytes 2359304 | tf_op jit(solution)/shard_map/ppermute | solution.py:67
  42.3 11.9 %collective-permute-start.10 = (bf16[530,384]{1,0:T(8,128)(2,1)S(1)}, bf16[530,384]{1,0:T(8,128)(2,1)S(1)}, u32[]{:S(2)}, u32[]{:S(2)}) collective-permute-start(bf16[530,384]{1,0:T(8,128)(2,1)S(1)} %collective-permute-done.9.refs_4_), channel_id=1, source_target_pairs={{8,0},{16,8},{24,16},{9,1},{17,9},{25,17},{10,2},{18,10},{26,18},{... | collective-permute-start | bytes 1221128 | tf_op jit(solution)/shard_map/ppermute | solution.py:740
  43.6 11.7 %collective-permute-start.7 = (bf16[530,384]{1,0:T(8,128)(2,1)S(1)}, bf16[530,384]{1,0:T(8,128)(2,1)S(1)}, u32[]{:S(2)}, u32[]{:S(2)}) collective-permute-start(bf16[530,384]{1,0:T(8,128)(2,1)S(1)} %collective-permute-done.6.refs_2_), channel_id=1, source_target_pairs={{0,8},{8,16},{16,24},{1,9},{9,17},{17,25},{2,10},{10,18},{18,26},{... | collective-permute-start | bytes 1221128 | tf_op jit(solution)/shard_map/ppermute | solution.py:740
  57.4 15.7 %collective-permute-start.8 = (bf16[530,384]{1,0:T(8,128)(2,1)}, bf16[530,384]{1,0:T(8,128)(2,1)}, u32[]{:S(2)}, u32[]{:S(2)}) collective-permute-start(bf16[530,384]{1,0:T(8,128)(2,1)} %copy-done.53), channel_id=1, source_target_pairs={{0,8},{8,16},{16,24},{1,9},{9,17},{17,25},{2,10},{10,18},{18,26},{... | collective-permute-start | bytes 1221128 | tf_op jit(solution)/shard_map/ppermute | solution.py:740
  64.6 17.1 %collective-permute-start.2 = (bf16[4,128,1536]{2,1,0:T(8,128)(2,1)S(1)}, bf16[4,128,1536]{2,1,0:T(8,128)(2,1)}, u32[]{:S(2)}, u32[]{:S(2)}) collective-permute-start(bf16[4,128,1536]{2,1,0:T(8,128)(2,1)S(1)} %pad_maximum_fusion.xa), channel_id=1, source_target_pairs={{0,1},{1,0},{2,3},{3,2},{4,5},{5,4},{6,7},{7,6},{8,9},{9,8},{10,11... | collective-permute-start | bytes 4718600 | tf_op jit(solution)/shard_map/ppermute | solution.py:67
  66.7 14.9 %collective-permute-start.5 = (bf16[4,128,1536]{2,1,0:T(8,128)(2,1)S(1)}, bf16[4,128,1536]{2,1,0:T(8,128)(2,1)}, u32[]{:S(2)}, u32[]{:S(2)}) collective-permute-start(bf16[4,128,1536]{2,1,0:T(8,128)(2,1)S(1)} %pad_maximum_fusion.1.xb), channel_id=1, source_target_pairs={{0,1},{1,0},{2,3},{3,2},{4,5},{5,4},{6,7},{7,6},{8,9},{9,8},{10,11... | collective-permute-start | bytes 4718600 | tf_op jit(solution)/shard_map/ppermute | solution.py:67
  66.9 12.0 %collective-permute-start.13 = (bf16[1,128,1536]{2,1,0:T(8,128)(2,1)S(1)}, bf16[1,128,1536]{2,1,0:T(8,128)(2,1)S(1)}, u32[]{:S(2)}, u32[]{:S(2)}) collective-permute-start(bf16[1,128,1536]{2,1,0:T(8,128)(2,1)S(1)} %get-tuple-element.147), channel_id=1, source_target_pairs={{0,2},{1,3},{2,0},{3,1},{4,6},{5,7},{6,4},{7,5},{8,10},{9,11},{10,... | collective-permute-start | bytes 1179656 | tf_op jit(solution)/shard_map/ppermute | solution.py:67
  68.5 13.1 %collective-permute-start.12 = (bf16[1,128,1536]{2,1,0:T(8,128)(2,1)S(1)}, bf16[1,128,1536]{2,1,0:T(8,128)(2,1)S(1)}, u32[]{:S(2)}, u32[]{:S(2)}) collective-permute-start(bf16[1,128,1536]{2,1,0:T(8,128)(2,1)S(1)} %get-tuple-element.145), channel_id=1, source_target_pairs={{0,4},{1,5},{2,6},{3,7},{4,0},{5,1},{6,2},{7,3},{8,12},{9,13},{10,... | collective-permute-start | bytes 1179656 | tf_op jit(solution)/shard_map/ppermute | solution.py:67
  77.3 16.6 %collective-permute-start.15 = (bf16[1,2,48,1536]{3,2,1,0:T(8,128)(2,1)S(1)}, bf16[1,2,48,1536]{3,2,1,0:T(8,128)(2,1)S(1)}, u32[]{:S(2)}, u32[]{:S(2)}) collective-permute-start(bf16[1,2,48,1536]{3,2,1,0:T(8,128)(2,1)S(1)} %get-tuple-element.151), channel_id=1, source_target_pairs={{0,2},{1,3},{2,0},{3,1},{4,6},{5,7},{6,4},{7,5},{8,10},{9,11},{10,... | collective-permute-start | bytes 884744 | tf_op jit(solution)/shard_map/ppermute | solution.py:67
  78.9 15.1 %collective-permute-start.14 = (bf16[1,2,48,1536]{3,2,1,0:T(8,128)(2,1)S(1)}, bf16[1,2,48,1536]{3,2,1,0:T(8,128)(2,1)S(1)}, u32[]{:S(2)}, u32[]{:S(2)}) collective-permute-start(bf16[1,2,48,1536]{3,2,1,0:T(8,128)(2,1)S(1)} %get-tuple-element.149), channel_id=1, source_target_pairs={{0,4},{1,5},{2,6},{3,7},{4,0},{5,1},{6,2},{7,3},{8,12},{9,13},{10,... | collective-permute-start | bytes 884744 | tf_op jit(solution)/shard_map/ppermute | solution.py:67
  95.5 31.0 %collective-permute-start.18 = (bf16[2,2,48,1536]{3,2,1,0:T(8,128)(2,1)}, bf16[2,2,48,1536]{3,2,1,0:T(8,128)(2,1)S(1)}, u32[]{:S(2)}, u32[]{:S(2)}) collective-permute-start(bf16[2,2,48,1536]{3,2,1,0:T(8,128)(2,1)} %get-tuple-element.316), channel_id=1, source_target_pairs={{0,2},{1,3},{2,0},{3,1},{4,6},{5,7},{6,4},{7,5},{8,10},{9,11},{10,... | collective-permute-start | bytes 1769480 | tf_op jit(solution)/shard_map/ppermute | solution.py:67
  100.1 26.3 %collective-permute-start.19 = (bf16[2,2,48,1536]{3,2,1,0:T(8,128)(2,1)}, bf16[2,2,48,1536]{3,2,1,0:T(8,128)(2,1)S(1)}, u32[]{:S(2)}, u32[]{:S(2)}) collective-permute-start(bf16[2,2,48,1536]{3,2,1,0:T(8,128)(2,1)} %get-tuple-element.312), channel_id=1, source_target_pairs={{0,4},{1,5},{2,6},{3,7},{4,0},{5,1},{6,2},{7,3},{8,12},{9,13},{10,... | collective-permute-start | bytes 1769480 | tf_op jit(solution)/shard_map/ppermute | solution.py:67
  102.1 24.4 %collective-permute-start.16 = (bf16[2,128,1536]{2,1,0:T(8,128)(2,1)S(1)}, bf16[2,128,1536]{2,1,0:T(8,128)(2,1)S(1)}, u32[]{:S(2)}, u32[]{:S(2)}) collective-permute-start(bf16[2,128,1536]{2,1,0:T(8,128)(2,1)S(1)} %get-tuple-element.306), channel_id=1, source_target_pairs={{0,2},{1,3},{2,0},{3,1},{4,6},{5,7},{6,4},{7,5},{8,10},{9,11},{10,... | collective-permute-start | bytes 2359304 | tf_op jit(solution)/shard_map/ppermute | solution.py:67
  103.8 25.5 %collective-permute-start.17 = (bf16[2,128,1536]{2,1,0:T(8,128)(2,1)S(1)}, bf16[2,128,1536]{2,1,0:T(8,128)(2,1)S(1)}, u32[]{:S(2)}, u32[]{:S(2)}) collective-permute-start(bf16[2,128,1536]{2,1,0:T(8,128)(2,1)S(1)} %get-tuple-element.302), channel_id=1, source_target_pairs={{0,4},{1,5},{2,6},{3,7},{4,0},{5,1},{6,2},{7,3},{8,12},{9,13},{10,... | collective-permute-start | bytes 2359304 | tf_op jit(solution)/shard_map/ppermute | solution.py:67
  131.6 16.1 %all-to-all-start.1 = ((bf16[8,192,256]{2,1,0:T(8,128)(2,1)}), bf16[8,192,256]{2,1,0:T(8,128)(2,1)S(1)}, u32[]{:S(2)}, u32[]{:S(2)}) async-start(bf16[8,192,256]{2,1,0:T(8,128)(2,1)} %get-tuple-element.157), calls=%async_computation.1 | async-start | bytes 1572864 | tf_op jit(solution)/shard_map/all_to_all | solution.py:857
  135.1 103.3 %all-gather.7.cloned.1.call-start = ((), (), s32[]{:S(2)}) async-start(), calls=%async_computation.11 | async-start | bytes 5898240 | tf_op jit(solution)/shard_map/all_gather | solution.py:772
  135.9 189.3 %reduce-scatter.4.cloned.1.call-start = ((), (), s32[]{:S(2)}) async-start(), calls=%async_computation.7 | async-start | bytes 5898240 | tf_op jit(solution)/shard_map/reduce_scatter | solution.py:938
  155.7 31.8 %collective-permute-start.28 = (bf16[4,128,1536]{2,1,0:T(8,128)(2,1)}, bf16[4,128,1536]{2,1,0:T(8,128)(2,1)}, u32[]{:S(2)}, u32[]{:S(2)}) collective-permute-start(bf16[4,128,1536]{2,1,0:T(8,128)(2,1)} %constant_dynamic-update-slice_fusion.20.refs_4_), channel_id=1, source_target_pairs={{0,1},{1,0},{2,3},{3,2},{4,5},{5,4},{6,7},{7,6},{8,9},{9,8},{10,11... | collective-permute-start | bytes 4718600 | tf_op jit(solution)/shard_map/ppermute | solution.py:67
  155.7 11.9 %collective-permute-start.22 = (bf16[1,128,1536]{2,1,0:T(8,128)(2,1)S(1)}, bf16[1,128,1536]{2,1,0:T(8,128)(2,1)S(1)}, u32[]{:S(2)}, u32[]{:S(2)}) collective-permute-start(bf16[1,128,1536]{2,1,0:T(8,128)(2,1)S(1)} %copy-done.30), channel_id=1, source_target_pairs={{0,4},{1,5},{2,6},{3,7},{4,0},{5,1},{6,2},{7,3},{8,12},{9,13},{10,... | collective-permute-start | bytes 1179656 | tf_op jit(solution)/shard_map/ppermute | solution.py:67
  157.5 30.0 %collective-permute-start.29 = (bf16[4,128,1536]{2,1,0:T(8,128)(2,1)}, bf16[4,128,1536]{2,1,0:T(8,128)(2,1)}, u32[]{:S(2)}, u32[]{:S(2)}) collective-permute-start(bf16[4,128,1536]{2,1,0:T(8,128)(2,1)} %constant_dynamic-update-slice_fusion.23.refs_6_), channel_id=1, source_target_pairs={{0,1},{1,0},{2,3},{3,2},{4,5},{5,4},{6,7},{7,6},{8,9},{9,8},{10,11... | collective-permute-start | bytes 4718600 | tf_op jit(solution)/shard_map/ppermute | solution.py:67
  164.5 19.6 %collective-permute-start.26 = (bf16[2,128,1536]{2,1,0:T(8,128)(2,1)S(1)}, bf16[2,128,1536]{2,1,0:T(8,128)(2,1)S(1)}, u32[]{:S(2)}, u32[]{:S(2)}) collective-permute-start(bf16[2,128,1536]{2,1,0:T(8,128)(2,1)S(1)} %pad_maximum_fusion.7), channel_id=1, source_target_pairs={{0,4},{1,5},{2,6},{3,7},{4,0},{5,1},{6,2},{7,3},{8,12},{9,13},{10,... | collective-permute-start | bytes 2359304 | tf_op jit(solution)/shard_map/ppermute | solution.py:67
  167.7 19.0 %collective-permute-start.23 = (bf16[2,128,1536]{2,1,0:T(8,128)(2,1)S(1)}, bf16[2,128,1536]{2,1,0:T(8,128)(2,1)S(1)}, u32[]{:S(2)}, u32[]{:S(2)}) collective-permute-start(bf16[2,128,1536]{2,1,0:T(8,128)(2,1)S(1)} %pad_maximum_fusion.6), channel_id=1, source_target_pairs={{0,2},{1,3},{2,0},{3,1},{4,6},{5,7},{6,4},{7,5},{8,10},{9,11},{10,... | collective-permute-start | bytes 2359304 | tf_op jit(solution)/shard_map/ppermute | solution.py:67
  235.9 198.2 %reduce-scatter.8.cloned.1.call-start = ((), (), s32[]{:S(2)}) async-start(), calls=%async_computation.9 | async-start | bytes 5898240 | tf_op jit(solution)/shard_map/reduce_scatter | solution.py:938
  283.6 21.5 %collective-permute-start.32 = (bf16[2,128,1664]{2,1,0:T(8,128)(2,1)}, bf16[2,128,1664]{2,1,0:T(8,128)(2,1)S(1)}, u32[]{:S(2)}, u32[]{:S(2)}) collective-permute-start(bf16[2,128,1664]{2,1,0:T(8,128)(2,1)} %get-tuple-element.182), channel_id=1, source_target_pairs={{0,2},{1,3},{2,0},{3,1},{4,6},{5,7},{6,4},{7,5},{8,10},{9,11},{10,... | collective-permute-start | bytes 2555912 | tf_op jit(solution)/shard_map/ppermute | solution.py:67
  285.2 20.9 %collective-permute-start.33 = (bf16[2,128,1664]{2,1,0:T(8,128)(2,1)}, bf16[2,128,1664]{2,1,0:T(8,128)(2,1)S(1)}, u32[]{:S(2)}, u32[]{:S(2)}) collective-permute-start(bf16[2,128,1664]{2,1,0:T(8,128)(2,1)} %get-tuple-element.183), channel_id=1, source_target_pairs={{0,4},{1,5},{2,6},{3,7},{4,0},{5,1},{6,2},{7,3},{8,12},{9,13},{10,... | collective-permute-start | bytes 2555912 | tf_op jit(solution)/shard_map/ppermute | solution.py:67
  309.0 16.2 %collective-permute-start.34 = (bf16[1,128,1664]{2,1,0:T(8,128)(2,1)}, bf16[1,128,1664]{2,1,0:T(8,128)(2,1)S(1)}, u32[]{:S(2)}, u32[]{:S(2)}) collective-permute-start(bf16[1,128,1664]{2,1,0:T(8,128)(2,1)} %get-tuple-element.192), channel_id=1, source_target_pairs={{0,4},{1,5},{2,6},{3,7},{4,0},{5,1},{6,2},{7,3},{8,12},{9,13},{10,... | collective-permute-start | bytes 1277960 | tf_op jit(solution)/shard_map/ppermute | solution.py:67
  310.1 15.1 %collective-permute-start.35 = (bf16[1,128,1664]{2,1,0:T(8,128)(2,1)}, bf16[1,128,1664]{2,1,0:T(8,128)(2,1)S(1)}, u32[]{:S(2)}, u32[]{:S(2)}) collective-permute-start(bf16[1,128,1664]{2,1,0:T(8,128)(2,1)} %get-tuple-element.193), channel_id=1, source_target_pairs={{0,2},{1,3},{2,0},{3,1},{4,6},{5,7},{6,4},{7,5},{8,10},{9,11},{10,... | collective-permute-start | bytes 1277960 | tf_op jit(solution)/shard_map/ppermute | solution.py:67
  323.4 23.4 %collective-permute-start.38 = (bf16[4,128,1536]{2,1,0:T(8,128)(2,1)}, bf16[4,128,1536]{2,1,0:T(8,128)(2,1)}, u32[]{:S(2)}, u32[]{:S(2)}) collective-permute-start(bf16[4,128,1536]{2,1,0:T(8,128)(2,1)} %get-tuple-element.195), channel_id=1, source_target_pairs={{0,1},{1,0},{2,3},{3,2},{4,5},{5,4},{6,7},{7,6},{8,9},{9,8},{10,11... | collective-permute-start | bytes 4718600 | tf_op jit(solution)/shard_map/ppermute | solution.py:67
  323.4 23.4 %collective-permute-start.39 = (bf16[4,128,1536]{2,1,0:T(8,128)(2,1)}, bf16[4,128,1536]{2,1,0:T(8,128)(2,1)}, u32[]{:S(2)}, u32[]{:S(2)}) collective-permute-start(bf16[4,128,1536]{2,1,0:T(8,128)(2,1)} %get-tuple-element.197), channel_id=1, source_target_pairs={{0,1},{1,0},{2,3},{3,2},{4,5},{5,4},{6,7},{7,6},{8,9},{9,8},{10,11... | collective-permute-start | bytes 4718600 | tf_op jit(solution)/shard_map/ppermute | solution.py:67
  341.2 17.4 %collective-permute-start.36 = (bf16[4,2,48,1536]{3,2,1,0:T(8,128)(2,1)}, bf16[4,2,48,1536]{3,2,1,0:T(8,128)(2,1)}, u32[]{:S(2)}, u32[]{:S(2)}) collective-permute-start(bf16[4,2,48,1536]{3,2,1,0:T(8,128)(2,1)} %get-tuple-element.201), channel_id=1, source_target_pairs={{0,1},{1,0},{2,3},{3,2},{4,5},{5,4},{6,7},{7,6},{8,9},{9,8},{10,11... | collective-permute-start | bytes 3538952 | tf_op jit(solution)/shard_map/ppermute | solution.py:67
  341.3 17.3 %collective-permute-start.37 = (bf16[4,2,48,1536]{3,2,1,0:T(8,128)(2,1)}, bf16[4,2,48,1536]{3,2,1,0:T(8,128)(2,1)}, u32[]{:S(2)}, u32[]{:S(2)}) collective-permute-start(bf16[4,2,48,1536]{3,2,1,0:T(8,128)(2,1)} %get-tuple-element.202), channel_id=1, source_target_pairs={{0,1},{1,0},{2,3},{3,2},{4,5},{5,4},{6,7},{7,6},{8,9},{9,8},{10,11... | collective-permute-start | bytes 3538952 | tf_op jit(solution)/shard_map/ppermute | solution.py:67
  341.7 16.8 %all-to-all-start.2 = ((bf16[8,192,256]{2,1,0:T(8,128)(2,1)}), bf16[8,192,256]{2,1,0:T(8,128)(2,1)}, u32[]{:S(2)}, u32[]{:S(2)}) async-start(bf16[8,192,256]{2,1,0:T(8,128)(2,1)} %bitcast.72), calls=%async_computation.3 | async-start | bytes 1572864 | tf_op jit(solution)/shard_map/all_to_all | solution.py:973
  345.9 134.8 %reduce-scatter.6.cloned.1.call-start = ((), (), s32[]{:S(2)}) async-start(), calls=%async_computation.8 | async-start | bytes 2088960 | tf_op jit(solution)/shard_map/reduce_scatter | solution.py:1062
  365.8 30.6 %collective-permute-start.40 = (bf16[2,2,48,1536]{3,2,1,0:T(8,128)(2,1)}, bf16[2,2,48,1536]{3,2,1,0:T(8,128)(2,1)S(1)}, u32[]{:S(2)}, u32[]{:S(2)}) collective-permute-start(bf16[2,2,48,1536]{3,2,1,0:T(8,128)(2,1)} %get-tuple-element.220), channel_id=1, source_target_pairs={{0,2},{1,3},{2,0},{3,1},{4,6},{5,7},{6,4},{7,5},{8,10},{9,11},{10,... | collective-permute-start | bytes 1769480 | tf_op jit(solution)/shard_map/ppermute | solution.py:67
  366.3 30.1 %collective-permute-start.41 = (bf16[2,2,48,1536]{3,2,1,0:T(8,128)(2,1)S(1)}, bf16[2,2,48,1536]{3,2,1,0:T(8,128)(2,1)S(1)}, u32[]{:S(2)}, u32[]{:S(2)}) collective-permute-start(bf16[2,2,48,1536]{3,2,1,0:T(8,128)(2,1)S(1)} %get-tuple-element.221), channel_id=1, source_target_pairs={{0,4},{1,5},{2,6},{3,7},{4,0},{5,1},{6,2},{7,3},{8,12},{9,13},{10,... | collective-permute-start | bytes 1769480 | tf_op jit(solution)/shard_map/ppermute | solution.py:67
  366.9 30.0 %collective-permute-start.42 = (bf16[2,128,1536]{2,1,0:T(8,128)(2,1)}, bf16[2,128,1536]{2,1,0:T(8,128)(2,1)S(1)}, u32[]{:S(2)}, u32[]{:S(2)}) collective-permute-start(bf16[2,128,1536]{2,1,0:T(8,128)(2,1)} %get-tuple-element.222), channel_id=1, source_target_pairs={{0,2},{1,3},{2,0},{3,1},{4,6},{5,7},{6,4},{7,5},{8,10},{9,11},{10,... | collective-permute-start | bytes 2359304 | tf_op jit(solution)/shard_map/ppermute | solution.py:67
  368.4 29.8 %collective-permute-start.43 = (bf16[2,128,1536]{2,1,0:T(8,128)(2,1)S(1)}, bf16[2,128,1536]{2,1,0:T(8,128)(2,1)S(1)}, u32[]{:S(2)}, u32[]{:S(2)}) collective-permute-start(bf16[2,128,1536]{2,1,0:T(8,128)(2,1)S(1)} %get-tuple-element.223), channel_id=1, source_target_pairs={{0,4},{1,5},{2,6},{3,7},{4,0},{5,1},{6,2},{7,3},{8,12},{9,13},{10,... | collective-permute-start | bytes 2359304 | tf_op jit(solution)/shard_map/ppermute | solution.py:67
  401.1 20.0 %collective-permute-start.52 = (bf16[1,2,48,1536]{3,2,1,0:T(8,128)(2,1)S(1)}, bf16[1,2,48,1536]{3,2,1,0:T(8,128)(2,1)S(1)}, u32[]{:S(2)}, u32[]{:S(2)}) collective-permute-start(bf16[1,2,48,1536]{3,2,1,0:T(8,128)(2,1)S(1)} %get-tuple-element.256), channel_id=1, source_target_pairs={{0,4},{1,5},{2,6},{3,7},{4,0},{5,1},{6,2},{7,3},{8,12},{9,13},{10,... | collective-permute-start | bytes 884744 | tf_op jit(solution)/shard_map/ppermute | solution.py:67
  420.0 21.1 %collective-permute-start.46 = (bf16[4,128,1536]{2,1,0:T(8,128)(2,1)}, bf16[4,128,1536]{2,1,0:T(8,128)(2,1)S(1)}, u32[]{:S(2)}, u32[]{:S(2)}) collective-permute-start(bf16[4,128,1536]{2,1,0:T(8,128)(2,1)} %get-tuple-element.240), channel_id=1, source_target_pairs={{0,1},{1,0},{2,3},{3,2},{4,5},{5,4},{6,7},{7,6},{8,9},{9,8},{10,11... | collective-permute-start | bytes 4718600 | tf_op jit(solution)/shard_map/ppermute | solution.py:67
  420.0 21.1 %collective-permute-start.47 = (bf16[4,128,1536]{2,1,0:T(8,128)(2,1)}, bf16[4,128,1536]{2,1,0:T(8,128)(2,1)S(1)}, u32[]{:S(2)}, u32[]{:S(2)}) collective-permute-start(bf16[4,128,1536]{2,1,0:T(8,128)(2,1)} %get-tuple-element.242), channel_id=1, source_target_pairs={{0,1},{1,0},{2,3},{3,2},{4,5},{5,4},{6,7},{7,6},{8,9},{9,8},{10,11... | collective-permute-start | bytes 4718600 | tf_op jit(solution)/shard_map/ppermute | solution.py:67
  440.3 12.1 %collective-permute-start.45 = (bf16[1,128,1536]{2,1,0:T(8,128)(2,1)S(1)}, bf16[1,128,1536]{2,1,0:T(8,128)(2,1)S(1)}, u32[]{:S(2)}, u32[]{:S(2)}) collective-permute-start(bf16[1,128,1536]{2,1,0:T(8,128)(2,1)S(1)} %copy-done.14), channel_id=1, source_target_pairs={{0,2},{1,3},{2,0},{3,1},{4,6},{5,7},{6,4},{7,5},{8,10},{9,11},{10,... | collective-permute-start | bytes 1179656 | tf_op jit(solution)/shard_map/ppermute | solution.py:67
  441.9 23.8 %collective-permute-start.48 = (bf16[2,128,1536]{2,1,0:T(8,128)(2,1)S(1)}, bf16[2,128,1536]{2,1,0:T(8,128)(2,1)S(1)}, u32[]{:S(2)}, u32[]{:S(2)}) collective-permute-start(bf16[2,128,1536]{2,1,0:T(8,128)(2,1)S(1)} %get-tuple-element.244), channel_id=1, source_target_pairs={{0,2},{1,3},{2,0},{3,1},{4,6},{5,7},{6,4},{7,5},{8,10},{9,11},{10,... | collective-permute-start | bytes 2359304 | tf_op jit(solution)/shard_map/ppermute | solution.py:67
  443.2 22.5 %collective-permute-start.49 = (bf16[2,128,1536]{2,1,0:T(8,128)(2,1)S(1)}, bf16[2,128,1536]{2,1,0:T(8,128)(2,1)S(1)}, u32[]{:S(2)}, u32[]{:S(2)}) collective-permute-start(bf16[2,128,1536]{2,1,0:T(8,128)(2,1)S(1)} %get-tuple-element.246), channel_id=1, source_target_pairs={{0,4},{1,5},{2,6},{3,7},{4,0},{5,1},{6,2},{7,3},{8,12},{9,13},{10,... | collective-permute-start | bytes 2359304 | tf_op jit(solution)/shard_map/ppermute | solution.py:67
  (72 other events, 356.4 us)
Sparse Core Ops, SparseCore 0:
  56.2 91.0 all-gather.4
  148.9 89.4 all-gather.6
  240.7 84.4 reduce-scatter.3
  327.3 85.7 reduce-scatter.7
  434.2 37.0 reduce-scatter.5

commit v3 on v2

--- a/solution.py
+++ b/solution.py
@@ -135,12 +135,19 @@
         self.got = [swap(a_far, 1, count), swap(b_far, 1, count)]
         self.at = 1
 
-    def step(self):
-        self.keep, send = fold(self.keep, self.got)
+    def fold(self):
+        self.keep, self.send = fold(self.keep, self.got)
+
+    def start(self):
         self.got = [
-            swap(part, order[self.at], self.count) for part, order in zip(send, self.orders)
+            swap(part, order[self.at], self.count)
+            for part, order in zip(self.send, self.orders)
         ]
         self.at += 1
+
+    def step(self):
+        self.fold()
+        self.start()
 
     def run(self):
         while self.at < len(self.orders[0]):
@@ -373,10 +380,26 @@
             dv_o[b] = dv_s[b].T.astype(bf16)
 
 
-def qkv_bwd_kernel(
-    share, far, blocks_ref, dqa, dka, dva, dqb, dkb, dvb, aa, ab, xa, xaf, xb, xbf, wt,
-    da_o, daf_o, db_o, dbf_o, gw_o, gg_o, acc, gacc,
-):
+def qkv_grads_kernel(share, dq, dk, dv, ain, wt, gain, gw_o, gg_o, acc):
+    i = pl.program_id(0)
+    d = jnp.concatenate([dq[0], dk[0], dv[0]], axis=0)
+
+    @pl.when(i == 0)
+    def _():
+        acc[...] = jnp.zeros_like(acc)
+
+    acc[...] += dot_nn(d, ain[0])
+
+    @pl.when(i == pl.num_programs(0) - 1)
+    def _():
+        width = gw_o.shape[2]
+        for z in range(gw_o.shape[0]):
+            gw_o[z] = acc[:, z * width : (z + 1) * width].astype(bf16)
+        total = jnp.sum(acc[...] * wt[...].astype(f32), axis=0, keepdims=True)
+        gg_o[...] = total * share / gain[...]
+
+
+def qkv_back_kernel(share, far, blocks_ref, dqa, dka, dva, dqb, dkb, dvb, wt, *outs):
     i = pl.program_id(0)
     flags = (i < far, i < far)
     d = jnp.concatenate(
@@ -386,25 +409,51 @@
         ],
         axis=1,
     )
-    part = dot_tn(d, wt[...]) * share
-    x = pick(flags, (xa, xaf, xb, xbf)).astype(f32)
-    inv = lax.rsqrt(jnp.mean(x * x, axis=-1, keepdims=True) + EPS)
-    put(flags, (da_o, daf_o, db_o, dbf_o), part.astype(bf16))
-
-    @pl.when(i == 0)
-    def _():
-        acc[...] = jnp.zeros_like(acc)
-        gacc[...] = jnp.zeros_like(gacc)
-
-    acc[...] += dot_nn(d, jnp.concatenate([aa[0], ab[0]], axis=0))
-    gacc[...] += jnp.sum(part * (x * inv), axis=0, keepdims=True)
-
-    @pl.when(i == pl.num_programs(0) - 1)
-    def _():
-        width = gw_o.shape[2]
-        for z in range(gw_o.shape[0]):
-            gw_o[z] = acc[:, z * width : (z + 1) * width].astype(bf16)
-        gg_o[...] = gacc[...]
+    put(flags, outs, (dot_tn(d, wt[...]) * share).astype(bf16))
+
+
+def bundle_kernel(gw, gain_a, gain_f, router, p0, p1, q0, q1, out):
+    shards, rows, slab = out.shape
+    half, rp, _ = p0.shape
+    first = shards * rp
+    small = jnp.concatenate([gain_a[...], gain_f[...], router[...]], axis=0).astype(bf16)
+    count = small.shape[0]
+    for z in range(shards):
+        near, got = (p0, p1) if z < half else (q0, q1)
+        w_out = add_up(near[z % half], got[z % half])
+        for j in range(shards):
+            out[z, j * rp : (j + 1) * rp, :] = w_out[:, j * slab : (j + 1) * slab]
+        out[z, first : first + QKV, :] = gw[z]
+        out[z, first + QKV : first + QKV + count, :] = small[:, z * slab : (z + 1) * slab]
+        rest = first + QKV + count
+        if rest < rows:
+            out[z, rest:, :] = jnp.zeros((rows - rest, slab), bf16)
+
+
+def share_kernel(own, send, w_out_o):
+    count, rp, columns = send.shape
+    shards = w_out_o.shape[1] // own.shape[1]
+    slab = own.shape[1]
+    first = shards * rp
+    for j in range(shards):
+        w_out_o[:, j * slab : (j + 1) * slab] = own[j * rp : (j + 1) * rp, :].astype(f32)
+    rows = own[first:, :].astype(f32)
+    rows = jnp.concatenate([rows, jnp.zeros((columns - rows.shape[0], slab), f32)], axis=0)
+    send[...] = rows.T.reshape(count, rp, columns).astype(bf16)
+
+
+def finish_kernel(copies, given, query, key, value, sums):
+    count = given.shape[0]
+    parts = [given[c].astype(f32) for c in range(count)]
+    for c in range(0, count, copies):
+        g = c // copies
+        query[:, g * QW : (g + 1) * QW] = parts[c][:, :QW]
+        key[:, g * HD : (g + 1) * HD] = parts[c][:, QW : QW + HD]
+        value[:, g * HD : (g + 1) * HD] = parts[c][:, QW + HD : QKV]
+    total = parts[0][:, QKV:]
+    for part in parts[1:]:
+        total = total + part[:, QKV:]
+    sums[...] = total[:, : sums.shape[1]]
 
 
 def expert_terms(expert, x, y, router, code, w_gate, w_up, w_down):
@@ -763,7 +812,7 @@
             whole((dp, rp, width)),
         ],
         tables=[lax.axis_index("dp").reshape(1).astype(i32)],
-        limit=58,
+        limit=30,
     )
     gain_a, gain_f = (gains[0:1], gains[1:2])
 
@@ -826,15 +875,15 @@
             at_step((1, HD, tok)),
         ],
         tables=[slot_at],
-        limit=58,
-    )
-
-    qt, y_rows.have, y_rows.got, o_rows.have, o_rows.got = after(
-        (qt, y_rows.have, y_rows.got, o_rows.have, o_rows.got)
+        limit=30,
+    )
+
+    qt, code_mine, y_rows.have, y_rows.got, o_rows.have, o_rows.got = after(
+        (qt, code_mine, y_rows.have, y_rows.got, o_rows.have, o_rows.got)
     )
     y_rows.step()
     o_rows.step()
-    qt = after(qt, y_rows.have, o_rows.have)
+    qt = after(qt, code_mine, y_rows.have, o_rows.have)
     of, attn_t, lse = call(
         attn_fwd_kernel,
         "attn_fwd",
@@ -848,7 +897,7 @@
         grid=n,
         specs=[at_step((1, QW, tok)), whole((n, tok, HD)), whole((n, HD, tok))],
         out_specs=[at_step((1, QW, tok))] * 2 + [at_step((1, 1, GROUP * tok))],
-        limit=58,
+        limit=30,
     )
 
     attn_t, y_rows.got, o_rows.got = after((attn_t, y_rows.got, o_rows.got))
@@ -876,7 +925,7 @@
         6,
         [shape_of(tok, width, dtype=f32)] + [shape_of(1, half, width)] * 2,
         [attn_b, w_out_all, hidden, gain_f],
-        limit=58,
+        limit=30,
     )
     ms = Gather(ma[0], mb[0], n).run()
 
@@ -955,11 +1004,11 @@
         limit=58,
     )
     mix = Scatter(outs, n)
-    resid_in = after(resid, expert_grads[0], outs)
+    resid_in = after(resid, outs)
     d_resid, d_branch, d_attn, d_router, d_gain_ffn = call(
         before_attn_kernel,
         "before_attn",
-        8,
+        14,
         [
             shape_of(tok, width, dtype=f32),
             shape_of(tok, width),
@@ -968,7 +1017,7 @@
             shape_of(1, width, dtype=f32),
         ],
         [a0, a1, b0, b1, resid_in, ma, mb, grad_out, code_mine, router_t, gain_f, w_out_all],
-        limit=58,
+        limit=30,
     )
     d_heads = lax.all_to_all(
         jnp.repeat(d_attn.reshape(KV, QW, tok), copies, axis=0),
@@ -987,18 +1036,19 @@
         specs=[whole((KV * QW, tok)), whole((tok, width))],
         out_specs=[whole((far, dp // 2, rp, width))] * 4,
         tables=[slot_at],
-        limit=58,
-    )
-
-    wout = Scatter(d_wout, n)
-    d_heads, wout.got, mix.got = after((d_heads, wout.got, mix.got))
-    wout.step()
-    mix.step()
-    d_heads = after(d_heads, wout.keep, mix.keep)
+        limit=30,
+    )
+
+    mix.fold()
+    mix.send, mix.keep, d_heads, expert_grads[0] = after(
+        (mix.send, mix.keep, d_heads, expert_grads[0])
+    )
+    mix.start()
+    wout = Scatter(after(d_wout, d_heads), n)
     dq, dk, dv = call(
         attn_bwd_kernel,
         "attn_bwd",
-        24,
+        40,
         [shape_of(n, QW, tok), shape_of(n, HD, tok), shape_of(n, HD, tok)],
         [qt, d_heads, of, lse, k, kt, v, cos, sin],
         grid=n,
@@ -1015,71 +1065,102 @@
         ],
         out_specs=[at_step((1, QW, tok)), whole((n, HD, tok)), whole((n, HD, tok))],
         scratch=[pltpu.VMEM((n, tok, HD), f32), pltpu.VMEM((n, tok, HD), f32)],
-        limit=58,
-    )
-
-    dq, wout.got, mix.got = after((dq, wout.got, mix.got))
-    (p0, p1), (q0, q1) = wout.run()
-    (r0, r1), (s0, s1) = mix.run()
-    dq = after(dq, wout.keep, mix.keep)
+        limit=30,
+    )
+
+    dq, wout.keep, wout.got = after((dq, wout.keep, wout.got))
+    wout.step()
+    dq = after(dq, wout.keep)
+
+    gw, d_gain_attn = call(
+        functools.partial(qkv_grads_kernel, 1.0 / copies),
+        "qkv_grads",
+        20,
+        [shape_of(dp, QKV, slab), shape_of(1, width, dtype=f32)],
+        [dq, dk, dv, ain, wt, gain_a],
+        grid=n,
+        specs=[
+            at_step((1, QW, tok)),
+            at_step((1, HD, tok)),
+            at_step((1, HD, tok)),
+            at_step((1, tok, width)),
+            whole((QKV, width)),
+            whole((1, width)),
+        ],
+        out_specs=[whole((dp, QKV, slab)), whole((1, width))],
+        scratch=[pltpu.VMEM((QKV, width), f32)],
+        limit=30,
+    )
 
     def columns(rows, lane):
         return pl.BlockSpec((1, rows, half), lambda i, blocks: (blocks[lane, i], 0, lane))
 
-    def tokens(lane):
-        return pl.BlockSpec((1, half, width), lambda i, blocks: (blocks[lane, i], lane, 0))
-
-    *d_in, gw, d_gain_attn = call(
-        functools.partial(qkv_bwd_kernel, 1.0 / copies, far),
-        "qkv_bwd",
-        12,
-        [shape_of(far, half, width)] * 4
-        + [shape_of(dp, QKV, slab), shape_of(1, width, dtype=f32)],
-        [dq, dk, dv, dq, dk, dv, ain, ain, *xs, wt],
+    dq, wout.keep, wout.got, mix.keep, mix.got = after(
+        (dq, wout.keep, wout.got, mix.keep, mix.got), gw
+    )
+    wout.step()
+    mix.step()
+    dq = after(dq, wout.keep, mix.keep)
+    d_in = call(
+        functools.partial(qkv_back_kernel, 1.0 / copies, far),
+        "qkv_back",
+        20,
+        [shape_of(far, half, width)] * 4,
+        [dq, dk, dv, dq, dk, dv, wt],
         grid=n,
         specs=[columns(rows, lane) for lane in range(2) for rows in (QW, HD, HD)]
-        + [tokens(0), tokens(1)]
-        + lanes_at_step((1, half, width), far)
         + [whole((QKV, width))],
-        out_specs=lanes_at_step((1, half, width), far)
-        + [whole((dp, QKV, slab)), whole((1, width))],
-        scratch=[pltpu.VMEM((QKV, width), f32), pltpu.VMEM((1, width), f32)],
+        out_specs=lanes_at_step((1, half, width), far),
         tables=[blocks],
-        limit=58,
-    )
-
-    d_wout = jnp.concatenate([add_up(p0, p1), add_up(q0, q1)], axis=0)
-    rest = jnp.concatenate([d_gain_attn, d_gain_ffn, d_router], axis=0).astype(bf16)
-    grads = jnp.concatenate(
+        limit=30,
+    )
+
+    wout.got = after(wout.got, d_in)
+    (p0, p1), (q0, q1) = wout.run()
+    bundle = call(
+        bundle_kernel,
+        "bundle",
+        2,
+        shape_of(dp, side + rp * dp + pad, slab),
+        [gw, d_gain_attn, d_gain_ffn, d_router, p0, p1, q0, q1],
+        limit=30,
+    )
+    own = lax.psum_scatter(bundle, "dp", scatter_dimension=0, tiled=True)[0]
+    send, grad_out_proj = call(
+        share_kernel,
+        "share",
+        2,
+        [shape_of(n, rp, -(-(side + pad) // 128) * 128), shape_of(rp, width, dtype=f32)],
+        [own],
+        limit=30,
+    )
+    given = lax.all_to_all(send, "ctx", split_axis=0, concat_axis=0, tiled=True)
+    grad_query, grad_key, grad_value, sums = call(
+        functools.partial(finish_kernel, copies),
+        "finish",
+        2,
         [
-            gw,
-            rest.reshape(2 + experts, dp, slab).transpose(1, 0, 2),
-            d_wout.reshape(dp, rp * dp, slab),
-            jnp.zeros((dp, pad, slab), bf16),
-        ],
-        axis=1,
-    )
-    own = lax.psum_scatter(grads, "dp", scatter_dimension=0, tiled=True)[0]
-    (c0, c1), (e0, e1) = Scatter(d_in, n).run()
+            shape_of(rp, KV * QW, dtype=f32),
+            shape_of(rp, KV * HD, dtype=f32),
+            shape_of(rp, KV * HD, dtype=f32),
+            shape_of(rp, 2 + experts, dtype=f32),
+        ],
+        [given],
+        limit=30,
+    )
+
+    back_in = Scatter(d_in, n)
+    (c0, c1), (e0, e1) = back_in.run()
     d_hidden = call(
         last_kernel,
         "last",
         3,
         shape_of(tok, width, dtype=f32),
-        [c0, c1, e0, e1, after(d_resid, own), hidden, gain_a],
-        limit=58,
-    )
-
-    given = lax.all_to_all(
-        own[:side].T.reshape(n, rp, side), "ctx", split_axis=0, concat_axis=0, tiled=True
-    ).astype(f32)
-    heads = given[::copies].transpose(1, 0, 2)
-    grad_query = heads[:, :, :QW].reshape(rp, KV * QW)
-    grad_key = heads[:, :, QW : QW + HD].reshape(rp, KV * HD)
-    grad_value = heads[:, :, QW + HD : QKV].reshape(rp, KV * HD)
-    sums = jnp.sum(given[:, :, QKV:], axis=0)
-    grad_out_proj = own[side : side + rp * dp].reshape(rp, width).astype(f32)
-
+        [c0, c1, e0, e1, after(d_resid, send), hidden, gain_a],
+        limit=30,
+    )
+
+    (r0, r1), (s0, s1) = mix.run()
     mixed = jnp.concatenate(
         [r0.astype(f32) + r1.astype(f32), s0.astype(f32) + s1.astype(f32)], axis=0
     )

time: 513 us -> 487 us (0.949)
  Pallas kernels: 243 us -> 213 us
  local copies, waits for them, and re-layouts: 47.7 us -> 64.9 us
  waiting for transfers between devices: 107 us -> 100 us
  other arithmetic: 19.9 us -> 13.9 us
    unnamed x126 -> x186, local copies, waits for them, and re-layouts: 24.8 us -> 52.7 us
    pallas_call x17 -> x21, Pallas kernels: 232 us -> 205 us  [call(): pl.pallas_call(kernel, grid_spec=pltpu.PrefetchScalarGridSpec(num_scalar_...]
    all_to_all x1, waiting for transfers between devices: 11.8 us -> 0.01 us  [shards(): lax.all_to_all(jnp.repeat(d_attn.reshape(KV, QW, tok), copies, axis=0), '...]
    all_gather x2, waiting for transfers between devices: 2.2 us -> 10.7 us  [shards(): expert_w = [lax.all_gather(stack, 'dp', axis=0) for stack in stacks]]
  transfers between devices with their start and end apart: 63 -> 63, of which waited for: 29 -> 26; matrix products, arithmetic and copies ran while one was open for 8% -> 7% of each run, Pallas kernels for 48% -> 44%
where the time goes in v3:
time: 487 us; the launch traced here: 479 us
  Pallas kernels  213 us (44%)
  waiting for transfers between devices  100 us (21%)
  starting transfers between devices  71 us (15%)
  local copies, waits for them, and re-layouts  64.9 us (13%)
  between operations  15.2 us (3%)
  other arithmetic  13.9 us (3%)
    pallas_call x21, Pallas kernels, call(): pl.pallas_call(kernel, grid_spec=pltpu.PrefetchScalarGridSpec(num_scalar_...  205 us
    ppermute x48, waiting for transfers between devices, swap(): return lax.ppermute(value, 'ctx', [(i, i ^ bit) for i in range(count)])  73.5 us
    unnamed x186, local copies, waits for them, and re-layouts  52.7 us
    ppermute x48, starting transfers between devices, swap(): return lax.ppermute(value, 'ctx', [(i, i ^ bit) for i in range(count)])  35.2 us
    ppermute x6, starting transfers between devices, along(): return lax.ppermute(value, 'dp', pairs)  18.5 us
    all_gather x2, waiting for transfers between devices, shards(): expert_w = [lax.all_gather(stack, 'dp', axis=0) for stack in stacks]  10.7 us
  transfers between devices with their start and end apart: 63, of which 26 were waited for; matrix products, arithmetic and copies ran while one was open for 7% of the time, Pallas kernels for 44%

profile of v3, /device:TPU:0, one launch (start us, length us, event | category | flops | bytes accessed | tf_op | source)
XLA Modules:
  0.0 478.6 jit_solution(7198217405879355926)
XLA Ops:
  9.2 5.2 %all-to-all-start = ((bf16[8,64,384]{2,1,0:T(8,128)(2,1)}), bf16[8,64,384]{2,1,0:T(8,128)(2,1)}, u32[]{:S(2)}, u32[]{:S(2)}) async-start(bf16[8,64,384]{2,1,0:T(8,128)(2,1)} %prep.1), calls=%async_computation | async-start | bytes 786432 | tf_op jit(solution)/shard_map/all_to_all | solution.py:777
  15.2 2.0 fusion.3
  19.2 3.6 all-to-all-done.took.table
  23.5 2.9 pad_maximum_fusion.2
  30.2 4.6 collective-permute-start.6
  43.1 5.3 %collective-permute-start.7 = (bf16[530,384]{1,0:T(8,128)(2,1)S(1)}, bf16[530,384]{1,0:T(8,128)(2,1)}, u32[]{:S(2)}, u32[]{:S(2)}) collective-permute-start(bf16[530,384]{1,0:T(8,128)(2,1)S(1)} %collective-permute-done.6.refs_2_), channel_id=1, source_target_pairs={{0,8},{8,16},{16,24},{1,9},{9,17},{17,25},{2,10},{10,18},{18,26},{... | collective-permute-start | bytes 1221128 | tf_op jit(solution)/shard_map/ppermute | solution.py:789
  48.5 6.0 %code.1.refs_9_.refs_10_ = f32[8,256,16]{2,1,0:T(8,128)} custom-call(bf16[8,64,384]{2,1,0:T(8,128)(2,1)} %all-to-all-done.took.table), custom_call_target="tpu_custom_call" | custom-call | flops 6600000000 | bytes 6000000 | tf_op jit(solution)/shard_map/code/pallas_call | solution.py:707
  57.5 4.6 collective-permute-start.8
  67.6 2.0 collective-permute-start.12
  69.7 3.9 collective-permute-done.8.refs_0_
  75.1 2.6 collective-permute-done.13
  79.4 6.9 %qkv.1 = (bf16[8,256,1536]{2,1,0:T(8,128)(2,1)S(1)}, bf16[8,192,256]{2,1,0:T(8,128)(2,1)S(1)}, bf16[8,256,64]{2,1,0:T(8,128)(2,1)S(1)}, bf16[8,64,256]{2,1,0:T(8...) custom-call(s32[2,8]{1,0:T(2,128)S(1)} %select_bitcast_fusion.slot_ref, ...), custom_call_target="tpu_custom_call" | custom-call | flops 6600000000 | bytes 6000000 | tf_op jit(solution)/shard_map/qkv/pallas_call | solution.py:707
  86.3 2.7 copy-done.59
  99.4 19.6 %attn_fwd.1 = (f32[8,192,256]{2,1,0:T(8,128)S(1)}, bf16[8,192,256]{2,1,0:T(8,128)(2,1)}, f32[8,1,768]{2,1,0:T(1,128)S(1)}) custom-call(bf16[8,192,256]{2,1,0:T(8,128)(2,1)S(1)} %get-tuple-element.178.qt, bf16[8,256,64]{2,1,0:T(8,128)(2,1)S(1)} %get-tuple-element.179.k, bf16[8,64,256]{2,1,0:T(8,128)(2,1)S(1)} %get-tuple-element.180.vt), custom_call_target="tpu_custom_call" | custom-call | flops 20899999744 | bytes 19000000 | tf_op jit(solution)/shard_map/attn_fwd/pallas_call | solution.py:707
  124.9 3.5 all-to-all-start.1
  129.4 8.0 %place.1 = bf16[4,8,48,1536]{3,2,1,0:T(8,128)(2,1)} custom-call(s32[2,8]{1,0:T(2,128)} %copy-done.26, bf16[4,2,48,1536]{3,2,1,0:T(8,128)(2,1)} %constant_dynamic-update-slice_fusion.8.a, bf16[4,2,48,1536]{3,2,1,0:T(8,128)(2,1)} %collective-permute-done.20.af, bf16[4,2,48,1536]{3,2,1,0:T(8,128)(2,1)} %constant_dynamic-update-slice_fusion.11.b, ...), custom_call_target="tpu_custom_call" | custom-call | flops 4400000000 | bytes 4000000 | tf_op jit(solution)/shard_map/place/pallas_call | solution.py:707
  137.4 3.5 all-to-all-done.1
  141.0 2.6 copy-done.45
  148.6 6.7 %collective-permute-done.25 = bf16[1,128,1536]{2,1,0:T(8,128)(2,1)S(1)} collective-permute-done((bf16[1,128,1536]{2,1,0:T(8,128)(2,1)S(1)}, bf16[1,128,1536]{2,1,0:T(8,128)(2,1)S(1)}, u32[]{:S(2)}, u32[]{:S(2)}) %collective-permute-start.25) | collective-permute-done | bytes 393248 | tf_op jit(solution)/shard_map/ppermute | solution.py:67
  155.7 2.9 collective-permute-done.22
  160.5 14.7 %collective-permute-done.26 = bf16[2,128,1536]{2,1,0:T(8,128)(2,1)S(1)} collective-permute-done((bf16[2,128,1536]{2,1,0:T(8,128)(2,1)S(1)}, bf16[2,128,1536]{2,1,0:T(8,128)(2,1)S(1)}, u32[]{:S(2)}, u32[]{:S(2)}) %collective-permute-start.26) | collective-permute-done | bytes 786464 | tf_op jit(solution)/shard_map/ppermute | solution.py:67
  175.3 2.3 collective-permute-done.23
  178.8 2.5 collective-permute-done.24.refs_1_
  181.3 45.5 %moe_first.1 = (bf16[4,128,1664]{2,1,0:T(8,128)(2,1)}, bf16[4,128,1664]{2,1,0:T(8,128)(2,1)}, bf16[4,128,1664]{2,1,0:T(8,128)(2,1)}, bf16[4,128,1664]{2,1,0:T(8,...) custom-call(s32[1]{0:T(128)} %bitcast.16.which, s32[2,8]{1,0:T(2,128)} %broadcast_xor_fusion.blocks.blocks_ref, ...), custom_call_target="tpu_custom_call" | custom-call | flops 41799999488 | bytes 38000000 | tf_op jit(solution)/shard_map/moe_first/pallas_call | solution.py:707
  227.1 10.7 %all-gather.7.cloned.1.call-done = bf16[12,384,512]{2,1,0:T(8,128)(2,1)} async-done(((bf16[3,384,512]{2,1,0:T(8,128)(2,1)}), bf16[12,384,512]{2,1,0:T(8,128)(2,1)}) %all-gather.7.cloned.1.call-update) | async-done | bytes 4718608 | tf_op jit(solution)/shard_map/all_gather | solution.py:821
  237.8 32.5 %moe_second.1 = (bf16[4,128,1664]{2,1,0:T(8,128)(2,1)}, bf16[4,128,1664]{2,1,0:T(8,128)(2,1)}, bf16[4,128,1664]{2,1,0:T(8,128)(2,1)}, bf16[4,128,1664]{2,1,0:T(8...) custom-call(s32[1]{0:T(128)S(6)} %add.55.which, ...), custom_call_target="tpu_custom_call" | custom-call | flops 27499999232 | bytes 25000000 | tf_op jit(solution)/shard_map/moe_second/pallas_call | solution.py:707
  270.9 3.3 collective-permute-done.30.refs_1_.refs_3_
  274.2 2.4 collective-permute-done.31.refs_5_.refs_7_
  284.2 18.5 %moe_grads.1 = bf16[4,3,384,512]{3,2,1,0:T(8,128)(2,1)} custom-call(bf16[4,128,1536]{2,1,0:T(8,128)(2,1)} %copy-done.84, bf16[4,128,1536]{2,1,0:T(8,128)(2,1)} %collective-permute-done.24.refs_1_, bf16[4,128,1536]{2,1,0:T(8,128)(2,1)} %copy-done.83, bf16[4,128,1536]{2,1,0:T(8,128)(2,1)} %collective-permute-done.27.refs_3_, ...), custom_call_target="tpu_custom_call" | custom-call | flops 16499999744 | bytes 15000000 | tf_op jit(solution)/shard_map/moe_grads/pallas_call | solution.py:707
  303.7 2.3 fold.9
  309.6 13.0 %moe_out.1 = (bf16[4,128,1536]{2,1,0:T(8,128)(2,1)}, bf16[4,128,1536]{2,1,0:T(8,128)(2,1)}, bf16[4,128,1536]{2,1,0:T(8,128)(2,1)}, bf16[4,128,1536]{2,1,0:T(8,128)(2,1)}) custom-call(bf16[8,256,512]{2,1,0:T(8,128)(2,1)} %get-tuple-element.193.b0, bf16[8,256,512]{2,1,0:T(8,128)(2,1)} %get-tuple-element.215.refs_8_.b1, bf16[4,3,384,512]{3,2,1,0:T(8,128)(2,1)} %bitcast.70, ...), custom_call_target="tpu_custom_call" | custom-call | flops 8800000000 | bytes 8000000 | tf_op jit(solution)/shard_map/moe_out/pallas_call | solution.py:707
  324.3 2.3 copy-done.46
  328.7 4.1 before_attn.1
  336.4 4.2 all-to-all-start.2
  342.9 3.4 wout_grad.1
  364.5 24.7 %attn_bwd.1 = (bf16[8,192,256]{2,1,0:T(8,128)(2,1)S(1)}, bf16[8,64,256]{2,1,0:T(8,128)(2,1)S(1)}, bf16[8,64,256]{2,1,0:T(8,128)(2,1)S(1)}) custom-call(bf16[8,192,256]{2,1,0:T(8,128)(2,1)S(1)} %copy-done.64, bf16[8,192,256]{2,1,0:T(8,128)(2,1)} %all-to-all-done.2.dot_, f32[8,192,256]{2,1,0:T(8,128)S(1)} %copy-done.76, f32[8,1,768]{2,1,0:T(1,128)S(1)} %copy-done.78, ...), custom_call_target="tpu_custom_call" | custom-call | flops 44000002048 | bytes 40000000 | tf_op jit(solution)/shard_map/attn_bwd/pallas_call | solution.py:707
  390.7 2.8 copy-done.60
  393.5 4.0 qkv_grads.1
  397.6 7.6 %collective-permute-done.40.refs_1_.refs_3_ = bf16[2,2,48,1536]{3,2,1,0:T(8,128)(2,1)S(1)} collective-permute-done((bf16[2,2,48,1536]{3,2,1,0:T(8,128)(2,1)S(1)}, bf16[2,2,48,1536]{3,2,1,0:T(8,128)(2,1)S(1)}, u32[]{:S(2)}, u32[]{:S(2)}) %collective-permute-start.40) | collective-permute-done | bytes 589856 | tf_op jit(solution)/shard_map/ppermute | solution.py:67
  410.5 7.8 %qkv_back.1 = (bf16[4,128,1536]{2,1,0:T(8,128)(2,1)S(1)}, bf16[4,128,1536]{2,1,0:T(8,128)(2,1)}, bf16[4,128,1536]{2,1,0:T(8,128)(2,1)S(1)}, bf16[4,128,1536]{2,1,0:T(8,128)(2,1)}) custom-call(s32[2,8]{1,0:T(2,128)S(1)} %copy-done.28, bf16[8,192,256]{2,1,0:T(8,128)(2,1)S(1)} %get-tuple-element.277.dq.dqa.dqb, ...), custom_call_target="tpu_custom_call" | custom-call | flops 22000001024 | bytes 20000000 | tf_op jit(solution)/shard_map/qkv_back/pallas_call | solution.py:707
  420.3 2.0 maximum_convert_fusion
  423.9 2.3 slice_bitcast_fusion
  426.7 2.2 fold.14
  431.0 3.3 collective-permute-done.44
  434.5 3.8 collective-permute-done.45
  438.3 15.5 %collective-permute-done.48.refs_1_.refs_3_ = bf16[2,128,1536]{2,1,0:T(8,128)(2,1)S(1)} collective-permute-done((bf16[2,128,1536]{2,1,0:T(8,128)(2,1)S(1)}, bf16[2,128,1536]{2,1,0:T(8,128)(2,1)S(1)}, u32[]{:S(2)}, u32[]{:S(2)}) %collective-permute-start.48) | collective-permute-done | bytes 786464 | tf_op jit(solution)/shard_map/ppermute | solution.py:67
  458.3 3.8 all-to-all-start.3
  462.0 2.1 collective-permute-done.50
  (336 shorter events, 120.7 us)
Async XLA Ops:
  9.2 13.6 %all-to-all-start = ((bf16[8,64,384]{2,1,0:T(8,128)(2,1)}), bf16[8,64,384]{2,1,0:T(8,128)(2,1)}, u32[]{:S(2)}, u32[]{:S(2)}) async-start(bf16[8,64,384]{2,1,0:T(8,128)(2,1)} %prep.1), calls=%async_computation | async-start | bytes 786432 | tf_op jit(solution)/shard_map/all_to_all | solution.py:777
  14.3 166.9 %all-gather.5.cloned.1.call-start = ((), (), s32[]{:S(2)}) async-start(), calls=%async_computation.10 | async-start | bytes 5898240 | tf_op jit(solution)/shard_map/all_gather | solution.py:821
  22.9 11.9 %collective-permute-start = (bf16[1,128,1536]{2,1,0:T(8,128)(2,1)S(1)}, bf16[1,128,1536]{2,1,0:T(8,128)(2,1)}, u32[]{:S(2)}, u32[]{:S(2)}) collective-permute-start(bf16[1,128,1536]{2,1,0:T(8,128)(2,1)S(1)} %get-tuple-element.356), channel_id=1, source_target_pairs={{0,4},{1,5},{2,6},{3,7},{4,0},{5,1},{6,2},{7,3},{8,12},{9,13},{10,... | collective-permute-start | bytes 1179656 | tf_op jit(solution)/shard_map/ppermute | solution.py:67
  26.4 11.8 %collective-permute-start.3 = (bf16[1,128,1536]{2,1,0:T(8,128)(2,1)S(1)}, bf16[1,128,1536]{2,1,0:T(8,128)(2,1)S(1)}, u32[]{:S(2)}, u32[]{:S(2)}) collective-permute-start(bf16[1,128,1536]{2,1,0:T(8,128)(2,1)S(1)} %get-tuple-element.355), channel_id=1, source_target_pairs={{0,2},{1,3},{2,0},{3,1},{4,6},{5,7},{6,4},{7,5},{8,10},{9,11},{10,... | collective-permute-start | bytes 1179656 | tf_op jit(solution)/shard_map/ppermute | solution.py:67
  28.9 12.9 %collective-permute-start.9 = (bf16[530,384]{1,0:T(8,128)(2,1)}, bf16[530,384]{1,0:T(8,128)(2,1)S(1)}, u32[]{:S(2)}, u32[]{:S(2)}) collective-permute-start(bf16[530,384]{1,0:T(8,128)(2,1)} %pack.1.refs_3_), channel_id=1, source_target_pairs={{8,0},{16,8},{24,16},{9,1},{17,9},{25,17},{10,2},{18,10},{26,18},{... | collective-permute-start | bytes 1221128 | tf_op jit(solution)/shard_map/ppermute | solution.py:789
  30.2 12.9 %collective-permute-start.6 = (bf16[530,384]{1,0:T(8,128)(2,1)}, bf16[530,384]{1,0:T(8,128)(2,1)S(1)}, u32[]{:S(2)}, u32[]{:S(2)}) collective-permute-start(bf16[530,384]{1,0:T(8,128)(2,1)} %pack.1.refs_3_), channel_id=1, source_target_pairs={{0,8},{8,16},{16,24},{1,9},{9,17},{17,25},{2,10},{10,18},{18,26},{... | collective-permute-start | bytes 1221128 | tf_op jit(solution)/shard_map/ppermute | solution.py:789
  36.7 25.4 %collective-permute-start.1 = (bf16[2,128,1536]{2,1,0:T(8,128)(2,1)}, bf16[2,128,1536]{2,1,0:T(8,128)(2,1)}, u32[]{:S(2)}, u32[]{:S(2)}) collective-permute-start(bf16[2,128,1536]{2,1,0:T(8,128)(2,1)} %pad_maximum_fusion.4), channel_id=1, source_target_pairs={{0,2},{1,3},{2,0},{3,1},{4,6},{5,7},{6,4},{7,5},{8,10},{9,11},{10,... | collective-permute-start | bytes 2359304 | tf_op jit(solution)/shard_map/ppermute | solution.py:67
  39.2 24.4 %collective-permute-start.4 = (bf16[2,128,1536]{2,1,0:T(8,128)(2,1)}, bf16[2,128,1536]{2,1,0:T(8,128)(2,1)}, u32[]{:S(2)}, u32[]{:S(2)}) collective-permute-start(bf16[2,128,1536]{2,1,0:T(8,128)(2,1)} %pad_maximum_fusion.5), channel_id=1, source_target_pairs={{0,4},{1,5},{2,6},{3,7},{4,0},{5,1},{6,2},{7,3},{8,12},{9,13},{10,... | collective-permute-start | bytes 2359304 | tf_op jit(solution)/shard_map/ppermute | solution.py:67
  41.8 14.2 %collective-permute-start.10 = (bf16[530,384]{1,0:T(8,128)(2,1)S(1)}, bf16[530,384]{1,0:T(8,128)(2,1)}, u32[]{:S(2)}, u32[]{:S(2)}) collective-permute-start(bf16[530,384]{1,0:T(8,128)(2,1)S(1)} %collective-permute-done.9.refs_4_), channel_id=1, source_target_pairs={{8,0},{16,8},{24,16},{9,1},{17,9},{25,17},{10,2},{18,10},{26,18},{... | collective-permute-start | bytes 1221128 | tf_op jit(solution)/shard_map/ppermute | solution.py:789
  43.1 12.9 %collective-permute-start.7 = (bf16[530,384]{1,0:T(8,128)(2,1)S(1)}, bf16[530,384]{1,0:T(8,128)(2,1)}, u32[]{:S(2)}, u32[]{:S(2)}) collective-permute-start(bf16[530,384]{1,0:T(8,128)(2,1)S(1)} %collective-permute-done.6.refs_2_), channel_id=1, source_target_pairs={{0,8},{8,16},{16,24},{1,9},{9,17},{17,25},{2,10},{10,18},{18,26},{... | collective-permute-start | bytes 1221128 | tf_op jit(solution)/shard_map/ppermute | solution.py:789
  56.1 11.6 %collective-permute-start.11 = (bf16[530,384]{1,0:T(8,128)(2,1)}, bf16[530,384]{1,0:T(8,128)(2,1)S(1)}, u32[]{:S(2)}, u32[]{:S(2)}) collective-permute-start(bf16[530,384]{1,0:T(8,128)(2,1)} %collective-permute-done.10.refs_5_), channel_id=1, source_target_pairs={{8,0},{16,8},{24,16},{9,1},{17,9},{25,17},{10,2},{18,10},{26,18},{... | collective-permute-start | bytes 1221128 | tf_op jit(solution)/shard_map/ppermute | solution.py:789
  57.5 16.1 %collective-permute-start.8 = (bf16[530,384]{1,0:T(8,128)(2,1)}, bf16[530,384]{1,0:T(8,128)(2,1)S(1)}, u32[]{:S(2)}, u32[]{:S(2)}) collective-permute-start(bf16[530,384]{1,0:T(8,128)(2,1)} %collective-permute-done.7.refs_1_), channel_id=1, source_target_pairs={{0,8},{8,16},{16,24},{1,9},{9,17},{17,25},{2,10},{10,18},{18,26},{... | collective-permute-start | bytes 1221128 | tf_op jit(solution)/shard_map/ppermute | solution.py:789
  63.5 15.8 %collective-permute-start.2 = (bf16[4,128,1536]{2,1,0:T(8,128)(2,1)S(1)}, bf16[4,128,1536]{2,1,0:T(8,128)(2,1)S(1)}, u32[]{:S(2)}, u32[]{:S(2)}) collective-permute-start(bf16[4,128,1536]{2,1,0:T(8,128)(2,1)S(1)} %pad_maximum_fusion.xa), channel_id=1, source_target_pairs={{0,1},{1,0},{2,3},{3,2},{4,5},{5,4},{6,7},{7,6},{8,9},{9,8},{10,11... | collective-permute-start | bytes 4718600 | tf_op jit(solution)/shard_map/ppermute | solution.py:67
  65.1 14.2 %collective-permute-start.5 = (bf16[4,128,1536]{2,1,0:T(8,128)(2,1)S(1)}, bf16[4,128,1536]{2,1,0:T(8,128)(2,1)S(1)}, u32[]{:S(2)}, u32[]{:S(2)}) collective-permute-start(bf16[4,128,1536]{2,1,0:T(8,128)(2,1)S(1)} %pad_maximum_fusion.1.xb), channel_id=1, source_target_pairs={{0,1},{1,0},{2,3},{3,2},{4,5},{5,4},{6,7},{7,6},{8,9},{9,8},{10,11... | collective-permute-start | bytes 4718600 | tf_op jit(solution)/shard_map/ppermute | solution.py:67
  65.6 12.0 %collective-permute-start.13 = (bf16[1,128,1536]{2,1,0:T(8,128)(2,1)S(1)}, bf16[1,128,1536]{2,1,0:T(8,128)(2,1)S(1)}, u32[]{:S(2)}, u32[]{:S(2)}) collective-permute-start(bf16[1,128,1536]{2,1,0:T(8,128)(2,1)S(1)} %get-tuple-element.172), channel_id=1, source_target_pairs={{0,2},{1,3},{2,0},{3,1},{4,6},{5,7},{6,4},{7,5},{8,10},{9,11},{10,... | collective-permute-start | bytes 1179656 | tf_op jit(solution)/shard_map/ppermute | solution.py:67
  67.6 11.7 %collective-permute-start.12 = (bf16[1,128,1536]{2,1,0:T(8,128)(2,1)S(1)}, bf16[1,128,1536]{2,1,0:T(8,128)(2,1)S(1)}, u32[]{:S(2)}, u32[]{:S(2)}) collective-permute-start(bf16[1,128,1536]{2,1,0:T(8,128)(2,1)S(1)} %get-tuple-element.170), channel_id=1, source_target_pairs={{0,4},{1,5},{2,6},{3,7},{4,0},{5,1},{6,2},{7,3},{8,12},{9,13},{10,... | collective-permute-start | bytes 1179656 | tf_op jit(solution)/shard_map/ppermute | solution.py:67
  75.0 14.1 %collective-permute-start.15 = (bf16[1,2,48,1536]{3,2,1,0:T(8,128)(2,1)S(1)}, bf16[1,2,48,1536]{3,2,1,0:T(8,128)(2,1)S(1)}, u32[]{:S(2)}, u32[]{:S(2)}) collective-permute-start(bf16[1,2,48,1536]{3,2,1,0:T(8,128)(2,1)S(1)} %get-tuple-element.176), channel_id=1, source_target_pairs={{0,2},{1,3},{2,0},{3,1},{4,6},{5,7},{6,4},{7,5},{8,10},{9,11},{10,... | collective-permute-start | bytes 884744 | tf_op jit(solution)/shard_map/ppermute | solution.py:67
  90.6 30.2 %collective-permute-start.18 = (bf16[2,2,48,1536]{3,2,1,0:T(8,128)(2,1)S(1)}, bf16[2,2,48,1536]{3,2,1,0:T(8,128)(2,1)S(1)}, u32[]{:S(2)}, u32[]{:S(2)}) collective-permute-start(bf16[2,2,48,1536]{3,2,1,0:T(8,128)(2,1)S(1)} %get-tuple-element.372), channel_id=1, source_target_pairs={{0,2},{1,3},{2,0},{3,1},{4,6},{5,7},{6,4},{7,5},{8,10},{9,11},{10,... | collective-permute-start | bytes 1769480 | tf_op jit(solution)/shard_map/ppermute | solution.py:67
  92.7 28.1 %collective-permute-start.19 = (bf16[2,2,48,1536]{3,2,1,0:T(8,128)(2,1)S(1)}, bf16[2,2,48,1536]{3,2,1,0:T(8,128)(2,1)S(1)}, u32[]{:S(2)}, u32[]{:S(2)}) collective-permute-start(bf16[2,2,48,1536]{3,2,1,0:T(8,128)(2,1)S(1)} %get-tuple-element.368), channel_id=1, source_target_pairs={{0,4},{1,5},{2,6},{3,7},{4,0},{5,1},{6,2},{7,3},{8,12},{9,13},{10,... | collective-permute-start | bytes 1769480 | tf_op jit(solution)/shard_map/ppermute | solution.py:67
  94.7 26.4 %collective-permute-start.16 = (bf16[2,128,1536]{2,1,0:T(8,128)(2,1)S(1)}, bf16[2,128,1536]{2,1,0:T(8,128)(2,1)S(1)}, u32[]{:S(2)}, u32[]{:S(2)}) collective-permute-start(bf16[2,128,1536]{2,1,0:T(8,128)(2,1)S(1)} %get-tuple-element.364), channel_id=1, source_target_pairs={{0,2},{1,3},{2,0},{3,1},{4,6},{5,7},{6,4},{7,5},{8,10},{9,11},{10,... | collective-permute-start | bytes 2359304 | tf_op jit(solution)/shard_map/ppermute | solution.py:67
  97.7 24.9 %collective-permute-start.17 = (bf16[2,128,1536]{2,1,0:T(8,128)(2,1)S(1)}, bf16[2,128,1536]{2,1,0:T(8,128)(2,1)S(1)}, u32[]{:S(2)}, u32[]{:S(2)}) collective-permute-start(bf16[2,128,1536]{2,1,0:T(8,128)(2,1)S(1)} %get-tuple-element.360), channel_id=1, source_target_pairs={{0,4},{1,5},{2,6},{3,7},{4,0},{5,1},{6,2},{7,3},{8,12},{9,13},{10,... | collective-permute-start | bytes 2359304 | tf_op jit(solution)/shard_map/ppermute | solution.py:67
  124.9 16.1 %all-to-all-start.1 = ((bf16[8,192,256]{2,1,0:T(8,128)(2,1)}), bf16[8,192,256]{2,1,0:T(8,128)(2,1)S(1)}, u32[]{:S(2)}, u32[]{:S(2)}) async-start(bf16[8,192,256]{2,1,0:T(8,128)(2,1)} %get-tuple-element.182), calls=%async_computation.1 | async-start | bytes 1572864 | tf_op jit(solution)/shard_map/all_to_all | solution.py:906
  128.5 109.4 %all-gather.7.cloned.1.call-start = ((), (), s32[]{:S(2)}) async-start(), calls=%async_computation.11 | async-start | bytes 5898240 | tf_op jit(solution)/shard_map/all_gather | solution.py:821
  129.2 224.9 %reduce-scatter.4.cloned.1.call-start = ((), (), s32[]{:S(2)}) async-start(), calls=%async_computation.7 | async-start | bytes 5898240 | tf_op jit(solution)/shard_map/reduce_scatter | solution.py:987
  146.7 31.7 %collective-permute-start.28 = (bf16[4,128,1536]{2,1,0:T(8,128)(2,1)}, bf16[4,128,1536]{2,1,0:T(8,128)(2,1)}, u32[]{:S(2)}, u32[]{:S(2)}) collective-permute-start(bf16[4,128,1536]{2,1,0:T(8,128)(2,1)} %constant_dynamic-update-slice_fusion.20.refs_4_), channel_id=1, source_target_pairs={{0,1},{1,0},{2,3},{3,2},{4,5},{5,4},{6,7},{7,6},{8,9},{9,8},{10,11... | collective-permute-start | bytes 4718600 | tf_op jit(solution)/shard_map/ppermute | solution.py:67
  146.7 11.9 %collective-permute-start.22 = (bf16[1,128,1536]{2,1,0:T(8,128)(2,1)S(1)}, bf16[1,128,1536]{2,1,0:T(8,128)(2,1)S(1)}, u32[]{:S(2)}, u32[]{:S(2)}) collective-permute-start(bf16[1,128,1536]{2,1,0:T(8,128)(2,1)S(1)} %get-tuple-element.186.ma), channel_id=1, source_target_pairs={{0,4},{1,5},{2,6},{3,7},{4,0},{5,1},{6,2},{7,3},{8,12},{9,13},{10,... | collective-permute-start | bytes 1179656 | tf_op jit(solution)/shard_map/ppermute | solution.py:67
  148.3 30.1 %collective-permute-start.29 = (bf16[4,128,1536]{2,1,0:T(8,128)(2,1)}, bf16[4,128,1536]{2,1,0:T(8,128)(2,1)}, u32[]{:S(2)}, u32[]{:S(2)}) collective-permute-start(bf16[4,128,1536]{2,1,0:T(8,128)(2,1)} %constant_dynamic-update-slice_fusion.23.refs_6_), channel_id=1, source_target_pairs={{0,1},{1,0},{2,3},{3,2},{4,5},{5,4},{6,7},{7,6},{8,9},{9,8},{10,11... | collective-permute-start | bytes 4718600 | tf_op jit(solution)/shard_map/ppermute | solution.py:67
  155.3 19.8 %collective-permute-start.26 = (bf16[2,128,1536]{2,1,0:T(8,128)(2,1)S(1)}, bf16[2,128,1536]{2,1,0:T(8,128)(2,1)S(1)}, u32[]{:S(2)}, u32[]{:S(2)}) collective-permute-start(bf16[2,128,1536]{2,1,0:T(8,128)(2,1)S(1)} %pad_maximum_fusion.7), channel_id=1, source_target_pairs={{0,4},{1,5},{2,6},{3,7},{4,0},{5,1},{6,2},{7,3},{8,12},{9,13},{10,... | collective-permute-start | bytes 2359304 | tf_op jit(solution)/shard_map/ppermute | solution.py:67
  158.7 18.9 %collective-permute-start.23 = (bf16[2,128,1536]{2,1,0:T(8,128)(2,1)S(1)}, bf16[2,128,1536]{2,1,0:T(8,128)(2,1)S(1)}, u32[]{:S(2)}, u32[]{:S(2)}) collective-permute-start(bf16[2,128,1536]{2,1,0:T(8,128)(2,1)S(1)} %pad_maximum_fusion.6), channel_id=1, source_target_pairs={{0,2},{1,3},{2,0},{3,1},{4,6},{5,7},{6,4},{7,5},{8,10},{9,11},{10,... | collective-permute-start | bytes 2359304 | tf_op jit(solution)/shard_map/ppermute | solution.py:67
  226.9 193.4 %reduce-scatter.8.cloned.1.call-start = ((), (), s32[]{:S(2)}) async-start(), calls=%async_computation.9 | async-start | bytes 5898240 | tf_op jit(solution)/shard_map/reduce_scatter | solution.py:987
  281.2 21.5 %collective-permute-start.32 = (bf16[2,128,1664]{2,1,0:T(8,128)(2,1)}, bf16[2,128,1664]{2,1,0:T(8,128)(2,1)S(1)}, u32[]{:S(2)}, u32[]{:S(2)}) collective-permute-start(bf16[2,128,1664]{2,1,0:T(8,128)(2,1)} %get-tuple-element.207), channel_id=1, source_target_pairs={{0,2},{1,3},{2,0},{3,1},{4,6},{5,7},{6,4},{7,5},{8,10},{9,11},{10,... | collective-permute-start | bytes 2555912 | tf_op jit(solution)/shard_map/ppermute | solution.py:67
  282.7 21.0 %collective-permute-start.33 = (bf16[2,128,1664]{2,1,0:T(8,128)(2,1)}, bf16[2,128,1664]{2,1,0:T(8,128)(2,1)}, u32[]{:S(2)}, u32[]{:S(2)}) collective-permute-start(bf16[2,128,1664]{2,1,0:T(8,128)(2,1)} %get-tuple-element.208), channel_id=1, source_target_pairs={{0,4},{1,5},{2,6},{3,7},{4,0},{5,1},{6,2},{7,3},{8,12},{9,13},{10,... | collective-permute-start | bytes 2555912 | tf_op jit(solution)/shard_map/ppermute | solution.py:67
  307.6 15.5 %collective-permute-start.36 = (bf16[1,128,1664]{2,1,0:T(8,128)(2,1)}, bf16[1,128,1664]{2,1,0:T(8,128)(2,1)S(1)}, u32[]{:S(2)}, u32[]{:S(2)}) collective-permute-start(bf16[1,128,1664]{2,1,0:T(8,128)(2,1)} %get-tuple-element.224), channel_id=1, source_target_pairs={{0,4},{1,5},{2,6},{3,7},{4,0},{5,1},{6,2},{7,3},{8,12},{9,13},{10,... | collective-permute-start | bytes 1277960 | tf_op jit(solution)/shard_map/ppermute | solution.py:67
  309.0 14.1 %collective-permute-start.37 = (bf16[1,128,1664]{2,1,0:T(8,128)(2,1)}, bf16[1,128,1664]{2,1,0:T(8,128)(2,1)}, u32[]{:S(2)}, u32[]{:S(2)}) collective-permute-start(bf16[1,128,1664]{2,1,0:T(8,128)(2,1)} %get-tuple-element.225), channel_id=1, source_target_pairs={{0,2},{1,3},{2,0},{3,1},{4,6},{5,7},{6,4},{7,5},{8,10},{9,11},{10,... | collective-permute-start | bytes 1277960 | tf_op jit(solution)/shard_map/ppermute | solution.py:67
  322.6 25.8 %collective-permute-start.34 = (bf16[4,128,1536]{2,1,0:T(8,128)(2,1)}, bf16[4,128,1536]{2,1,0:T(8,128)(2,1)S(1)}, u32[]{:S(2)}, u32[]{:S(2)}) collective-permute-start(bf16[4,128,1536]{2,1,0:T(8,128)(2,1)} %get-tuple-element.217), channel_id=1, source_target_pairs={{0,1},{1,0},{2,3},{3,2},{4,5},{5,4},{6,7},{7,6},{8,9},{9,8},{10,11... | collective-permute-start | bytes 4718600 | tf_op jit(solution)/shard_map/ppermute | solution.py:67
  322.6 25.8 %collective-permute-start.35 = (bf16[4,128,1536]{2,1,0:T(8,128)(2,1)}, bf16[4,128,1536]{2,1,0:T(8,128)(2,1)S(1)}, u32[]{:S(2)}, u32[]{:S(2)}) collective-permute-start(bf16[4,128,1536]{2,1,0:T(8,128)(2,1)} %get-tuple-element.219), channel_id=1, source_target_pairs={{0,1},{1,0},{2,3},{3,2},{4,5},{5,4},{6,7},{7,6},{8,9},{9,8},{10,11... | collective-permute-start | bytes 4718600 | tf_op jit(solution)/shard_map/ppermute | solution.py:67
  336.4 17.8 %all-to-all-start.2 = ((bf16[8,192,256]{2,1,0:T(8,128)(2,1)}), bf16[8,192,256]{2,1,0:T(8,128)(2,1)}, u32[]{:S(2)}, u32[]{:S(2)}) async-start(bf16[8,192,256]{2,1,0:T(8,128)(2,1)} %bitcast.54), calls=%async_computation.2 | async-start | bytes 1572864 | tf_op jit(solution)/shard_map/all_to_all | solution.py:1022
  340.6 115.7 %reduce-scatter.6.cloned.1.call-start = ((), (), s32[]{:S(2)}) async-start(), calls=%async_computation.8 | async-start | bytes 2088960 | tf_op jit(solution)/shard_map/reduce_scatter | solution.py:1128
  354.2 43.4 %collective-permute-start.42 = (bf16[2,128,1536]{2,1,0:T(8,128)(2,1)}, bf16[2,128,1536]{2,1,0:T(8,128)(2,1)S(1)}, u32[]{:S(2)}, u32[]{:S(2)}) collective-permute-start(bf16[2,128,1536]{2,1,0:T(8,128)(2,1)} %copy-done.36), channel_id=1, source_target_pairs={{0,2},{1,3},{2,0},{3,1},{4,6},{5,7},{6,4},{7,5},{8,10},{9,11},{10,... | collective-permute-start | bytes 2359304 | tf_op jit(solution)/shard_map/ppermute | solution.py:67
  356.0 41.6 %collective-permute-start.43 = (bf16[2,128,1536]{2,1,0:T(8,128)(2,1)}, bf16[2,128,1536]{2,1,0:T(8,128)(2,1)S(1)}, u32[]{:S(2)}, u32[]{:S(2)}) collective-permute-start(bf16[2,128,1536]{2,1,0:T(8,128)(2,1)} %copy-done.35), channel_id=1, source_target_pairs={{0,4},{1,5},{2,6},{3,7},{4,0},{5,1},{6,2},{7,3},{8,12},{9,13},{10,... | collective-permute-start | bytes 2359304 | tf_op jit(solution)/shard_map/ppermute | solution.py:67
  357.5 31.8 %collective-permute-start.38 = (bf16[4,2,48,1536]{3,2,1,0:T(8,128)(2,1)}, bf16[4,2,48,1536]{3,2,1,0:T(8,128)(2,1)S(1)}, u32[]{:S(2)}, u32[]{:S(2)}) collective-permute-start(bf16[4,2,48,1536]{3,2,1,0:T(8,128)(2,1)} %copy-done.30), channel_id=1, source_target_pairs={{0,1},{1,0},{2,3},{3,2},{4,5},{5,4},{6,7},{7,6},{8,9},{9,8},{10,11... | collective-permute-start | bytes 3538952 | tf_op jit(solution)/shard_map/ppermute | solution.py:67
  357.5 31.8 %collective-permute-start.39 = (bf16[4,2,48,1536]{3,2,1,0:T(8,128)(2,1)}, bf16[4,2,48,1536]{3,2,1,0:T(8,128)(2,1)S(1)}, u32[]{:S(2)}, u32[]{:S(2)}) collective-permute-start(bf16[4,2,48,1536]{3,2,1,0:T(8,128)(2,1)} %copy-done.29), channel_id=1, source_target_pairs={{0,1},{1,0},{2,3},{3,2},{4,5},{5,4},{6,7},{7,6},{8,9},{9,8},{10,11... | collective-permute-start | bytes 3538952 | tf_op jit(solution)/shard_map/ppermute | solution.py:67
  389.9 15.3 %collective-permute-start.40 = (bf16[2,2,48,1536]{3,2,1,0:T(8,128)(2,1)S(1)}, bf16[2,2,48,1536]{3,2,1,0:T(8,128)(2,1)S(1)}, u32[]{:S(2)}, u32[]{:S(2)}) collective-permute-start(bf16[2,2,48,1536]{3,2,1,0:T(8,128)(2,1)S(1)} %get-tuple-element.252), channel_id=1, source_target_pairs={{0,2},{1,3},{2,0},{3,1},{4,6},{5,7},{6,4},{7,5},{8,10},{9,11},{10,... | collective-permute-start | bytes 1769480 | tf_op jit(solution)/shard_map/ppermute | solution.py:67
  390.5 14.9 %collective-permute-start.41 = (bf16[2,2,48,1536]{3,2,1,0:T(8,128)(2,1)S(1)}, bf16[2,2,48,1536]{3,2,1,0:T(8,128)(2,1)S(1)}, u32[]{:S(2)}, u32[]{:S(2)}) collective-permute-start(bf16[2,2,48,1536]{3,2,1,0:T(8,128)(2,1)S(1)} %get-tuple-element.253), channel_id=1, source_target_pairs={{0,4},{1,5},{2,6},{3,7},{4,0},{5,1},{6,2},{7,3},{8,12},{9,13},{10,... | collective-permute-start | bytes 1769480 | tf_op jit(solution)/shard_map/ppermute | solution.py:67
  422.3 12.0 %collective-permute-start.44 = (bf16[1,128,1536]{2,1,0:T(8,128)(2,1)S(1)}, bf16[1,128,1536]{2,1,0:T(8,128)(2,1)S(1)}, u32[]{:S(2)}, u32[]{:S(2)}) collective-permute-start(bf16[1,128,1536]{2,1,0:T(8,128)(2,1)S(1)} %copy-done.44), channel_id=1, source_target_pairs={{0,4},{1,5},{2,6},{3,7},{4,0},{5,1},{6,2},{7,3},{8,12},{9,13},{10,... | collective-permute-start | bytes 1179656 | tf_op jit(solution)/shard_map/ppermute | solution.py:67
  426.2 12.0 %collective-permute-start.45 = (bf16[1,128,1536]{2,1,0:T(8,128)(2,1)S(1)}, bf16[1,128,1536]{2,1,0:T(8,128)(2,1)S(1)}, u32[]{:S(2)}, u32[]{:S(2)}) collective-permute-start(bf16[1,128,1536]{2,1,0:T(8,128)(2,1)S(1)} %copy-done.42), channel_id=1, source_target_pairs={{0,2},{1,3},{2,0},{3,1},{4,6},{5,7},{6,4},{7,5},{8,10},{9,11},{10,... | collective-permute-start | bytes 1179656 | tf_op jit(solution)/shard_map/ppermute | solution.py:67
  429.0 24.8 %collective-permute-start.48 = (bf16[2,128,1536]{2,1,0:T(8,128)(2,1)S(1)}, bf16[2,128,1536]{2,1,0:T(8,128)(2,1)S(1)}, u32[]{:S(2)}, u32[]{:S(2)}) collective-permute-start(bf16[2,128,1536]{2,1,0:T(8,128)(2,1)S(1)} %get-tuple-element.283), channel_id=1, source_target_pairs={{0,2},{1,3},{2,0},{3,1},{4,6},{5,7},{6,4},{7,5},{8,10},{9,11},{10,... | collective-permute-start | bytes 2359304 | tf_op jit(solution)/shard_map/ppermute | solution.py:67
  430.5 23.3 %collective-permute-start.49 = (bf16[2,128,1536]{2,1,0:T(8,128)(2,1)S(1)}, bf16[2,128,1536]{2,1,0:T(8,128)(2,1)S(1)}, u32[]{:S(2)}, u32[]{:S(2)}) collective-permute-start(bf16[2,128,1536]{2,1,0:T(8,128)(2,1)S(1)} %get-tuple-element.285), channel_id=1, source_target_pairs={{0,4},{1,5},{2,6},{3,7},{4,0},{5,1},{6,2},{7,3},{8,12},{9,13},{10,... | collective-permute-start | bytes 2359304 | tf_op jit(solution)/shard_map/ppermute | solution.py:67
  (102 other events, 730.4 us)
Sparse Core Ops, SparseCore 0:
  56.2 90.7 all-gather.4
  148.5 89.2 all-gather.6
  240.1 83.6 reduce-scatter.3
  326.0 85.7 reduce-scatter.7
  420.4 34.2 reduce-scatter.5

commit v4 on v3

--- a/solution.py
+++ b/solution.py
@@ -812,27 +812,13 @@
             whole((dp, rp, width)),
         ],
         tables=[lax.axis_index("dp").reshape(1).astype(i32)],
-        limit=30,
+        limit=58,
     )
     gain_a, gain_f = (gains[0:1], gains[1:2])
 
     stacks = [jnp.stack([w_gate[e], w_up[e], w_down[e]]) for e in range(w_gate.shape[0])]
     stacks = after(stacks, below[:-1], above[:-1])
     expert_w = [lax.all_gather(stack, "dp", axis=0) for stack in stacks]
-
-    code = call(
-        functools.partial(code_kernel, rp),
-        "code",
-        6,
-        shape_of(n, tok, experts, dtype=f32),
-        [took],
-        grid=n,
-        specs=[at_step((1,) + took.shape[1:])],
-        out_specs=at_step((1, tok, experts)),
-        scratch=[pltpu.VMEM((experts, 1), f32)],
-        limit=58,
-    )
-    code_mine = lax.dynamic_index_in_dim(code, me, 0, keepdims=False)
 
     x_rows = after(hidden, took)
     x_rows = Gather(x_rows[:half], x_rows[half:], n)
@@ -847,7 +833,7 @@
     cos, sin = (jnp.cos(angles), jnp.sin(angles))
 
     o_rows = Gather(out_rows[: dp // 2], out_rows[dp // 2 :], n)
-    gain_a, code, y_rows.got = after((gain_a, code, y_rows.got))
+    gain_a, y_rows.got = after((gain_a, y_rows.got))
 
     ain, qt, k, kt, v, vt = call(
         functools.partial(qkv_kernel, far),
@@ -875,15 +861,15 @@
             at_step((1, HD, tok)),
         ],
         tables=[slot_at],
-        limit=30,
-    )
-
-    qt, code_mine, y_rows.have, y_rows.got, o_rows.have, o_rows.got = after(
-        (qt, code_mine, y_rows.have, y_rows.got, o_rows.have, o_rows.got)
+        limit=58,
+    )
+
+    qt, y_rows.have, y_rows.got, o_rows.have, o_rows.got = after(
+        (qt, y_rows.have, y_rows.got, o_rows.have, o_rows.got)
     )
     y_rows.step()
     o_rows.step()
-    qt = after(qt, code_mine, y_rows.have, o_rows.have)
+    qt = after(qt, y_rows.have, o_rows.have)
     of, attn_t, lse = call(
         attn_fwd_kernel,
         "attn_fwd",
@@ -897,7 +883,7 @@
         grid=n,
         specs=[at_step((1, QW, tok)), whole((n, tok, HD)), whole((n, HD, tok))],
         out_specs=[at_step((1, QW, tok))] * 2 + [at_step((1, 1, GROUP * tok))],
-        limit=30,
+        limit=58,
     )
 
     attn_t, y_rows.got, o_rows.got = after((attn_t, y_rows.got, o_rows.got))
@@ -925,9 +911,27 @@
         6,
         [shape_of(tok, width, dtype=f32)] + [shape_of(1, half, width)] * 2,
         [attn_b, w_out_all, hidden, gain_f],
-        limit=30,
-    )
-    ms = Gather(ma[0], mb[0], n).run()
+        limit=58,
+    )
+    m_rows = Gather(ma[0], mb[0], n)
+    took = after(took, ma)
+
+    code = call(
+        functools.partial(code_kernel, rp),
+        "code",
+        6,
+        shape_of(n, tok, experts, dtype=f32),
+        [took],
+        grid=n,
+        specs=[at_step((1,) + took.shape[1:])],
+        out_specs=at_step((1, tok, experts)),
+        scratch=[pltpu.VMEM((experts, 1), f32)],
+        limit=58,
+    )
+    code_mine = lax.dynamic_index_in_dim(code, me, 0, keepdims=False)
+
+    m_rows.got, code, code_mine = after((m_rows.got, code, code_mine))
+    ms = m_rows.run()
 
     side_w = width + EXTRA
     wide = [shape_of(far, half, side_w)] * 4
@@ -1017,7 +1021,7 @@
             shape_of(1, width, dtype=f32),
         ],
         [a0, a1, b0, b1, resid_in, ma, mb, grad_out, code_mine, router_t, gain_f, w_out_all],
-        limit=30,
+        limit=58,
     )
     d_heads = lax.all_to_all(
         jnp.repeat(d_attn.reshape(KV, QW, tok), copies, axis=0),
@@ -1036,7 +1040,7 @@
         specs=[whole((KV * QW, tok)), whole((tok, width))],
         out_specs=[whole((far, dp // 2, rp, width))] * 4,
         tables=[slot_at],
-        limit=30,
+        limit=58,
     )
 
     mix.fold()
@@ -1065,7 +1069,7 @@
         ],
         out_specs=[at_step((1, QW, tok)), whole((n, HD, tok)), whole((n, HD, tok))],
         scratch=[pltpu.VMEM((n, tok, HD), f32), pltpu.VMEM((n, tok, HD), f32)],
-        limit=30,
+        limit=58,
     )
 
     dq, wout.keep, wout.got = after((dq, wout.keep, wout.got))
@@ -1150,6 +1154,9 @@
     )
 
     back_in = Scatter(d_in, n)
+    back_in.got = after(back_in.got, bundle)
+    back_in.step()
+    expert_grads, mix.got = after((expert_grads, mix.got), back_in.keep)
     (c0, c1), (e0, e1) = back_in.run()
     d_hidden = call(
         last_kernel,

time: 487 us -> 480 us (0.986)
  Pallas kernels: 213 us -> 236 us
  local copies, waits for them, and re-layouts: 64.9 us -> 43.4 us
  waiting for transfers between devices: 100 us -> 88.3 us
    pallas_call x21, Pallas kernels: 205 us -> 227 us  [call(): pl.pallas_call(kernel, grid_spec=pltpu.PrefetchScalarGridSpec(num_scalar_...]
    unnamed x186 -> x138, local copies, waits for them, and re-layouts: 52.7 us -> 30.7 us
    ppermute x48, waiting for transfers between devices: 73.5 us -> 63.6 us  [swap(): return lax.ppermute(value, 'ctx', [(i, i ^ bit) for i in range(count)])]
    all_gather x2, waiting for transfers between devices: 10.7 us -> 4.38 us  [shards(): expert_w = [lax.all_gather(stack, 'dp', axis=0) for stack in stacks]]
  transfers between devices with their start and end apart: 63 -> 63, of which waited for: 26 -> 29; matrix products, arithmetic and copies ran while one was open for 7% -> 6% of each run, Pallas kernels for 44% -> 49%
where the time goes in v4:
time: 480 us; the launch traced here: 472 us
  Pallas kernels  236 us (49%)
  waiting for transfers between devices  88.3 us (18%)
  starting transfers between devices  75.3 us (16%)
  local copies, waits for them, and re-layouts  43.4 us (9%)
  between operations  15.1 us (3%)
  other arithmetic  14.1 us (3%)
    pallas_call x21, Pallas kernels, call(): pl.pallas_call(kernel, grid_spec=pltpu.PrefetchScalarGridSpec(num_scalar_...  227 us
    ppermute x48, waiting for transfers between devices, swap(): return lax.ppermute(value, 'ctx', [(i, i ^ bit) for i in range(count)])  63.6 us
    ppermute x48, starting transfers between devices, swap(): return lax.ppermute(value, 'ctx', [(i, i ^ bit) for i in range(count)])  38.3 us
    unnamed x138, local copies, waits for them, and re-layouts  30.7 us
    ppermute x6, starting transfers between devices, along(): return lax.ppermute(value, 'dp', pairs)  19.7 us
  transfers between devices with their start and end apart: 63, of which 29 were waited for; matrix products, arithmetic and copies ran while one was open for 6% of the time, Pallas kernels for 49%

profile of v4, /device:TPU:0, one launch (start us, length us, event | category | flops | bytes accessed | tf_op | source)
XLA Modules:
  0.0 471.9 jit_solution(5596252855201707014)
XLA Ops:
  7.2 2.0 prep.1
  9.2 5.3 %all-to-all-start = ((bf16[8,64,384]{2,1,0:T(8,128)(2,1)}), bf16[8,64,384]{2,1,0:T(8,128)(2,1)S(1)}, u32[]{:S(2)}, u32[]{:S(2)}) async-start(bf16[8,64,384]{2,1,0:T(8,128)(2,1)} %prep.1), calls=%async_computation | async-start | bytes 786432 | tf_op jit(solution)/shard_map/all_to_all | solution.py:777
  17.3 5.6 %all-to-all-done.took.table = bf16[8,64,384]{2,1,0:T(8,128)(2,1)S(1)} async-done(((bf16[8,64,384]{2,1,0:T(8,128)(2,1)}), bf16[8,64,384]{2,1,0:T(8,128)(2,1)S(1)}, u32[]{:S(2)}, u32[]{:S(2)}) %all-to-all-start) | async-done | bytes 393248 | tf_op jit(solution)/shard_map/all_to_all | solution.py:777
  24.7 1.9 pack.1.refs_3_
  28.0 5.3 %collective-permute-start.6 = (bf16[530,384]{1,0:T(8,128)(2,1)}, bf16[530,384]{1,0:T(8,128)(2,1)}, u32[]{:S(2)}, u32[]{:S(2)}) collective-permute-start(bf16[530,384]{1,0:T(8,128)(2,1)} %pack.1.refs_3_), channel_id=1, source_target_pairs={{0,8},{8,16},{16,24},{1,9},{9,17},{17,25},{2,10},{10,18},{18,26},{... | collective-permute-start | bytes 1221128 | tf_op jit(solution)/shard_map/ppermute | solution.py:789
  41.0 5.3 %collective-permute-start.7 = (bf16[530,384]{1,0:T(8,128)(2,1)}, bf16[530,384]{1,0:T(8,128)(2,1)}, u32[]{:S(2)}, u32[]{:S(2)}) collective-permute-start(bf16[530,384]{1,0:T(8,128)(2,1)} %collective-permute-done.6.refs_2_), channel_id=1, source_target_pairs={{0,8},{8,16},{16,24},{1,9},{9,17},{17,25},{2,10},{10,18},{18,26},{... | collective-permute-start | bytes 1221128 | tf_op jit(solution)/shard_map/ppermute | solution.py:789
  49.7 1.9 collective-permute-done.10.refs_5_
  54.2 5.0 %collective-permute-start.8 = (bf16[530,384]{1,0:T(8,128)(2,1)}, bf16[530,384]{1,0:T(8,128)(2,1)S(1)}, u32[]{:S(2)}, u32[]{:S(2)}) collective-permute-start(bf16[530,384]{1,0:T(8,128)(2,1)} %collective-permute-done.7.refs_1_), channel_id=1, source_target_pairs={{0,8},{8,16},{16,24},{1,9},{9,17},{17,25},{2,10},{10,18},{18,26},{... | collective-permute-start | bytes 1221128 | tf_op jit(solution)/shard_map/ppermute | solution.py:789
  60.7 2.0 pad_maximum_fusion.1.xb
  64.4 2.1 collective-permute-start.12
  68.6 3.1 unpack.1
  74.8 2.3 collective-permute-start.14
  77.2 12.3 %qkv.1 = (bf16[8,256,1536]{2,1,0:T(8,128)(2,1)}, bf16[8,192,256]{2,1,0:T(8,128)(2,1)}, bf16[8,256,64]{2,1,0:T(8,128)(2,1)}, bf16[8,64,256]{2,1,0:T(8,128)(2,1)},...) custom-call(s32[2,8]{1,0:T(2,128)} %select_bitcast_fusion.slot_ref, bf16[4,128,1536]{2,1,0:T(8,128)(2,1)} %copy-done.37, ...), custom_call_target="tpu_custom_call" | custom-call | flops 6600000000 | bytes 6000000 | tf_op jit(solution)/shard_map/qkv/pallas_call | solution.py:707
  91.0 2.0 collective-permute-start.18
  98.5 21.0 %attn_fwd.1 = (f32[8,192,256]{2,1,0:T(8,128)}, bf16[8,192,256]{2,1,0:T(8,128)(2,1)}, f32[8,1,768]{2,1,0:T(1,128)}) custom-call(bf16[8,192,256]{2,1,0:T(8,128)(2,1)} %get-tuple-element.186.qt, bf16[8,256,64]{2,1,0:T(8,128)(2,1)} %get-tuple-element.187.k, bf16[8,64,256]{2,1,0:T(8,128)(2,1)} %get-tuple-element.188.vt), custom_call_target="tpu_custom_call" | custom-call | flops 20899999744 | bytes 19000000 | tf_op jit(solution)/shard_map/attn_fwd/pallas_call | solution.py:707
  119.4 2.6 collective-permute-done.16
  125.5 3.6 all-to-all-start.1
  131.8 8.0 %place.1 = bf16[4,8,48,1536]{3,2,1,0:T(8,128)(2,1)} custom-call(s32[2,8]{1,0:T(2,128)} %select_bitcast_fusion.slot_ref, bf16[4,2,48,1536]{3,2,1,0:T(8,128)(2,1)} %constant_dynamic-update-slice_fusion.8.a, bf16[4,2,48,1536]{3,2,1,0:T(8,128)(2,1)} %collective-permute-done.20.af, bf16[4,2,48,1536]{3,2,1,0:T(8,128)(2,1)} %constant_dynamic-update-slice_fusion.11.b, ...), custom_call_target="tpu_custom_call" | custom-call | flops 4400000000 | bytes 4000000 | tf_op jit(solution)/shard_map/place/pallas_call | solution.py:707
  142.5 5.7 %after_attn.1 = (f32[256,1536]{1,0:T(8,128)}, bf16[1,128,1536]{2,1,0:T(8,128)(2,1)}, bf16[1,128,1536]{2,1,0:T(8,128)(2,1)}) custom-call(bf16[1536,256]{1,0:T(8,128)(2,1)} %bitcast.63, bf16[1536,1536]{1,0:T(8,128)(2,1)} %bitcast.76, bf16[256,1536]{1,0:T(8,128)(2,1)} %hidden.3, f32[1,1536]{1,0:T(1,128)} %get-tuple-element.393.gain), custom_call_target="tpu_custom_call" | custom-call | flops 6600000000 | bytes 6000000 | tf_op jit(solution)/shard_map/after_attn/pallas_call | solution.py:707
  150.2 6.0 %code.1.refs_9_.refs_10_ = f32[8,256,16]{2,1,0:T(8,128)} custom-call(bf16[8,64,384]{2,1,0:T(8,128)(2,1)} %copy-done.51), custom_call_target="tpu_custom_call" | custom-call | flops 6600000000 | bytes 6000000 | tf_op jit(solution)/shard_map/code/pallas_call | solution.py:707
  157.8 2.2 collective-permute-done.23
  162.3 16.5 %collective-permute-done.26 = bf16[2,128,1536]{2,1,0:T(8,128)(2,1)S(1)} collective-permute-done((bf16[2,128,1536]{2,1,0:T(8,128)(2,1)S(1)}, bf16[2,128,1536]{2,1,0:T(8,128)(2,1)S(1)}, u32[]{:S(2)}, u32[]{:S(2)}) %collective-permute-start.26) | collective-permute-done | bytes 786464 | tf_op jit(solution)/shard_map/ppermute | solution.py:67
  180.5 2.0 collective-permute-done.27.refs_3_
  182.5 2.2 collective-permute-done.25.refs_1_
  184.8 45.6 %moe_first.1 = (bf16[4,128,1664]{2,1,0:T(8,128)(2,1)}, bf16[4,128,1664]{2,1,0:T(8,128)(2,1)}, bf16[4,128,1664]{2,1,0:T(8,128)(2,1)}, bf16[4,128,1664]{2,1,0:T(8,...) custom-call(s32[1]{0:T(128)} %bitcast.15.which, s32[2,8]{1,0:T(2,128)} %broadcast_xor_fusion.blocks.blocks_ref, ...), custom_call_target="tpu_custom_call" | custom-call | flops 41799999488 | bytes 38000000 | tf_op jit(solution)/shard_map/moe_first/pallas_call | solution.py:707
  230.7 4.4 all-gather.7.cloned.1.call-done
  235.1 32.5 %moe_second.1 = (bf16[4,128,1664]{2,1,0:T(8,128)(2,1)}, bf16[4,128,1664]{2,1,0:T(8,128)(2,1)}, bf16[4,128,1664]{2,1,0:T(8,128)(2,1)}, bf16[4,128,1664]{2,1,0:T(8...) custom-call(s32[1]{0:T(128)S(6)} %add.55.which, ...), custom_call_target="tpu_custom_call" | custom-call | flops 27499999232 | bytes 25000000 | tf_op jit(solution)/shard_map/moe_second/pallas_call | solution.py:707
  268.1 3.3 collective-permute-done.30.refs_1_.refs_3_
  271.4 2.4 collective-permute-done.31.refs_5_.refs_7_
  281.3 18.4 %moe_grads.1 = bf16[4,3,384,512]{3,2,1,0:T(8,128)(2,1)} custom-call(bf16[4,128,1536]{2,1,0:T(8,128)(2,1)} %copy-done.54, bf16[4,128,1536]{2,1,0:T(8,128)(2,1)} %collective-permute-done.25.refs_1_, bf16[4,128,1536]{2,1,0:T(8,128)(2,1)} %copy-done.53, bf16[4,128,1536]{2,1,0:T(8,128)(2,1)} %collective-permute-done.27.refs_3_, ...), custom_call_target="tpu_custom_call" | custom-call | flops 16499999744 | bytes 15000000 | tf_op jit(solution)/shard_map/moe_grads/pallas_call | solution.py:707
  305.7 12.7 %moe_out.1 = (bf16[4,128,1536]{2,1,0:T(8,128)(2,1)}, bf16[4,128,1536]{2,1,0:T(8,128)(2,1)}, bf16[4,128,1536]{2,1,0:T(8,128)(2,1)}, bf16[4,128,1536]{2,1,0:T(8,128)(2,1)}) custom-call(bf16[8,256,512]{2,1,0:T(8,128)(2,1)} %get-tuple-element.204.b0, bf16[8,256,512]{2,1,0:T(8,128)(2,1)} %get-tuple-element.226.refs_8_.b1, bf16[4,3,384,512]{3,2,1,0:T(8,128)(2,1)} %bitcast.67, ...), custom_call_target="tpu_custom_call" | custom-call | flops 8800000000 | bytes 8000000 | tf_op jit(solution)/shard_map/moe_out/pallas_call | solution.py:707
  319.9 8.0 %before_attn.1 = (f32[256,1536]{1,0:T(8,128)}, bf16[256,1536]{1,0:T(8,128)(2,1)}, bf16[1536,256]{1,0:T(8,128)(2,1)}, f32[16,1536]{1,0:T(8,128)}, f32[1,1536]{1,0:T(1,128)}) custom-call(bf16[128,1664]{1,0:T(8,128)(2,1)} %bitcast.57, bf16[128,1664]{1,0:T(8,128)(2,1)} %bitcast.70, bf16[128,1664]{1,0:T(8,128)(2,1)} %bitcast.58, bf16[128,1664]{1,0:T(8,128)(2,1)} %bitcast.71, ...), custom_call_target="tpu_custom_call" | custom-call | flops 15399999488 | bytes 14000000 | tf_op jit(solution)/shard_map/before_attn/pallas_call | solution.py:707
  327.8 4.2 all-to-all-start.2
  332.1 7.4 %wout_grad.1 = (bf16[4,2,48,1536]{3,2,1,0:T(8,128)(2,1)}, bf16[4,2,48,1536]{3,2,1,0:T(8,128)(2,1)}, bf16[4,2,48,1536]{3,2,1,0:T(8,128)(2,1)}, bf16[4,2,48,1536]{3,2,1,0:T(8,128)(2,1)}) custom-call(s32[2,8]{1,0:T(2,128)} %select_bitcast_fusion.slot_ref, bf16[1536,256]{1,0:T(8,128)(2,1)} %bitcast.64, bf16[256,1536]{1,0:T(8,128)(2,1)} %get-tuple-element.247.d_branch), custom_call_target="tpu_custom_call" | custom-call | flops 6600000000 | bytes 6000000 | tf_op jit(solution)/shard_map/wout_grad/pallas_call | solution.py:707
  339.5 1.9 fold.10
  345.0 1.9 collective-permute-start.42
  348.8 26.6 %attn_bwd.1 = (bf16[8,192,256]{2,1,0:T(8,128)(2,1)}, bf16[8,64,256]{2,1,0:T(8,128)(2,1)}, bf16[8,64,256]{2,1,0:T(8,128)(2,1)}) custom-call(bf16[8,192,256]{2,1,0:T(8,128)(2,1)} %get-tuple-element.186.qt, bf16[8,192,256]{2,1,0:T(8,128)(2,1)} %all-to-all-done.2.dot_, f32[8,192,256]{2,1,0:T(8,128)} %get-tuple-element.242.of, ...), custom_call_target="tpu_custom_call" | custom-call | flops 44000002048 | bytes 40000000 | tf_op jit(solution)/shard_map/attn_bwd/pallas_call | solution.py:707
  378.3 2.8 copy-done.31
  381.1 4.0 qkv_grads.1
  385.2 7.5 %collective-permute-done.40.refs_1_.refs_3_ = bf16[2,2,48,1536]{3,2,1,0:T(8,128)(2,1)S(1)} collective-permute-done((bf16[2,2,48,1536]{3,2,1,0:T(8,128)(2,1)S(1)}, bf16[2,2,48,1536]{3,2,1,0:T(8,128)(2,1)S(1)}, u32[]{:S(2)}, u32[]{:S(2)}) %collective-permute-start.40) | collective-permute-done | bytes 589856 | tf_op jit(solution)/shard_map/ppermute | solution.py:67
  395.0 7.8 %qkv_back.1 = (bf16[4,128,1536]{2,1,0:T(8,128)(2,1)S(1)}, bf16[4,128,1536]{2,1,0:T(8,128)(2,1)}, bf16[4,128,1536]{2,1,0:T(8,128)(2,1)S(1)}, bf16[4,128,1536]{2,1,0:T(8,128)(2,1)}) custom-call(s32[2,8]{1,0:T(2,128)S(1)} %copy-done.9, bf16[8,192,256]{2,1,0:T(8,128)(2,1)S(1)} %copy-done.34, bf16[8,64,256]{2,1,0:T(8,128)(2,1)S(1)} %copy-done.35, ...), custom_call_target="tpu_custom_call" | custom-call | flops 22000001024 | bytes 20000000 | tf_op jit(solution)/shard_map/qkv_back/pallas_call | solution.py:707
  405.4 6.9 %collective-permute-done.48 = bf16[1,2,48,1536]{3,2,1,0:T(8,128)(2,1)S(1)} collective-permute-done((bf16[1,2,48,1536]{3,2,1,0:T(8,128)(2,1)S(1)}, bf16[1,2,48,1536]{3,2,1,0:T(8,128)(2,1)S(1)}, u32[]{:S(2)}, u32[]{:S(2)}) %collective-permute-start.48) | collective-permute-done | bytes 294944 | tf_op jit(solution)/shard_map/ppermute | solution.py:67
  416.9 2.3 fold.14
  432.4 10.3 %collective-permute-done.50.refs_1_.refs_3_ = bf16[2,128,1536]{2,1,0:T(8,128)(2,1)S(1)} collective-permute-done((bf16[2,128,1536]{2,1,0:T(8,128)(2,1)}, bf16[2,128,1536]{2,1,0:T(8,128)(2,1)S(1)}, u32[]{:S(2)}, u32[]{:S(2)}) %collective-permute-start.50) | collective-permute-done | bytes 786464 | tf_op jit(solution)/shard_map/ppermute | solution.py:67
  445.8 2.3 slice_bitcast_fusion
  451.6 3.7 all-to-all-start.3
  456.7 2.0 last.1
  458.7 3.9 all-to-all-done.3.given
  (288 shorter events, 108.2 us)
Async XLA Ops:
  9.2 13.6 %all-to-all-start = ((bf16[8,64,384]{2,1,0:T(8,128)(2,1)}), bf16[8,64,384]{2,1,0:T(8,128)(2,1)S(1)}, u32[]{:S(2)}, u32[]{:S(2)}) async-start(bf16[8,64,384]{2,1,0:T(8,128)(2,1)} %prep.1), calls=%async_computation | async-start | bytes 786432 | tf_op jit(solution)/shard_map/all_to_all | solution.py:777
  14.5 170.3 %all-gather.5.cloned.1.call-start = ((), (), s32[]{:S(2)}) async-start(), calls=%async_computation.10 | async-start | bytes 5898240 | tf_op jit(solution)/shard_map/all_gather | solution.py:821
  24.1 11.7 %collective-permute-start.3 = (bf16[1,128,1536]{2,1,0:T(8,128)(2,1)S(1)}, bf16[1,128,1536]{2,1,0:T(8,128)(2,1)S(1)}, u32[]{:S(2)}, u32[]{:S(2)}) collective-permute-start(bf16[1,128,1536]{2,1,0:T(8,128)(2,1)S(1)} %get-tuple-element.373), channel_id=1, source_target_pairs={{0,2},{1,3},{2,0},{3,1},{4,6},{5,7},{6,4},{7,5},{8,10},{9,11},{10,... | collective-permute-start | bytes 1179656 | tf_op jit(solution)/shard_map/ppermute | solution.py:67
  26.6 13.0 %collective-permute-start.9 = (bf16[530,384]{1,0:T(8,128)(2,1)}, bf16[530,384]{1,0:T(8,128)(2,1)}, u32[]{:S(2)}, u32[]{:S(2)}) collective-permute-start(bf16[530,384]{1,0:T(8,128)(2,1)} %pack.1.refs_3_), channel_id=1, source_target_pairs={{8,0},{16,8},{24,16},{9,1},{17,9},{25,17},{10,2},{18,10},{26,18},{... | collective-permute-start | bytes 1221128 | tf_op jit(solution)/shard_map/ppermute | solution.py:789
  28.0 12.9 %collective-permute-start.6 = (bf16[530,384]{1,0:T(8,128)(2,1)}, bf16[530,384]{1,0:T(8,128)(2,1)}, u32[]{:S(2)}, u32[]{:S(2)}) collective-permute-start(bf16[530,384]{1,0:T(8,128)(2,1)} %pack.1.refs_3_), channel_id=1, source_target_pairs={{0,8},{8,16},{16,24},{1,9},{9,17},{17,25},{2,10},{10,18},{18,26},{... | collective-permute-start | bytes 1221128 | tf_op jit(solution)/shard_map/ppermute | solution.py:789
  34.3 24.9 %collective-permute-start.1 = (bf16[2,128,1536]{2,1,0:T(8,128)(2,1)}, bf16[2,128,1536]{2,1,0:T(8,128)(2,1)}, u32[]{:S(2)}, u32[]{:S(2)}) collective-permute-start(bf16[2,128,1536]{2,1,0:T(8,128)(2,1)} %pad_maximum_fusion.4), channel_id=1, source_target_pairs={{0,2},{1,3},{2,0},{3,1},{4,6},{5,7},{6,4},{7,5},{8,10},{9,11},{10,... | collective-permute-start | bytes 2359304 | tf_op jit(solution)/shard_map/ppermute | solution.py:67
  36.8 23.9 %collective-permute-start.4 = (bf16[2,128,1536]{2,1,0:T(8,128)(2,1)}, bf16[2,128,1536]{2,1,0:T(8,128)(2,1)}, u32[]{:S(2)}, u32[]{:S(2)}) collective-permute-start(bf16[2,128,1536]{2,1,0:T(8,128)(2,1)} %pad_maximum_fusion.5), channel_id=1, source_target_pairs={{0,4},{1,5},{2,6},{3,7},{4,0},{5,1},{6,2},{7,3},{8,12},{9,13},{10,... | collective-permute-start | bytes 2359304 | tf_op jit(solution)/shard_map/ppermute | solution.py:67
  39.7 12.0 %collective-permute-start.10 = (bf16[530,384]{1,0:T(8,128)(2,1)}, bf16[530,384]{1,0:T(8,128)(2,1)}, u32[]{:S(2)}, u32[]{:S(2)}) collective-permute-start(bf16[530,384]{1,0:T(8,128)(2,1)} %collective-permute-done.9.refs_4_), channel_id=1, source_target_pairs={{8,0},{16,8},{24,16},{9,1},{17,9},{25,17},{10,2},{18,10},{26,18},{... | collective-permute-start | bytes 1221128 | tf_op jit(solution)/shard_map/ppermute | solution.py:789
  41.0 11.9 %collective-permute-start.7 = (bf16[530,384]{1,0:T(8,128)(2,1)}, bf16[530,384]{1,0:T(8,128)(2,1)}, u32[]{:S(2)}, u32[]{:S(2)}) collective-permute-start(bf16[530,384]{1,0:T(8,128)(2,1)} %collective-permute-done.6.refs_2_), channel_id=1, source_target_pairs={{0,8},{8,16},{16,24},{1,9},{9,17},{17,25},{2,10},{10,18},{18,26},{... | collective-permute-start | bytes 1221128 | tf_op jit(solution)/shard_map/ppermute | solution.py:789
  52.9 182.2 %all-gather.7.cloned.1.call-start = ((), (), s32[]{:S(2)}) async-start(), calls=%async_computation.11 | async-start | bytes 5898240 | tf_op jit(solution)/shard_map/all_gather | solution.py:821
  52.9 11.4 %collective-permute-start.11 = (bf16[530,384]{1,0:T(8,128)(2,1)}, bf16[530,384]{1,0:T(8,128)(2,1)S(1)}, u32[]{:S(2)}, u32[]{:S(2)}) collective-permute-start(bf16[530,384]{1,0:T(8,128)(2,1)} %collective-permute-done.10.refs_5_), channel_id=1, source_target_pairs={{8,0},{16,8},{24,16},{9,1},{17,9},{25,17},{10,2},{18,10},{26,18},{... | collective-permute-start | bytes 1221128 | tf_op jit(solution)/shard_map/ppermute | solution.py:789
  54.2 13.7 %collective-permute-start.8 = (bf16[530,384]{1,0:T(8,128)(2,1)}, bf16[530,384]{1,0:T(8,128)(2,1)S(1)}, u32[]{:S(2)}, u32[]{:S(2)}) collective-permute-start(bf16[530,384]{1,0:T(8,128)(2,1)} %collective-permute-done.7.refs_1_), channel_id=1, source_target_pairs={{0,8},{8,16},{16,24},{1,9},{9,17},{17,25},{2,10},{10,18},{18,26},{... | collective-permute-start | bytes 1221128 | tf_op jit(solution)/shard_map/ppermute | solution.py:789
  60.6 16.6 %collective-permute-start.2 = (bf16[4,128,1536]{2,1,0:T(8,128)(2,1)S(1)}, bf16[4,128,1536]{2,1,0:T(8,128)(2,1)}, u32[]{:S(2)}, u32[]{:S(2)}) collective-permute-start(bf16[4,128,1536]{2,1,0:T(8,128)(2,1)S(1)} %pad_maximum_fusion.xa), channel_id=1, source_target_pairs={{0,1},{1,0},{2,3},{3,2},{4,5},{5,4},{6,7},{7,6},{8,9},{9,8},{10,11... | collective-permute-start | bytes 4718600 | tf_op jit(solution)/shard_map/ppermute | solution.py:67
  62.7 14.5 %collective-permute-start.5 = (bf16[4,128,1536]{2,1,0:T(8,128)(2,1)S(1)}, bf16[4,128,1536]{2,1,0:T(8,128)(2,1)}, u32[]{:S(2)}, u32[]{:S(2)}) collective-permute-start(bf16[4,128,1536]{2,1,0:T(8,128)(2,1)S(1)} %pad_maximum_fusion.1.xb), channel_id=1, source_target_pairs={{0,1},{1,0},{2,3},{3,2},{4,5},{5,4},{6,7},{7,6},{8,9},{9,8},{10,11... | collective-permute-start | bytes 4718600 | tf_op jit(solution)/shard_map/ppermute | solution.py:67
  62.8 12.0 %collective-permute-start.13 = (bf16[1,128,1536]{2,1,0:T(8,128)(2,1)S(1)}, bf16[1,128,1536]{2,1,0:T(8,128)(2,1)S(1)}, u32[]{:S(2)}, u32[]{:S(2)}) collective-permute-start(bf16[1,128,1536]{2,1,0:T(8,128)(2,1)S(1)} %get-tuple-element.180), channel_id=1, source_target_pairs={{0,2},{1,3},{2,0},{3,1},{4,6},{5,7},{6,4},{7,5},{8,10},{9,11},{10,... | collective-permute-start | bytes 1179656 | tf_op jit(solution)/shard_map/ppermute | solution.py:67
  64.4 12.8 %collective-permute-start.12 = (bf16[1,128,1536]{2,1,0:T(8,128)(2,1)S(1)}, bf16[1,128,1536]{2,1,0:T(8,128)(2,1)S(1)}, u32[]{:S(2)}, u32[]{:S(2)}) collective-permute-start(bf16[1,128,1536]{2,1,0:T(8,128)(2,1)S(1)} %get-tuple-element.178), channel_id=1, source_target_pairs={{0,4},{1,5},{2,6},{3,7},{4,0},{5,1},{6,2},{7,3},{8,12},{9,13},{10,... | collective-permute-start | bytes 1179656 | tf_op jit(solution)/shard_map/ppermute | solution.py:67
  72.8 16.7 %collective-permute-start.15 = (bf16[1,2,48,1536]{3,2,1,0:T(8,128)(2,1)S(1)}, bf16[1,2,48,1536]{3,2,1,0:T(8,128)(2,1)S(1)}, u32[]{:S(2)}, u32[]{:S(2)}) collective-permute-start(bf16[1,2,48,1536]{3,2,1,0:T(8,128)(2,1)S(1)} %get-tuple-element.184), channel_id=1, source_target_pairs={{0,2},{1,3},{2,0},{3,1},{4,6},{5,7},{6,4},{7,5},{8,10},{9,11},{10,... | collective-permute-start | bytes 884744 | tf_op jit(solution)/shard_map/ppermute | solution.py:67
  74.8 14.7 %collective-permute-start.14 = (bf16[1,2,48,1536]{3,2,1,0:T(8,128)(2,1)S(1)}, bf16[1,2,48,1536]{3,2,1,0:T(8,128)(2,1)S(1)}, u32[]{:S(2)}, u32[]{:S(2)}) collective-permute-start(bf16[1,2,48,1536]{3,2,1,0:T(8,128)(2,1)S(1)} %get-tuple-element.182), channel_id=1, source_target_pairs={{0,4},{1,5},{2,6},{3,7},{4,0},{5,1},{6,2},{7,3},{8,12},{9,13},{10,... | collective-permute-start | bytes 884744 | tf_op jit(solution)/shard_map/ppermute | solution.py:67
  91.0 28.4 %collective-permute-start.18 = (bf16[2,2,48,1536]{3,2,1,0:T(8,128)(2,1)}, bf16[2,2,48,1536]{3,2,1,0:T(8,128)(2,1)S(1)}, u32[]{:S(2)}, u32[]{:S(2)}) collective-permute-start(bf16[2,2,48,1536]{3,2,1,0:T(8,128)(2,1)} %get-tuple-element.390), channel_id=1, source_target_pairs={{0,2},{1,3},{2,0},{3,1},{4,6},{5,7},{6,4},{7,5},{8,10},{9,11},{10,... | collective-permute-start | bytes 1769480 | tf_op jit(solution)/shard_map/ppermute | solution.py:67
  94.2 25.3 %collective-permute-start.19 = (bf16[2,2,48,1536]{3,2,1,0:T(8,128)(2,1)S(1)}, bf16[2,2,48,1536]{3,2,1,0:T(8,128)(2,1)S(1)}, u32[]{:S(2)}, u32[]{:S(2)}) collective-permute-start(bf16[2,2,48,1536]{3,2,1,0:T(8,128)(2,1)S(1)} %get-tuple-element.386), channel_id=1, source_target_pairs={{0,4},{1,5},{2,6},{3,7},{4,0},{5,1},{6,2},{7,3},{8,12},{9,13},{10,... | collective-permute-start | bytes 1769480 | tf_op jit(solution)/shard_map/ppermute | solution.py:67
  94.6 27.5 %collective-permute-start.16 = (bf16[2,128,1536]{2,1,0:T(8,128)(2,1)S(1)}, bf16[2,128,1536]{2,1,0:T(8,128)(2,1)S(1)}, u32[]{:S(2)}, u32[]{:S(2)}) collective-permute-start(bf16[2,128,1536]{2,1,0:T(8,128)(2,1)S(1)} %get-tuple-element.382), channel_id=1, source_target_pairs={{0,2},{1,3},{2,0},{3,1},{4,6},{5,7},{6,4},{7,5},{8,10},{9,11},{10,... | collective-permute-start | bytes 2359304 | tf_op jit(solution)/shard_map/ppermute | solution.py:67
  96.8 26.5 %collective-permute-start.17 = (bf16[2,128,1536]{2,1,0:T(8,128)(2,1)S(1)}, bf16[2,128,1536]{2,1,0:T(8,128)(2,1)S(1)}, u32[]{:S(2)}, u32[]{:S(2)}) collective-permute-start(bf16[2,128,1536]{2,1,0:T(8,128)(2,1)S(1)} %get-tuple-element.378), channel_id=1, source_target_pairs={{0,4},{1,5},{2,6},{3,7},{4,0},{5,1},{6,2},{7,3},{8,12},{9,13},{10,... | collective-permute-start | bytes 2359304 | tf_op jit(solution)/shard_map/ppermute | solution.py:67
  125.5 16.1 %all-to-all-start.1 = ((bf16[8,192,256]{2,1,0:T(8,128)(2,1)}), bf16[8,192,256]{2,1,0:T(8,128)(2,1)S(1)}, u32[]{:S(2)}, u32[]{:S(2)}) async-start(bf16[8,192,256]{2,1,0:T(8,128)(2,1)} %get-tuple-element.190), calls=%async_computation.1 | async-start | bytes 1572864 | tf_op jit(solution)/shard_map/all_to_all | solution.py:892
  129.1 215.9 %reduce-scatter.4.cloned.1.call-start = ((), (), s32[]{:S(2)}) async-start(), calls=%async_computation.7 | async-start | bytes 5898240 | tf_op jit(solution)/shard_map/reduce_scatter | solution.py:991
  130.3 50.2 %collective-permute-start.28 = (bf16[4,128,1536]{2,1,0:T(8,128)(2,1)}, bf16[4,128,1536]{2,1,0:T(8,128)(2,1)}, u32[]{:S(2)}, u32[]{:S(2)}) collective-permute-start(bf16[4,128,1536]{2,1,0:T(8,128)(2,1)} %constant_dynamic-update-slice_fusion.20.refs_4_), channel_id=1, source_target_pairs={{0,1},{1,0},{2,3},{3,2},{4,5},{5,4},{6,7},{7,6},{8,9},{9,8},{10,11... | collective-permute-start | bytes 4718600 | tf_op jit(solution)/shard_map/ppermute | solution.py:67
  131.6 48.8 %collective-permute-start.29 = (bf16[4,128,1536]{2,1,0:T(8,128)(2,1)}, bf16[4,128,1536]{2,1,0:T(8,128)(2,1)}, u32[]{:S(2)}, u32[]{:S(2)}) collective-permute-start(bf16[4,128,1536]{2,1,0:T(8,128)(2,1)} %constant_dynamic-update-slice_fusion.23.refs_6_), channel_id=1, source_target_pairs={{0,1},{1,0},{2,3},{3,2},{4,5},{5,4},{6,7},{7,6},{8,9},{9,8},{10,11... | collective-permute-start | bytes 4718600 | tf_op jit(solution)/shard_map/ppermute | solution.py:67
  148.2 11.8 %collective-permute-start.22 = (bf16[1,128,1536]{2,1,0:T(8,128)(2,1)}, bf16[1,128,1536]{2,1,0:T(8,128)(2,1)S(1)}, u32[]{:S(2)}, u32[]{:S(2)}) collective-permute-start(bf16[1,128,1536]{2,1,0:T(8,128)(2,1)} %get-tuple-element.194.ma), channel_id=1, source_target_pairs={{0,4},{1,5},{2,6},{3,7},{4,0},{5,1},{6,2},{7,3},{8,12},{9,13},{10,... | collective-permute-start | bytes 1179656 | tf_op jit(solution)/shard_map/ppermute | solution.py:67
  160.1 18.8 %collective-permute-start.26 = (bf16[2,128,1536]{2,1,0:T(8,128)(2,1)S(1)}, bf16[2,128,1536]{2,1,0:T(8,128)(2,1)S(1)}, u32[]{:S(2)}, u32[]{:S(2)}) collective-permute-start(bf16[2,128,1536]{2,1,0:T(8,128)(2,1)S(1)} %pad_maximum_fusion.7), channel_id=1, source_target_pairs={{0,4},{1,5},{2,6},{3,7},{4,0},{5,1},{6,2},{7,3},{8,12},{9,13},{10,... | collective-permute-start | bytes 2359304 | tf_op jit(solution)/shard_map/ppermute | solution.py:67
  160.5 18.8 %collective-permute-start.24 = (bf16[2,128,1536]{2,1,0:T(8,128)(2,1)S(1)}, bf16[2,128,1536]{2,1,0:T(8,128)(2,1)S(1)}, u32[]{:S(2)}, u32[]{:S(2)}) collective-permute-start(bf16[2,128,1536]{2,1,0:T(8,128)(2,1)S(1)} %pad_maximum_fusion.6), channel_id=1, source_target_pairs={{0,2},{1,3},{2,0},{3,1},{4,6},{5,7},{6,4},{7,5},{8,10},{9,11},{10,... | collective-permute-start | bytes 2359304 | tf_op jit(solution)/shard_map/ppermute | solution.py:67
  230.4 192.3 %reduce-scatter.6.cloned.1.call-start = ((), (), s32[]{:S(2)}) async-start(), calls=%async_computation.8 | async-start | bytes 5898240 | tf_op jit(solution)/shard_map/reduce_scatter | solution.py:991
  278.3 21.4 %collective-permute-start.32 = (bf16[2,128,1664]{2,1,0:T(8,128)(2,1)}, bf16[2,128,1664]{2,1,0:T(8,128)(2,1)S(1)}, u32[]{:S(2)}, u32[]{:S(2)}) collective-permute-start(bf16[2,128,1664]{2,1,0:T(8,128)(2,1)} %get-tuple-element.218), channel_id=1, source_target_pairs={{0,2},{1,3},{2,0},{3,1},{4,6},{5,7},{6,4},{7,5},{8,10},{9,11},{10,... | collective-permute-start | bytes 2555912 | tf_op jit(solution)/shard_map/ppermute | solution.py:67
  279.8 20.8 %collective-permute-start.33 = (bf16[2,128,1664]{2,1,0:T(8,128)(2,1)S(1)}, bf16[2,128,1664]{2,1,0:T(8,128)(2,1)}, u32[]{:S(2)}, u32[]{:S(2)}) collective-permute-start(bf16[2,128,1664]{2,1,0:T(8,128)(2,1)S(1)} %get-tuple-element.219), channel_id=1, source_target_pairs={{0,4},{1,5},{2,6},{3,7},{4,0},{5,1},{6,2},{7,3},{8,12},{9,13},{10,... | collective-permute-start | bytes 2555912 | tf_op jit(solution)/shard_map/ppermute | solution.py:67
  303.7 15.3 %collective-permute-start.36 = (bf16[1,128,1664]{2,1,0:T(8,128)(2,1)S(1)}, bf16[1,128,1664]{2,1,0:T(8,128)(2,1)S(1)}, u32[]{:S(2)}, u32[]{:S(2)}) collective-permute-start(bf16[1,128,1664]{2,1,0:T(8,128)(2,1)S(1)} %get-tuple-element.235), channel_id=1, source_target_pairs={{0,4},{1,5},{2,6},{3,7},{4,0},{5,1},{6,2},{7,3},{8,12},{9,13},{10,... | collective-permute-start | bytes 1277960 | tf_op jit(solution)/shard_map/ppermute | solution.py:67
  305.1 13.8 %collective-permute-start.37 = (bf16[1,128,1664]{2,1,0:T(8,128)(2,1)S(1)}, bf16[1,128,1664]{2,1,0:T(8,128)(2,1)S(1)}, u32[]{:S(2)}, u32[]{:S(2)}) collective-permute-start(bf16[1,128,1664]{2,1,0:T(8,128)(2,1)S(1)} %get-tuple-element.236), channel_id=1, source_target_pairs={{0,2},{1,3},{2,0},{3,1},{4,6},{5,7},{6,4},{7,5},{8,10},{9,11},{10,... | collective-permute-start | bytes 1277960 | tf_op jit(solution)/shard_map/ppermute | solution.py:67
  318.4 21.1 %collective-permute-start.34 = (bf16[4,128,1536]{2,1,0:T(8,128)(2,1)}, bf16[4,128,1536]{2,1,0:T(8,128)(2,1)S(1)}, u32[]{:S(2)}, u32[]{:S(2)}) collective-permute-start(bf16[4,128,1536]{2,1,0:T(8,128)(2,1)} %get-tuple-element.228), channel_id=1, source_target_pairs={{0,1},{1,0},{2,3},{3,2},{4,5},{5,4},{6,7},{7,6},{8,9},{9,8},{10,11... | collective-permute-start | bytes 4718600 | tf_op jit(solution)/shard_map/ppermute | solution.py:67
  318.4 21.1 %collective-permute-start.35 = (bf16[4,128,1536]{2,1,0:T(8,128)(2,1)}, bf16[4,128,1536]{2,1,0:T(8,128)(2,1)}, u32[]{:S(2)}, u32[]{:S(2)}) collective-permute-start(bf16[4,128,1536]{2,1,0:T(8,128)(2,1)} %get-tuple-element.230), channel_id=1, source_target_pairs={{0,1},{1,0},{2,3},{3,2},{4,5},{5,4},{6,7},{7,6},{8,9},{9,8},{10,11... | collective-permute-start | bytes 4718600 | tf_op jit(solution)/shard_map/ppermute | solution.py:67
  327.8 17.2 %all-to-all-start.2 = ((bf16[8,192,256]{2,1,0:T(8,128)(2,1)}), bf16[8,192,256]{2,1,0:T(8,128)(2,1)}, u32[]{:S(2)}, u32[]{:S(2)}) async-start(bf16[8,192,256]{2,1,0:T(8,128)(2,1)} %bitcast.65), calls=%async_computation.2 | async-start | bytes 1572864 | tf_op jit(solution)/shard_map/all_to_all | solution.py:1026
  332.1 117.6 %reduce-scatter.8.cloned.1.call-start = ((), (), s32[]{:S(2)}) async-start(), calls=%async_computation.9 | async-start | bytes 2088960 | tf_op jit(solution)/shard_map/reduce_scatter | solution.py:1132
  345.0 40.2 %collective-permute-start.42 = (bf16[2,128,1536]{2,1,0:T(8,128)(2,1)}, bf16[2,128,1536]{2,1,0:T(8,128)(2,1)S(1)}, u32[]{:S(2)}, u32[]{:S(2)}) collective-permute-start(bf16[2,128,1536]{2,1,0:T(8,128)(2,1)} %copy-done.15), channel_id=1, source_target_pairs={{0,2},{1,3},{2,0},{3,1},{4,6},{5,7},{6,4},{7,5},{8,10},{9,11},{10,... | collective-permute-start | bytes 2359304 | tf_op jit(solution)/shard_map/ppermute | solution.py:67
  346.8 38.3 %collective-permute-start.43 = (bf16[2,128,1536]{2,1,0:T(8,128)(2,1)}, bf16[2,128,1536]{2,1,0:T(8,128)(2,1)S(1)}, u32[]{:S(2)}, u32[]{:S(2)}) collective-permute-start(bf16[2,128,1536]{2,1,0:T(8,128)(2,1)} %copy-done.14), channel_id=1, source_target_pairs={{0,4},{1,5},{2,6},{3,7},{4,0},{5,1},{6,2},{7,3},{8,12},{9,13},{10,... | collective-permute-start | bytes 2359304 | tf_op jit(solution)/shard_map/ppermute | solution.py:67
  348.3 27.1 %collective-permute-start.38 = (bf16[4,2,48,1536]{3,2,1,0:T(8,128)(2,1)}, bf16[4,2,48,1536]{3,2,1,0:T(8,128)(2,1)S(1)}, u32[]{:S(2)}, u32[]{:S(2)}) collective-permute-start(bf16[4,2,48,1536]{3,2,1,0:T(8,128)(2,1)} %get-tuple-element.254), channel_id=1, source_target_pairs={{0,1},{1,0},{2,3},{3,2},{4,5},{5,4},{6,7},{7,6},{8,9},{9,8},{10,11... | collective-permute-start | bytes 3538952 | tf_op jit(solution)/shard_map/ppermute | solution.py:67
  348.3 27.1 %collective-permute-start.39 = (bf16[4,2,48,1536]{3,2,1,0:T(8,128)(2,1)}, bf16[4,2,48,1536]{3,2,1,0:T(8,128)(2,1)S(1)}, u32[]{:S(2)}, u32[]{:S(2)}) collective-permute-start(bf16[4,2,48,1536]{3,2,1,0:T(8,128)(2,1)} %get-tuple-element.255), channel_id=1, source_target_pairs={{0,1},{1,0},{2,3},{3,2},{4,5},{5,4},{6,7},{7,6},{8,9},{9,8},{10,11... | collective-permute-start | bytes 3538952 | tf_op jit(solution)/shard_map/ppermute | solution.py:67
  377.4 15.3 %collective-permute-start.40 = (bf16[2,2,48,1536]{3,2,1,0:T(8,128)(2,1)S(1)}, bf16[2,2,48,1536]{3,2,1,0:T(8,128)(2,1)S(1)}, u32[]{:S(2)}, u32[]{:S(2)}) collective-permute-start(bf16[2,2,48,1536]{3,2,1,0:T(8,128)(2,1)S(1)} %get-tuple-element.264), channel_id=1, source_target_pairs={{0,2},{1,3},{2,0},{3,1},{4,6},{5,7},{6,4},{7,5},{8,10},{9,11},{10,... | collective-permute-start | bytes 1769480 | tf_op jit(solution)/shard_map/ppermute | solution.py:67
  378.0 15.0 %collective-permute-start.41 = (bf16[2,2,48,1536]{3,2,1,0:T(8,128)(2,1)S(1)}, bf16[2,2,48,1536]{3,2,1,0:T(8,128)(2,1)S(1)}, u32[]{:S(2)}, u32[]{:S(2)}) collective-permute-start(bf16[2,2,48,1536]{3,2,1,0:T(8,128)(2,1)S(1)} %get-tuple-element.265), channel_id=1, source_target_pairs={{0,4},{1,5},{2,6},{3,7},{4,0},{5,1},{6,2},{7,3},{8,12},{9,13},{10,... | collective-permute-start | bytes 1769480 | tf_op jit(solution)/shard_map/ppermute | solution.py:67
  402.8 14.1 %collective-permute-start.46 = (bf16[4,128,1536]{2,1,0:T(8,128)(2,1)}, bf16[4,128,1536]{2,1,0:T(8,128)(2,1)}, u32[]{:S(2)}, u32[]{:S(2)}) collective-permute-start(bf16[4,128,1536]{2,1,0:T(8,128)(2,1)} %get-tuple-element.292), channel_id=1, source_target_pairs={{0,1},{1,0},{2,3},{3,2},{4,5},{5,4},{6,7},{7,6},{8,9},{9,8},{10,11... | collective-permute-start | bytes 4718600 | tf_op jit(solution)/shard_map/ppermute | solution.py:67
  402.8 14.1 %collective-permute-start.47 = (bf16[4,128,1536]{2,1,0:T(8,128)(2,1)}, bf16[4,128,1536]{2,1,0:T(8,128)(2,1)}, u32[]{:S(2)}, u32[]{:S(2)}) collective-permute-start(bf16[4,128,1536]{2,1,0:T(8,128)(2,1)} %get-tuple-element.293), channel_id=1, source_target_pairs={{0,1},{1,0},{2,3},{3,2},{4,5},{5,4},{6,7},{7,6},{8,9},{9,8},{10,11... | collective-permute-start | bytes 4718600 | tf_op jit(solution)/shard_map/ppermute | solution.py:67
  425.4 17.3 %collective-permute-start.50 = (bf16[2,128,1536]{2,1,0:T(8,128)(2,1)}, bf16[2,128,1536]{2,1,0:T(8,128)(2,1)S(1)}, u32[]{:S(2)}, u32[]{:S(2)}) collective-permute-start(bf16[2,128,1536]{2,1,0:T(8,128)(2,1)} %copy-done.21), channel_id=1, source_target_pairs={{0,2},{1,3},{2,0},{3,1},{4,6},{5,7},{6,4},{7,5},{8,10},{9,11},{10,... | collective-permute-start | bytes 2359304 | tf_op jit(solution)/shard_map/ppermute | solution.py:67
  426.8 17.4 %collective-permute-start.51 = (bf16[2,128,1536]{2,1,0:T(8,128)(2,1)}, bf16[2,128,1536]{2,1,0:T(8,128)(2,1)S(1)}, u32[]{:S(2)}, u32[]{:S(2)}) collective-permute-start(bf16[2,128,1536]{2,1,0:T(8,128)(2,1)} %copy-done.20), channel_id=1, source_target_pairs={{0,4},{1,5},{2,6},{3,7},{4,0},{5,1},{6,2},{7,3},{8,12},{9,13},{10,... | collective-permute-start | bytes 2359304 | tf_op jit(solution)/shard_map/ppermute | solution.py:67
  (78 other events, 426.3 us)
Sparse Core Ops, SparseCore 0:
  53.0 91.8 all-gather.4
  146.4 88.5 all-gather.6
  237.4 83.6 reduce-scatter.3
  323.3 85.7 reduce-scatter.5
  413.9 35.7 reduce-scatter.7

commit v5 on v4

--- a/solution.py
+++ b/solution.py
@@ -453,7 +453,7 @@
     total = parts[0][:, QKV:]
     for part in parts[1:]:
         total = total + part[:, QKV:]
-    sums[...] = total[:, : sums.shape[1]]
+    sums[...] = total.T[: sums.shape[0]]
 
 
 def expert_terms(expert, x, y, router, code, w_gate, w_up, w_down):
@@ -1005,7 +1005,7 @@
         grid=n,
         specs=hidden_o * 2 + [down] * 2,
         out_specs=lanes_at_step((1, half, width), far),
-        limit=58,
+        limit=40,
     )
     mix = Scatter(outs, n)
     resid_in = after(resid, outs)
@@ -1069,7 +1069,7 @@
         ],
         out_specs=[at_step((1, QW, tok)), whole((n, HD, tok)), whole((n, HD, tok))],
         scratch=[pltpu.VMEM((n, tok, HD), f32), pltpu.VMEM((n, tok, HD), f32)],
-        limit=58,
+        limit=40,
     )
 
     dq, wout.keep, wout.got = after((dq, wout.keep, wout.got))
@@ -1147,14 +1147,13 @@
             shape_of(rp, KV * QW, dtype=f32),
             shape_of(rp, KV * HD, dtype=f32),
             shape_of(rp, KV * HD, dtype=f32),
-            shape_of(rp, 2 + experts, dtype=f32),
+            shape_of(2 + experts, rp, dtype=f32),
         ],
         [given],
         limit=30,
     )
 
-    back_in = Scatter(d_in, n)
-    back_in.got = after(back_in.got, bundle)
+    back_in = Scatter(after(d_in, bundle), n)
     back_in.step()
     expert_grads, mix.got = after((expert_grads, mix.got), back_in.keep)
     (c0, c1), (e0, e1) = back_in.run()
@@ -1177,13 +1176,13 @@
     return (
         output,
         d_hidden,
-        sums[:, 0],
+        sums[0],
         grad_query,
         grad_key,
         grad_value,
         grad_out_proj,
-        sums[:, 1],
-        sums[:, 2:],
+        sums[1],
+        sums[2:].T,
         expert_grads[:, 0],
         expert_grads[:, 1],
         expert_grads[:, 2],

time: 480 us -> 478 us (level)
  local copies, waits for them, and re-layouts: 43.4 us -> 50.6 us
    unnamed x138 -> x151, local copies, waits for them, and re-layouts: 30.7 us -> 37.5 us
where the time goes in v5:
time: 478 us; the launch traced here: 470 us
  Pallas kernels  232 us (49%)
  waiting for transfers between devices  83.8 us (18%)
  starting transfers between devices  74.6 us (16%)
  local copies, waits for them, and re-layouts  50.6 us (11%)
  between operations  15.1 us (3%)
  other arithmetic  14.1 us (3%)
    pallas_call x21, Pallas kernels, call(): pl.pallas_call(kernel, grid_spec=pltpu.PrefetchScalarGridSpec(num_scalar_...  223 us
    ppermute x48, waiting for transfers between devices, swap(): return lax.ppermute(value, 'ctx', [(i, i ^ bit) for i in range(count)])  59.6 us
    ppermute x48, starting transfers between devices, swap(): return lax.ppermute(value, 'ctx', [(i, i ^ bit) for i in range(count)])  37.6 us
    unnamed x151, local copies, waits for them, and re-layouts  37.5 us
    ppermute x6, starting transfers between devices, along(): return lax.ppermute(value, 'dp', pairs)  19.7 us
  transfers between devices with their start and end apart: 63, of which 29 were waited for; matrix products, arithmetic and copies ran while one was open for 6% of the time, Pallas kernels for 49%

profile of v5, /device:TPU:0, one launch (start us, length us, event | category | flops | bytes accessed | tf_op | source)
XLA Modules:
  0.0 470.5 jit_solution(14417155712510999170)
XLA Ops:
  7.2 2.0 prep.1
  9.2 5.3 %all-to-all-start = ((bf16[8,64,384]{2,1,0:T(8,128)(2,1)}), bf16[8,64,384]{2,1,0:T(8,128)(2,1)S(1)}, u32[]{:S(2)}, u32[]{:S(2)}) async-start(bf16[8,64,384]{2,1,0:T(8,128)(2,1)} %prep.1), calls=%async_computation | async-start | bytes 786432 | tf_op jit(solution)/shard_map/all_to_all | solution.py:777
  17.3 5.6 %all-to-all-done.took.table = bf16[8,64,384]{2,1,0:T(8,128)(2,1)S(1)} async-done(((bf16[8,64,384]{2,1,0:T(8,128)(2,1)}), bf16[8,64,384]{2,1,0:T(8,128)(2,1)S(1)}, u32[]{:S(2)}, u32[]{:S(2)}) %all-to-all-start) | async-done | bytes 393248 | tf_op jit(solution)/shard_map/all_to_all | solution.py:777
  24.7 1.9 pack.1.refs_3_
  28.0 5.3 %collective-permute-start.6 = (bf16[530,384]{1,0:T(8,128)(2,1)}, bf16[530,384]{1,0:T(8,128)(2,1)}, u32[]{:S(2)}, u32[]{:S(2)}) collective-permute-start(bf16[530,384]{1,0:T(8,128)(2,1)} %pack.1.refs_3_), channel_id=1, source_target_pairs={{0,8},{8,16},{16,24},{1,9},{9,17},{17,25},{2,10},{10,18},{18,26},{... | collective-permute-start | bytes 1221128 | tf_op jit(solution)/shard_map/ppermute | solution.py:789
  40.9 5.3 %collective-permute-start.7 = (bf16[530,384]{1,0:T(8,128)(2,1)}, bf16[530,384]{1,0:T(8,128)(2,1)}, u32[]{:S(2)}, u32[]{:S(2)}) collective-permute-start(bf16[530,384]{1,0:T(8,128)(2,1)} %collective-permute-done.6.refs_2_), channel_id=1, source_target_pairs={{0,8},{8,16},{16,24},{1,9},{9,17},{17,25},{2,10},{10,18},{18,26},{... | collective-permute-start | bytes 1221128 | tf_op jit(solution)/shard_map/ppermute | solution.py:789
  49.7 1.9 collective-permute-done.10.refs_5_
  54.2 5.0 %collective-permute-start.8 = (bf16[530,384]{1,0:T(8,128)(2,1)}, bf16[530,384]{1,0:T(8,128)(2,1)S(1)}, u32[]{:S(2)}, u32[]{:S(2)}) collective-permute-start(bf16[530,384]{1,0:T(8,128)(2,1)} %collective-permute-done.7.refs_1_), channel_id=1, source_target_pairs={{0,8},{8,16},{16,24},{1,9},{9,17},{17,25},{2,10},{10,18},{18,26},{... | collective-permute-start | bytes 1221128 | tf_op jit(solution)/shard_map/ppermute | solution.py:789
  60.7 2.0 pad_maximum_fusion.1.xb
  64.3 2.1 collective-permute-start.12
  68.6 3.1 unpack.1
  74.8 2.3 collective-permute-start.14
  77.1 12.3 %qkv.1 = (bf16[8,256,1536]{2,1,0:T(8,128)(2,1)}, bf16[8,192,256]{2,1,0:T(8,128)(2,1)}, bf16[8,256,64]{2,1,0:T(8,128)(2,1)}, bf16[8,64,256]{2,1,0:T(8,128)(2,1)},...) custom-call(s32[2,8]{1,0:T(2,128)} %select_bitcast_fusion.slot_ref, bf16[4,128,1536]{2,1,0:T(8,128)(2,1)} %copy-done.44, ...), custom_call_target="tpu_custom_call" | custom-call | flops 6600000000 | bytes 6000000 | tf_op jit(solution)/shard_map/qkv/pallas_call | solution.py:707
  91.0 2.1 collective-permute-start.18
  98.4 21.0 %attn_fwd.1 = (f32[8,192,256]{2,1,0:T(8,128)}, bf16[8,192,256]{2,1,0:T(8,128)(2,1)}, f32[8,1,768]{2,1,0:T(1,128)}) custom-call(bf16[8,192,256]{2,1,0:T(8,128)(2,1)} %get-tuple-element.188.qt, bf16[8,256,64]{2,1,0:T(8,128)(2,1)} %get-tuple-element.189.k, bf16[8,64,256]{2,1,0:T(8,128)(2,1)} %get-tuple-element.190.vt), custom_call_target="tpu_custom_call" | custom-call | flops 20899999744 | bytes 19000000 | tf_op jit(solution)/shard_map/attn_fwd/pallas_call | solution.py:707
  119.4 2.7 collective-permute-done.16
  125.5 3.6 all-to-all-start.1
  131.8 8.0 %place.1 = bf16[4,8,48,1536]{3,2,1,0:T(8,128)(2,1)} custom-call(s32[2,8]{1,0:T(2,128)} %select_bitcast_fusion.slot_ref, bf16[4,2,48,1536]{3,2,1,0:T(8,128)(2,1)} %constant_dynamic-update-slice_fusion.8.a, bf16[4,2,48,1536]{3,2,1,0:T(8,128)(2,1)} %collective-permute-done.20.af, bf16[4,2,48,1536]{3,2,1,0:T(8,128)(2,1)} %constant_dynamic-update-slice_fusion.11.b, ...), custom_call_target="tpu_custom_call" | custom-call | flops 4400000000 | bytes 4000000 | tf_op jit(solution)/shard_map/place/pallas_call | solution.py:707
  142.5 5.7 %after_attn.1 = (f32[256,1536]{1,0:T(8,128)}, bf16[1,128,1536]{2,1,0:T(8,128)(2,1)}, bf16[1,128,1536]{2,1,0:T(8,128)(2,1)}) custom-call(bf16[1536,256]{1,0:T(8,128)(2,1)} %bitcast.69, bf16[1536,1536]{1,0:T(8,128)(2,1)} %bitcast.82, bf16[256,1536]{1,0:T(8,128)(2,1)} %hidden.3, f32[1,1536]{1,0:T(1,128)} %get-tuple-element.361.gain), custom_call_target="tpu_custom_call" | custom-call | flops 6600000000 | bytes 6000000 | tf_op jit(solution)/shard_map/after_attn/pallas_call | solution.py:707
  150.3 6.0 %code.1.refs_9_.refs_10_ = f32[8,256,16]{2,1,0:T(8,128)} custom-call(bf16[8,64,384]{2,1,0:T(8,128)(2,1)} %copy-done.58), custom_call_target="tpu_custom_call" | custom-call | flops 6600000000 | bytes 6000000 | tf_op jit(solution)/shard_map/code/pallas_call | solution.py:707
  157.9 2.1 collective-permute-done.23
  162.4 16.4 %collective-permute-done.26 = bf16[2,128,1536]{2,1,0:T(8,128)(2,1)S(1)} collective-permute-done((bf16[2,128,1536]{2,1,0:T(8,128)(2,1)S(1)}, bf16[2,128,1536]{2,1,0:T(8,128)(2,1)S(1)}, u32[]{:S(2)}, u32[]{:S(2)}) %collective-permute-start.26) | collective-permute-done | bytes 786464 | tf_op jit(solution)/shard_map/ppermute | solution.py:67
  180.4 2.1 collective-permute-done.27.refs_3_
  182.5 2.2 collective-permute-done.25.refs_1_
  184.7 45.6 %moe_first.1 = (bf16[4,128,1664]{2,1,0:T(8,128)(2,1)}, bf16[4,128,1664]{2,1,0:T(8,128)(2,1)}, bf16[4,128,1664]{2,1,0:T(8,128)(2,1)}, bf16[4,128,1664]{2,1,0:T(8,...) custom-call(s32[1]{0:T(128)} %bitcast.15.which, s32[2,8]{1,0:T(2,128)} %broadcast_xor_fusion.blocks.blocks_ref, ...), custom_call_target="tpu_custom_call" | custom-call | flops 41799999488 | bytes 38000000 | tf_op jit(solution)/shard_map/moe_first/pallas_call | solution.py:707
  230.6 4.5 all-gather.7.cloned.1.call-done
  235.0 32.5 %moe_second.1 = (bf16[4,128,1664]{2,1,0:T(8,128)(2,1)}, bf16[4,128,1664]{2,1,0:T(8,128)(2,1)}, bf16[4,128,1664]{2,1,0:T(8,128)(2,1)}, bf16[4,128,1664]{2,1,0:T(8...) custom-call(s32[1]{0:T(128)S(6)} %add.55.which, ...), custom_call_target="tpu_custom_call" | custom-call | flops 27499999232 | bytes 25000000 | tf_op jit(solution)/shard_map/moe_second/pallas_call | solution.py:707
  268.1 3.3 collective-permute-done.30.refs_1_.refs_3_
  271.4 2.4 collective-permute-done.31.refs_5_.refs_7_
  281.1 18.4 %moe_grads.1 = bf16[4,3,384,512]{3,2,1,0:T(8,128)(2,1)} custom-call(bf16[4,128,1536]{2,1,0:T(8,128)(2,1)} %copy-done.61, bf16[4,128,1536]{2,1,0:T(8,128)(2,1)} %collective-permute-done.25.refs_1_, bf16[4,128,1536]{2,1,0:T(8,128)(2,1)} %copy-done.60, bf16[4,128,1536]{2,1,0:T(8,128)(2,1)} %collective-permute-done.27.refs_3_, ...), custom_call_target="tpu_custom_call" | custom-call | flops 16499999744 | bytes 15000000 | tf_op jit(solution)/shard_map/moe_grads/pallas_call | solution.py:707
  305.7 11.7 %moe_out.1 = (bf16[4,128,1536]{2,1,0:T(8,128)(2,1)S(1)}, bf16[4,128,1536]{2,1,0:T(8,128)(2,1)}, bf16[4,128,1536]{2,1,0:T(8,128)(2,1)S(1)}, bf16[4,128,1536]{2,1,0:T(8,128)(2,1)}) custom-call(bf16[8,256,512]{2,1,0:T(8,128)(2,1)S(1)} %copy-done.34, bf16[8,256,512]{2,1,0:T(8,128)(2,1)S(1)} %copy-done.35, bf16[4,3,384,512]{3,2,1,0:T(8,128)(2,1)} %bitcast.73, ...), custom_call_target="tpu_custom_call" | custom-call | flops 8800000000 | bytes 8000000 | tf_op jit(solution)/shard_map/moe_out/pallas_call | solution.py:707
  318.8 7.9 %before_attn.1 = (f32[256,1536]{1,0:T(8,128)}, bf16[256,1536]{1,0:T(8,128)(2,1)}, bf16[1536,256]{1,0:T(8,128)(2,1)}, f32[16,1536]{1,0:T(8,128)}, f32[1,1536]{1,0:T(1,128)}) custom-call(bf16[128,1664]{1,0:T(8,128)(2,1)} %bitcast.63, bf16[128,1664]{1,0:T(8,128)(2,1)} %bitcast.76, bf16[128,1664]{1,0:T(8,128)(2,1)} %bitcast.64, bf16[128,1664]{1,0:T(8,128)(2,1)} %bitcast.77, ...), custom_call_target="tpu_custom_call" | custom-call | flops 15399999488 | bytes 14000000 | tf_op jit(solution)/shard_map/before_attn/pallas_call | solution.py:707
  326.8 4.2 all-to-all-start.2
  331.1 7.1 %wout_grad.1 = (bf16[4,2,48,1536]{3,2,1,0:T(8,128)(2,1)}, bf16[4,2,48,1536]{3,2,1,0:T(8,128)(2,1)}, bf16[4,2,48,1536]{3,2,1,0:T(8,128)(2,1)}, bf16[4,2,48,1536]{3,2,1,0:T(8,128)(2,1)}) custom-call(s32[2,8]{1,0:T(2,128)} %select_bitcast_fusion.slot_ref, bf16[1536,256]{1,0:T(8,128)(2,1)} %bitcast.70, bf16[256,1536]{1,0:T(8,128)(2,1)} %get-tuple-element.249.d_branch), custom_call_target="tpu_custom_call" | custom-call | flops 6600000000 | bytes 6000000 | tf_op jit(solution)/shard_map/wout_grad/pallas_call | solution.py:707
  338.2 2.3 fold.10
  344.0 1.9 collective-permute-start.42
  354.5 24.7 %attn_bwd.1 = (bf16[8,192,256]{2,1,0:T(8,128)(2,1)S(1)}, bf16[8,64,256]{2,1,0:T(8,128)(2,1)S(1)}, bf16[8,64,256]{2,1,0:T(8,128)(2,1)S(1)}) custom-call(bf16[8,192,256]{2,1,0:T(8,128)(2,1)S(1)} %copy-done.37, bf16[8,192,256]{2,1,0:T(8,128)(2,1)} %all-to-all-done.2.dot_, f32[8,192,256]{2,1,0:T(8,128)S(1)} %copy-done.42, f32[8,1,768]{2,1,0:T(1,128)S(1)} %copy-done.43, ...), custom_call_target="tpu_custom_call" | custom-call | flops 44000002048 | bytes 40000000 | tf_op jit(solution)/shard_map/attn_bwd/pallas_call | solution.py:707
  380.6 2.9 copy-done.33
  383.5 4.0 qkv_grads.1
  387.5 7.6 %collective-permute-done.40.refs_1_.refs_3_ = bf16[2,2,48,1536]{3,2,1,0:T(8,128)(2,1)S(1)} collective-permute-done((bf16[2,2,48,1536]{3,2,1,0:T(8,128)(2,1)S(1)}, bf16[2,2,48,1536]{3,2,1,0:T(8,128)(2,1)S(1)}, u32[]{:S(2)}, u32[]{:S(2)}) %collective-permute-start.40) | collective-permute-done | bytes 589856 | tf_op jit(solution)/shard_map/ppermute | solution.py:67
  399.4 6.8 %qkv_back.1 = (bf16[4,128,1536]{2,1,0:T(8,128)(2,1)S(1)}, bf16[4,128,1536]{2,1,0:T(8,128)(2,1)S(1)}, bf16[4,128,1536]{2,1,0:T(8,128)(2,1)S(1)}, bf16[4,128,1536]{2,1,0:T(8,128)(2,1)S(1)}) custom-call(s32[2,8]{1,0:T(2,128)S(1)} %copy-done.9, bf16[8,192,256]{2,1,0:T(8,128)(2,1)S(1)} %get-tuple-element.292.dq.dqa.dqb, ...), custom_call_target="tpu_custom_call" | custom-call | flops 22000001024 | bytes 20000000 | tf_op jit(solution)/shard_map/qkv_back/pallas_call | solution.py:707
  413.7 2.2 collective-permute-done.49.refs_5_.refs_7_
  416.0 2.3 fold.14
  429.1 12.5 %collective-permute-done.50.refs_1_.refs_3_ = bf16[2,128,1536]{2,1,0:T(8,128)(2,1)S(1)} collective-permute-done((bf16[2,128,1536]{2,1,0:T(8,128)(2,1)}, bf16[2,128,1536]{2,1,0:T(8,128)(2,1)S(1)}, u32[]{:S(2)}, u32[]{:S(2)}) %collective-permute-start.50) | collective-permute-done | bytes 786464 | tf_op jit(solution)/shard_map/ppermute | solution.py:67
  445.3 2.3 slice_bitcast_fusion
  450.5 3.7 all-to-all-start.3
  455.6 2.0 last.1
  457.6 3.9 all-to-all-done.3.given
  (301 shorter events, 112.5 us)
Async XLA Ops:
  9.2 13.6 %all-to-all-start = ((bf16[8,64,384]{2,1,0:T(8,128)(2,1)}), bf16[8,64,384]{2,1,0:T(8,128)(2,1)S(1)}, u32[]{:S(2)}, u32[]{:S(2)}) async-start(bf16[8,64,384]{2,1,0:T(8,128)(2,1)} %prep.1), calls=%async_computation | async-start | bytes 786432 | tf_op jit(solution)/shard_map/all_to_all | solution.py:777
  14.5 170.2 %all-gather.5.cloned.1.call-start = ((), (), s32[]{:S(2)}) async-start(), calls=%async_computation.10 | async-start | bytes 5898240 | tf_op jit(solution)/shard_map/all_gather | solution.py:821
  24.1 11.7 %collective-permute-start.3 = (bf16[1,128,1536]{2,1,0:T(8,128)(2,1)S(1)}, bf16[1,128,1536]{2,1,0:T(8,128)(2,1)S(1)}, u32[]{:S(2)}, u32[]{:S(2)}) collective-permute-start(bf16[1,128,1536]{2,1,0:T(8,128)(2,1)S(1)} %get-tuple-element.339), channel_id=1, source_target_pairs={{0,2},{1,3},{2,0},{3,1},{4,6},{5,7},{6,4},{7,5},{8,10},{9,11},{10,... | collective-permute-start | bytes 1179656 | tf_op jit(solution)/shard_map/ppermute | solution.py:67
  26.6 13.0 %collective-permute-start.9 = (bf16[530,384]{1,0:T(8,128)(2,1)}, bf16[530,384]{1,0:T(8,128)(2,1)}, u32[]{:S(2)}, u32[]{:S(2)}) collective-permute-start(bf16[530,384]{1,0:T(8,128)(2,1)} %pack.1.refs_3_), channel_id=1, source_target_pairs={{8,0},{16,8},{24,16},{9,1},{17,9},{25,17},{10,2},{18,10},{26,18},{... | collective-permute-start | bytes 1221128 | tf_op jit(solution)/shard_map/ppermute | solution.py:789
  28.0 12.9 %collective-permute-start.6 = (bf16[530,384]{1,0:T(8,128)(2,1)}, bf16[530,384]{1,0:T(8,128)(2,1)}, u32[]{:S(2)}, u32[]{:S(2)}) collective-permute-start(bf16[530,384]{1,0:T(8,128)(2,1)} %pack.1.refs_3_), channel_id=1, source_target_pairs={{0,8},{8,16},{16,24},{1,9},{9,17},{17,25},{2,10},{10,18},{18,26},{... | collective-permute-start | bytes 1221128 | tf_op jit(solution)/shard_map/ppermute | solution.py:789
  34.3 25.0 %collective-permute-start.1 = (bf16[2,128,1536]{2,1,0:T(8,128)(2,1)}, bf16[2,128,1536]{2,1,0:T(8,128)(2,1)}, u32[]{:S(2)}, u32[]{:S(2)}) collective-permute-start(bf16[2,128,1536]{2,1,0:T(8,128)(2,1)} %pad_maximum_fusion.4), channel_id=1, source_target_pairs={{0,2},{1,3},{2,0},{3,1},{4,6},{5,7},{6,4},{7,5},{8,10},{9,11},{10,... | collective-permute-start | bytes 2359304 | tf_op jit(solution)/shard_map/ppermute | solution.py:67
  36.8 23.9 %collective-permute-start.4 = (bf16[2,128,1536]{2,1,0:T(8,128)(2,1)}, bf16[2,128,1536]{2,1,0:T(8,128)(2,1)}, u32[]{:S(2)}, u32[]{:S(2)}) collective-permute-start(bf16[2,128,1536]{2,1,0:T(8,128)(2,1)} %pad_maximum_fusion.5), channel_id=1, source_target_pairs={{0,4},{1,5},{2,6},{3,7},{4,0},{5,1},{6,2},{7,3},{8,12},{9,13},{10,... | collective-permute-start | bytes 2359304 | tf_op jit(solution)/shard_map/ppermute | solution.py:67
  39.6 12.0 %collective-permute-start.10 = (bf16[530,384]{1,0:T(8,128)(2,1)}, bf16[530,384]{1,0:T(8,128)(2,1)}, u32[]{:S(2)}, u32[]{:S(2)}) collective-permute-start(bf16[530,384]{1,0:T(8,128)(2,1)} %collective-permute-done.9.refs_4_), channel_id=1, source_target_pairs={{8,0},{16,8},{24,16},{9,1},{17,9},{25,17},{10,2},{18,10},{26,18},{... | collective-permute-start | bytes 1221128 | tf_op jit(solution)/shard_map/ppermute | solution.py:789
  40.9 11.9 %collective-permute-start.7 = (bf16[530,384]{1,0:T(8,128)(2,1)}, bf16[530,384]{1,0:T(8,128)(2,1)}, u32[]{:S(2)}, u32[]{:S(2)}) collective-permute-start(bf16[530,384]{1,0:T(8,128)(2,1)} %collective-permute-done.6.refs_2_), channel_id=1, source_target_pairs={{0,8},{8,16},{16,24},{1,9},{9,17},{17,25},{2,10},{10,18},{18,26},{... | collective-permute-start | bytes 1221128 | tf_op jit(solution)/shard_map/ppermute | solution.py:789
  52.9 182.2 %all-gather.7.cloned.1.call-start = ((), (), s32[]{:S(2)}) async-start(), calls=%async_computation.11 | async-start | bytes 5898240 | tf_op jit(solution)/shard_map/all_gather | solution.py:821
  52.9 11.4 %collective-permute-start.11 = (bf16[530,384]{1,0:T(8,128)(2,1)}, bf16[530,384]{1,0:T(8,128)(2,1)S(1)}, u32[]{:S(2)}, u32[]{:S(2)}) collective-permute-start(bf16[530,384]{1,0:T(8,128)(2,1)} %collective-permute-done.10.refs_5_), channel_id=1, source_target_pairs={{8,0},{16,8},{24,16},{9,1},{17,9},{25,17},{10,2},{18,10},{26,18},{... | collective-permute-start | bytes 1221128 | tf_op jit(solution)/shard_map/ppermute | solution.py:789
  54.2 13.7 %collective-permute-start.8 = (bf16[530,384]{1,0:T(8,128)(2,1)}, bf16[530,384]{1,0:T(8,128)(2,1)S(1)}, u32[]{:S(2)}, u32[]{:S(2)}) collective-permute-start(bf16[530,384]{1,0:T(8,128)(2,1)} %collective-permute-done.7.refs_1_), channel_id=1, source_target_pairs={{0,8},{8,16},{16,24},{1,9},{9,17},{17,25},{2,10},{10,18},{18,26},{... | collective-permute-start | bytes 1221128 | tf_op jit(solution)/shard_map/ppermute | solution.py:789
  60.6 16.6 %collective-permute-start.2 = (bf16[4,128,1536]{2,1,0:T(8,128)(2,1)S(1)}, bf16[4,128,1536]{2,1,0:T(8,128)(2,1)}, u32[]{:S(2)}, u32[]{:S(2)}) collective-permute-start(bf16[4,128,1536]{2,1,0:T(8,128)(2,1)S(1)} %pad_maximum_fusion.xa), channel_id=1, source_target_pairs={{0,1},{1,0},{2,3},{3,2},{4,5},{5,4},{6,7},{7,6},{8,9},{9,8},{10,11... | collective-permute-start | bytes 4718600 | tf_op jit(solution)/shard_map/ppermute | solution.py:67
  62.7 14.5 %collective-permute-start.5 = (bf16[4,128,1536]{2,1,0:T(8,128)(2,1)S(1)}, bf16[4,128,1536]{2,1,0:T(8,128)(2,1)}, u32[]{:S(2)}, u32[]{:S(2)}) collective-permute-start(bf16[4,128,1536]{2,1,0:T(8,128)(2,1)S(1)} %pad_maximum_fusion.1.xb), channel_id=1, source_target_pairs={{0,1},{1,0},{2,3},{3,2},{4,5},{5,4},{6,7},{7,6},{8,9},{9,8},{10,11... | collective-permute-start | bytes 4718600 | tf_op jit(solution)/shard_map/ppermute | solution.py:67
  62.8 12.0 %collective-permute-start.13 = (bf16[1,128,1536]{2,1,0:T(8,128)(2,1)S(1)}, bf16[1,128,1536]{2,1,0:T(8,128)(2,1)S(1)}, u32[]{:S(2)}, u32[]{:S(2)}) collective-permute-start(bf16[1,128,1536]{2,1,0:T(8,128)(2,1)S(1)} %get-tuple-element.182), channel_id=1, source_target_pairs={{0,2},{1,3},{2,0},{3,1},{4,6},{5,7},{6,4},{7,5},{8,10},{9,11},{10,... | collective-permute-start | bytes 1179656 | tf_op jit(solution)/shard_map/ppermute | solution.py:67
  64.3 12.8 %collective-permute-start.12 = (bf16[1,128,1536]{2,1,0:T(8,128)(2,1)S(1)}, bf16[1,128,1536]{2,1,0:T(8,128)(2,1)S(1)}, u32[]{:S(2)}, u32[]{:S(2)}) collective-permute-start(bf16[1,128,1536]{2,1,0:T(8,128)(2,1)S(1)} %get-tuple-element.180), channel_id=1, source_target_pairs={{0,4},{1,5},{2,6},{3,7},{4,0},{5,1},{6,2},{7,3},{8,12},{9,13},{10,... | collective-permute-start | bytes 1179656 | tf_op jit(solution)/shard_map/ppermute | solution.py:67
  72.8 16.6 %collective-permute-start.15 = (bf16[1,2,48,1536]{3,2,1,0:T(8,128)(2,1)S(1)}, bf16[1,2,48,1536]{3,2,1,0:T(8,128)(2,1)S(1)}, u32[]{:S(2)}, u32[]{:S(2)}) collective-permute-start(bf16[1,2,48,1536]{3,2,1,0:T(8,128)(2,1)S(1)} %get-tuple-element.186), channel_id=1, source_target_pairs={{0,2},{1,3},{2,0},{3,1},{4,6},{5,7},{6,4},{7,5},{8,10},{9,11},{10,... | collective-permute-start | bytes 884744 | tf_op jit(solution)/shard_map/ppermute | solution.py:67
  74.8 14.6 %collective-permute-start.14 = (bf16[1,2,48,1536]{3,2,1,0:T(8,128)(2,1)S(1)}, bf16[1,2,48,1536]{3,2,1,0:T(8,128)(2,1)S(1)}, u32[]{:S(2)}, u32[]{:S(2)}) collective-permute-start(bf16[1,2,48,1536]{3,2,1,0:T(8,128)(2,1)S(1)} %get-tuple-element.184), channel_id=1, source_target_pairs={{0,4},{1,5},{2,6},{3,7},{4,0},{5,1},{6,2},{7,3},{8,12},{9,13},{10,... | collective-permute-start | bytes 884744 | tf_op jit(solution)/shard_map/ppermute | solution.py:67
  91.0 28.4 %collective-permute-start.18 = (bf16[2,2,48,1536]{3,2,1,0:T(8,128)(2,1)}, bf16[2,2,48,1536]{3,2,1,0:T(8,128)(2,1)S(1)}, u32[]{:S(2)}, u32[]{:S(2)}) collective-permute-start(bf16[2,2,48,1536]{3,2,1,0:T(8,128)(2,1)} %get-tuple-element.356), channel_id=1, source_target_pairs={{0,2},{1,3},{2,0},{3,1},{4,6},{5,7},{6,4},{7,5},{8,10},{9,11},{10,... | collective-permute-start | bytes 1769480 | tf_op jit(solution)/shard_map/ppermute | solution.py:67
  94.1 25.2 %collective-permute-start.19 = (bf16[2,2,48,1536]{3,2,1,0:T(8,128)(2,1)S(1)}, bf16[2,2,48,1536]{3,2,1,0:T(8,128)(2,1)S(1)}, u32[]{:S(2)}, u32[]{:S(2)}) collective-permute-start(bf16[2,2,48,1536]{3,2,1,0:T(8,128)(2,1)S(1)} %get-tuple-element.352), channel_id=1, source_target_pairs={{0,4},{1,5},{2,6},{3,7},{4,0},{5,1},{6,2},{7,3},{8,12},{9,13},{10,... | collective-permute-start | bytes 1769480 | tf_op jit(solution)/shard_map/ppermute | solution.py:67
  94.6 27.5 %collective-permute-start.16 = (bf16[2,128,1536]{2,1,0:T(8,128)(2,1)S(1)}, bf16[2,128,1536]{2,1,0:T(8,128)(2,1)S(1)}, u32[]{:S(2)}, u32[]{:S(2)}) collective-permute-start(bf16[2,128,1536]{2,1,0:T(8,128)(2,1)S(1)} %get-tuple-element.348), channel_id=1, source_target_pairs={{0,2},{1,3},{2,0},{3,1},{4,6},{5,7},{6,4},{7,5},{8,10},{9,11},{10,... | collective-permute-start | bytes 2359304 | tf_op jit(solution)/shard_map/ppermute | solution.py:67
  96.7 26.6 %collective-permute-start.17 = (bf16[2,128,1536]{2,1,0:T(8,128)(2,1)S(1)}, bf16[2,128,1536]{2,1,0:T(8,128)(2,1)S(1)}, u32[]{:S(2)}, u32[]{:S(2)}) collective-permute-start(bf16[2,128,1536]{2,1,0:T(8,128)(2,1)S(1)} %get-tuple-element.344), channel_id=1, source_target_pairs={{0,4},{1,5},{2,6},{3,7},{4,0},{5,1},{6,2},{7,3},{8,12},{9,13},{10,... | collective-permute-start | bytes 2359304 | tf_op jit(solution)/shard_map/ppermute | solution.py:67
  125.5 16.1 %all-to-all-start.1 = ((bf16[8,192,256]{2,1,0:T(8,128)(2,1)}), bf16[8,192,256]{2,1,0:T(8,128)(2,1)S(1)}, u32[]{:S(2)}, u32[]{:S(2)}) async-start(bf16[8,192,256]{2,1,0:T(8,128)(2,1)} %get-tuple-element.192), calls=%async_computation.1 | async-start | bytes 1572864 | tf_op jit(solution)/shard_map/all_to_all | solution.py:892
  129.1 214.9 %reduce-scatter.4.cloned.1.call-start = ((), (), s32[]{:S(2)}) async-start(), calls=%async_computation.7 | async-start | bytes 5898240 | tf_op jit(solution)/shard_map/reduce_scatter | solution.py:991
  130.3 50.1 %collective-permute-start.28 = (bf16[4,128,1536]{2,1,0:T(8,128)(2,1)}, bf16[4,128,1536]{2,1,0:T(8,128)(2,1)}, u32[]{:S(2)}, u32[]{:S(2)}) collective-permute-start(bf16[4,128,1536]{2,1,0:T(8,128)(2,1)} %constant_dynamic-update-slice_fusion.20.refs_4_), channel_id=1, source_target_pairs={{0,1},{1,0},{2,3},{3,2},{4,5},{5,4},{6,7},{7,6},{8,9},{9,8},{10,11... | collective-permute-start | bytes 4718600 | tf_op jit(solution)/shard_map/ppermute | solution.py:67
  131.6 48.8 %collective-permute-start.29 = (bf16[4,128,1536]{2,1,0:T(8,128)(2,1)}, bf16[4,128,1536]{2,1,0:T(8,128)(2,1)}, u32[]{:S(2)}, u32[]{:S(2)}) collective-permute-start(bf16[4,128,1536]{2,1,0:T(8,128)(2,1)} %constant_dynamic-update-slice_fusion.23.refs_6_), channel_id=1, source_target_pairs={{0,1},{1,0},{2,3},{3,2},{4,5},{5,4},{6,7},{7,6},{8,9},{9,8},{10,11... | collective-permute-start | bytes 4718600 | tf_op jit(solution)/shard_map/ppermute | solution.py:67
  148.3 11.7 %collective-permute-start.22 = (bf16[1,128,1536]{2,1,0:T(8,128)(2,1)}, bf16[1,128,1536]{2,1,0:T(8,128)(2,1)S(1)}, u32[]{:S(2)}, u32[]{:S(2)}) collective-permute-start(bf16[1,128,1536]{2,1,0:T(8,128)(2,1)} %get-tuple-element.196.ma), channel_id=1, source_target_pairs={{0,4},{1,5},{2,6},{3,7},{4,0},{5,1},{6,2},{7,3},{8,12},{9,13},{10,... | collective-permute-start | bytes 1179656 | tf_op jit(solution)/shard_map/ppermute | solution.py:67
  160.1 18.7 %collective-permute-start.26 = (bf16[2,128,1536]{2,1,0:T(8,128)(2,1)S(1)}, bf16[2,128,1536]{2,1,0:T(8,128)(2,1)S(1)}, u32[]{:S(2)}, u32[]{:S(2)}) collective-permute-start(bf16[2,128,1536]{2,1,0:T(8,128)(2,1)S(1)} %pad_maximum_fusion.7), channel_id=1, source_target_pairs={{0,4},{1,5},{2,6},{3,7},{4,0},{5,1},{6,2},{7,3},{8,12},{9,13},{10,... | collective-permute-start | bytes 2359304 | tf_op jit(solution)/shard_map/ppermute | solution.py:67
  160.5 18.7 %collective-permute-start.24 = (bf16[2,128,1536]{2,1,0:T(8,128)(2,1)S(1)}, bf16[2,128,1536]{2,1,0:T(8,128)(2,1)S(1)}, u32[]{:S(2)}, u32[]{:S(2)}) collective-permute-start(bf16[2,128,1536]{2,1,0:T(8,128)(2,1)S(1)} %pad_maximum_fusion.6), channel_id=1, source_target_pairs={{0,2},{1,3},{2,0},{3,1},{4,6},{5,7},{6,4},{7,5},{8,10},{9,11},{10,... | collective-permute-start | bytes 2359304 | tf_op jit(solution)/shard_map/ppermute | solution.py:67
  230.3 191.5 %reduce-scatter.6.cloned.1.call-start = ((), (), s32[]{:S(2)}) async-start(), calls=%async_computation.8 | async-start | bytes 5898240 | tf_op jit(solution)/shard_map/reduce_scatter | solution.py:991
  278.2 21.4 %collective-permute-start.32 = (bf16[2,128,1664]{2,1,0:T(8,128)(2,1)}, bf16[2,128,1664]{2,1,0:T(8,128)(2,1)S(1)}, u32[]{:S(2)}, u32[]{:S(2)}) collective-permute-start(bf16[2,128,1664]{2,1,0:T(8,128)(2,1)} %get-tuple-element.220), channel_id=1, source_target_pairs={{0,2},{1,3},{2,0},{3,1},{4,6},{5,7},{6,4},{7,5},{8,10},{9,11},{10,... | collective-permute-start | bytes 2555912 | tf_op jit(solution)/shard_map/ppermute | solution.py:67
  279.7 20.8 %collective-permute-start.33 = (bf16[2,128,1664]{2,1,0:T(8,128)(2,1)S(1)}, bf16[2,128,1664]{2,1,0:T(8,128)(2,1)}, u32[]{:S(2)}, u32[]{:S(2)}) collective-permute-start(bf16[2,128,1664]{2,1,0:T(8,128)(2,1)S(1)} %get-tuple-element.221), channel_id=1, source_target_pairs={{0,4},{1,5},{2,6},{3,7},{4,0},{5,1},{6,2},{7,3},{8,12},{9,13},{10,... | collective-permute-start | bytes 2555912 | tf_op jit(solution)/shard_map/ppermute | solution.py:67
  303.9 14.0 %collective-permute-start.36 = (bf16[1,128,1664]{2,1,0:T(8,128)(2,1)S(1)}, bf16[1,128,1664]{2,1,0:T(8,128)(2,1)S(1)}, u32[]{:S(2)}, u32[]{:S(2)}) collective-permute-start(bf16[1,128,1664]{2,1,0:T(8,128)(2,1)S(1)} %get-tuple-element.237), channel_id=1, source_target_pairs={{0,4},{1,5},{2,6},{3,7},{4,0},{5,1},{6,2},{7,3},{8,12},{9,13},{10,... | collective-permute-start | bytes 1277960 | tf_op jit(solution)/shard_map/ppermute | solution.py:67
  305.1 12.8 %collective-permute-start.37 = (bf16[1,128,1664]{2,1,0:T(8,128)(2,1)S(1)}, bf16[1,128,1664]{2,1,0:T(8,128)(2,1)S(1)}, u32[]{:S(2)}, u32[]{:S(2)}) collective-permute-start(bf16[1,128,1664]{2,1,0:T(8,128)(2,1)S(1)} %get-tuple-element.238), channel_id=1, source_target_pairs={{0,2},{1,3},{2,0},{3,1},{4,6},{5,7},{6,4},{7,5},{8,10},{9,11},{10,... | collective-permute-start | bytes 1277960 | tf_op jit(solution)/shard_map/ppermute | solution.py:67
  317.4 20.8 %collective-permute-start.34 = (bf16[4,128,1536]{2,1,0:T(8,128)(2,1)}, bf16[4,128,1536]{2,1,0:T(8,128)(2,1)}, u32[]{:S(2)}, u32[]{:S(2)}) collective-permute-start(bf16[4,128,1536]{2,1,0:T(8,128)(2,1)} %get-tuple-element.230), channel_id=1, source_target_pairs={{0,1},{1,0},{2,3},{3,2},{4,5},{5,4},{6,7},{7,6},{8,9},{9,8},{10,11... | collective-permute-start | bytes 4718600 | tf_op jit(solution)/shard_map/ppermute | solution.py:67
  317.4 20.8 %collective-permute-start.35 = (bf16[4,128,1536]{2,1,0:T(8,128)(2,1)}, bf16[4,128,1536]{2,1,0:T(8,128)(2,1)}, u32[]{:S(2)}, u32[]{:S(2)}) collective-permute-start(bf16[4,128,1536]{2,1,0:T(8,128)(2,1)} %get-tuple-element.232), channel_id=1, source_target_pairs={{0,1},{1,0},{2,3},{3,2},{4,5},{5,4},{6,7},{7,6},{8,9},{9,8},{10,11... | collective-permute-start | bytes 4718600 | tf_op jit(solution)/shard_map/ppermute | solution.py:67
  326.8 17.3 %all-to-all-start.2 = ((bf16[8,192,256]{2,1,0:T(8,128)(2,1)}), bf16[8,192,256]{2,1,0:T(8,128)(2,1)}, u32[]{:S(2)}, u32[]{:S(2)}) async-start(bf16[8,192,256]{2,1,0:T(8,128)(2,1)} %bitcast.71), calls=%async_computation.2 | async-start | bytes 1572864 | tf_op jit(solution)/shard_map/all_to_all | solution.py:1026
  331.0 117.6 %reduce-scatter.8.cloned.1.call-start = ((), (), s32[]{:S(2)}) async-start(), calls=%async_computation.9 | async-start | bytes 2088960 | tf_op jit(solution)/shard_map/reduce_scatter | solution.py:1132
  344.0 43.5 %collective-permute-start.42 = (bf16[2,128,1536]{2,1,0:T(8,128)(2,1)}, bf16[2,128,1536]{2,1,0:T(8,128)(2,1)S(1)}, u32[]{:S(2)}, u32[]{:S(2)}) collective-permute-start(bf16[2,128,1536]{2,1,0:T(8,128)(2,1)} %copy-done.17), channel_id=1, source_target_pairs={{0,2},{1,3},{2,0},{3,1},{4,6},{5,7},{6,4},{7,5},{8,10},{9,11},{10,... | collective-permute-start | bytes 2359304 | tf_op jit(solution)/shard_map/ppermute | solution.py:67
  345.9 41.6 %collective-permute-start.43 = (bf16[2,128,1536]{2,1,0:T(8,128)(2,1)}, bf16[2,128,1536]{2,1,0:T(8,128)(2,1)S(1)}, u32[]{:S(2)}, u32[]{:S(2)}) collective-permute-start(bf16[2,128,1536]{2,1,0:T(8,128)(2,1)} %copy-done.16), channel_id=1, source_target_pairs={{0,4},{1,5},{2,6},{3,7},{4,0},{5,1},{6,2},{7,3},{8,12},{9,13},{10,... | collective-permute-start | bytes 2359304 | tf_op jit(solution)/shard_map/ppermute | solution.py:67
  347.4 31.8 %collective-permute-start.38 = (bf16[4,2,48,1536]{3,2,1,0:T(8,128)(2,1)}, bf16[4,2,48,1536]{3,2,1,0:T(8,128)(2,1)S(1)}, u32[]{:S(2)}, u32[]{:S(2)}) collective-permute-start(bf16[4,2,48,1536]{3,2,1,0:T(8,128)(2,1)} %get-tuple-element.256), channel_id=1, source_target_pairs={{0,1},{1,0},{2,3},{3,2},{4,5},{5,4},{6,7},{7,6},{8,9},{9,8},{10,11... | collective-permute-start | bytes 3538952 | tf_op jit(solution)/shard_map/ppermute | solution.py:67
  347.4 31.8 %collective-permute-start.39 = (bf16[4,2,48,1536]{3,2,1,0:T(8,128)(2,1)}, bf16[4,2,48,1536]{3,2,1,0:T(8,128)(2,1)S(1)}, u32[]{:S(2)}, u32[]{:S(2)}) collective-permute-start(bf16[4,2,48,1536]{3,2,1,0:T(8,128)(2,1)} %get-tuple-element.257), channel_id=1, source_target_pairs={{0,1},{1,0},{2,3},{3,2},{4,5},{5,4},{6,7},{7,6},{8,9},{9,8},{10,11... | collective-permute-start | bytes 3538952 | tf_op jit(solution)/shard_map/ppermute | solution.py:67
  379.8 15.3 %collective-permute-start.40 = (bf16[2,2,48,1536]{3,2,1,0:T(8,128)(2,1)S(1)}, bf16[2,2,48,1536]{3,2,1,0:T(8,128)(2,1)S(1)}, u32[]{:S(2)}, u32[]{:S(2)}) collective-permute-start(bf16[2,2,48,1536]{3,2,1,0:T(8,128)(2,1)S(1)} %get-tuple-element.266), channel_id=1, source_target_pairs={{0,2},{1,3},{2,0},{3,1},{4,6},{5,7},{6,4},{7,5},{8,10},{9,11},{10,... | collective-permute-start | bytes 1769480 | tf_op jit(solution)/shard_map/ppermute | solution.py:67
  380.5 14.9 %collective-permute-start.41 = (bf16[2,2,48,1536]{3,2,1,0:T(8,128)(2,1)S(1)}, bf16[2,2,48,1536]{3,2,1,0:T(8,128)(2,1)S(1)}, u32[]{:S(2)}, u32[]{:S(2)}) collective-permute-start(bf16[2,2,48,1536]{3,2,1,0:T(8,128)(2,1)S(1)} %get-tuple-element.267), channel_id=1, source_target_pairs={{0,4},{1,5},{2,6},{3,7},{4,0},{5,1},{6,2},{7,3},{8,12},{9,13},{10,... | collective-permute-start | bytes 1769480 | tf_op jit(solution)/shard_map/ppermute | solution.py:67
  410.5 11.4 %collective-permute-start.44 = (bf16[1,128,1536]{2,1,0:T(8,128)(2,1)}, bf16[1,128,1536]{2,1,0:T(8,128)(2,1)}, u32[]{:S(2)}, u32[]{:S(2)}) collective-permute-start(bf16[1,128,1536]{2,1,0:T(8,128)(2,1)} %copy-done.26), channel_id=1, source_target_pairs={{0,4},{1,5},{2,6},{3,7},{4,0},{5,1},{6,2},{7,3},{8,12},{9,13},{10,... | collective-permute-start | bytes 1179656 | tf_op jit(solution)/shard_map/ppermute | solution.py:67
  423.1 18.5 %collective-permute-start.50 = (bf16[2,128,1536]{2,1,0:T(8,128)(2,1)}, bf16[2,128,1536]{2,1,0:T(8,128)(2,1)S(1)}, u32[]{:S(2)}, u32[]{:S(2)}) collective-permute-start(bf16[2,128,1536]{2,1,0:T(8,128)(2,1)} %copy-done.23), channel_id=1, source_target_pairs={{0,2},{1,3},{2,0},{3,1},{4,6},{5,7},{6,4},{7,5},{8,10},{9,11},{10,... | collective-permute-start | bytes 2359304 | tf_op jit(solution)/shard_map/ppermute | solution.py:67
  423.7 18.2 %collective-permute-start.51 = (bf16[2,128,1536]{2,1,0:T(8,128)(2,1)}, bf16[2,128,1536]{2,1,0:T(8,128)(2,1)S(1)}, u32[]{:S(2)}, u32[]{:S(2)}) collective-permute-start(bf16[2,128,1536]{2,1,0:T(8,128)(2,1)} %copy-done.22), channel_id=1, source_target_pairs={{0,4},{1,5},{2,6},{3,7},{4,0},{5,1},{6,2},{7,3},{8,12},{9,13},{10,... | collective-permute-start | bytes 2359304 | tf_op jit(solution)/shard_map/ppermute | solution.py:67
  442.3 11.9 %collective-permute-start.52 = (bf16[1,128,1536]{2,1,0:T(8,128)(2,1)S(1)}, bf16[1,128,1536]{2,1,0:T(8,128)(2,1)S(1)}, u32[]{:S(2)}, u32[]{:S(2)}) collective-permute-start(bf16[1,128,1536]{2,1,0:T(8,128)(2,1)S(1)} %get-tuple-element.315), channel_id=1, source_target_pairs={{0,4},{1,5},{2,6},{3,7},{4,0},{5,1},{6,2},{7,3},{8,12},{9,13},{10,... | collective-permute-start | bytes 1179656 | tf_op jit(solution)/shard_map/ppermute | solution.py:67
  (85 other events, 454.1 us)
Sparse Core Ops, SparseCore 0:
  53.0 91.8 all-gather.4
  146.4 88.5 all-gather.6
  237.4 83.6 reduce-scatter.3
  323.2 85.7 reduce-scatter.5
  411.2 37.3 reduce-scatter.7

commit v6 on v5

--- a/solution.py
+++ b/solution.py
@@ -1103,8 +1103,7 @@
         (dq, wout.keep, wout.got, mix.keep, mix.got), gw
     )
     wout.step()
-    mix.step()
-    dq = after(dq, wout.keep, mix.keep)
+    dq = after(dq, wout.keep)
     d_in = call(
         functools.partial(qkv_back_kernel, 1.0 / copies, far),
         "qkv_back",
@@ -1154,6 +1153,9 @@
     )
 
     back_in = Scatter(after(d_in, bundle), n)
+    mix.keep, mix.got = after((mix.keep, mix.got), bundle)
+    mix.step()
+    back_in.got = after(back_in.got, mix.keep)
     back_in.step()
     expert_grads, mix.got = after((expert_grads, mix.got), back_in.keep)
     (c0, c1), (e0, e1) = back_in.run()

time: 478 us -> 481 us (level)
    unnamed x151 -> x155, local copies, waits for them, and re-layouts: 37.5 us -> 41.5 us
  transfers between devices with their start and end apart: 63 -> 63, of which waited for: 29 -> 26; matrix products, arithmetic and copies ran while one was open for 6% -> 6% of each run, Pallas kernels for 49% -> 49%
where the time goes in v6:
time: 481 us; the launch traced here: 473 us
  Pallas kernels  233 us (48%)
  waiting for transfers between devices  82.6 us (17%)
  starting transfers between devices  73.4 us (15%)
  local copies, waits for them, and re-layouts  54.6 us (11%)
  between operations  15.1 us (3%)
  other arithmetic  14.2 us (3%)
    pallas_call x21, Pallas kernels, call(): pl.pallas_call(kernel, grid_spec=pltpu.PrefetchScalarGridSpec(num_scalar_...  223 us
    ppermute x48, waiting for transfers between devices, swap(): return lax.ppermute(value, 'ctx', [(i, i ^ bit) for i in range(count)])  59.6 us
    unnamed x155, local copies, waits for them, and re-layouts  41.5 us
    ppermute x48, starting transfers between devices, swap(): return lax.ppermute(value, 'ctx', [(i, i ^ bit) for i in range(count)])  36.7 us
    ppermute x6, starting transfers between devices, along(): return lax.ppermute(value, 'dp', pairs)  19.7 us
    pallas_call x8, Pallas kernels, fold(): pl.pallas_call(fold_kernel, grid=(half,), in_specs=[near, near, far, far]...  10.3 us
  transfers between devices with their start and end apart: 63, of which 26 were waited for; matrix products, arithmetic and copies ran while one was open for 6% of the time, Pallas kernels for 49%

profile of v6, /device:TPU:0, one launch (start us, length us, event | category | flops | bytes accessed | tf_op | source)
XLA Modules:
  0.0 473.1 jit_solution(9412936158078083290)
XLA Ops:
  7.2 2.0 prep.1
  9.2 5.3 %all-to-all-start = ((bf16[8,64,384]{2,1,0:T(8,128)(2,1)}), bf16[8,64,384]{2,1,0:T(8,128)(2,1)S(1)}, u32[]{:S(2)}, u32[]{:S(2)}) async-start(bf16[8,64,384]{2,1,0:T(8,128)(2,1)} %prep.1), calls=%async_computation | async-start | bytes 786432 | tf_op jit(solution)/shard_map/all_to_all | solution.py:777
  17.3 5.6 %all-to-all-done.took.table = bf16[8,64,384]{2,1,0:T(8,128)(2,1)S(1)} async-done(((bf16[8,64,384]{2,1,0:T(8,128)(2,1)}), bf16[8,64,384]{2,1,0:T(8,128)(2,1)S(1)}, u32[]{:S(2)}, u32[]{:S(2)}) %all-to-all-start) | async-done | bytes 393248 | tf_op jit(solution)/shard_map/all_to_all | solution.py:777
  24.7 1.9 pack.1.refs_3_
  28.0 5.3 %collective-permute-start.6 = (bf16[530,384]{1,0:T(8,128)(2,1)}, bf16[530,384]{1,0:T(8,128)(2,1)}, u32[]{:S(2)}, u32[]{:S(2)}) collective-permute-start(bf16[530,384]{1,0:T(8,128)(2,1)} %pack.1.refs_3_), channel_id=1, source_target_pairs={{0,8},{8,16},{16,24},{1,9},{9,17},{17,25},{2,10},{10,18},{18,26},{... | collective-permute-start | bytes 1221128 | tf_op jit(solution)/shard_map/ppermute | solution.py:789
  41.0 5.3 %collective-permute-start.7 = (bf16[530,384]{1,0:T(8,128)(2,1)}, bf16[530,384]{1,0:T(8,128)(2,1)}, u32[]{:S(2)}, u32[]{:S(2)}) collective-permute-start(bf16[530,384]{1,0:T(8,128)(2,1)} %collective-permute-done.6.refs_2_), channel_id=1, source_target_pairs={{0,8},{8,16},{16,24},{1,9},{9,17},{17,25},{2,10},{10,18},{18,26},{... | collective-permute-start | bytes 1221128 | tf_op jit(solution)/shard_map/ppermute | solution.py:789
  49.7 1.9 collective-permute-done.10.refs_5_
  54.2 5.0 %collective-permute-start.8 = (bf16[530,384]{1,0:T(8,128)(2,1)}, bf16[530,384]{1,0:T(8,128)(2,1)S(1)}, u32[]{:S(2)}, u32[]{:S(2)}) collective-permute-start(bf16[530,384]{1,0:T(8,128)(2,1)} %collective-permute-done.7.refs_1_), channel_id=1, source_target_pairs={{0,8},{8,16},{16,24},{1,9},{9,17},{17,25},{2,10},{10,18},{18,26},{... | collective-permute-start | bytes 1221128 | tf_op jit(solution)/shard_map/ppermute | solution.py:789
  60.7 2.0 pad_maximum_fusion.1.xb
  64.4 2.1 collective-permute-start.12
  68.6 3.1 unpack.1
  74.8 2.3 collective-permute-start.14
  77.2 12.3 %qkv.1 = (bf16[8,256,1536]{2,1,0:T(8,128)(2,1)}, bf16[8,192,256]{2,1,0:T(8,128)(2,1)}, bf16[8,256,64]{2,1,0:T(8,128)(2,1)}, bf16[8,64,256]{2,1,0:T(8,128)(2,1)},...) custom-call(s32[2,8]{1,0:T(2,128)} %select_bitcast_fusion.slot_ref, bf16[4,128,1536]{2,1,0:T(8,128)(2,1)} %copy-done.46, ...), custom_call_target="tpu_custom_call" | custom-call | flops 6600000000 | bytes 6000000 | tf_op jit(solution)/shard_map/qkv/pallas_call | solution.py:707
  91.0 2.1 collective-permute-start.18
  98.4 21.0 %attn_fwd.1 = (f32[8,192,256]{2,1,0:T(8,128)}, bf16[8,192,256]{2,1,0:T(8,128)(2,1)}, f32[8,1,768]{2,1,0:T(1,128)}) custom-call(bf16[8,192,256]{2,1,0:T(8,128)(2,1)} %get-tuple-element.194.qt, bf16[8,256,64]{2,1,0:T(8,128)(2,1)} %get-tuple-element.195.k, bf16[8,64,256]{2,1,0:T(8,128)(2,1)} %get-tuple-element.196.vt), custom_call_target="tpu_custom_call" | custom-call | flops 20899999744 | bytes 19000000 | tf_op jit(solution)/shard_map/attn_fwd/pallas_call | solution.py:707
  119.4 2.7 collective-permute-done.16
  125.5 3.6 all-to-all-start.1
  131.8 8.0 %place.1 = bf16[4,8,48,1536]{3,2,1,0:T(8,128)(2,1)} custom-call(s32[2,8]{1,0:T(2,128)} %select_bitcast_fusion.slot_ref, bf16[4,2,48,1536]{3,2,1,0:T(8,128)(2,1)} %constant_dynamic-update-slice_fusion.8.a, bf16[4,2,48,1536]{3,2,1,0:T(8,128)(2,1)} %collective-permute-done.20.af, bf16[4,2,48,1536]{3,2,1,0:T(8,128)(2,1)} %constant_dynamic-update-slice_fusion.11.b, ...), custom_call_target="tpu_custom_call" | custom-call | flops 4400000000 | bytes 4000000 | tf_op jit(solution)/shard_map/place/pallas_call | solution.py:707
  142.5 5.8 %after_attn.1 = (f32[256,1536]{1,0:T(8,128)}, bf16[1,128,1536]{2,1,0:T(8,128)(2,1)}, bf16[1,128,1536]{2,1,0:T(8,128)(2,1)}) custom-call(bf16[1536,256]{1,0:T(8,128)(2,1)} %bitcast.69, bf16[1536,1536]{1,0:T(8,128)(2,1)} %bitcast.82, bf16[256,1536]{1,0:T(8,128)(2,1)} %hidden.3, f32[1,1536]{1,0:T(1,128)} %get-tuple-element.373.gain), custom_call_target="tpu_custom_call" | custom-call | flops 6600000000 | bytes 6000000 | tf_op jit(solution)/shard_map/after_attn/pallas_call | solution.py:707
  150.3 6.0 %code.1.refs_9_.refs_10_ = f32[8,256,16]{2,1,0:T(8,128)} custom-call(bf16[8,64,384]{2,1,0:T(8,128)(2,1)} %copy-done.60), custom_call_target="tpu_custom_call" | custom-call | flops 6600000000 | bytes 6000000 | tf_op jit(solution)/shard_map/code/pallas_call | solution.py:707
  158.0 2.1 collective-permute-done.23
  162.4 16.5 %collective-permute-done.26 = bf16[2,128,1536]{2,1,0:T(8,128)(2,1)S(1)} collective-permute-done((bf16[2,128,1536]{2,1,0:T(8,128)(2,1)S(1)}, bf16[2,128,1536]{2,1,0:T(8,128)(2,1)S(1)}, u32[]{:S(2)}, u32[]{:S(2)}) %collective-permute-start.26) | collective-permute-done | bytes 786464 | tf_op jit(solution)/shard_map/ppermute | solution.py:67
  180.5 2.0 collective-permute-done.27.refs_3_
  182.5 2.2 collective-permute-done.25.refs_1_
  184.8 45.6 %moe_first.1 = (bf16[4,128,1664]{2,1,0:T(8,128)(2,1)}, bf16[4,128,1664]{2,1,0:T(8,128)(2,1)}, bf16[4,128,1664]{2,1,0:T(8,128)(2,1)}, bf16[4,128,1664]{2,1,0:T(8,...) custom-call(s32[1]{0:T(128)} %bitcast.15.which, s32[2,8]{1,0:T(2,128)} %broadcast_xor_fusion.blocks.blocks_ref, ...), custom_call_target="tpu_custom_call" | custom-call | flops 41799999488 | bytes 38000000 | tf_op jit(solution)/shard_map/moe_first/pallas_call | solution.py:707
  230.6 4.4 all-gather.7.cloned.1.call-done
  235.1 32.5 %moe_second.1 = (bf16[4,128,1664]{2,1,0:T(8,128)(2,1)}, bf16[4,128,1664]{2,1,0:T(8,128)(2,1)}, bf16[4,128,1664]{2,1,0:T(8,128)(2,1)}, bf16[4,128,1664]{2,1,0:T(8...) custom-call(s32[1]{0:T(128)S(6)} %add.55.which, ...), custom_call_target="tpu_custom_call" | custom-call | flops 27499999232 | bytes 25000000 | tf_op jit(solution)/shard_map/moe_second/pallas_call | solution.py:707
  268.1 3.3 collective-permute-done.30.refs_1_.refs_3_
  271.4 2.4 collective-permute-done.31.refs_5_.refs_7_
  281.2 18.4 %moe_grads.1 = bf16[4,3,384,512]{3,2,1,0:T(8,128)(2,1)} custom-call(bf16[4,128,1536]{2,1,0:T(8,128)(2,1)} %copy-done.63, bf16[4,128,1536]{2,1,0:T(8,128)(2,1)} %collective-permute-done.25.refs_1_, bf16[4,128,1536]{2,1,0:T(8,128)(2,1)} %copy-done.62, bf16[4,128,1536]{2,1,0:T(8,128)(2,1)} %collective-permute-done.27.refs_3_, ...), custom_call_target="tpu_custom_call" | custom-call | flops 16499999744 | bytes 15000000 | tf_op jit(solution)/shard_map/moe_grads/pallas_call | solution.py:707
  305.7 11.7 %moe_out.1 = (bf16[4,128,1536]{2,1,0:T(8,128)(2,1)S(1)}, bf16[4,128,1536]{2,1,0:T(8,128)(2,1)}, bf16[4,128,1536]{2,1,0:T(8,128)(2,1)S(1)}, bf16[4,128,1536]{2,1,0:T(8,128)(2,1)}) custom-call(bf16[8,256,512]{2,1,0:T(8,128)(2,1)S(1)} %copy-done.36, bf16[8,256,512]{2,1,0:T(8,128)(2,1)S(1)} %copy-done.37, bf16[4,3,384,512]{3,2,1,0:T(8,128)(2,1)} %bitcast.73, ...), custom_call_target="tpu_custom_call" | custom-call | flops 8800000000 | bytes 8000000 | tf_op jit(solution)/shard_map/moe_out/pallas_call | solution.py:707
  318.8 7.9 %before_attn.1 = (f32[256,1536]{1,0:T(8,128)}, bf16[256,1536]{1,0:T(8,128)(2,1)}, bf16[1536,256]{1,0:T(8,128)(2,1)}, f32[16,1536]{1,0:T(8,128)}, f32[1,1536]{1,0:T(1,128)}) custom-call(bf16[128,1664]{1,0:T(8,128)(2,1)} %bitcast.63, bf16[128,1664]{1,0:T(8,128)(2,1)} %bitcast.76, bf16[128,1664]{1,0:T(8,128)(2,1)} %bitcast.64, bf16[128,1664]{1,0:T(8,128)(2,1)} %bitcast.77, ...), custom_call_target="tpu_custom_call" | custom-call | flops 15399999488 | bytes 14000000 | tf_op jit(solution)/shard_map/before_attn/pallas_call | solution.py:707
  326.8 4.2 all-to-all-start.2
  331.0 7.1 %wout_grad.1 = (bf16[4,2,48,1536]{3,2,1,0:T(8,128)(2,1)}, bf16[4,2,48,1536]{3,2,1,0:T(8,128)(2,1)}, bf16[4,2,48,1536]{3,2,1,0:T(8,128)(2,1)}, bf16[4,2,48,1536]{3,2,1,0:T(8,128)(2,1)}) custom-call(s32[2,8]{1,0:T(2,128)} %select_bitcast_fusion.slot_ref, bf16[1536,256]{1,0:T(8,128)(2,1)} %bitcast.70, bf16[256,1536]{1,0:T(8,128)(2,1)} %get-tuple-element.255.d_branch), custom_call_target="tpu_custom_call" | custom-call | flops 6600000000 | bytes 6000000 | tf_op jit(solution)/shard_map/wout_grad/pallas_call | solution.py:707
  338.2 2.3 fold.10
  344.0 1.9 collective-permute-start.42
  354.5 24.7 %attn_bwd.1 = (bf16[8,192,256]{2,1,0:T(8,128)(2,1)S(1)}, bf16[8,64,256]{2,1,0:T(8,128)(2,1)S(1)}, bf16[8,64,256]{2,1,0:T(8,128)(2,1)S(1)}) custom-call(bf16[8,192,256]{2,1,0:T(8,128)(2,1)S(1)} %copy-done.39, bf16[8,192,256]{2,1,0:T(8,128)(2,1)} %all-to-all-done.2.dot_, f32[8,192,256]{2,1,0:T(8,128)S(1)} %copy-done.44, f32[8,1,768]{2,1,0:T(1,128)S(1)} %copy-done.45, ...), custom_call_target="tpu_custom_call" | custom-call | flops 44000002048 | bytes 40000000 | tf_op jit(solution)/shard_map/attn_bwd/pallas_call | solution.py:707
  380.6 2.9 copy-done.35
  383.5 4.0 qkv_grads.1
  387.5 7.6 %collective-permute-done.40.refs_1_.refs_3_ = bf16[2,2,48,1536]{3,2,1,0:T(8,128)(2,1)S(1)} collective-permute-done((bf16[2,2,48,1536]{3,2,1,0:T(8,128)(2,1)S(1)}, bf16[2,2,48,1536]{3,2,1,0:T(8,128)(2,1)S(1)}, u32[]{:S(2)}, u32[]{:S(2)}) %collective-permute-start.40) | collective-permute-done | bytes 589856 | tf_op jit(solution)/shard_map/ppermute | solution.py:67
  397.8 6.8 %qkv_back.1 = (bf16[4,128,1536]{2,1,0:T(8,128)(2,1)S(1)}, bf16[4,128,1536]{2,1,0:T(8,128)(2,1)S(1)}, bf16[4,128,1536]{2,1,0:T(8,128)(2,1)S(1)}, bf16[4,128,1536]{2,1,0:T(8,128)(2,1)S(1)}) custom-call(s32[2,8]{1,0:T(2,128)S(1)} %copy-done.9, bf16[8,192,256]{2,1,0:T(8,128)(2,1)S(1)} %get-tuple-element.298.dq.dqa.dqb, ...), custom_call_target="tpu_custom_call" | custom-call | flops 22000001024 | bytes 20000000 | tf_op jit(solution)/shard_map/qkv_back/pallas_call | solution.py:707
  417.4 2.3 fold.14
  423.3 3.4 collective-permute-done.46
  433.9 12.5 %collective-permute-done.50.refs_1_.refs_3_ = bf16[2,128,1536]{2,1,0:T(8,128)(2,1)S(1)} collective-permute-done((bf16[2,128,1536]{2,1,0:T(8,128)(2,1)}, bf16[2,128,1536]{2,1,0:T(8,128)(2,1)S(1)}, u32[]{:S(2)}, u32[]{:S(2)}) %collective-permute-start.50) | collective-permute-done | bytes 786464 | tf_op jit(solution)/shard_map/ppermute | solution.py:67
  449.2 2.3 slice_bitcast_fusion
  453.4 3.4 all-to-all-start.3
  458.3 2.0 last.1
  460.3 3.8 all-to-all-done.3.given
  (305 shorter events, 114.4 us)
Async XLA Ops:
  9.2 13.6 %all-to-all-start = ((bf16[8,64,384]{2,1,0:T(8,128)(2,1)}), bf16[8,64,384]{2,1,0:T(8,128)(2,1)S(1)}, u32[]{:S(2)}, u32[]{:S(2)}) async-start(bf16[8,64,384]{2,1,0:T(8,128)(2,1)} %prep.1), calls=%async_computation | async-start | bytes 786432 | tf_op jit(solution)/shard_map/all_to_all | solution.py:777
  14.5 170.3 %all-gather.5.cloned.1.call-start = ((), (), s32[]{:S(2)}) async-start(), calls=%async_computation.10 | async-start | bytes 5898240 | tf_op jit(solution)/shard_map/all_gather | solution.py:821
  24.1 11.7 %collective-permute-start.3 = (bf16[1,128,1536]{2,1,0:T(8,128)(2,1)S(1)}, bf16[1,128,1536]{2,1,0:T(8,128)(2,1)S(1)}, u32[]{:S(2)}, u32[]{:S(2)}) collective-permute-start(bf16[1,128,1536]{2,1,0:T(8,128)(2,1)S(1)} %get-tuple-element.351), channel_id=1, source_target_pairs={{0,2},{1,3},{2,0},{3,1},{4,6},{5,7},{6,4},{7,5},{8,10},{9,11},{10,... | collective-permute-start | bytes 1179656 | tf_op jit(solution)/shard_map/ppermute | solution.py:67
  26.6 13.0 %collective-permute-start.9 = (bf16[530,384]{1,0:T(8,128)(2,1)}, bf16[530,384]{1,0:T(8,128)(2,1)}, u32[]{:S(2)}, u32[]{:S(2)}) collective-permute-start(bf16[530,384]{1,0:T(8,128)(2,1)} %pack.1.refs_3_), channel_id=1, source_target_pairs={{8,0},{16,8},{24,16},{9,1},{17,9},{25,17},{10,2},{18,10},{26,18},{... | collective-permute-start | bytes 1221128 | tf_op jit(solution)/shard_map/ppermute | solution.py:789
  28.0 12.9 %collective-permute-start.6 = (bf16[530,384]{1,0:T(8,128)(2,1)}, bf16[530,384]{1,0:T(8,128)(2,1)}, u32[]{:S(2)}, u32[]{:S(2)}) collective-permute-start(bf16[530,384]{1,0:T(8,128)(2,1)} %pack.1.refs_3_), channel_id=1, source_target_pairs={{0,8},{8,16},{16,24},{1,9},{9,17},{17,25},{2,10},{10,18},{18,26},{... | collective-permute-start | bytes 1221128 | tf_op jit(solution)/shard_map/ppermute | solution.py:789
  34.3 24.9 %collective-permute-start.1 = (bf16[2,128,1536]{2,1,0:T(8,128)(2,1)}, bf16[2,128,1536]{2,1,0:T(8,128)(2,1)}, u32[]{:S(2)}, u32[]{:S(2)}) collective-permute-start(bf16[2,128,1536]{2,1,0:T(8,128)(2,1)} %pad_maximum_fusion.4), channel_id=1, source_target_pairs={{0,2},{1,3},{2,0},{3,1},{4,6},{5,7},{6,4},{7,5},{8,10},{9,11},{10,... | collective-permute-start | bytes 2359304 | tf_op jit(solution)/shard_map/ppermute | solution.py:67
  36.8 23.9 %collective-permute-start.4 = (bf16[2,128,1536]{2,1,0:T(8,128)(2,1)}, bf16[2,128,1536]{2,1,0:T(8,128)(2,1)}, u32[]{:S(2)}, u32[]{:S(2)}) collective-permute-start(bf16[2,128,1536]{2,1,0:T(8,128)(2,1)} %pad_maximum_fusion.5), channel_id=1, source_target_pairs={{0,4},{1,5},{2,6},{3,7},{4,0},{5,1},{6,2},{7,3},{8,12},{9,13},{10,... | collective-permute-start | bytes 2359304 | tf_op jit(solution)/shard_map/ppermute | solution.py:67
  39.7 12.0 %collective-permute-start.10 = (bf16[530,384]{1,0:T(8,128)(2,1)}, bf16[530,384]{1,0:T(8,128)(2,1)}, u32[]{:S(2)}, u32[]{:S(2)}) collective-permute-start(bf16[530,384]{1,0:T(8,128)(2,1)} %collective-permute-done.9.refs_4_), channel_id=1, source_target_pairs={{8,0},{16,8},{24,16},{9,1},{17,9},{25,17},{10,2},{18,10},{26,18},{... | collective-permute-start | bytes 1221128 | tf_op jit(solution)/shard_map/ppermute | solution.py:789
  41.0 11.9 %collective-permute-start.7 = (bf16[530,384]{1,0:T(8,128)(2,1)}, bf16[530,384]{1,0:T(8,128)(2,1)}, u32[]{:S(2)}, u32[]{:S(2)}) collective-permute-start(bf16[530,384]{1,0:T(8,128)(2,1)} %collective-permute-done.6.refs_2_), channel_id=1, source_target_pairs={{0,8},{8,16},{16,24},{1,9},{9,17},{17,25},{2,10},{10,18},{18,26},{... | collective-permute-start | bytes 1221128 | tf_op jit(solution)/shard_map/ppermute | solution.py:789
  52.9 182.2 %all-gather.7.cloned.1.call-start = ((), (), s32[]{:S(2)}) async-start(), calls=%async_computation.11 | async-start | bytes 5898240 | tf_op jit(solution)/shard_map/all_gather | solution.py:821
  52.9 11.4 %collective-permute-start.11 = (bf16[530,384]{1,0:T(8,128)(2,1)}, bf16[530,384]{1,0:T(8,128)(2,1)S(1)}, u32[]{:S(2)}, u32[]{:S(2)}) collective-permute-start(bf16[530,384]{1,0:T(8,128)(2,1)} %collective-permute-done.10.refs_5_), channel_id=1, source_target_pairs={{8,0},{16,8},{24,16},{9,1},{17,9},{25,17},{10,2},{18,10},{26,18},{... | collective-permute-start | bytes 1221128 | tf_op jit(solution)/shard_map/ppermute | solution.py:789
  54.2 13.7 %collective-permute-start.8 = (bf16[530,384]{1,0:T(8,128)(2,1)}, bf16[530,384]{1,0:T(8,128)(2,1)S(1)}, u32[]{:S(2)}, u32[]{:S(2)}) collective-permute-start(bf16[530,384]{1,0:T(8,128)(2,1)} %collective-permute-done.7.refs_1_), channel_id=1, source_target_pairs={{0,8},{8,16},{16,24},{1,9},{9,17},{17,25},{2,10},{10,18},{18,26},{... | collective-permute-start | bytes 1221128 | tf_op jit(solution)/shard_map/ppermute | solution.py:789
  60.6 16.6 %collective-permute-start.2 = (bf16[4,128,1536]{2,1,0:T(8,128)(2,1)S(1)}, bf16[4,128,1536]{2,1,0:T(8,128)(2,1)}, u32[]{:S(2)}, u32[]{:S(2)}) collective-permute-start(bf16[4,128,1536]{2,1,0:T(8,128)(2,1)S(1)} %pad_maximum_fusion.xa), channel_id=1, source_target_pairs={{0,1},{1,0},{2,3},{3,2},{4,5},{5,4},{6,7},{7,6},{8,9},{9,8},{10,11... | collective-permute-start | bytes 4718600 | tf_op jit(solution)/shard_map/ppermute | solution.py:67
  62.7 14.5 %collective-permute-start.5 = (bf16[4,128,1536]{2,1,0:T(8,128)(2,1)S(1)}, bf16[4,128,1536]{2,1,0:T(8,128)(2,1)}, u32[]{:S(2)}, u32[]{:S(2)}) collective-permute-start(bf16[4,128,1536]{2,1,0:T(8,128)(2,1)S(1)} %pad_maximum_fusion.1.xb), channel_id=1, source_target_pairs={{0,1},{1,0},{2,3},{3,2},{4,5},{5,4},{6,7},{7,6},{8,9},{9,8},{10,11... | collective-permute-start | bytes 4718600 | tf_op jit(solution)/shard_map/ppermute | solution.py:67
  62.8 12.0 %collective-permute-start.13 = (bf16[1,128,1536]{2,1,0:T(8,128)(2,1)S(1)}, bf16[1,128,1536]{2,1,0:T(8,128)(2,1)S(1)}, u32[]{:S(2)}, u32[]{:S(2)}) collective-permute-start(bf16[1,128,1536]{2,1,0:T(8,128)(2,1)S(1)} %get-tuple-element.188), channel_id=1, source_target_pairs={{0,2},{1,3},{2,0},{3,1},{4,6},{5,7},{6,4},{7,5},{8,10},{9,11},{10,... | collective-permute-start | bytes 1179656 | tf_op jit(solution)/shard_map/ppermute | solution.py:67
  64.4 12.8 %collective-permute-start.12 = (bf16[1,128,1536]{2,1,0:T(8,128)(2,1)S(1)}, bf16[1,128,1536]{2,1,0:T(8,128)(2,1)S(1)}, u32[]{:S(2)}, u32[]{:S(2)}) collective-permute-start(bf16[1,128,1536]{2,1,0:T(8,128)(2,1)S(1)} %get-tuple-element.186), channel_id=1, source_target_pairs={{0,4},{1,5},{2,6},{3,7},{4,0},{5,1},{6,2},{7,3},{8,12},{9,13},{10,... | collective-permute-start | bytes 1179656 | tf_op jit(solution)/shard_map/ppermute | solution.py:67
  72.8 16.6 %collective-permute-start.15 = (bf16[1,2,48,1536]{3,2,1,0:T(8,128)(2,1)S(1)}, bf16[1,2,48,1536]{3,2,1,0:T(8,128)(2,1)S(1)}, u32[]{:S(2)}, u32[]{:S(2)}) collective-permute-start(bf16[1,2,48,1536]{3,2,1,0:T(8,128)(2,1)S(1)} %get-tuple-element.192), channel_id=1, source_target_pairs={{0,2},{1,3},{2,0},{3,1},{4,6},{5,7},{6,4},{7,5},{8,10},{9,11},{10,... | collective-permute-start | bytes 884744 | tf_op jit(solution)/shard_map/ppermute | solution.py:67
  74.8 14.6 %collective-permute-start.14 = (bf16[1,2,48,1536]{3,2,1,0:T(8,128)(2,1)S(1)}, bf16[1,2,48,1536]{3,2,1,0:T(8,128)(2,1)S(1)}, u32[]{:S(2)}, u32[]{:S(2)}) collective-permute-start(bf16[1,2,48,1536]{3,2,1,0:T(8,128)(2,1)S(1)} %get-tuple-element.190), channel_id=1, source_target_pairs={{0,4},{1,5},{2,6},{3,7},{4,0},{5,1},{6,2},{7,3},{8,12},{9,13},{10,... | collective-permute-start | bytes 884744 | tf_op jit(solution)/shard_map/ppermute | solution.py:67
  91.0 28.4 %collective-permute-start.18 = (bf16[2,2,48,1536]{3,2,1,0:T(8,128)(2,1)}, bf16[2,2,48,1536]{3,2,1,0:T(8,128)(2,1)S(1)}, u32[]{:S(2)}, u32[]{:S(2)}) collective-permute-start(bf16[2,2,48,1536]{3,2,1,0:T(8,128)(2,1)} %get-tuple-element.368), channel_id=1, source_target_pairs={{0,2},{1,3},{2,0},{3,1},{4,6},{5,7},{6,4},{7,5},{8,10},{9,11},{10,... | collective-permute-start | bytes 1769480 | tf_op jit(solution)/shard_map/ppermute | solution.py:67
  94.2 25.2 %collective-permute-start.19 = (bf16[2,2,48,1536]{3,2,1,0:T(8,128)(2,1)S(1)}, bf16[2,2,48,1536]{3,2,1,0:T(8,128)(2,1)S(1)}, u32[]{:S(2)}, u32[]{:S(2)}) collective-permute-start(bf16[2,2,48,1536]{3,2,1,0:T(8,128)(2,1)S(1)} %get-tuple-element.364), channel_id=1, source_target_pairs={{0,4},{1,5},{2,6},{3,7},{4,0},{5,1},{6,2},{7,3},{8,12},{9,13},{10,... | collective-permute-start | bytes 1769480 | tf_op jit(solution)/shard_map/ppermute | solution.py:67
  94.6 27.5 %collective-permute-start.16 = (bf16[2,128,1536]{2,1,0:T(8,128)(2,1)S(1)}, bf16[2,128,1536]{2,1,0:T(8,128)(2,1)S(1)}, u32[]{:S(2)}, u32[]{:S(2)}) collective-permute-start(bf16[2,128,1536]{2,1,0:T(8,128)(2,1)S(1)} %get-tuple-element.360), channel_id=1, source_target_pairs={{0,2},{1,3},{2,0},{3,1},{4,6},{5,7},{6,4},{7,5},{8,10},{9,11},{10,... | collective-permute-start | bytes 2359304 | tf_op jit(solution)/shard_map/ppermute | solution.py:67
  96.7 26.5 %collective-permute-start.17 = (bf16[2,128,1536]{2,1,0:T(8,128)(2,1)S(1)}, bf16[2,128,1536]{2,1,0:T(8,128)(2,1)S(1)}, u32[]{:S(2)}, u32[]{:S(2)}) collective-permute-start(bf16[2,128,1536]{2,1,0:T(8,128)(2,1)S(1)} %get-tuple-element.356), channel_id=1, source_target_pairs={{0,4},{1,5},{2,6},{3,7},{4,0},{5,1},{6,2},{7,3},{8,12},{9,13},{10,... | collective-permute-start | bytes 2359304 | tf_op jit(solution)/shard_map/ppermute | solution.py:67
  125.5 16.1 %all-to-all-start.1 = ((bf16[8,192,256]{2,1,0:T(8,128)(2,1)}), bf16[8,192,256]{2,1,0:T(8,128)(2,1)S(1)}, u32[]{:S(2)}, u32[]{:S(2)}) async-start(bf16[8,192,256]{2,1,0:T(8,128)(2,1)} %get-tuple-element.198), calls=%async_computation.1 | async-start | bytes 1572864 | tf_op jit(solution)/shard_map/all_to_all | solution.py:892
  129.1 214.9 %reduce-scatter.4.cloned.1.call-start = ((), (), s32[]{:S(2)}) async-start(), calls=%async_computation.7 | async-start | bytes 5898240 | tf_op jit(solution)/shard_map/reduce_scatter | solution.py:991
  130.3 50.2 %collective-permute-start.28 = (bf16[4,128,1536]{2,1,0:T(8,128)(2,1)}, bf16[4,128,1536]{2,1,0:T(8,128)(2,1)}, u32[]{:S(2)}, u32[]{:S(2)}) collective-permute-start(bf16[4,128,1536]{2,1,0:T(8,128)(2,1)} %constant_dynamic-update-slice_fusion.20.refs_4_), channel_id=1, source_target_pairs={{0,1},{1,0},{2,3},{3,2},{4,5},{5,4},{6,7},{7,6},{8,9},{9,8},{10,11... | collective-permute-start | bytes 4718600 | tf_op jit(solution)/shard_map/ppermute | solution.py:67
  131.6 48.9 %collective-permute-start.29 = (bf16[4,128,1536]{2,1,0:T(8,128)(2,1)}, bf16[4,128,1536]{2,1,0:T(8,128)(2,1)}, u32[]{:S(2)}, u32[]{:S(2)}) collective-permute-start(bf16[4,128,1536]{2,1,0:T(8,128)(2,1)} %constant_dynamic-update-slice_fusion.23.refs_6_), channel_id=1, source_target_pairs={{0,1},{1,0},{2,3},{3,2},{4,5},{5,4},{6,7},{7,6},{8,9},{9,8},{10,11... | collective-permute-start | bytes 4718600 | tf_op jit(solution)/shard_map/ppermute | solution.py:67
  148.3 11.7 %collective-permute-start.22 = (bf16[1,128,1536]{2,1,0:T(8,128)(2,1)}, bf16[1,128,1536]{2,1,0:T(8,128)(2,1)S(1)}, u32[]{:S(2)}, u32[]{:S(2)}) collective-permute-start(bf16[1,128,1536]{2,1,0:T(8,128)(2,1)} %get-tuple-element.202.ma), channel_id=1, source_target_pairs={{0,4},{1,5},{2,6},{3,7},{4,0},{5,1},{6,2},{7,3},{8,12},{9,13},{10,... | collective-permute-start | bytes 1179656 | tf_op jit(solution)/shard_map/ppermute | solution.py:67
  160.1 18.7 %collective-permute-start.26 = (bf16[2,128,1536]{2,1,0:T(8,128)(2,1)S(1)}, bf16[2,128,1536]{2,1,0:T(8,128)(2,1)S(1)}, u32[]{:S(2)}, u32[]{:S(2)}) collective-permute-start(bf16[2,128,1536]{2,1,0:T(8,128)(2,1)S(1)} %pad_maximum_fusion.7), channel_id=1, source_target_pairs={{0,4},{1,5},{2,6},{3,7},{4,0},{5,1},{6,2},{7,3},{8,12},{9,13},{10,... | collective-permute-start | bytes 2359304 | tf_op jit(solution)/shard_map/ppermute | solution.py:67
  160.6 18.7 %collective-permute-start.24 = (bf16[2,128,1536]{2,1,0:T(8,128)(2,1)S(1)}, bf16[2,128,1536]{2,1,0:T(8,128)(2,1)S(1)}, u32[]{:S(2)}, u32[]{:S(2)}) collective-permute-start(bf16[2,128,1536]{2,1,0:T(8,128)(2,1)S(1)} %pad_maximum_fusion.6), channel_id=1, source_target_pairs={{0,2},{1,3},{2,0},{3,1},{4,6},{5,7},{6,4},{7,5},{8,10},{9,11},{10,... | collective-permute-start | bytes 2359304 | tf_op jit(solution)/shard_map/ppermute | solution.py:67
  230.4 192.9 %reduce-scatter.6.cloned.1.call-start = ((), (), s32[]{:S(2)}) async-start(), calls=%async_computation.8 | async-start | bytes 5898240 | tf_op jit(solution)/shard_map/reduce_scatter | solution.py:991
  278.3 21.4 %collective-permute-start.32 = (bf16[2,128,1664]{2,1,0:T(8,128)(2,1)}, bf16[2,128,1664]{2,1,0:T(8,128)(2,1)S(1)}, u32[]{:S(2)}, u32[]{:S(2)}) collective-permute-start(bf16[2,128,1664]{2,1,0:T(8,128)(2,1)} %get-tuple-element.226), channel_id=1, source_target_pairs={{0,2},{1,3},{2,0},{3,1},{4,6},{5,7},{6,4},{7,5},{8,10},{9,11},{10,... | collective-permute-start | bytes 2555912 | tf_op jit(solution)/shard_map/ppermute | solution.py:67
  279.7 20.8 %collective-permute-start.33 = (bf16[2,128,1664]{2,1,0:T(8,128)(2,1)S(1)}, bf16[2,128,1664]{2,1,0:T(8,128)(2,1)}, u32[]{:S(2)}, u32[]{:S(2)}) collective-permute-start(bf16[2,128,1664]{2,1,0:T(8,128)(2,1)S(1)} %get-tuple-element.227), channel_id=1, source_target_pairs={{0,4},{1,5},{2,6},{3,7},{4,0},{5,1},{6,2},{7,3},{8,12},{9,13},{10,... | collective-permute-start | bytes 2555912 | tf_op jit(solution)/shard_map/ppermute | solution.py:67
  303.9 14.0 %collective-permute-start.36 = (bf16[1,128,1664]{2,1,0:T(8,128)(2,1)S(1)}, bf16[1,128,1664]{2,1,0:T(8,128)(2,1)S(1)}, u32[]{:S(2)}, u32[]{:S(2)}) collective-permute-start(bf16[1,128,1664]{2,1,0:T(8,128)(2,1)S(1)} %get-tuple-element.243), channel_id=1, source_target_pairs={{0,4},{1,5},{2,6},{3,7},{4,0},{5,1},{6,2},{7,3},{8,12},{9,13},{10,... | collective-permute-start | bytes 1277960 | tf_op jit(solution)/shard_map/ppermute | solution.py:67
  305.1 12.8 %collective-permute-start.37 = (bf16[1,128,1664]{2,1,0:T(8,128)(2,1)S(1)}, bf16[1,128,1664]{2,1,0:T(8,128)(2,1)S(1)}, u32[]{:S(2)}, u32[]{:S(2)}) collective-permute-start(bf16[1,128,1664]{2,1,0:T(8,128)(2,1)S(1)} %get-tuple-element.244), channel_id=1, source_target_pairs={{0,2},{1,3},{2,0},{3,1},{4,6},{5,7},{6,4},{7,5},{8,10},{9,11},{10,... | collective-permute-start | bytes 1277960 | tf_op jit(solution)/shard_map/ppermute | solution.py:67
  317.4 20.8 %collective-permute-start.34 = (bf16[4,128,1536]{2,1,0:T(8,128)(2,1)}, bf16[4,128,1536]{2,1,0:T(8,128)(2,1)}, u32[]{:S(2)}, u32[]{:S(2)}) collective-permute-start(bf16[4,128,1536]{2,1,0:T(8,128)(2,1)} %get-tuple-element.236), channel_id=1, source_target_pairs={{0,1},{1,0},{2,3},{3,2},{4,5},{5,4},{6,7},{7,6},{8,9},{9,8},{10,11... | collective-permute-start | bytes 4718600 | tf_op jit(solution)/shard_map/ppermute | solution.py:67
  317.4 20.8 %collective-permute-start.35 = (bf16[4,128,1536]{2,1,0:T(8,128)(2,1)}, bf16[4,128,1536]{2,1,0:T(8,128)(2,1)}, u32[]{:S(2)}, u32[]{:S(2)}) collective-permute-start(bf16[4,128,1536]{2,1,0:T(8,128)(2,1)} %get-tuple-element.238), channel_id=1, source_target_pairs={{0,1},{1,0},{2,3},{3,2},{4,5},{5,4},{6,7},{7,6},{8,9},{9,8},{10,11... | collective-permute-start | bytes 4718600 | tf_op jit(solution)/shard_map/ppermute | solution.py:67
  326.8 17.3 %all-to-all-start.2 = ((bf16[8,192,256]{2,1,0:T(8,128)(2,1)}), bf16[8,192,256]{2,1,0:T(8,128)(2,1)}, u32[]{:S(2)}, u32[]{:S(2)}) async-start(bf16[8,192,256]{2,1,0:T(8,128)(2,1)} %bitcast.71), calls=%async_computation.2 | async-start | bytes 1572864 | tf_op jit(solution)/shard_map/all_to_all | solution.py:1026
  331.0 120.5 %reduce-scatter.8.cloned.1.call-start = ((), (), s32[]{:S(2)}) async-start(), calls=%async_computation.9 | async-start | bytes 2088960 | tf_op jit(solution)/shard_map/reduce_scatter | solution.py:1131
  344.0 43.5 %collective-permute-start.42 = (bf16[2,128,1536]{2,1,0:T(8,128)(2,1)}, bf16[2,128,1536]{2,1,0:T(8,128)(2,1)S(1)}, u32[]{:S(2)}, u32[]{:S(2)}) collective-permute-start(bf16[2,128,1536]{2,1,0:T(8,128)(2,1)} %copy-done.21), channel_id=1, source_target_pairs={{0,2},{1,3},{2,0},{3,1},{4,6},{5,7},{6,4},{7,5},{8,10},{9,11},{10,... | collective-permute-start | bytes 2359304 | tf_op jit(solution)/shard_map/ppermute | solution.py:67
  345.9 41.6 %collective-permute-start.43 = (bf16[2,128,1536]{2,1,0:T(8,128)(2,1)}, bf16[2,128,1536]{2,1,0:T(8,128)(2,1)S(1)}, u32[]{:S(2)}, u32[]{:S(2)}) collective-permute-start(bf16[2,128,1536]{2,1,0:T(8,128)(2,1)} %copy-done.20), channel_id=1, source_target_pairs={{0,4},{1,5},{2,6},{3,7},{4,0},{5,1},{6,2},{7,3},{8,12},{9,13},{10,... | collective-permute-start | bytes 2359304 | tf_op jit(solution)/shard_map/ppermute | solution.py:67
  347.4 31.8 %collective-permute-start.38 = (bf16[4,2,48,1536]{3,2,1,0:T(8,128)(2,1)}, bf16[4,2,48,1536]{3,2,1,0:T(8,128)(2,1)S(1)}, u32[]{:S(2)}, u32[]{:S(2)}) collective-permute-start(bf16[4,2,48,1536]{3,2,1,0:T(8,128)(2,1)} %get-tuple-element.262), channel_id=1, source_target_pairs={{0,1},{1,0},{2,3},{3,2},{4,5},{5,4},{6,7},{7,6},{8,9},{9,8},{10,11... | collective-permute-start | bytes 3538952 | tf_op jit(solution)/shard_map/ppermute | solution.py:67
  347.4 31.8 %collective-permute-start.39 = (bf16[4,2,48,1536]{3,2,1,0:T(8,128)(2,1)}, bf16[4,2,48,1536]{3,2,1,0:T(8,128)(2,1)S(1)}, u32[]{:S(2)}, u32[]{:S(2)}) collective-permute-start(bf16[4,2,48,1536]{3,2,1,0:T(8,128)(2,1)} %get-tuple-element.263), channel_id=1, source_target_pairs={{0,1},{1,0},{2,3},{3,2},{4,5},{5,4},{6,7},{7,6},{8,9},{9,8},{10,11... | collective-permute-start | bytes 3538952 | tf_op jit(solution)/shard_map/ppermute | solution.py:67
  379.8 15.3 %collective-permute-start.40 = (bf16[2,2,48,1536]{3,2,1,0:T(8,128)(2,1)S(1)}, bf16[2,2,48,1536]{3,2,1,0:T(8,128)(2,1)S(1)}, u32[]{:S(2)}, u32[]{:S(2)}) collective-permute-start(bf16[2,2,48,1536]{3,2,1,0:T(8,128)(2,1)S(1)} %get-tuple-element.272), channel_id=1, source_target_pairs={{0,2},{1,3},{2,0},{3,1},{4,6},{5,7},{6,4},{7,5},{8,10},{9,11},{10,... | collective-permute-start | bytes 1769480 | tf_op jit(solution)/shard_map/ppermute | solution.py:67
  380.5 14.9 %collective-permute-start.41 = (bf16[2,2,48,1536]{3,2,1,0:T(8,128)(2,1)S(1)}, bf16[2,2,48,1536]{3,2,1,0:T(8,128)(2,1)S(1)}, u32[]{:S(2)}, u32[]{:S(2)}) collective-permute-start(bf16[2,2,48,1536]{3,2,1,0:T(8,128)(2,1)S(1)} %get-tuple-element.273), channel_id=1, source_target_pairs={{0,4},{1,5},{2,6},{3,7},{4,0},{5,1},{6,2},{7,3},{8,12},{9,13},{10,... | collective-permute-start | bytes 1769480 | tf_op jit(solution)/shard_map/ppermute | solution.py:67
  395.7 11.2 %collective-permute-start.44 = (bf16[1,2,48,1536]{3,2,1,0:T(8,128)(2,1)S(1)}, bf16[1,2,48,1536]{3,2,1,0:T(8,128)(2,1)S(1)}, u32[]{:S(2)}, u32[]{:S(2)}) collective-permute-start(bf16[1,2,48,1536]{3,2,1,0:T(8,128)(2,1)S(1)} %get-tuple-element.294), channel_id=1, source_target_pairs={{0,4},{1,5},{2,6},{3,7},{4,0},{5,1},{6,2},{7,3},{8,12},{9,13},{10,... | collective-permute-start | bytes 884744 | tf_op jit(solution)/shard_map/ppermute | solution.py:67
  415.4 11.3 %collective-permute-start.46 = (bf16[1,128,1536]{2,1,0:T(8,128)(2,1)}, bf16[1,128,1536]{2,1,0:T(8,128)(2,1)}, u32[]{:S(2)}, u32[]{:S(2)}) collective-permute-start(bf16[1,128,1536]{2,1,0:T(8,128)(2,1)} %get-tuple-element.311), channel_id=1, source_target_pairs={{0,4},{1,5},{2,6},{3,7},{4,0},{5,1},{6,2},{7,3},{8,12},{9,13},{10,... | collective-permute-start | bytes 1179656 | tf_op jit(solution)/shard_map/ppermute | solution.py:67
  427.9 18.5 %collective-permute-start.50 = (bf16[2,128,1536]{2,1,0:T(8,128)(2,1)}, bf16[2,128,1536]{2,1,0:T(8,128)(2,1)S(1)}, u32[]{:S(2)}, u32[]{:S(2)}) collective-permute-start(bf16[2,128,1536]{2,1,0:T(8,128)(2,1)} %copy-done.27), channel_id=1, source_target_pairs={{0,2},{1,3},{2,0},{3,1},{4,6},{5,7},{6,4},{7,5},{8,10},{9,11},{10,... | collective-permute-start | bytes 2359304 | tf_op jit(solution)/shard_map/ppermute | solution.py:67
  428.5 18.2 %collective-permute-start.51 = (bf16[2,128,1536]{2,1,0:T(8,128)(2,1)}, bf16[2,128,1536]{2,1,0:T(8,128)(2,1)S(1)}, u32[]{:S(2)}, u32[]{:S(2)}) collective-permute-start(bf16[2,128,1536]{2,1,0:T(8,128)(2,1)} %copy-done.26), channel_id=1, source_target_pairs={{0,4},{1,5},{2,6},{3,7},{4,0},{5,1},{6,2},{7,3},{8,12},{9,13},{10,... | collective-permute-start | bytes 2359304 | tf_op jit(solution)/shard_map/ppermute | solution.py:67
  (87 other events, 454.3 us)
Sparse Core Ops, SparseCore 0:
  53.0 91.8 all-gather.4
  146.4 88.5 all-gather.6
  237.4 83.7 reduce-scatter.3
  323.3 85.7 reduce-scatter.5
  411.3 37.3 reduce-scatter.7
